TPU v7x, 32 devices: a whole 2x2x4 slice. The times are simulated.
32 devices in a mesh: parts: 2 (over y), replica: 4 (over x, core), tensor: 4 (over z).
Axes of the slice: x: 2, y: 2, z: 4, core: 2. Of those that a mesh axis runs over, the one named last changes fastest.
Arguments:
- hidden: bfloat16 [112, 2, 8192], P(('parts', 'replica'), None, 'tensor'), parts along dimension 0, may hold values from -6 to 6
- queries: bfloat16 [112, 2, 64, 128], P(('parts', 'replica'), None, 'tensor'), parts along dimension 0, may hold values from -220 to 220
- kv_cache: bfloat16 [96, 128, 8, 256], P(('parts', 'replica'), None, 'tensor'), parts along dimension 0, may hold values from -6.5 to 6.5
- w_kv: bfloat16 [8192, 8, 256], P(None, 'tensor'), may hold values from -0.0625 to 0.0625
- store_a: bfloat16 [64, 2, 64, 8192], P(('parts', 'replica'), None, None, 'tensor'), parts along dimension 0, may hold values from -0.0625 to 0.0625
- store_b: bfloat16 [64, 2, 64, 1024], P(('parts', 'replica'), None, None, 'tensor'), parts along dimension 0, may hold values from -0.75 to 0.75
- lengths: int32 [96], P('parts'), parts along dimension 0, may hold values from 2 to 128, as said below
- arrival_from: int32 [8, 2], P('parts'), parts along dimension 0, may hold values from 0 to 3, as said below
- arrival_slot: int32 [8, 2], P('parts'), parts along dimension 0, may hold values from 0 to 11, as said below
- resident_adapter: int32 [96], P('parts'), parts along dimension 0, may hold values from 0 to 7
- arrival_adapter: int32 [8, 2], P('parts'), parts along dimension 0, may hold values from 0 to 3
- hot_holder: int32 [32], P('parts'), parts along dimension 0, may hold values from 0 to 31, as said below
- hot_dest: int32 [32, 1], P('parts'), parts along dimension 0, may hold values from 0 to 3, as said below
Outputs:
- attn_out: bfloat16 [112, 2, 8192], P(('parts', 'replica'), None, 'tensor'), parts along dimension 0
- new_kv: bfloat16 [112, 2, 8, 256], P(('parts', 'replica'), None, 'tensor'), parts along dimension 0
- arrival_cache: bfloat16 [16, 128, 8, 256], P(('parts', 'replica'), None, 'tensor'), parts along dimension 0
- installed_a: bfloat16 [32, 2, 64, 8192], P(('parts', 'replica'), None, None, 'tensor'), parts along dimension 0
- installed_b: bfloat16 [32, 2, 64, 1024], P(('parts', 'replica'), None, None, 'tensor'), parts along dimension 0
There are 2 independent parts, one for each index of `parts`. A program takes and returns all parts, laid end to end along the dimension named above; an argument that names none is the same for every part. Nothing has to cross between parts.
Inputs may be any that keep to these rules, and one draw needn't show every extreme that they name: `lengths`: every request listed by arrival_from and arrival_slot holds more than 96 rows; some request holds exactly 128. `arrival_from`: row r lists 2 distinct replicas, none equal to r; each replica appears exactly 2 times in the whole array. `arrival_slot`: no request (replica and slot) is listed twice. `hot_holder`: entry h is the holder's replica times 8 plus its slot; the holder's replica is not in row h of hot_dest; the holders of rows c * 4 to c * 4 + 3 lie on distinct replicas. `hot_dest`: for each c below 4, rows c * 4 to c * 4 + 3 together list every replica exactly once.
All inputs are finite; a program needn't handle non-finite values.
Results may differ from a plain program's by a relative error of at most 0.0071.
Values may be sent and summed in bfloat16 or wider, within the bound.
No kernel may reach another device: no remote copies, remote signals or barrier semaphores. Data moves between devices by JAX's collectives and lax.ppermute only.
A program may use at most 64 MiB of HBM per device.

v0:
```python
import functools
import math

import jax
import jax.numpy as jnp
from jax import lax
from jax.experimental import pallas as pl
from jax.experimental.pallas import tpu as pltpu
from jax.sharding import PartitionSpec as P


COPIES = 4


ADAPTER_SCALE = 2.0
ROPE_BASE = 500000.0


def rotate_keys(key_rows, positions):
    head_length = key_rows.shape[-1]
    half_size = head_length // 2
    frequency = ROPE_BASE ** (-(jnp.arange(half_size, dtype=jnp.float32) * 2.0 / head_length))
    angles = positions.astype(jnp.float32)[:, :, None, None] * frequency
    cosine = jnp.cos(angles)
    sine_val = jnp.sin(angles)
    first_half = key_rows[..., :half_size]
    second_half = key_rows[..., half_size:]
    return jnp.concatenate(
        [
            first_half * cosine - second_half * sine_val,
            second_half * cosine + first_half * sine_val,
        ],
        axis=-1,
    )


def attend(queries, stored, lengths_now, fresh_kv):
    request_slot_count, decode_step_count, heads_local, head_length = queries.shape
    local_key_value = stored.shape[2]
    group_size = heads_local // local_key_value
    grouped = queries.reshape(
        request_slot_count, decode_step_count, local_key_value, group_size, head_length
    )
    score_scale = 1.0 / math.sqrt(head_length)
    past_scores = (
        jnp.einsum(
            "msgjd,mcgd->msgjc",
            grouped,
            stored[..., :head_length],
            preferred_element_type=jnp.float32,
        )
        * score_scale
    )
    recent_scores = (
        jnp.einsum(
            "msgjd,mtgd->msgjt",
            grouped,
            fresh_kv[..., :head_length],
            preferred_element_type=jnp.float32,
        )
        * score_scale
    )
    row_ids = jnp.arange(stored.shape[1], dtype=jnp.int32)
    past_ok = (row_ids[None, :] < lengths_now[:, None])[:, None, None, None, :]
    step_ids = jnp.arange(decode_step_count, dtype=jnp.int32)
    recent_ok = (step_ids[None, :] <= step_ids[:, None])[None, :, None, None, :]
    past_scores = jnp.where(past_ok, past_scores, -jnp.inf)
    recent_scores = jnp.where(recent_ok, recent_scores, -jnp.inf)
    peak_score = jnp.maximum(jnp.max(past_scores, -1), jnp.max(recent_scores, -1))[..., None]
    past_exp = jnp.exp(past_scores - peak_score)
    recent_exp = jnp.exp(recent_scores - peak_score)
    denom_sum = jnp.sum(past_exp, -1, keepdims=True) + jnp.sum(recent_exp, -1, keepdims=True)
    past_w = (past_exp / denom_sum).astype(jnp.bfloat16)
    recent_w = (recent_exp / denom_sum).astype(jnp.bfloat16)
    mixed_out = jnp.einsum(
        "msgjc,mcgd->msgjd", past_w, stored[..., head_length:], preferred_element_type=jnp.float32
    )
    mixed_out = mixed_out + jnp.einsum(
        "msgjt,mtgd->msgjd",
        recent_w,
        fresh_kv[..., head_length:],
        preferred_element_type=jnp.float32,
    )
    return mixed_out.reshape(request_slot_count, decode_step_count, heads_local * head_length)


def local_general(
    hidden,
    queries,
    kv_cache,
    w_kv,
    store_a,
    store_b,
    lengths,
    arrival_from,
    arrival_slot,
    resident_adapter,
    arrival_adapter,
    hot_holder,
    hot_dest,
):
    my_index = lax.axis_index("replica")
    replicas = lax.axis_size("replica")
    resident = kv_cache.shape[0]
    arrive = arrival_from.shape[1]
    request_slot_count = resident + arrive
    decode_step_count = hidden.shape[1]
    head_length = queries.shape[3]
    local_key_value = kv_cache.shape[2]
    slot_total = store_a.shape[0]
    hot_total = hot_holder.shape[0]
    spans = hot_total // COPIES
    my_from = lax.dynamic_index_in_dim(arrival_from, my_index, 0, keepdims=False)
    my_slot = lax.dynamic_index_in_dim(arrival_slot, my_index, 0, keepdims=False)
    own_ids = my_index * resident + jnp.arange(resident, dtype=jnp.int32)
    leaving_ids = (arrival_from * resident + arrival_slot).reshape(-1)
    staying = jnp.logical_not(jnp.any(own_ids[:, None] == leaving_ids[None, :], axis=1))
    live_mask = jnp.concatenate([staying, jnp.ones((arrive,), bool)])
    own_len = lax.dynamic_slice_in_dim(lengths, my_index * resident, resident)
    arrival_len = jnp.take(lengths, my_from * resident + my_slot)
    seen_len = jnp.concatenate([own_len, arrival_len])
    takes_mine = arrival_from == my_index
    sends_any = jnp.any(takes_mine, axis=1)
    send_slot = jnp.sum(jnp.where(takes_mine, arrival_slot, 0), axis=1)
    outgoing = jnp.take(kv_cache, send_slot, axis=0)
    outgoing = jnp.where(sends_any[:, None, None, None], outgoing, jnp.zeros((), jnp.bfloat16))
    incoming = lax.all_to_all(outgoing, "replica", split_axis=0, concat_axis=0, tiled=True)
    blocks = hot_dest.reshape(COPIES, spans, hot_dest.shape[1])
    holder_grid = hot_holder.reshape(COPIES, spans)
    holder_rep = holder_grid // slot_total
    mine = holder_rep == my_index
    has_one = jnp.any(mine, axis=1)
    local_pick = jnp.sum(jnp.where(mine, holder_grid % slot_total, 0), axis=1)

    def spread_rows(store):
        rows = jnp.take(store, local_pick, axis=0)
        rows = jnp.where(has_one[:, None, None, None], rows, jnp.zeros((), jnp.bfloat16))
        return rows.reshape(COPIES, replicas, -1).transpose(1, 0, 2)

    got_a, got_b = (
        lax.all_to_all(spread_rows(store_a), "replica", split_axis=0, concat_axis=0, tiled=True),
        lax.all_to_all(spread_rows(store_b), "replica", split_axis=0, concat_axis=0, tiled=True),
    )
    replica_ids = jnp.arange(replicas, dtype=jnp.int32)
    member = jnp.any(blocks[:, :, :, None] == replica_ids[None, None, None, :], axis=2).astype(
        jnp.int32
    )
    source_rep = jnp.sum(member * holder_rep[:, :, None], axis=1)
    copy_ids = jnp.arange(COPIES, dtype=jnp.int32)
    route_a = got_a[source_rep.T, copy_ids[None, :]]
    route_b = got_b[source_rep.T, copy_ids[None, :]]
    recv_a, recv_b = (
        lax.all_to_all(route_a, "replica", split_axis=0, concat_axis=0, tiled=True),
        lax.all_to_all(route_b, "replica", split_axis=0, concat_axis=0, tiled=True),
    )
    installed_a = recv_a.transpose(1, 0, 2).reshape((COPIES,) + store_a.shape[1:])
    installed_b = recv_b.transpose(1, 0, 2).reshape((COPIES,) + store_b.shape[1:])
    own_adapter = lax.dynamic_slice_in_dim(resident_adapter, my_index * resident, resident)
    my_choice = lax.dynamic_index_in_dim(arrival_adapter, my_index, 0, keepdims=False)
    adapt_a = jnp.concatenate(
        [jnp.take(store_a, own_adapter, axis=0), jnp.take(installed_a, my_choice, axis=0)]
    )
    adapter_up_weight = jnp.concatenate(
        [jnp.take(store_b, own_adapter, axis=0), jnp.take(installed_b, my_choice, axis=0)]
    )
    partial_value = jnp.einsum(
        "msd,mpkd->mspk", hidden, adapt_a, preferred_element_type=jnp.float32
    )
    base_projection = jnp.einsum(
        "msd,dgc->msgc",
        lax.all_gather(hidden, "tensor", axis=2, tiled=True),
        w_kv,
        preferred_element_type=jnp.float32,
    )
    down_projected = lax.psum(partial_value, "tensor")
    down_projected = down_projected.astype(jnp.bfloat16)
    adapter_update = jnp.einsum(
        "gnot,gote->gnoe", down_projected, adapter_up_weight, preferred_element_type=jnp.float32
    )
    adapter_update = (
        adapter_update.reshape(
            request_slot_count, decode_step_count, 2, local_key_value, head_length
        )
        .transpose(0, 1, 3, 2, 4)
        .reshape(request_slot_count, decode_step_count, local_key_value, 2 * head_length)
    )
    unrotated_key_value = base_projection + ADAPTER_SCALE * adapter_update
    positions = seen_len[:, None] + jnp.arange(decode_step_count, dtype=jnp.int32)[None, :]
    fresh_kv = jnp.concatenate(
        [
            rotate_keys(unrotated_key_value[..., :head_length], positions),
            unrotated_key_value[..., head_length:],
        ],
        axis=-1,
    ).astype(jnp.bfloat16)
    stay_out = attend(queries[:resident], kv_cache, own_len, fresh_kv[:resident])
    arrived = jnp.take(incoming, my_from, axis=0)
    row_ids = jnp.arange(kv_cache.shape[1], dtype=jnp.int32)
    arrived = jnp.where(
        (row_ids[None, :] < arrival_len[:, None])[:, :, None, None],
        arrived,
        jnp.zeros((), jnp.bfloat16),
    )
    move_out = attend(queries[resident:], arrived, arrival_len, fresh_kv[resident:])
    mixed_out = jnp.concatenate([stay_out, move_out], axis=0)
    attn_out = jnp.where(live_mask[:, None, None], mixed_out, 0.0).astype(jnp.bfloat16)
    new_kv = jnp.where(live_mask[:, None, None, None], fresh_kv, jnp.zeros((), jnp.bfloat16))
    return (attn_out, new_kv, arrived, installed_a, installed_b)


def partner(array, mask):
    return lax.ppermute(array, "replica", [(i, i ^ mask) for i in range(lax.axis_size("replica"))])


def shifted(array, step):
    size = lax.axis_size("tensor")
    return lax.ppermute(array, "tensor", [(i, (i + step) % size) for i in range(size)])


HEAD_UNITS = 5
SMEM = pl.BlockSpec(memory_space=pltpu.SMEM)
VMEM = pl.BlockSpec(memory_space=pltpu.VMEM)


def wanted_by(holder, dest, spans, replica, copy_id):
    row = jnp.int32(0)
    for span in range(spans):
        at = copy_id * spans + span
        row += jnp.where(dest[0, at] == replica, holder[at], 0)
    return row


def crossing(holder, dest, spans, slot_total, chip):
    items, count = [], jnp.int32(0)
    for copy_id in range(COPIES):
        for core in range(2):
            row = wanted_by(holder, dest, spans, 2 * chip + core, copy_id)
            crosses = row // (2 * slot_total) != chip
            items.append((copy_id, core, row, crosses, count))
            count = count + crosses.astype(jnp.int32)
    return items


def staged(moves, buffer, sems):
    def when(condition, action):
        if condition is None:
            action()
        else:
            pl.when(condition)(action)

    def begin(at, sources):
        for condition, source in sources:
            when(condition, pltpu.make_async_copy(source, buffer.at[at], sems.at[0, at]).start)

    def forward(at, targets):
        pltpu.make_async_copy(buffer.at[at], buffer.at[at], sems.at[0, at]).wait()
        for condition, target in targets:
            when(condition, pltpu.make_async_copy(buffer.at[at], target, sems.at[1, at]).start)

    def finish(at):
        pltpu.make_async_copy(buffer.at[at], buffer.at[at], sems.at[1, at]).wait()

    for at, (condition, sources, _) in enumerate(moves):
        when(condition, functools.partial(begin, at, sources))
    for at, (condition, _, targets) in enumerate(moves):
        when(condition, functools.partial(forward, at, targets))
    for at, (condition, _, _) in enumerate(moves):
        when(condition, functools.partial(finish, at))


def collect_kernel(spans, slot_total, masks, *refs):
    (me_ref, arrival_from, arrival_slot, holder, kv_cache, store_a, store_b) = refs[:7]
    leaving, (rows_b, rows_a) = refs[7 : 7 + len(masks)], refs[7 + len(masks) : 9 + len(masks)]
    buffers, semaphores = refs[9 + len(masks) : 12 + len(masks)], refs[12 + len(masks) :]
    me = me_ref[0]
    moves = []
    for i, mask in enumerate(masks):
        to = me ^ mask
        slot = jnp.int32(0)
        for a in range(arrival_from.shape[0]):
            slot += jnp.where(arrival_from[a, to] == me, arrival_slot[a, to], 0)
        moves.append((None, [(None, kv_cache.at[slot])], [(None, leaving[i])]))
    groups = [moves]
    held = []
    for copy_id in range(COPIES):
        slot = jnp.int32(0)
        for span in range(spans):
            row = holder[copy_id * spans + span]
            slot += jnp.where(row // slot_total == me, row % slot_total, 0)
        held.append(slot)
    for table, rows in ((store_a, rows_a), (store_b, rows_b)):
        groups.append(
            [
                (None, [(None, table.at[slot])], [(None, rows.at[copy_id])])
                for copy_id, slot in enumerate(held)
            ]
        )
    for moves, buffer, sems in zip(groups, buffers, semaphores):
        for at, (_, ((_, source),), _) in enumerate(moves):
            pltpu.make_async_copy(source, buffer.at[at], sems.at[0, at]).start()
    for moves, buffer, sems in zip(groups, buffers, semaphores):
        for at, (_, _, ((_, target),)) in enumerate(moves):
            pltpu.make_async_copy(buffer.at[at], buffer.at[at], sems.at[0, at]).wait()
            pltpu.make_async_copy(buffer.at[at], target, sems.at[1, at]).start()
    for moves, buffer, sems in zip(groups, buffers, semaphores):
        for at in range(len(moves)):
            pltpu.make_async_copy(buffer.at[at], buffer.at[at], sems.at[1, at]).wait()


def pack_kernel(spans, slot_total, *refs):
    (me_ref, holder, dest, store_a, store_b, sibling_a, sibling_b) = refs[:7]
    across_b, head, *tails = refs[7:-5]
    extra, buffer_b, buffer_a, sems_b, sems_a = refs[-5:]
    me = me_ref[0]
    core = me % 2
    chip = 1 - me // 2
    items = crossing(holder, dest, spans, slot_total, chip)
    moves_b, moves_a = [], []
    for copy_id in range(COPIES):
        row = wanted_by(holder, dest, spans, 2 * chip + core, copy_id)
        own = row // slot_total == me
        sources = [
            (own, store_b.at[row % slot_total]),
            (jnp.logical_not(own), sibling_b.at[copy_id]),
        ]
        moves_b.append((None, sources, [(None, across_b.at[copy_id])]))
    for at, (copy_id, _, row, crosses, unit) in enumerate(items):
        own = row // slot_total == me
        sources = [
            (own, store_a.at[row % slot_total, core]),
            (jnp.logical_not(own), sibling_a.at[copy_id, core]),
        ]
        targets = [(unit < HEAD_UNITS, head.at[jnp.minimum(unit, HEAD_UNITS - 1)])]
        for i, tail in enumerate(tails):
            if at >= HEAD_UNITS + i:
                targets.append((unit == HEAD_UNITS + i, tail))
        moves_a.append((crosses, sources, targets))
    count = items[-1][4] + items[-1][3].astype(jnp.int32)
    extra[0] = jnp.clip(count - HEAD_UNITS, 0, len(tails))
    staged(moves_b, buffer_b, sems_b)
    staged(moves_a, buffer_a, sems_a)


def place_down_kernel(spans, slot_total, tail_units, *refs):
    (me_ref, holder, dest, sibling_a, head, head_other) = refs[:6]
    tails, tails_other = refs[6 : 6 + tail_units], refs[6 + tail_units : 6 + 2 * tail_units]
    out, buffer, sems = refs[-3:]
    me = me_ref[0]
    core = me % 2
    items = crossing(holder, dest, spans, slot_total, me // 2)
    moves = []
    for copy_id in range(COPIES):
        first, second = items[2 * copy_id], items[2 * copy_id + 1]
        crosses = jnp.where(core == 0, first[3].astype(jnp.int32), second[3].astype(jnp.int32))
        unit = jnp.where(core == 0, first[4], second[4])
        near = crosses == 0
        for side, (group, last) in enumerate(((head, tails), (head_other, tails_other))):
            half = core if side == 0 else 1 - core
            early = jnp.logical_and(crosses != 0, unit < HEAD_UNITS)
            sources = [
                (near, sibling_a.at[copy_id, half]),
                (early, group.at[jnp.minimum(unit, HEAD_UNITS - 1)]),
            ]
            for i, tail in enumerate(last):
                sources.append((jnp.logical_and(crosses != 0, unit == HEAD_UNITS + i), tail))
            moves.append((None, sources, [(None, out.at[copy_id, half])]))
    staged(moves, buffer, sems)


def copy_call(kernel, tables, arrays, shapes, scratch, scalars=()):
    hbm = pl.BlockSpec(memory_space=pl.ANY)
    return pl.pallas_call(
        kernel,
        out_shape=[jax.ShapeDtypeStruct(shape, arrays[0].dtype) for shape in shapes]
        + [jax.ShapeDtypeStruct(shape, jnp.int32) for shape in scalars],
        in_specs=[SMEM] * len(tables) + [hbm] * len(arrays),
        out_specs=[hbm] * len(shapes) + [SMEM] * len(scalars),
        scratch_shapes=[pltpu.VMEM(shape, arrays[0].dtype) for shape in scratch]
        + [pltpu.SemaphoreType.DMA((2, shape[0])) for shape in scratch],
    )(*tables, *arrays)


def project_kernel(spans, slot_total, resident, steps, masks, *refs):
    (me_ref, resident_adapter, arrival_adapter, holder, dest, hidden, *others) = refs[: 6 + len(masks)]
    store, out, left, adapters = refs[-4:]
    me = me_ref[0]
    adapter = pl.program_id(0)
    base = hidden.shape[0]
    block = others[0].shape[0]

    @pl.when(adapter == 0)
    def _():
        left[0:base] = hidden[...]
        for i, other in enumerate(others):
            left[base + i * block : base + (i + 1) * block] = other[...]
        out[...] = jnp.zeros_like(out)
        ids = lax.broadcasted_iota(jnp.int32, out.shape, 0) // steps
        own = jnp.full(out.shape, -1, jnp.int32)
        for slot in range(resident):
            own = jnp.where(ids == slot, resident_adapter[me * resident + slot], own)
        for i, mask in enumerate((0,) + masks):
            replica = me ^ mask
            first = resident if i == 0 else (base + (i - 1) * block) // steps
            for a in range(arrival_adapter.shape[0]):
                chosen = arrival_adapter[a, replica]
                row = jnp.int32(0)
                for copy_id in range(COPIES):
                    wanted = wanted_by(holder, dest, spans, replica, copy_id)
                    row += jnp.where(chosen == copy_id, wanted, 0)
                here = jnp.where(row // slot_total == me, row % slot_total, -1)
                own = jnp.where(ids == first + a, here, own)
        adapters[...] = own

    product = lax.dot_general(
        left[...], store[0], (((1,), (1,)), ((), ())), preferred_element_type=jnp.float32
    )
    out[...] += jnp.where(adapters[...] == adapter, product, 0.0)


def gather_kernel(shard_ref, *refs):
    out = refs[-1]
    count = len(refs) - 1
    width = refs[0].shape[1]
    for step, ref in enumerate(refs[:-1]):
        source = lax.rem(shard_ref[0] + count - step, count)
        out[:, pl.ds(pl.multiple_of(source * width, width), width)] = ref[...]


def attend_kernel(spans, masks, resident, steps, kv_heads, head_length, *refs):
    (me_ref, lengths, arrival_from, arrival_slot, resident_adapter, arrival_adapter) = refs[:6]
    holder, dest, total, *returned = refs[6 : 9 + len(masks)]
    came = refs[9 + len(masks) : 9 + 2 * len(masks)]
    store_b, sibling_b, across_b, base, queries, cache = refs[9 + 2 * len(masks) : -5]
    out, new_kv, arrived, installed_b, fresh_ref = refs[-5:]
    me = me_ref[0]
    arrive = arrival_from.shape[0]
    replicas = arrival_from.shape[1]
    slots = resident + arrive
    row_count = base.shape[1]
    rank = store_b.shape[1] // 2
    slot_total = store_b.shape[0]
    half = head_length // 2
    seen = [lengths[me * resident + slot] for slot in range(resident)]
    for a in range(arrive):
        seen.append(lengths[arrival_from[a, me] * resident + arrival_slot[a, me]])

    for a in range(arrive):
        for ref, mask in zip(came, masks):

            @pl.when(arrival_from[a, me] == me ^ mask)
            def _():
                arrived[a] = ref[...]

        def clear(row, carry):
            arrived[a, row] = jnp.zeros(arrived.shape[2:], arrived.dtype)
            return carry

        lax.fori_loop(seen[resident + a], arrived.shape[1], clear, 0)
    for copy_id in range(COPIES):
        near = wanted_by(holder, dest, spans, me, copy_id) // (2 * slot_total) == me // 2

        @pl.when(near)
        def _():
            installed_b[copy_id] = sibling_b[copy_id]

        @pl.when(jnp.logical_not(near))
        def _():
            installed_b[copy_id] = across_b[copy_id]

    first = resident * steps
    last = total[first:row_count]
    for ref in returned:
        last = last + ref[...]
    down = jnp.concatenate([total[0:first], last], axis=0).astype(jnp.bfloat16)

    ids = lax.broadcasted_iota(jnp.int32, (row_count, 1), 0) // steps
    adapters = jnp.zeros((row_count, 1), jnp.int32)
    position = lax.broadcasted_iota(jnp.int32, (row_count, 1), 0) % steps
    for slot in range(slots):
        if slot < resident:
            adapter = resident_adapter[me * resident + slot]
        else:
            adapter = store_b.shape[0] + arrival_adapter[slot - resident, me]
        adapters = jnp.where(ids == slot, adapter, adapters)
        position = jnp.where(ids == slot, position + seen[slot], position)
    deltas = [jnp.zeros((row_count, store_b.shape[2]), jnp.float32) for _ in range(2)]
    for adapter in range(store_b.shape[0] + COPIES):
        if adapter < store_b.shape[0]:
            table = store_b[adapter]
        else:
            table = installed_b[adapter - store_b.shape[0]]
        for part in range(2):
            product = jnp.dot(
                down[:, part * rank : (part + 1) * rank],
                table[part * rank : (part + 1) * rank],
                preferred_element_type=jnp.float32,
            )
            deltas[part] = jnp.where(adapters == adapter, product, deltas[part])

    lane = lax.broadcasted_iota(jnp.int32, (1, half), 1).astype(jnp.float32)
    frequency = jnp.exp(lane * (-2.0 * math.log(ROPE_BASE) / head_length))
    angles = position.astype(jnp.float32) * frequency
    cosine, sine = jnp.cos(angles), jnp.sin(angles)
    dead = jnp.zeros((row_count, 1), jnp.bool_)
    gone = [jnp.int32(0)] * resident
    for q in range(replicas):
        for a in range(arrive):
            mine = arrival_from[a, q] == me
            slot = arrival_slot[a, q]
            dead = jnp.logical_or(dead, jnp.logical_and(ids == slot, mine))
            for n in range(resident):
                gone[n] = jnp.where(jnp.logical_and(mine, slot == n), 1, gone[n])
    for g in range(kv_heads):
        at = g * 2 * head_length
        columns = slice(g * head_length, (g + 1) * head_length)
        key = base[g, :, :head_length] + ADAPTER_SCALE * deltas[0][:, columns]
        value = base[g, :, head_length:] + ADAPTER_SCALE * deltas[1][:, columns]
        u, w = key[:, :half], key[:, half:]
        key = jnp.concatenate([u * cosine - w * sine, w * cosine + u * sine], axis=1)
        for part, piece in enumerate((key, value)):
            spot = slice(at + part * head_length, at + (part + 1) * head_length)
            rounded = piece.astype(jnp.bfloat16)
            fresh_ref[:, spot] = rounded.astype(jnp.float32)
            new_kv[:, spot] = jnp.where(dead, jnp.zeros_like(rounded), rounded)

    query_rows = queries.shape[1]
    heads = query_rows // steps
    row = lax.broadcasted_iota(jnp.int32, (query_rows, 1), 0)
    step_of = row // heads
    group_of = row % heads // (heads // kv_heads)
    cache_rows = cache.shape[1] * kv_heads
    column = lax.broadcasted_iota(jnp.int32, (query_rows, cache_rows), 1)
    same = column % kv_heads == group_of
    past_row = column // kv_heads
    scale = 1.0 / math.sqrt(head_length)
    for n in range(slots):
        stored = cache[n] if n < resident else arrived[n - resident]
        stored = stored.reshape(cache_rows, 2 * head_length)
        query = queries[n]
        score = (
            lax.dot_general(
                query,
                stored[:, :head_length],
                (((1,), (1,)), ((), ())),
                preferred_element_type=jnp.float32,
            )
            * scale
        )
        score = jnp.where(jnp.logical_and(same, past_row < seen[n]), score, -jnp.inf)
        query = query.astype(jnp.float32)
        recent, values = [], []
        for t in range(steps):
            line = fresh_ref[n * steps + t : n * steps + t + 1]
            key = jnp.zeros((query_rows, head_length), jnp.float32)
            value = key
            for g in range(kv_heads):
                at = g * 2 * head_length
                key = jnp.where(group_of == g, line[:, at : at + head_length], key)
                value = jnp.where(
                    group_of == g, line[:, at + head_length : at + 2 * head_length], value
                )
            fit = jnp.sum(query * key, axis=1, keepdims=True) * scale
            recent.append(jnp.where(step_of >= t, fit, -jnp.inf))
            values.append(value)
        peak = jnp.max(score, axis=1, keepdims=True)
        for fit in recent:
            peak = jnp.maximum(peak, fit)
        past_exp = jnp.exp(score - peak)
        recent_exp = [jnp.exp(fit - peak) for fit in recent]
        denom = jnp.sum(past_exp, axis=1, keepdims=True)
        for term in recent_exp:
            denom = denom + term
        weight = (past_exp / denom).astype(jnp.bfloat16)
        mixed = jnp.dot(weight, stored[:, head_length:], preferred_element_type=jnp.float32)
        for term, value in zip(recent_exp, values):
            mixed = mixed + (term / denom).astype(jnp.bfloat16).astype(jnp.float32) * value
        if n < resident:
            mixed = jnp.where(gone[n] != 0, 0.0, mixed)
        out[n] = mixed.astype(jnp.bfloat16)


def pairs_layer(
    hidden,
    queries,
    kv_cache,
    w_kv,
    store_a,
    store_b,
    lengths,
    arrival_from,
    arrival_slot,
    resident_adapter,
    arrival_adapter,
    hot_holder,
    hot_dest,
):
    me = lax.axis_index("replica")
    replicas = lax.axis_size("replica")
    shards = lax.axis_size("tensor")
    resident, _, kv_heads, head_pair = kv_cache.shape
    arrive = arrival_from.shape[1]
    slots = resident + arrive
    steps, features = hidden.shape[1:]
    heads, head_length = queries.shape[2:]
    slot_total = store_a.shape[0]
    rank = store_a.shape[2]
    spans = hot_holder.shape[0] // COPIES
    row_a, row_b = store_a.shape[1:], store_b.shape[1:]
    columns = store_b.shape[3]
    masks = tuple(range(1, replicas))
    me_table = jnp.reshape(me, (1,)).astype(jnp.int32)
    shard_table = jnp.reshape(lax.axis_index("tensor"), (1,)).astype(jnp.int32)
    from_table, slot_table, choice_table = arrival_from.T, arrival_slot.T, arrival_adapter.T
    dest_table = hot_dest.T

    used = slots * steps
    padded = -(-used // 8) * 8
    rows = jnp.pad(hidden.reshape(used, features), ((0, padded - used), (0, 0)))
    first = resident * steps
    block = padded - first
    other_rows = [partner(rows[first:], mask) for mask in masks]

    *leaving, rows_b, rows_a = copy_call(
        functools.partial(collect_kernel, spans, slot_total, masks),
        (me_table, from_table, slot_table, hot_holder),
        (kv_cache, store_a, store_b),
        [kv_cache.shape[1:]] * len(masks) + [(COPIES,) + row_b, (COPIES,) + row_a],
        [(len(masks),) + kv_cache.shape[1:], (COPIES,) + row_a, (COPIES,) + row_b],
    )
    sibling_a = partner(rows_a, 1)
    sibling_b = partner(rows_b, 1)
    came = [partner(array, mask) for array, mask in zip(leaving, masks)]
    around = [rows] + [shifted(rows, step) for step in range(1, shards)]

    line_count = padded + len(masks) * block
    partial = pl.pallas_call(
        functools.partial(project_kernel, spans, slot_total, resident, steps, masks),
        out_shape=jax.ShapeDtypeStruct((line_count, 2 * rank), jnp.float32),
        grid=(slot_total,),
        in_specs=[SMEM] * 5
        + [pl.BlockSpec((padded, features), lambda i: (0, 0))]
        + [pl.BlockSpec((block, features), lambda i: (0, 0))] * len(masks)
        + [pl.BlockSpec((1, 2 * rank, features), lambda i: (i, 0, 0))],
        out_specs=pl.BlockSpec((line_count, 2 * rank), lambda i: (0, 0)),
        scratch_shapes=[
            pltpu.VMEM((line_count, features), hidden.dtype),
            pltpu.VMEM((line_count, 2 * rank), jnp.int32),
        ],
        name="project",
    )(
        me_table,
        resident_adapter,
        choice_table,
        hot_holder,
        dest_table,
        rows,
        *other_rows,
        store_a.reshape(slot_total, 2 * rank, features),
    )
    parts = [partial] + [shifted(partial, step) for step in range(1, shards)]

    unit_shape = row_a[1:]
    tail_units = 2 * COPIES - HEAD_UNITS
    across_b, head, *tails, extra = copy_call(
        functools.partial(pack_kernel, spans, slot_total),
        (me_table, hot_holder, dest_table),
        (store_a, store_b, sibling_a, sibling_b),
        [(COPIES,) + row_b, (HEAD_UNITS,) + unit_shape] + [unit_shape] * tail_units,
        [(COPIES,) + row_b, (2 * COPIES,) + unit_shape],
        [(1,)],
    )
    across_b = partner(across_b, 2)
    head = partner(head, 2)
    total = parts[0]
    for array in parts[1:]:
        total = total + array
    returned = [
        partner(total[padded + i * block : padded + (i + 1) * block], mask)
        for i, mask in enumerate(masks)
    ]

    full = pl.pallas_call(
        gather_kernel,
        out_shape=jax.ShapeDtypeStruct((padded, shards * features), hidden.dtype),
        in_specs=[SMEM] + [VMEM] * shards,
        out_specs=VMEM,
        name="gather",
    )(shard_table, *around)
    base = jnp.einsum("md,dgc->gmc", full, w_kv, preferred_element_type=jnp.float32)

    attn_out, new_kv, arrived, installed_b = pl.pallas_call(
        functools.partial(attend_kernel, spans, masks, resident, steps, kv_heads, head_length),
        out_shape=[
            jax.ShapeDtypeStruct((slots, steps * heads, head_length), jnp.bfloat16),
            jax.ShapeDtypeStruct((padded, kv_heads * head_pair), jnp.bfloat16),
            jax.ShapeDtypeStruct((arrive,) + kv_cache.shape[1:], jnp.bfloat16),
            jax.ShapeDtypeStruct((COPIES, 2 * rank, columns), jnp.bfloat16),
        ],
        in_specs=[SMEM] * 8 + [VMEM] * (1 + 2 * len(masks) + 6),
        out_specs=[VMEM] * 4,
        scratch_shapes=[pltpu.VMEM((padded, kv_heads * head_pair), jnp.float32)],
        name="attend",
    )(
        me_table,
        lengths,
        from_table,
        slot_table,
        resident_adapter,
        choice_table,
        hot_holder,
        dest_table,
        total,
        *returned,
        *came,
        store_b.reshape(slot_total, 2 * rank, columns),
        sibling_b.reshape(COPIES, 2 * rank, columns),
        across_b.reshape(COPIES, 2 * rank, columns),
        base,
        queries.reshape(slots, steps * heads, head_length),
        kv_cache,
    )
    installed_b = installed_b.reshape((COPIES,) + row_b)
    head, attn_out, new_kv = lax.optimization_barrier((head, attn_out, new_kv))
    attn_out = attn_out.reshape(slots, steps, heads * head_length)
    new_kv = new_kv[:used].reshape(slots, steps, kv_heads, head_pair)

    def finish(units):
        def branch(sibling_a, head, *tails):
            got = [partner(array, 2) for array in tails[:units]]
            head_other = partner(head, 1)
            other = [partner(array, 1) for array in got]
            (placed,) = copy_call(
                functools.partial(place_down_kernel, spans, slot_total, units),
                (me_table, hot_holder, dest_table),
                (sibling_a, head, head_other, *got, *other),
                [(COPIES,) + row_a],
                [(2 * COPIES,) + unit_shape],
            )
            return placed

        return branch

    branches = [finish(units) for units in range(tail_units + 1)]
    installed_a = lax.switch(extra[0], branches, sibling_a, head, *tails)
    return (attn_out, new_kv, arrived, installed_a, installed_b)


def local(*args):
    fan = args[-1].shape[1]
    if lax.axis_size("replica") == 4 and fan == 1:
        return pairs_layer(*args)
    return local_general(*args)


def solution(mesh):
    in_specs = (
        P(("parts", "replica"), None, "tensor"),
        P(("parts", "replica"), None, "tensor", None),
        P(("parts", "replica"), None, "tensor", None),
        P(None, "tensor", None),
        P(("parts", "replica"), None, None, "tensor"),
        P(("parts", "replica"), None, None, "tensor"),
        P("parts"),
        P("parts", None),
        P("parts", None),
        P("parts"),
        P("parts", None),
        P("parts"),
        P("parts", None),
    )
    out_specs = (
        P(("parts", "replica"), None, "tensor"),
        P(("parts", "replica"), None, "tensor", None),
        P(("parts", "replica"), None, "tensor", None),
        P(("parts", "replica"), None, None, "tensor"),
        P(("parts", "replica"), None, None, "tensor"),
    )
    return jax.shard_map(local, mesh=mesh, in_specs=in_specs, out_specs=out_specs, check_vma=False)
```

profile of v0, /device:TPU:7, one launch (start us, length us, event | category | flops | bytes accessed | tf_op | source)
XLA Modules:
  0.0 118.0 jit_solution(16440998688566638029)
XLA Ops:
  0.7 4.1 %shard_map.164 = (bf16[128,2,256]{2,1,0:T(2,128)(2,1)}, bf16[128,2,256]{2,1,0:T(2,128)(2,1)}, bf16[128,2,256]{2,1,0:T(2,128)(2,1)}, bf16[4,2,64,256]{3,2,1,0:T(8,128)(2,1)}, bf16[4,2,64,2048]{3,2,1,0:T(8,128)(2,1)}) custom-call(s32[1]{0:T(128)} %bitcast.refs_0_, s32[2,4]{1,0:T(2,128)} %bitcast.31, s32[2,4]{1,0:T(2,128)} %bitcast.33, s32[16]{0:T(128)} %refs_6_.3, ...), custom_call_target="tpu_custom_call" | custom-call | tf_op jit(solution)/shard_map/pallas_call | solution.py:372
  4.8 0.8 collective-permute-start.16
  5.6 0.1 collective-permute-start.17
  5.7 4.2 %collective-permute-done.17.refs_6_ = bf16[4,2,64,256]{3,2,1,0:T(8,128)(2,1)S(1)} collective-permute-done((bf16[4,2,64,256]{3,2,1,0:T(8,128)(2,1)}, bf16[4,2,64,256]{3,2,1,0:T(8,128)(2,1)S(1)}, u32[]{:S(2)}, u32[]{:S(2)}) %collective-permute-start.17) | collective-permute-done | bytes 262176 | tf_op jit(solution)/shard_map/ppermute | solution.py:212
  10.0 0.0 collective-permute-done.16.refs_5_
  10.0 0.7 copy-done.5
  10.6 5.0 %shard_map.165 = (bf16[4,2,64,256]{3,2,1,0:T(8,128)(2,1)}, bf16[5,64,2048]{2,1,0:T(8,128)(2,1)}, bf16[64,2048]{1,0:T(8,128)(2,1)}, bf16[64,2048]{1,0:T(8,128)(2,1)}, bf16[64,2048]{1,0:T(8,128)(2,1)}, /*index=5*/s32[1]{0:T(128)}) custom-call(s32[1]{0:T(128)} %bitcast.refs_0_, s32[16]{0:T(128)S(1)} %copy-done.26, s32[1,16]{1,0:T(1,128)S(1)} %bitcast.24, ...), custom_call_target="tpu_custom_call" | custom-call | tf_op jit(solution)/shard_map/pallas_call | solution.py:372
  15.7 0.1 collective-permute-start.18
  15.8 2.0 %collective-permute-start.21 = (bf16[8,2048]{1,0:T(8,128)(2,1)S(1)}, bf16[8,2048]{1,0:T(8,128)(2,1)S(1)}, u32[]{:S(2)}, u32[]{:S(2)}) collective-permute-start(bf16[8,2048]{1,0:T(8,128)(2,1)S(1)} %pad_slice_fusion), channel_id=1, source_target_pairs={{0,12},{4,8},{8,4},{12,0},{1,13},{5,9},{9,5},{13,1},{2,14},{6,10},... | collective-permute-start | bytes 98312 | tf_op jit(solution)/shard_map/ppermute | solution.py:212
  17.8 0.2 collective-permute-start.20
  17.9 0.3 collective-permute-start.19
  18.2 0.7 pad.4.refs_5_.refs_0_
  18.9 28.6 %collective-permute-done.21.refs_8_ = bf16[8,2048]{1,0:T(8,128)(2,1)S(1)} collective-permute-done((bf16[8,2048]{1,0:T(8,128)(2,1)S(1)}, bf16[8,2048]{1,0:T(8,128)(2,1)S(1)}, u32[]{:S(2)}, u32[]{:S(2)}) %collective-permute-start.21) | collective-permute-done | bytes 32800 | tf_op jit(solution)/shard_map/ppermute | solution.py:212
  47.5 0.0 collective-permute-done.20.refs_7_
  47.5 0.0 collective-permute-done.19.refs_6_
  47.5 0.0 copy-start.25
  47.5 0.6 copy-done.23
  48.1 0.0 copy-done.24
  48.1 0.0 copy-done.25
  48.1 6.9 %project.1 = f32[56,128]{1,0:T(8,128)} custom-call(s32[1]{0:T(128)} %bitcast.refs_0_, s32[48]{0:T(128)} %refs_4_.5, s32[2,4]{1,0:T(2,128)} %bitcast.35, s32[16]{0:T(128)S(1)} %copy-done.26, s32[1,16]{1,0:T(1,128)S(1)} %bitcast.25, bf16[32,2048]{1,0:T(8,128)(2,1)} %pad.4.refs_5_.refs_0_, bf16[8,2048]{1,0:T(8,128)(2,1)} %copy-done.25, ...), custom_call_target="tpu_custom_call" | custom-call | tf_op jit(solution)/shard_map/project/pallas_call | solution.py:636
  55.0 3.3 %collective-permute-start.24 = (f32[56,128]{1,0:T(8,128)}, f32[56,128]{1,0:T(8,128)S(1)}, u32[]{:S(2)}, u32[]{:S(2)}) collective-permute-start(f32[56,128]{1,0:T(8,128)} %project.1), channel_id=1, source_target_pairs={{0,3},{1,0},{2,1},{3,2},{4,7},{5,4},{6,5},{7,6},{8,11},{9,8},{10,9... | collective-permute-start | bytes 86024 | tf_op jit(solution)/shard_map/ppermute | solution.py:217
  58.3 0.0 collective-permute-start.23
  58.4 0.4 collective-permute-start.22
  58.8 2.8 %collective-permute-start.34 = (bf16[32,2048]{1,0:T(8,128)(2,1)S(1)}, bf16[32,2048]{1,0:T(8,128)(2,1)S(1)}, u32[]{:S(2)}, u32[]{:S(2)}) collective-permute-start(bf16[32,2048]{1,0:T(8,128)(2,1)S(1)} %copy-done.4), channel_id=1, source_target_pairs={{0,3},{1,0},{2,1},{3,2},{4,7},{5,4},{6,5},{7,6},{8,11},{9,8},{10,9... | collective-permute-start | bytes 393224 | tf_op jit(solution)/shard_map/ppermute | solution.py:217
  61.6 0.0 collective-permute-done.24
  61.6 0.6 collective-permute-start.33
  62.2 0.0 collective-permute-done.23
  62.2 1.2 collective-permute-start.32
  63.4 0.0 collective-permute-done.22
  63.4 0.8 add_add_fusion.refs_8_
  64.1 0.6 fusion.6
  64.7 2.8 %collective-permute-start.27 = (f32[8,128]{1,0:T(8,128)}, f32[8,128]{1,0:T(8,128)S(1)}, u32[]{:S(2)}, u32[]{:S(2)}) collective-permute-start(f32[8,128]{1,0:T(8,128)} %get-tuple-element.124), channel_id=1, source_target_pairs={{0,12},{4,8},{8,4},{12,0},{1,13},{5,9},{9,5},{13,1},{2,14},{6,10},... | collective-permute-start | bytes 12296 | tf_op jit(solution)/shard_map/ppermute | solution.py:212
  67.5 0.0 collective-permute-done.34.refs_3_
  67.5 1.4 %collective-permute-start.26 = (f32[8,128]{1,0:T(8,128)}, f32[8,128]{1,0:T(8,128)S(1)}, u32[]{:S(2)}, u32[]{:S(2)}) collective-permute-start(f32[8,128]{1,0:T(8,128)} %get-tuple-element.125), channel_id=1, source_target_pairs={{0,8},{4,12},{8,0},{12,4},{1,9},{5,13},{9,1},{13,5},{2,10},{6,14},... | collective-permute-start | bytes 12296 | tf_op jit(solution)/shard_map/ppermute | solution.py:212
  68.9 5.1 %collective-permute-done.33.refs_2_ = bf16[32,2048]{1,0:T(8,128)(2,1)S(1)} collective-permute-done((bf16[32,2048]{1,0:T(8,128)(2,1)S(1)}, bf16[32,2048]{1,0:T(8,128)(2,1)S(1)}, u32[]{:S(2)}, u32[]{:S(2)}) %collective-permute-start.33) | collective-permute-done | bytes 131104 | tf_op jit(solution)/shard_map/ppermute | solution.py:217
  74.1 0.7 copy-done.21
  74.7 1.6 %collective-permute-start.25 = (f32[8,128]{1,0:T(8,128)}, f32[8,128]{1,0:T(8,128)}, u32[]{:S(2)}, u32[]{:S(2)}) collective-permute-start(f32[8,128]{1,0:T(8,128)} %get-tuple-element.126), channel_id=1, source_target_pairs={{0,4},{4,0},{8,12},{12,8},{1,5},{5,1},{9,13},{13,9},{2,6},{6,2},{1... | collective-permute-start | bytes 12296 | tf_op jit(solution)/shard_map/ppermute | solution.py:212
  76.3 0.0 collective-permute-done.32.refs_1_
  76.3 0.0 collective-permute-start.28
  76.3 2.0 %gather.1 = bf16[32,8192]{1,0:T(8,128)(2,1)} custom-call(s32[1]{0:T(128)} %bitcast.9.shard_ref, bf16[32,2048]{1,0:T(8,128)(2,1)} %pad.4.refs_5_.refs_0_, bf16[32,2048]{1,0:T(8,128)(2,1)} %collective-permute-done.32.refs_1_, bf16[32,2048]{1,0:T(8,128)(2,1)} %copy-done.21, bf16[32,2048]{1,0:T(8,128)(2,1)} %copy-done.20), custom_call_target="tpu_custom_call" | custom-call | tf_op jit(solution)/shard_map/gather/pallas_call | solution.py:682
  78.3 0.0 collective-permute-done.27.refs_11_
  78.3 0.0 collective-permute-start.29
  78.4 0.0 collective-permute-done.26.refs_10_
  78.4 2.1 %collective-permute-start.30 = (bf16[128,2,256]{2,1,0:T(2,128)(2,1)}, bf16[128,2,256]{2,1,0:T(2,128)(2,1)}, u32[]{:S(2)}, u32[]{:S(2)}) collective-permute-start(bf16[128,2,256]{2,1,0:T(2,128)(2,1)} %get-tuple-element.111), channel_id=1, source_target_pairs={{0,12},{4,8},{8,4},{12,0},{1,13},{5,9},{9,5},{13,1},{2,14},{6,10},... | collective-permute-start | bytes 393224 | tf_op jit(solution)/shard_map/ppermute | solution.py:212
  80.4 0.0 collective-permute-done.25.refs_9_
  80.5 0.0 collective-permute-start.31
  80.5 5.8 %fusion.2.refs_18_ = f32[2,32,256]{2,1,0:T(8,128)} fusion(bf16[8192,2,256]{2,1,0:T(2,128)(2,1)} %param.20, bf16[32,8192]{1,0:T(8,128)(2,1)} %gather.1), kind=kOutput, calls=%fused_computation.2 | convolution fusion | flops 268435456 | bytes 8978432 | tf_op jit(solution)/shard_map/md,dgc->gmc/dot_general | solution.py:689
  86.8 0.0 collective-permute-done.29.refs_13_
  86.8 0.8 collective-permute-done.30.refs_14_
  87.6 4.0 %collective-permute-done.31 = bf16[4,2,64,256]{3,2,1,0:T(8,128)(2,1)} collective-permute-done((bf16[4,2,64,256]{3,2,1,0:T(8,128)(2,1)}, bf16[4,2,64,256]{3,2,1,0:T(8,128)(2,1)}, u32[]{:S(2)}, u32[]{:S(2)}) %collective-permute-start.31) | collective-permute-done | bytes 262176 | tf_op jit(solution)/shard_map/ppermute | solution.py:212
  91.6 7.9 %attend.1 = (bf16[14,32,128]{2,1,0:T(8,128)(2,1)}, bf16[32,512]{1,0:T(8,128)(2,1)}, bf16[2,128,2,256]{3,2,1,0:T(2,128)(2,1)}, bf16[4,128,256]{2,1,0:T(8,128)(2,1)}) custom-call(s32[1]{0:T(128)} %bitcast.refs_0_, s32[48]{0:T(128)} %refs_1_.5, s32[2,4]{1,0:T(2,128)} %bitcast.32, s32[2,4]{1,0:T(2,128)} %bitcast.34, s32[48]{0:T(128)} %refs_4_.5, ...), custom_call_target="tpu_custom_call" | custom-call | tf_op jit(solution)/shard_map/attend/pallas_call | solution.py:691
  99.5 0.0 collective-permute-done.18
  99.5 1.6 %reshape.54 = bf16[14,2,2048]{2,1,0:T(2,128)(2,1)} reshape(bf16[14,32,128]{2,1,0:T(8,128)(2,1)} %get-tuple-element.115) | data formatting | bytes 229376 | tf_op jit(solution)/shard_map/reshape | solution.py:724
  101.1 1.4 %reshape.55 = bf16[14,2,2,256]{3,2,1,0:T(2,128)(2,1)} reshape(bf16[28,512]{1,0:T(8,128)(2,1)} %bitcast.23) | data formatting | bytes 57344 | tf_op jit(solution)/shard_map/reshape | solution.py:725
  102.4 15.6 %conditional.1 = (bf16[4,2,64,2048]{3,2,1,0:T(8,128)(2,1)}) conditional(s32[]{:T(128)} %bitcast.13, (bf16[5,64,2048]{2,1,0:T(8,128)(2,1)S(1)}, s32[1]{0:T(128)}, s32[16]{0:T(128)S(1)}, s32[1,16]{1,0:T(1,128)S(1)}, bf16[4,2,64,2048]{3,2,1,0:T(8,128)(2,1)S(1)}) %tuple.37, (bf16[5,64,2048]{2,1,0:T(8,128)(2,1)S(1)}, ...), branch_computations={%region_0.1_spmd, %region_1.2_spmd, %region_2.3_spmd, %region_3.4_... | conditional | bytes 23069156 | solution.py:744
  102.4 1.3 %collective-permute-start.1 = (bf16[5,64,2048]{2,1,0:T(8,128)(2,1)S(1)}, bf16[5,64,2048]{2,1,0:T(8,128)(2,1)S(1)}, u32[]{:S(2)}, u32[]{:S(2)}) collective-permute-start(bf16[5,64,2048]{2,1,0:T(8,128)(2,1)S(1)} %get-tuple-element.66.refs_4_), channel_id=1, source_target_pairs={{0,4},{4,0},{8,12},{12,8},{1,5},{5,1},{9,13},{13,9},{2,6},{6,2},{1... | collective-permute-start | bytes 3932168 | tf_op jit(solution)/shard_map/cond/branch_1_fun/ppermute | solution.py:212
  103.8 0.0 collective-permute-start.2
  103.8 8.0 %collective-permute-done.2.refs_6_ = bf16[64,2048]{1,0:T(8,128)(2,1)S(1)} collective-permute-done((bf16[64,2048]{1,0:T(8,128)(2,1)}, bf16[64,2048]{1,0:T(8,128)(2,1)S(1)}, u32[]{:S(2)}, u32[]{:S(2)}) %collective-permute-start.2) | collective-permute-done | bytes 262176 | tf_op jit(solution)/shard_map/cond/branch_1_fun/ppermute | solution.py:212
  111.8 0.9 collective-permute-start.3
  112.7 1.2 collective-permute-done.3.refs_7_
  113.9 0.0 collective-permute-done.1.refs_5_
  113.9 1.1 copy-done.2
  115.0 0.0 copy-done.17
  115.0 3.0 %branch_1_fun.1 = bf16[4,2,64,2048]{3,2,1,0:T(8,128)(2,1)} custom-call(s32[1]{0:T(128)} %get-tuple-element.62.refs_0_, s32[16]{0:T(128)S(1)} %get-tuple-element.63.refs_1_, s32[1,16]{1,0:T(1,128)S(1)} %get-tuple-element.64.refs_2_, bf16[4,2,64,2048]{3,2,1,0:T(8,128)(2,1)S(1)} %get-tuple-element.65.refs_3_, ...), custom_call_target="tpu_custom_call" | custom-call | tf_op jit(solution)/shard_map/cond/branch_1_fun/pallas_call | solution.py:372
  (29 shorter events, 0.1 us)
Async XLA Ops:
  0.6 5.0 %copy-start.22 = (bf16[14,2,2048]{2,1,0:T(2,128)(2,1)S(1)}, bf16[14,2,2048]{2,1,0:T(2,128)(2,1)}, u32[]{:S(2)}) copy-start(bf16[14,2,2048]{2,1,0:T(2,128)(2,1)} %param.17) | copy-start | bytes 344068
  0.6 10.0 %copy-start.26 = (s32[16]{0:T(128)S(1)}, s32[16]{0:T(128)}, u32[]{:S(2)}) copy-start(s32[16]{0:T(128)} %refs_6_.3) | copy-start | bytes 196
  0.7 10.0 %copy-start.27 = (s32[16,1]{0,1:T(1,128)S(1)}, s32[16,1]{0,1:T(1,128)}, u32[]{:S(2)}) copy-start(s32[16,1]{0,1:T(1,128)} %param.29) | copy-start | bytes 196
  4.8 5.2 %collective-permute-start.16 = (bf16[4,2,64,2048]{3,2,1,0:T(8,128)(2,1)}, bf16[4,2,64,2048]{3,2,1,0:T(8,128)(2,1)S(1)}, u32[]{:S(2)}, u32[]{:S(2)}) collective-permute-start(bf16[4,2,64,2048]{3,2,1,0:T(8,128)(2,1)} %get-tuple-element.106), channel_id=1, source_target_pairs={{0,4},{4,0},{8,12},{12,8},{1,5},{5,1},{9,13},{13,9},{2,6},{6,2},{1... | collective-permute-start | bytes 6291464 | tf_op jit(solution)/shard_map/ppermute | solution.py:212
  5.6 4.4 %collective-permute-start.17 = (bf16[4,2,64,256]{3,2,1,0:T(8,128)(2,1)}, bf16[4,2,64,256]{3,2,1,0:T(8,128)(2,1)S(1)}, u32[]{:S(2)}, u32[]{:S(2)}) collective-permute-start(bf16[4,2,64,256]{3,2,1,0:T(8,128)(2,1)} %get-tuple-element.107), channel_id=1, source_target_pairs={{0,4},{4,0},{8,12},{12,8},{1,5},{5,1},{9,13},{13,9},{2,6},{6,2},{1... | collective-permute-start | bytes 786440 | tf_op jit(solution)/shard_map/ppermute | solution.py:212
  9.9 0.7 copy-start.5
  15.7 83.8 %collective-permute-start.18 = (bf16[5,64,2048]{2,1,0:T(8,128)(2,1)}, bf16[5,64,2048]{2,1,0:T(8,128)(2,1)S(1)}, u32[]{:S(2)}, u32[]{:S(2)}) collective-permute-start(bf16[5,64,2048]{2,1,0:T(8,128)(2,1)} %get-tuple-element.108), channel_id=1, source_target_pairs={{0,8},{4,12},{8,0},{12,4},{1,9},{5,13},{9,1},{13,5},{2,10},{6,14},... | collective-permute-start | bytes 3932168 | tf_op jit(solution)/shard_map/ppermute | solution.py:212
  15.8 31.7 %collective-permute-start.21 = (bf16[8,2048]{1,0:T(8,128)(2,1)S(1)}, bf16[8,2048]{1,0:T(8,128)(2,1)S(1)}, u32[]{:S(2)}, u32[]{:S(2)}) collective-permute-start(bf16[8,2048]{1,0:T(8,128)(2,1)S(1)} %pad_slice_fusion), channel_id=1, source_target_pairs={{0,12},{4,8},{8,4},{12,0},{1,13},{5,9},{9,5},{13,1},{2,14},{6,10},... | collective-permute-start | bytes 98312 | tf_op jit(solution)/shard_map/ppermute | solution.py:212
  17.8 29.8 %collective-permute-start.20 = (bf16[8,2048]{1,0:T(8,128)(2,1)S(1)}, bf16[8,2048]{1,0:T(8,128)(2,1)S(1)}, u32[]{:S(2)}, u32[]{:S(2)}) collective-permute-start(bf16[8,2048]{1,0:T(8,128)(2,1)S(1)} %pad_slice_fusion), channel_id=1, source_target_pairs={{0,8},{4,12},{8,0},{12,4},{1,9},{5,13},{9,1},{13,5},{2,10},{6,14},... | collective-permute-start | bytes 98312 | tf_op jit(solution)/shard_map/ppermute | solution.py:212
  17.9 29.6 %collective-permute-start.19 = (bf16[8,2048]{1,0:T(8,128)(2,1)S(1)}, bf16[8,2048]{1,0:T(8,128)(2,1)S(1)}, u32[]{:S(2)}, u32[]{:S(2)}) collective-permute-start(bf16[8,2048]{1,0:T(8,128)(2,1)S(1)} %pad_slice_fusion), channel_id=1, source_target_pairs={{0,4},{4,0},{8,12},{12,8},{1,5},{5,1},{9,13},{13,9},{2,6},{6,2},{1... | collective-permute-start | bytes 98312 | tf_op jit(solution)/shard_map/ppermute | solution.py:212
  47.5 0.6 copy-start.23
  47.5 0.6 copy-start.24
  47.5 0.6 copy-start.25
  48.1 10.7 %copy-start.4 = (bf16[32,2048]{1,0:T(8,128)(2,1)S(1)}, bf16[32,2048]{1,0:T(8,128)(2,1)}, u32[]{:S(2)}) copy-start(bf16[32,2048]{1,0:T(8,128)(2,1)} %pad.4.refs_5_.refs_0_) | copy-start | bytes 393220
  55.0 6.6 %collective-permute-start.24 = (f32[56,128]{1,0:T(8,128)}, f32[56,128]{1,0:T(8,128)S(1)}, u32[]{:S(2)}, u32[]{:S(2)}) collective-permute-start(f32[56,128]{1,0:T(8,128)} %project.1), channel_id=1, source_target_pairs={{0,3},{1,0},{2,1},{3,2},{4,7},{5,4},{6,5},{7,6},{8,11},{9,8},{10,9... | collective-permute-start | bytes 86024 | tf_op jit(solution)/shard_map/ppermute | solution.py:217
  58.3 3.9 %collective-permute-start.23 = (f32[56,128]{1,0:T(8,128)}, f32[56,128]{1,0:T(8,128)S(1)}, u32[]{:S(2)}, u32[]{:S(2)}) collective-permute-start(f32[56,128]{1,0:T(8,128)} %project.1), channel_id=1, source_target_pairs={{0,2},{1,3},{2,0},{3,1},{4,6},{5,7},{6,4},{7,5},{8,10},{9,11},{10,... | collective-permute-start | bytes 86024 | tf_op jit(solution)/shard_map/ppermute | solution.py:217
  58.4 5.0 %collective-permute-start.22 = (f32[56,128]{1,0:T(8,128)}, f32[56,128]{1,0:T(8,128)S(1)}, u32[]{:S(2)}, u32[]{:S(2)}) collective-permute-start(f32[56,128]{1,0:T(8,128)} %project.1), channel_id=1, source_target_pairs={{0,1},{1,2},{2,3},{3,0},{4,5},{5,6},{6,7},{7,4},{8,9},{9,10},{10,1... | collective-permute-start | bytes 86024 | tf_op jit(solution)/shard_map/ppermute | solution.py:217
  58.8 8.7 %collective-permute-start.34 = (bf16[32,2048]{1,0:T(8,128)(2,1)S(1)}, bf16[32,2048]{1,0:T(8,128)(2,1)S(1)}, u32[]{:S(2)}, u32[]{:S(2)}) collective-permute-start(bf16[32,2048]{1,0:T(8,128)(2,1)S(1)} %copy-done.4), channel_id=1, source_target_pairs={{0,3},{1,0},{2,1},{3,2},{4,7},{5,4},{6,5},{7,6},{8,11},{9,8},{10,9... | collective-permute-start | bytes 393224 | tf_op jit(solution)/shard_map/ppermute | solution.py:217
  61.6 12.5 %collective-permute-start.33 = (bf16[32,2048]{1,0:T(8,128)(2,1)S(1)}, bf16[32,2048]{1,0:T(8,128)(2,1)S(1)}, u32[]{:S(2)}, u32[]{:S(2)}) collective-permute-start(bf16[32,2048]{1,0:T(8,128)(2,1)S(1)} %copy-done.4), channel_id=1, source_target_pairs={{0,2},{1,3},{2,0},{3,1},{4,6},{5,7},{6,4},{7,5},{8,10},{9,11},{10,... | collective-permute-start | bytes 393224 | tf_op jit(solution)/shard_map/ppermute | solution.py:217
  62.2 14.1 %collective-permute-start.32 = (bf16[32,2048]{1,0:T(8,128)(2,1)S(1)}, bf16[32,2048]{1,0:T(8,128)(2,1)}, u32[]{:S(2)}, u32[]{:S(2)}) collective-permute-start(bf16[32,2048]{1,0:T(8,128)(2,1)S(1)} %copy-done.4), channel_id=1, source_target_pairs={{0,1},{1,2},{2,3},{3,0},{4,5},{5,6},{6,7},{7,4},{8,9},{9,10},{10,1... | collective-permute-start | bytes 393224 | tf_op jit(solution)/shard_map/ppermute | solution.py:217
  64.1 9.9 %copy-start.18 = (f32[56,128]{1,0:T(8,128)}, f32[56,128]{1,0:T(8,128)S(1)}, u32[]{:S(2)}) copy-start(f32[56,128]{1,0:T(8,128)S(1)} %add_add_fusion.refs_8_) | copy-start | bytes 86020
  64.7 13.6 %collective-permute-start.27 = (f32[8,128]{1,0:T(8,128)}, f32[8,128]{1,0:T(8,128)S(1)}, u32[]{:S(2)}, u32[]{:S(2)}) collective-permute-start(f32[8,128]{1,0:T(8,128)} %get-tuple-element.124), channel_id=1, source_target_pairs={{0,12},{4,8},{8,4},{12,0},{1,13},{5,9},{9,5},{13,1},{2,14},{6,10},... | collective-permute-start | bytes 12296 | tf_op jit(solution)/shard_map/ppermute | solution.py:212
  67.5 6.6 %copy-start.20 = (bf16[32,2048]{1,0:T(8,128)(2,1)}, bf16[32,2048]{1,0:T(8,128)(2,1)S(1)}, u32[]{:S(2)}) copy-start(bf16[32,2048]{1,0:T(8,128)(2,1)S(1)} %collective-permute-done.34.refs_3_) | copy-start | bytes 393220
  67.5 10.8 %collective-permute-start.26 = (f32[8,128]{1,0:T(8,128)}, f32[8,128]{1,0:T(8,128)S(1)}, u32[]{:S(2)}, u32[]{:S(2)}) collective-permute-start(f32[8,128]{1,0:T(8,128)} %get-tuple-element.125), channel_id=1, source_target_pairs={{0,8},{4,12},{8,0},{12,4},{1,9},{5,13},{9,1},{13,5},{2,10},{6,14},... | collective-permute-start | bytes 12296 | tf_op jit(solution)/shard_map/ppermute | solution.py:212
  74.1 0.7 copy-start.21
  74.7 5.7 %collective-permute-start.25 = (f32[8,128]{1,0:T(8,128)}, f32[8,128]{1,0:T(8,128)}, u32[]{:S(2)}, u32[]{:S(2)}) collective-permute-start(f32[8,128]{1,0:T(8,128)} %get-tuple-element.126), channel_id=1, source_target_pairs={{0,4},{4,0},{8,12},{12,8},{1,5},{5,1},{9,13},{13,9},{2,6},{6,2},{1... | collective-permute-start | bytes 12296 | tf_op jit(solution)/shard_map/ppermute | solution.py:212
  76.3 10.5 %collective-permute-start.28 = (bf16[128,2,256]{2,1,0:T(2,128)(2,1)}, bf16[128,2,256]{2,1,0:T(2,128)(2,1)S(1)}, u32[]{:S(2)}, u32[]{:S(2)}) collective-permute-start(bf16[128,2,256]{2,1,0:T(2,128)(2,1)} %get-tuple-element.109), channel_id=1, source_target_pairs={{0,4},{4,0},{8,12},{12,8},{1,5},{5,1},{9,13},{13,9},{2,6},{6,2},{1... | collective-permute-start | bytes 393224 | tf_op jit(solution)/shard_map/ppermute | solution.py:212
  78.3 8.0 %copy-start.28 = (f32[8,128]{1,0:T(8,128)}, f32[8,128]{1,0:T(8,128)S(1)}, u32[]{:S(2)}) copy-start(f32[8,128]{1,0:T(8,128)S(1)} %collective-permute-done.27.refs_11_) | copy-start | bytes 12292
  78.3 8.5 %collective-permute-start.29 = (bf16[128,2,256]{2,1,0:T(2,128)(2,1)}, bf16[128,2,256]{2,1,0:T(2,128)(2,1)}, u32[]{:S(2)}, u32[]{:S(2)}) collective-permute-start(bf16[128,2,256]{2,1,0:T(2,128)(2,1)} %get-tuple-element.110), channel_id=1, source_target_pairs={{0,8},{4,12},{8,0},{12,4},{1,9},{5,13},{9,1},{13,5},{2,10},{6,14},... | collective-permute-start | bytes 393224 | tf_op jit(solution)/shard_map/ppermute | solution.py:212
  78.4 7.9 %copy-start.29 = (f32[8,128]{1,0:T(8,128)}, f32[8,128]{1,0:T(8,128)S(1)}, u32[]{:S(2)}) copy-start(f32[8,128]{1,0:T(8,128)S(1)} %collective-permute-done.26.refs_10_) | copy-start | bytes 12292
  78.4 9.3 %collective-permute-start.30 = (bf16[128,2,256]{2,1,0:T(2,128)(2,1)}, bf16[128,2,256]{2,1,0:T(2,128)(2,1)}, u32[]{:S(2)}, u32[]{:S(2)}) collective-permute-start(bf16[128,2,256]{2,1,0:T(2,128)(2,1)} %get-tuple-element.111), channel_id=1, source_target_pairs={{0,12},{4,8},{8,4},{12,0},{1,13},{5,9},{9,5},{13,1},{2,14},{6,10},... | collective-permute-start | bytes 393224 | tf_op jit(solution)/shard_map/ppermute | solution.py:212
  80.5 11.1 %collective-permute-start.31 = (bf16[4,2,64,256]{3,2,1,0:T(8,128)(2,1)}, bf16[4,2,64,256]{3,2,1,0:T(8,128)(2,1)}, u32[]{:S(2)}, u32[]{:S(2)}) collective-permute-start(bf16[4,2,64,256]{3,2,1,0:T(8,128)(2,1)} %get-tuple-element.112), channel_id=1, source_target_pairs={{0,8},{4,12},{8,0},{12,4},{1,9},{5,13},{9,1},{13,5},{2,10},{6,14},... | collective-permute-start | bytes 786440 | tf_op jit(solution)/shard_map/ppermute | solution.py:212
  86.8 4.8 %copy-start.19 = (bf16[128,2,256]{2,1,0:T(2,128)(2,1)}, bf16[128,2,256]{2,1,0:T(2,128)(2,1)S(1)}, u32[]{:S(2)}) copy-start(bf16[128,2,256]{2,1,0:T(2,128)(2,1)S(1)} %collective-permute-done.28.refs_12_) | copy-start | bytes 393220
  102.4 11.4 %collective-permute-start.1 = (bf16[5,64,2048]{2,1,0:T(8,128)(2,1)S(1)}, bf16[5,64,2048]{2,1,0:T(8,128)(2,1)S(1)}, u32[]{:S(2)}, u32[]{:S(2)}) collective-permute-start(bf16[5,64,2048]{2,1,0:T(8,128)(2,1)S(1)} %get-tuple-element.66.refs_4_), channel_id=1, source_target_pairs={{0,4},{4,0},{8,12},{12,8},{1,5},{5,1},{9,13},{13,9},{2,6},{6,2},{1... | collective-permute-start | bytes 3932168 | tf_op jit(solution)/shard_map/cond/branch_1_fun/ppermute | solution.py:212
  103.8 8.1 %collective-permute-start.2 = (bf16[64,2048]{1,0:T(8,128)(2,1)}, bf16[64,2048]{1,0:T(8,128)(2,1)S(1)}, u32[]{:S(2)}, u32[]{:S(2)}) collective-permute-start(bf16[64,2048]{1,0:T(8,128)(2,1)} %get-tuple-element.67), channel_id=1, source_target_pairs={{0,8},{4,12},{8,0},{12,4},{1,9},{5,13},{9,1},{13,5},{2,10},{6,14},... | collective-permute-start | bytes 786440 | tf_op jit(solution)/shard_map/cond/branch_1_fun/ppermute | solution.py:212
  111.8 3.2 %copy-start.15 = (bf16[64,2048]{1,0:T(8,128)(2,1)}, bf16[64,2048]{1,0:T(8,128)(2,1)S(1)}, u32[]{:S(2)}) copy-start(bf16[64,2048]{1,0:T(8,128)(2,1)S(1)} %collective-permute-done.2.refs_6_) | copy-start | bytes 786436 | tf_op jit(solution)/shard_map/cond
  111.8 2.0 %collective-permute-start.3 = (bf16[64,2048]{1,0:T(8,128)(2,1)S(1)}, bf16[64,2048]{1,0:T(8,128)(2,1)S(1)}, u32[]{:S(2)}, u32[]{:S(2)}) collective-permute-start(bf16[64,2048]{1,0:T(8,128)(2,1)S(1)} %collective-permute-done.2.refs_6_), channel_id=1, source_target_pairs={{0,4},{4,0},{8,12},{12,8},{1,5},{5,1},{9,13},{13,9},{2,6},{6,2},{1... | collective-permute-start | bytes 786440 | tf_op jit(solution)/shard_map/cond/branch_1_fun/ppermute | solution.py:212
  113.9 1.2 copy-start.17
  113.9 1.1 copy-start.2
where the time goes:
time: 119 us; the launch traced here: 118 us
  waiting for transfers between devices  52 us (44%)
  Pallas kernels  28.8 us (24%)
  starting transfers between devices  21.9 us (18%)
  local copies, waits for them, and re-layouts  7.43 us (6%)
  matrix products  5.76 us (5%)
  between operations  1.32 us (1%)
    ppermute x16, waiting for transfers between devices, partner(): lax.ppermute(array, 'replica', [(i, i ^ mask) for i in range(lax.axis_siz...  46.8 us
    ppermute x16, starting transfers between devices, partner(): lax.ppermute(array, 'replica', [(i, i ^ mask) for i in range(lax.axis_siz...  13.6 us
    pallas_call x3, Pallas kernels, copy_call(): pl.pallas_call(kernel, out_shape=[jax.ShapeDtypeStruct(shape, arrays[0].d...  12.1 us
    ppermute x6, starting transfers between devices, shifted(): lax.ppermute(array, 'tensor', [(i, (i + step) % size) for i in range(size)])  8.32 us
    pallas_call x1, Pallas kernels, pairs_layer(): pl.pallas_call(functools.partial(attend_kernel, spans, masks, resident, s...  7.87 us
    pallas_call x1, Pallas kernels, pairs_layer(): pl.pallas_call(functools.partial(project_kernel, spans, slot_total, resid...  6.88 us
    dot_general x1, matrix products, pairs_layer(): jnp.einsum('md,dgc->gmc', full, w_kv, preferred_element_type=jnp.float32)  5.76 us
    ppermute x6, waiting for transfers between devices, shifted(): lax.ppermute(array, 'tensor', [(i, (i + step) % size) for i in range(size)])  5.17 us
  transfers between devices with their start and end apart: 22, of which 7 were waited for; matrix products, arithmetic and copies ran while one was open for 7% of the time, Pallas kernels for 14%

commit v1 on v0

--- a/solution.py
+++ b/solution.py
@@ -218,6 +218,7 @@
 
 
 HEAD_UNITS = 5
+EARLY_UNITS = 4
 SMEM = pl.BlockSpec(memory_space=pltpu.SMEM)
 VMEM = pl.BlockSpec(memory_space=pltpu.VMEM)
 
@@ -241,31 +242,34 @@
     return items
 
 
-def staged(moves, buffer, sems):
+def staged(groups):
     def when(condition, action):
         if condition is None:
             action()
         else:
             pl.when(condition)(action)
 
-    def begin(at, sources):
+    def begin(at, sources, buffer, sems):
         for condition, source in sources:
             when(condition, pltpu.make_async_copy(source, buffer.at[at], sems.at[0, at]).start)
 
-    def forward(at, targets):
+    def forward(at, targets, buffer, sems):
         pltpu.make_async_copy(buffer.at[at], buffer.at[at], sems.at[0, at]).wait()
         for condition, target in targets:
             when(condition, pltpu.make_async_copy(buffer.at[at], target, sems.at[1, at]).start)
 
-    def finish(at):
+    def finish(at, buffer, sems):
         pltpu.make_async_copy(buffer.at[at], buffer.at[at], sems.at[1, at]).wait()
 
-    for at, (condition, sources, _) in enumerate(moves):
-        when(condition, functools.partial(begin, at, sources))
-    for at, (condition, _, targets) in enumerate(moves):
-        when(condition, functools.partial(forward, at, targets))
-    for at, (condition, _, _) in enumerate(moves):
-        when(condition, functools.partial(finish, at))
+    for moves, buffer, sems in groups:
+        for at, (condition, sources, _) in enumerate(moves):
+            when(condition, functools.partial(begin, at, sources, buffer, sems))
+    for moves, buffer, sems in groups:
+        for at, (condition, _, targets) in enumerate(moves):
+            when(condition, functools.partial(forward, at, targets, buffer, sems))
+    for moves, buffer, sems in groups:
+        for at, (condition, _, _) in enumerate(moves):
+            when(condition, functools.partial(finish, at, buffer, sems))
 
 
 def collect_kernel(spans, slot_total, masks, *refs):
@@ -295,21 +299,12 @@
                 for copy_id, slot in enumerate(held)
             ]
         )
-    for moves, buffer, sems in zip(groups, buffers, semaphores):
-        for at, (_, ((_, source),), _) in enumerate(moves):
-            pltpu.make_async_copy(source, buffer.at[at], sems.at[0, at]).start()
-    for moves, buffer, sems in zip(groups, buffers, semaphores):
-        for at, (_, _, ((_, target),)) in enumerate(moves):
-            pltpu.make_async_copy(buffer.at[at], buffer.at[at], sems.at[0, at]).wait()
-            pltpu.make_async_copy(buffer.at[at], target, sems.at[1, at]).start()
-    for moves, buffer, sems in zip(groups, buffers, semaphores):
-        for at in range(len(moves)):
-            pltpu.make_async_copy(buffer.at[at], buffer.at[at], sems.at[1, at]).wait()
+    staged(list(zip(groups, buffers, semaphores)))
 
 
 def pack_kernel(spans, slot_total, *refs):
     (me_ref, holder, dest, store_a, store_b, sibling_a, sibling_b) = refs[:7]
-    across_b, head, *tails = refs[7:-5]
+    across_b, *units = refs[7:-5]
     extra, buffer_b, buffer_a, sems_b, sems_a = refs[-5:]
     me = me_ref[0]
     core = me % 2
@@ -317,7 +312,7 @@
     items = crossing(holder, dest, spans, slot_total, chip)
     moves_b, moves_a = [], []
     for copy_id in range(COPIES):
-        row = wanted_by(holder, dest, spans, 2 * chip + core, copy_id)
+        row = jnp.where(core == 0, items[2 * copy_id][2], items[2 * copy_id + 1][2])
         own = row // slot_total == me
         sources = [
             (own, store_b.at[row % slot_total]),
@@ -330,72 +325,75 @@
             (own, store_a.at[row % slot_total, core]),
             (jnp.logical_not(own), sibling_a.at[copy_id, core]),
         ]
-        targets = [(unit < HEAD_UNITS, head.at[jnp.minimum(unit, HEAD_UNITS - 1)])]
-        for i, tail in enumerate(tails):
-            if at >= HEAD_UNITS + i:
-                targets.append((unit == HEAD_UNITS + i, tail))
+        targets = [(unit == i, units[i]) for i in range(at + 1)]
         moves_a.append((crosses, sources, targets))
     count = items[-1][4] + items[-1][3].astype(jnp.int32)
-    extra[0] = jnp.clip(count - HEAD_UNITS, 0, len(tails))
-    staged(moves_b, buffer_b, sems_b)
-    staged(moves_a, buffer_a, sems_a)
-
-
-def place_down_kernel(spans, slot_total, tail_units, *refs):
-    (me_ref, holder, dest, sibling_a, head, head_other) = refs[:6]
-    tails, tails_other = refs[6 : 6 + tail_units], refs[6 + tail_units : 6 + 2 * tail_units]
+    extra[0] = jnp.clip(count - HEAD_UNITS, 0, len(units) - HEAD_UNITS)
+    staged([(moves_b, buffer_b, sems_b), (moves_a, buffer_a, sems_a)])
+
+
+def place_kernel(spans, slot_total, first_unit, unit_count, *refs):
+    (me_ref, holder, dest, earlier) = refs[:4]
+    got, other = refs[4 : 4 + unit_count], refs[4 + unit_count : 4 + 2 * unit_count]
     out, buffer, sems = refs[-3:]
     me = me_ref[0]
     core = me % 2
     items = crossing(holder, dest, spans, slot_total, me // 2)
     moves = []
     for copy_id in range(COPIES):
-        first, second = items[2 * copy_id], items[2 * copy_id + 1]
-        crosses = jnp.where(core == 0, first[3].astype(jnp.int32), second[3].astype(jnp.int32))
-        unit = jnp.where(core == 0, first[4], second[4])
-        near = crosses == 0
-        for side, (group, last) in enumerate(((head, tails), (head_other, tails_other))):
-            half = core if side == 0 else 1 - core
-            early = jnp.logical_and(crosses != 0, unit < HEAD_UNITS)
-            sources = [
-                (near, sibling_a.at[copy_id, half]),
-                (early, group.at[jnp.minimum(unit, HEAD_UNITS - 1)]),
-            ]
-            for i, tail in enumerate(last):
-                sources.append((jnp.logical_and(crosses != 0, unit == HEAD_UNITS + i), tail))
-            moves.append((None, sources, [(None, out.at[copy_id, half])]))
-    staged(moves, buffer, sems)
-
-
-def copy_call(kernel, tables, arrays, shapes, scratch, scalars=()):
-    hbm = pl.BlockSpec(memory_space=pl.ANY)
+        one, two = items[2 * copy_id], items[2 * copy_id + 1]
+        crosses = jnp.where(core == 0, one[3].astype(jnp.int32), two[3].astype(jnp.int32)) != 0
+        unit = jnp.where(core == 0, one[4], two[4])
+        possible = [i for i in range(unit_count) if first_unit + i <= 2 * copy_id + 1]
+        if first_unit and not possible:
+            continue
+        for half, arrays in ((core, got), (1 - core, other)):
+            sources = []
+            if first_unit:
+                active = jnp.logical_and(crosses, unit >= first_unit)
+            else:
+                near = jnp.logical_not(crosses)
+                active = jnp.logical_or(near, unit < unit_count)
+                sources.append((near, earlier.at[copy_id, half]))
+            for i in possible:
+                hit = jnp.logical_and(crosses, unit == first_unit + i)
+                sources.append((hit, arrays[i]))
+            moves.append((active, sources, [(None, out.at[copy_id, half])]))
+    staged([(moves, buffer, sems)])
+
+
+def copy_call(kernel, tables, arrays, shapes, scratch, scalars=(), aliases=None):
+    hbm = pl.BlockSpec(memory_space=pltpu.HBM)
     return pl.pallas_call(
         kernel,
-        out_shape=[jax.ShapeDtypeStruct(shape, arrays[0].dtype) for shape in shapes]
+        out_shape=[pltpu.HBM(shape, arrays[0].dtype) for shape in shapes]
         + [jax.ShapeDtypeStruct(shape, jnp.int32) for shape in scalars],
         in_specs=[SMEM] * len(tables) + [hbm] * len(arrays),
         out_specs=[hbm] * len(shapes) + [SMEM] * len(scalars),
         scratch_shapes=[pltpu.VMEM(shape, arrays[0].dtype) for shape in scratch]
         + [pltpu.SemaphoreType.DMA((2, shape[0])) for shape in scratch],
+        input_output_aliases=aliases or {},
     )(*tables, *arrays)
 
 
 def project_kernel(spans, slot_total, resident, steps, masks, *refs):
     (me_ref, resident_adapter, arrival_adapter, holder, dest, hidden, *others) = refs[: 6 + len(masks)]
-    store, out, left, adapters = refs[-4:]
+    store, *outs, left, adapters, sums = refs[6 + len(masks) :]
     me = me_ref[0]
-    adapter = pl.program_id(0)
+    group = pl.program_id(0)
     base = hidden.shape[0]
     block = others[0].shape[0]
-
-    @pl.when(adapter == 0)
+    width = sums.shape[1]
+    per_step = store.shape[1] // width
+
+    @pl.when(group == 0)
     def _():
         left[0:base] = hidden[...]
         for i, other in enumerate(others):
             left[base + i * block : base + (i + 1) * block] = other[...]
-        out[...] = jnp.zeros_like(out)
-        ids = lax.broadcasted_iota(jnp.int32, out.shape, 0) // steps
-        own = jnp.full(out.shape, -1, jnp.int32)
+        sums[...] = jnp.zeros_like(sums)
+        ids = lax.broadcasted_iota(jnp.int32, sums.shape, 0) // steps
+        own = jnp.full(sums.shape, -1, jnp.int32)
         for slot in range(resident):
             own = jnp.where(ids == slot, resident_adapter[me * resident + slot], own)
         for i, mask in enumerate((0,) + masks):
@@ -404,9 +402,9 @@
             for a in range(arrival_adapter.shape[0]):
                 chosen = arrival_adapter[a, replica]
                 row = jnp.int32(0)
-                for copy_id in range(COPIES):
-                    wanted = wanted_by(holder, dest, spans, replica, copy_id)
-                    row += jnp.where(chosen == copy_id, wanted, 0)
+                for span in range(spans):
+                    at = chosen * spans + span
+                    row += jnp.where(dest[0, at] == replica, holder[at], 0)
                 here = jnp.where(row // slot_total == me, row % slot_total, -1)
                 own = jnp.where(ids == first + a, here, own)
         adapters[...] = own
@@ -414,7 +412,15 @@
     product = lax.dot_general(
         left[...], store[0], (((1,), (1,)), ((), ())), preferred_element_type=jnp.float32
     )
-    out[...] += jnp.where(adapters[...] == adapter, product, 0.0)
+    for i in range(per_step):
+        hit = adapters[...] == group * per_step + i
+        sums[...] += jnp.where(hit, product[:, i * width : (i + 1) * width], 0.0)
+
+    @pl.when(group == pl.num_programs(0) - 1)
+    def _():
+        outs[0][...] = sums[0:base]
+        for i, out in enumerate(outs[1:]):
+            out[...] = sums[base + i * block : base + (i + 1) * block]
 
 
 def gather_kernel(shard_ref, *refs):
@@ -428,9 +434,9 @@
 
 def attend_kernel(spans, masks, resident, steps, kv_heads, head_length, *refs):
     (me_ref, lengths, arrival_from, arrival_slot, resident_adapter, arrival_adapter) = refs[:6]
-    holder, dest, total, *returned = refs[6 : 9 + len(masks)]
-    came = refs[9 + len(masks) : 9 + 2 * len(masks)]
-    store_b, sibling_b, across_b, base, queries, cache = refs[9 + 2 * len(masks) : -5]
+    holder, dest, *parts = refs[6 : -11 - len(masks)]
+    came = refs[-11 - len(masks) : -11]
+    store_b, sibling_b, across_b, base, queries, cache = refs[-11:-5]
     out, new_kv, arrived, installed_b, fresh_ref = refs[-5:]
     me = me_ref[0]
     arrive = arrival_from.shape[0]
@@ -467,11 +473,10 @@
         def _():
             installed_b[copy_id] = across_b[copy_id]
 
-    first = resident * steps
-    last = total[first:row_count]
-    for ref in returned:
-        last = last + ref[...]
-    down = jnp.concatenate([total[0:first], last], axis=0).astype(jnp.bfloat16)
+    total = parts[0][...]
+    for part in parts[1:]:
+        total = total + part[...]
+    down = total.astype(jnp.bfloat16)
 
     ids = lax.broadcasted_iota(jnp.int32, (row_count, 1), 0) // steps
     adapters = jnp.zeros((row_count, 1), jnp.int32)
@@ -633,18 +638,22 @@
     around = [rows] + [shifted(rows, step) for step in range(1, shards)]
 
     line_count = padded + len(masks) * block
-    partial = pl.pallas_call(
+    per_step = 2 if slot_total % 2 == 0 else 1
+    partial, *sent = pl.pallas_call(
         functools.partial(project_kernel, spans, slot_total, resident, steps, masks),
-        out_shape=jax.ShapeDtypeStruct((line_count, 2 * rank), jnp.float32),
-        grid=(slot_total,),
+        out_shape=[jax.ShapeDtypeStruct((padded, 2 * rank), jnp.float32)]
+        + [jax.ShapeDtypeStruct((block, 2 * rank), jnp.float32)] * len(masks),
+        grid=(slot_total // per_step,),
         in_specs=[SMEM] * 5
         + [pl.BlockSpec((padded, features), lambda i: (0, 0))]
         + [pl.BlockSpec((block, features), lambda i: (0, 0))] * len(masks)
-        + [pl.BlockSpec((1, 2 * rank, features), lambda i: (i, 0, 0))],
-        out_specs=pl.BlockSpec((line_count, 2 * rank), lambda i: (0, 0)),
+        + [pl.BlockSpec((1, per_step * 2 * rank, features), lambda i: (i, 0, 0))],
+        out_specs=[pl.BlockSpec((padded, 2 * rank), lambda i: (0, 0))]
+        + [pl.BlockSpec((block, 2 * rank), lambda i: (0, 0))] * len(masks),
         scratch_shapes=[
             pltpu.VMEM((line_count, features), hidden.dtype),
             pltpu.VMEM((line_count, 2 * rank), jnp.int32),
+            pltpu.VMEM((line_count, 2 * rank), jnp.float32),
         ],
         name="project",
     )(
@@ -655,29 +664,28 @@
         dest_table,
         rows,
         *other_rows,
-        store_a.reshape(slot_total, 2 * rank, features),
-    )
+        store_a.reshape(slot_total // per_step, per_step * 2 * rank, features),
+    )
+    returned = [partner(array, mask) for array, mask in zip(sent, masks)]
+    last = partial[first:]
+    for array in returned:
+        last = last + array
+    partial = jnp.concatenate([partial[:first], last])
     parts = [partial] + [shifted(partial, step) for step in range(1, shards)]
 
     unit_shape = row_a[1:]
-    tail_units = 2 * COPIES - HEAD_UNITS
-    across_b, head, *tails, extra = copy_call(
+    unit_total = 2 * COPIES
+    across_b, *units, extra = copy_call(
         functools.partial(pack_kernel, spans, slot_total),
         (me_table, hot_holder, dest_table),
         (store_a, store_b, sibling_a, sibling_b),
-        [(COPIES,) + row_b, (HEAD_UNITS,) + unit_shape] + [unit_shape] * tail_units,
-        [(COPIES,) + row_b, (2 * COPIES,) + unit_shape],
+        [(COPIES,) + row_b] + [unit_shape] * unit_total,
+        [(COPIES,) + row_b, (unit_total,) + unit_shape],
         [(1,)],
     )
     across_b = partner(across_b, 2)
-    head = partner(head, 2)
-    total = parts[0]
-    for array in parts[1:]:
-        total = total + array
-    returned = [
-        partner(total[padded + i * block : padded + (i + 1) * block], mask)
-        for i, mask in enumerate(masks)
-    ]
+    got = [partner(array, 2) for array in units[:EARLY_UNITS]]
+    got += [partner(array, 2) for array in units[EARLY_UNITS:HEAD_UNITS]]
 
     full = pl.pallas_call(
         gather_kernel,
@@ -696,7 +704,7 @@
             jax.ShapeDtypeStruct((arrive,) + kv_cache.shape[1:], jnp.bfloat16),
             jax.ShapeDtypeStruct((COPIES, 2 * rank, columns), jnp.bfloat16),
         ],
-        in_specs=[SMEM] * 8 + [VMEM] * (1 + 2 * len(masks) + 6),
+        in_specs=[SMEM] * 8 + [VMEM] * (shards + len(masks) + 6),
         out_specs=[VMEM] * 4,
         scratch_shapes=[pltpu.VMEM((padded, kv_heads * head_pair), jnp.float32)],
         name="attend",
@@ -709,8 +717,7 @@
         choice_table,
         hot_holder,
         dest_table,
-        total,
-        *returned,
+        *parts,
         *came,
         store_b.reshape(slot_total, 2 * rank, columns),
         sibling_b.reshape(COPIES, 2 * rank, columns),
@@ -720,28 +727,39 @@
         kv_cache,
     )
     installed_b = installed_b.reshape((COPIES,) + row_b)
-    head, attn_out, new_kv = lax.optimization_barrier((head, attn_out, new_kv))
     attn_out = attn_out.reshape(slots, steps, heads * head_length)
     new_kv = new_kv[:used].reshape(slots, steps, kv_heads, head_pair)
 
-    def finish(units):
-        def branch(sibling_a, head, *tails):
-            got = [partner(array, 2) for array in tails[:units]]
-            head_other = partner(head, 1)
-            other = [partner(array, 1) for array in got]
-            (placed,) = copy_call(
-                functools.partial(place_down_kernel, spans, slot_total, units),
-                (me_table, hot_holder, dest_table),
-                (sibling_a, head, head_other, *got, *other),
+    tables = (me_table, hot_holder, dest_table)
+    other = [partner(array, 1) for array in got[:EARLY_UNITS]]
+    (placed,) = copy_call(
+        functools.partial(place_kernel, spans, slot_total, 0, EARLY_UNITS),
+        tables,
+        (sibling_a, *got[:EARLY_UNITS], *other),
+        [(COPIES,) + row_a],
+        [(unit_total,) + unit_shape],
+    )
+
+    def finish(count):
+        def branch(placed, *arrays):
+            late = list(arrays[: HEAD_UNITS - EARLY_UNITS])
+            late += [partner(array, 2) for array in arrays[len(late) :][:count]]
+            other = [partner(array, 1) for array in late]
+            return copy_call(
+                functools.partial(place_kernel, spans, slot_total, EARLY_UNITS, len(late)),
+                tables,
+                (placed, *late, *other),
                 [(COPIES,) + row_a],
-                [(2 * COPIES,) + unit_shape],
-            )
-            return placed
+                [(unit_total,) + unit_shape],
+                aliases={len(tables): 0},
+            )[0]
 
         return branch
 
-    branches = [finish(units) for units in range(tail_units + 1)]
-    installed_a = lax.switch(extra[0], branches, sibling_a, head, *tails)
+    branches = [finish(count) for count in range(unit_total - HEAD_UNITS + 1)]
+    installed_a = lax.switch(
+        extra[0], branches, placed, *got[EARLY_UNITS:], *units[HEAD_UNITS:]
+    )
     return (attn_out, new_kv, arrived, installed_a, installed_b)
 
 

time: 119 us -> 108 us (0.908)
  the two profiles are of different devices: /device:TPU:7 before, /device:TPU:5 now
where the time goes in v1:
time: 108 us; the launch traced here: 107 us
  starting transfers between devices  40.2 us (37%)
  Pallas kernels  28 us (26%)
  waiting for transfers between devices  23.7 us (22%)
  local copies, waits for them, and re-layouts  7.4 us (7%)
  matrix products  5.76 us (5%)
  between operations  1.56 us (1%)
    ppermute x24, starting transfers between devices, partner(): lax.ppermute(array, 'replica', [(i, i ^ mask) for i in range(lax.axis_siz...  34.5 us
    ppermute x24, waiting for transfers between devices, partner(): lax.ppermute(array, 'replica', [(i, i ^ mask) for i in range(lax.axis_siz...  19 us
    pallas_call x4, Pallas kernels, copy_call(): pl.pallas_call(kernel, out_shape=[pltpu.HBM(shape, arrays[0].dtype) for s...  13.4 us
    pallas_call x1, Pallas kernels, pairs_layer(): pl.pallas_call(functools.partial(attend_kernel, spans, masks, resident, s...  7.85 us
    dot_general x1, matrix products, pairs_layer(): jnp.einsum('md,dgc->gmc', full, w_kv, preferred_element_type=jnp.float32)  5.76 us
    ppermute x6, starting transfers between devices, shifted(): lax.ppermute(array, 'tensor', [(i, (i + step) % size) for i in range(size)])  5.61 us
    pallas_call x1, Pallas kernels, pairs_layer(): pl.pallas_call(functools.partial(project_kernel, spans, slot_total, resid...  4.88 us
    ppermute x6, waiting for transfers between devices, shifted(): lax.ppermute(array, 'tensor', [(i, (i + step) % size) for i in range(size)])  4.69 us
  transfers between devices with their start and end apart: 30, of which 12 were waited for; matrix products, arithmetic and copies ran while one was open for 10% of the time, Pallas kernels for 20%

profile of v1, /device:TPU:5, one launch (start us, length us, event | category | flops | bytes accessed | tf_op | source)
XLA Modules:
  0.0 107.3 jit_solution(15179676865750686468)
XLA Ops:
  0.7 4.2 %shard_map.164 = (bf16[128,2,256]{2,1,0:T(2,128)(2,1)}, bf16[128,2,256]{2,1,0:T(2,128)(2,1)}, bf16[128,2,256]{2,1,0:T(2,128)(2,1)}, bf16[4,2,64,256]{3,2,1,0:T(8,128)(2,1)}, bf16[4,2,64,2048]{3,2,1,0:T(8,128)(2,1)}) custom-call(s32[1]{0:T(128)} %bitcast.refs_0_, s32[2,4]{1,0:T(2,128)} %bitcast.33, s32[2,4]{1,0:T(2,128)} %bitcast.35, s32[16]{0:T(128)} %refs_1_.7, ...), custom_call_target="tpu_custom_call" | custom-call | tf_op jit(solution)/shard_map/pallas_call | solution.py:367
  4.9 0.6 collective-permute-start.29
  5.5 1.3 %collective-permute-start.18 = (bf16[8,2048]{1,0:T(8,128)(2,1)S(1)}, bf16[8,2048]{1,0:T(8,128)(2,1)S(1)}, u32[]{:S(2)}, u32[]{:S(2)}) collective-permute-start(bf16[8,2048]{1,0:T(8,128)(2,1)S(1)} %pad_slice_fusion), channel_id=1, source_target_pairs={{0,12},{4,8},{8,4},{12,0},{1,13},{5,9},{9,5},{13,1},{2,14},{6,10},... | collective-permute-start | bytes 98312 | tf_op jit(solution)/shard_map/ppermute | solution.py:212
  6.8 0.2 collective-permute-start.17
  7.0 0.7 collective-permute-start.16
  7.7 0.7 pad.4.refs_5_.refs_0_
  8.4 0.5 collective-permute-done.18.refs_8_
  8.9 0.7 collective-permute-done.17.refs_7_
  9.6 0.6 copy-done.38
  10.2 0.0 copy-done.39
  10.2 0.0 copy-start.48
  10.3 4.9 %project.1 = (f32[32,128]{1,0:T(8,128)}, f32[8,128]{1,0:T(8,128)}, f32[8,128]{1,0:T(8,128)}, f32[8,128]{1,0:T(8,128)}) custom-call(s32[1]{0:T(128)} %bitcast.refs_0_, s32[48]{0:T(128)} %refs_4_.5, s32[2,4]{1,0:T(2,128)} %bitcast.37, s32[16]{0:T(128)S(1)} %copy-done.36, s32[1,16]{1,0:T(1,128)S(1)} %bitcast.25, bf16[32,2048]{1,0:T(8,128)(2,1)} %pad.4.refs_5_.refs_0_, ...), custom_call_target="tpu_custom_call" | custom-call | tf_op jit(solution)/shard_map/project/pallas_call | solution.py:642
  15.1 1.7 %collective-permute-start.19 = (f32[8,128]{1,0:T(8,128)}, f32[8,128]{1,0:T(8,128)S(1)}, u32[]{:S(2)}, u32[]{:S(2)}) collective-permute-start(f32[8,128]{1,0:T(8,128)} %get-tuple-element.112), channel_id=1, source_target_pairs={{0,4},{4,0},{8,12},{12,8},{1,5},{5,1},{9,13},{13,9},{2,6},{6,2},{1... | collective-permute-start | bytes 12296 | tf_op jit(solution)/shard_map/ppermute | solution.py:212
  16.8 0.1 collective-permute-start.20
  16.9 1.6 %collective-permute-start.21 = (f32[8,128]{1,0:T(8,128)}, f32[8,128]{1,0:T(8,128)S(1)}, u32[]{:S(2)}, u32[]{:S(2)}) collective-permute-start(f32[8,128]{1,0:T(8,128)} %get-tuple-element.114), channel_id=1, source_target_pairs={{0,12},{4,8},{8,4},{12,0},{1,13},{5,9},{9,5},{13,1},{2,14},{6,10},... | collective-permute-start | bytes 12296 | tf_op jit(solution)/shard_map/ppermute | solution.py:212
  18.5 3.3 %collective-permute-start.33 = (bf16[32,2048]{1,0:T(8,128)(2,1)S(1)}, bf16[32,2048]{1,0:T(8,128)(2,1)S(1)}, u32[]{:S(2)}, u32[]{:S(2)}) collective-permute-start(bf16[32,2048]{1,0:T(8,128)(2,1)S(1)} %copy-done.1), channel_id=1, source_target_pairs={{0,3},{1,0},{2,1},{3,2},{4,7},{5,4},{6,5},{7,6},{8,11},{9,8},{10,9... | collective-permute-start | bytes 393224 | tf_op jit(solution)/shard_map/ppermute | solution.py:217
  21.9 0.7 slice.15
  22.6 0.4 collective-permute-start.28
  23.0 0.0 collective-permute-done.20
  23.0 0.0 collective-permute-done.21
  23.0 0.7 add_add_fusion
  23.7 0.6 collective-permute-start.24
  24.4 2.0 %collective-permute-done.24.refs_11_ = f32[32,128]{1,0:T(8,128)S(1)} collective-permute-done((f32[32,128]{1,0:T(8,128)S(1)}, f32[32,128]{1,0:T(8,128)S(1)}, u32[]{:S(2)}, u32[]{:S(2)}) %collective-permute-start.24) | collective-permute-done | bytes 16416 | tf_op jit(solution)/shard_map/ppermute | solution.py:217
  26.3 1.5 %collective-permute-done.23.refs_10_ = f32[32,128]{1,0:T(8,128)S(1)} collective-permute-done((f32[32,128]{1,0:T(8,128)S(1)}, f32[32,128]{1,0:T(8,128)S(1)}, u32[]{:S(2)}, u32[]{:S(2)}) %collective-permute-start.23) | collective-permute-done | bytes 16416 | tf_op jit(solution)/shard_map/ppermute | solution.py:217
  27.8 1.7 %collective-permute-start.32 = (bf16[32,2048]{1,0:T(8,128)(2,1)S(1)}, bf16[32,2048]{1,0:T(8,128)(2,1)S(1)}, u32[]{:S(2)}, u32[]{:S(2)}) collective-permute-start(bf16[32,2048]{1,0:T(8,128)(2,1)S(1)} %copy-done.1), channel_id=1, source_target_pairs={{0,2},{1,3},{2,0},{3,1},{4,6},{5,7},{6,4},{7,5},{8,10},{9,11},{10,... | collective-permute-start | bytes 393224 | tf_op jit(solution)/shard_map/ppermute | solution.py:217
  29.5 1.2 %collective-permute-done.22.refs_9_ = f32[32,128]{1,0:T(8,128)S(1)} collective-permute-done((f32[32,128]{1,0:T(8,128)S(1)}, f32[32,128]{1,0:T(8,128)S(1)}, u32[]{:S(2)}, u32[]{:S(2)}) %collective-permute-start.22) | collective-permute-done | bytes 16416 | tf_op jit(solution)/shard_map/ppermute | solution.py:217
  30.7 2.7 %collective-permute-start.25 = (bf16[128,2,256]{2,1,0:T(2,128)(2,1)}, bf16[128,2,256]{2,1,0:T(2,128)(2,1)S(1)}, u32[]{:S(2)}, u32[]{:S(2)}) collective-permute-start(bf16[128,2,256]{2,1,0:T(2,128)(2,1)} %get-tuple-element.115), channel_id=1, source_target_pairs={{0,4},{4,0},{8,12},{12,8},{1,5},{5,1},{9,13},{13,9},{2,6},{6,2},{1... | collective-permute-start | bytes 393224 | tf_op jit(solution)/shard_map/ppermute | solution.py:212
  33.4 0.0 collective-permute-done.28.refs_6_
  33.4 0.5 collective-permute-start.26
  33.9 1.3 %collective-permute-start.27 = (bf16[128,2,256]{2,1,0:T(2,128)(2,1)S(1)}, bf16[128,2,256]{2,1,0:T(2,128)(2,1)S(1)}, u32[]{:S(2)}, u32[]{:S(2)}) collective-permute-start(bf16[128,2,256]{2,1,0:T(2,128)(2,1)S(1)} %copy-done.48), channel_id=1, source_target_pairs={{0,12},{4,8},{8,4},{12,0},{1,13},{5,9},{9,5},{13,1},{2,14},{6,10},... | collective-permute-start | bytes 393224 | tf_op jit(solution)/shard_map/ppermute | solution.py:212
  35.2 3.8 %shard_map.165 = (bf16[4,2,64,256]{3,2,1,0:T(8,128)(2,1)}, bf16[64,2048]{1,0:T(8,128)(2,1)}, bf16[64,2048]{1,0:T(8,128)(2,1)}, bf16[64,2048]{1,0:T(8,128)(2,1)},...) custom-call(s32[1]{0:T(128)} %bitcast.refs_0_, ...), custom_call_target="tpu_custom_call" | custom-call | tf_op jit(solution)/shard_map/pallas_call | solution.py:367
  39.1 1.2 %collective-permute-start.30 = (bf16[4,2,64,256]{3,2,1,0:T(8,128)(2,1)}, bf16[4,2,64,256]{3,2,1,0:T(8,128)(2,1)S(1)}, u32[]{:S(2)}, u32[]{:S(2)}) collective-permute-start(bf16[4,2,64,256]{3,2,1,0:T(8,128)(2,1)} %get-tuple-element.120), channel_id=1, source_target_pairs={{0,8},{4,12},{8,0},{12,4},{1,9},{5,13},{9,1},{13,5},{2,10},{6,14},... | collective-permute-start | bytes 786440 | tf_op jit(solution)/shard_map/ppermute | solution.py:212
  40.3 0.3 collective-permute-start.35
  40.7 1.1 %collective-permute-start.36 = (bf16[64,2048]{1,0:T(8,128)(2,1)}, bf16[64,2048]{1,0:T(8,128)(2,1)S(1)}, u32[]{:S(2)}, u32[]{:S(2)}) collective-permute-start(bf16[64,2048]{1,0:T(8,128)(2,1)} %get-tuple-element.127), channel_id=1, source_target_pairs={{0,8},{4,12},{8,0},{12,4},{1,9},{5,13},{9,1},{13,5},{2,10},{6,14},... | collective-permute-start | bytes 786440 | tf_op jit(solution)/shard_map/ppermute | solution.py:212
  41.8 0.3 collective-permute-start.37
  42.1 1.1 %collective-permute-start.38 = (bf16[64,2048]{1,0:T(8,128)(2,1)}, bf16[64,2048]{1,0:T(8,128)(2,1)S(1)}, u32[]{:S(2)}, u32[]{:S(2)}) collective-permute-start(bf16[64,2048]{1,0:T(8,128)(2,1)} %get-tuple-element.129), channel_id=1, source_target_pairs={{0,8},{4,12},{8,0},{12,4},{1,9},{5,13},{9,1},{13,5},{2,10},{6,14},... | collective-permute-start | bytes 786440 | tf_op jit(solution)/shard_map/ppermute | solution.py:212
  43.3 1.9 %gather.1 = bf16[32,8192]{1,0:T(8,128)(2,1)} custom-call(s32[1]{0:T(128)} %bitcast.9.shard_ref, bf16[32,2048]{1,0:T(8,128)(2,1)} %pad.4.refs_5_.refs_0_, bf16[32,2048]{1,0:T(8,128)(2,1)} %copy-done.33, bf16[32,2048]{1,0:T(8,128)(2,1)} %copy-done.32, bf16[32,2048]{1,0:T(8,128)(2,1)} %copy-done.31), custom_call_target="tpu_custom_call" | custom-call | tf_op jit(solution)/shard_map/gather/pallas_call | solution.py:690
  45.2 0.8 collective-permute-done.30
  46.0 1.6 %collective-permute-start.34 = (bf16[64,2048]{1,0:T(8,128)(2,1)}, bf16[64,2048]{1,0:T(8,128)(2,1)S(1)}, u32[]{:S(2)}, u32[]{:S(2)}) collective-permute-start(bf16[64,2048]{1,0:T(8,128)(2,1)} %get-tuple-element.125), channel_id=1, source_target_pairs={{0,8},{4,12},{8,0},{12,4},{1,9},{5,13},{9,1},{13,5},{2,10},{6,14},... | collective-permute-start | bytes 786440 | tf_op jit(solution)/shard_map/ppermute | solution.py:212
  47.6 4.0 %collective-permute-done.35.refs_4_ = bf16[64,2048]{1,0:T(8,128)(2,1)S(1)} collective-permute-done((bf16[64,2048]{1,0:T(8,128)(2,1)}, bf16[64,2048]{1,0:T(8,128)(2,1)S(1)}, u32[]{:S(2)}, u32[]{:S(2)}) %collective-permute-start.35) | collective-permute-done | bytes 262176 | tf_op jit(solution)/shard_map/ppermute | solution.py:212
  51.6 3.8 %collective-permute-start.39 = (bf16[64,2048]{1,0:T(8,128)(2,1)S(1)}, bf16[64,2048]{1,0:T(8,128)(2,1)S(1)}, u32[]{:S(2)}, u32[]{:S(2)}) collective-permute-start(bf16[64,2048]{1,0:T(8,128)(2,1)S(1)} %collective-permute-done.35.refs_4_), channel_id=1, source_target_pairs={{0,4},{4,0},{8,12},{12,8},{1,5},{5,1},{9,13},{13,9},{2,6},{6,2},{1... | collective-permute-start | bytes 786440 | tf_op jit(solution)/shard_map/ppermute | solution.py:212
  55.5 1.8 %collective-permute-done.36.refs_5_ = bf16[64,2048]{1,0:T(8,128)(2,1)S(1)} collective-permute-done((bf16[64,2048]{1,0:T(8,128)(2,1)}, bf16[64,2048]{1,0:T(8,128)(2,1)S(1)}, u32[]{:S(2)}, u32[]{:S(2)}) %collective-permute-start.36) | collective-permute-done | bytes 262176 | tf_op jit(solution)/shard_map/ppermute | solution.py:212
  57.2 3.8 %collective-permute-start.40 = (bf16[64,2048]{1,0:T(8,128)(2,1)S(1)}, bf16[64,2048]{1,0:T(8,128)(2,1)S(1)}, u32[]{:S(2)}, u32[]{:S(2)}) collective-permute-start(bf16[64,2048]{1,0:T(8,128)(2,1)S(1)} %collective-permute-done.36.refs_5_), channel_id=1, source_target_pairs={{0,4},{4,0},{8,12},{12,8},{1,5},{5,1},{9,13},{13,9},{2,6},{6,2},{1... | collective-permute-start | bytes 786440 | tf_op jit(solution)/shard_map/ppermute | solution.py:212
  61.1 1.8 %collective-permute-done.37.refs_6_ = bf16[64,2048]{1,0:T(8,128)(2,1)S(1)} collective-permute-done((bf16[64,2048]{1,0:T(8,128)(2,1)}, bf16[64,2048]{1,0:T(8,128)(2,1)S(1)}, u32[]{:S(2)}, u32[]{:S(2)}) %collective-permute-start.37) | collective-permute-done | bytes 262176 | tf_op jit(solution)/shard_map/ppermute | solution.py:212
  62.8 3.8 %collective-permute-start.41 = (bf16[64,2048]{1,0:T(8,128)(2,1)S(1)}, bf16[64,2048]{1,0:T(8,128)(2,1)S(1)}, u32[]{:S(2)}, u32[]{:S(2)}) collective-permute-start(bf16[64,2048]{1,0:T(8,128)(2,1)S(1)} %collective-permute-done.37.refs_6_), channel_id=1, source_target_pairs={{0,4},{4,0},{8,12},{12,8},{1,5},{5,1},{9,13},{13,9},{2,6},{6,2},{1... | collective-permute-start | bytes 786440 | tf_op jit(solution)/shard_map/ppermute | solution.py:212
  66.7 1.8 %collective-permute-done.38.refs_7_ = bf16[64,2048]{1,0:T(8,128)(2,1)S(1)} collective-permute-done((bf16[64,2048]{1,0:T(8,128)(2,1)}, bf16[64,2048]{1,0:T(8,128)(2,1)S(1)}, u32[]{:S(2)}, u32[]{:S(2)}) %collective-permute-start.38) | collective-permute-done | bytes 262176 | tf_op jit(solution)/shard_map/ppermute | solution.py:212
  68.5 3.8 %collective-permute-start.42 = (bf16[64,2048]{1,0:T(8,128)(2,1)S(1)}, bf16[64,2048]{1,0:T(8,128)(2,1)S(1)}, u32[]{:S(2)}, u32[]{:S(2)}) collective-permute-start(bf16[64,2048]{1,0:T(8,128)(2,1)S(1)} %collective-permute-done.38.refs_7_), channel_id=1, source_target_pairs={{0,4},{4,0},{8,12},{12,8},{1,5},{5,1},{9,13},{13,9},{2,6},{6,2},{1... | collective-permute-start | bytes 786440 | tf_op jit(solution)/shard_map/ppermute | solution.py:212
  72.3 5.8 %fusion.2.refs_18_ = f32[2,32,256]{2,1,0:T(8,128)} fusion(bf16[8192,2,256]{2,1,0:T(2,128)(2,1)} %param.20, bf16[32,8192]{1,0:T(8,128)(2,1)} %gather.1), kind=kOutput, calls=%fused_computation.2 | convolution fusion | flops 268435456 | bytes 8978432 | tf_op jit(solution)/shard_map/md,dgc->gmc/dot_general | solution.py:697
  78.8 7.8 %attend.1 = (bf16[14,32,128]{2,1,0:T(8,128)(2,1)}, bf16[32,512]{1,0:T(8,128)(2,1)}, bf16[2,128,2,256]{3,2,1,0:T(2,128)(2,1)}, bf16[4,128,256]{2,1,0:T(8,128)(2,1)}) custom-call(s32[1]{0:T(128)} %bitcast.refs_0_, s32[48]{0:T(128)} %refs_1_.6, s32[2,4]{1,0:T(2,128)} %bitcast.34, s32[2,4]{1,0:T(2,128)} %bitcast.36, s32[48]{0:T(128)} %refs_4_.5, ...), custom_call_target="tpu_custom_call" | custom-call | tf_op jit(solution)/shard_map/attend/pallas_call | solution.py:699
  86.6 1.6 %reshape.54 = bf16[14,2,2048]{2,1,0:T(2,128)(2,1)} reshape(bf16[14,32,128]{2,1,0:T(8,128)(2,1)} %get-tuple-element.121) | data formatting | bytes 229376 | tf_op jit(solution)/shard_map/reshape | solution.py:730
  88.2 1.4 %reshape.55 = bf16[14,2,2,256]{3,2,1,0:T(2,128)(2,1)} reshape(bf16[28,512]{1,0:T(8,128)(2,1)} %bitcast.24) | data formatting | bytes 57344 | tf_op jit(solution)/shard_map/reshape | solution.py:731
  89.7 0.7 copy-done.8
  90.3 0.1 copy-done.9
  90.4 0.1 copy-done.10
  90.5 0.7 copy-done.12
  91.2 2.8 %shard_map.166 = bf16[4,2,64,2048]{3,2,1,0:T(8,128)(2,1)} custom-call(s32[1]{0:T(128)} %bitcast.refs_0_, s32[16]{0:T(128)S(1)} %copy-done.36, s32[1,16]{1,0:T(1,128)S(1)} %bitcast.28, bf16[4,2,64,2048]{3,2,1,0:T(8,128)(2,1)} %copy-done, bf16[64,2048]{1,0:T(8,128)(2,1)} %copy-done.3, bf16[64,2048]{1,0:T(8,128)(2,1)} %copy-done.4, bf16[64,2048]{1,0:T(8,128)(2,1)} %copy-done.6, ...), custom_call_target="tpu_custom_call" | custom-call | tf_op jit(solution)/shard_map/pallas_call | solution.py:367
  94.1 13.2 %conditional.1 = (bf16[4,2,64,2048]{3,2,1,0:T(8,128)(2,1)}) conditional(s32[]{:T(128)} %bitcast.13, (bf16[64,2048]{1,0:T(8,128)(2,1)S(1)}, s32[1]{0:T(128)}, s32[16]{0:T(128)S(1)}, s32[1,16]{1,0:T(1,128)S(1)}, bf16[4,2,64,2048]{3,2,1,0:T(8,128)(2,1)}) %tuple.33, (bf16[64,2048]{1,0:T(8,128)(2,1)S(1)}, ...), branch_computations={%region_0.1_spmd, %region_1.2_spmd, %region_2.3_spmd, %region_3.4_... | conditional | bytes 14680548 | solution.py:760
  94.1 0.6 collective-permute-start.1
  94.8 0.7 collective-permute-start.2
  95.4 6.5 %collective-permute-done.1.refs_5_ = bf16[64,2048]{1,0:T(8,128)(2,1)S(1)} collective-permute-done((bf16[64,2048]{1,0:T(8,128)(2,1)S(1)}, bf16[64,2048]{1,0:T(8,128)(2,1)S(1)}, u32[]{:S(2)}, u32[]{:S(2)}) %collective-permute-start.1) | collective-permute-done | bytes 262176 | tf_op jit(solution)/shard_map/cond/branch_1_fun/ppermute | solution.py:212
  101.9 1.0 collective-permute-start.3
  102.9 1.2 %collective-permute-done.3.refs_7_ = bf16[64,2048]{1,0:T(8,128)(2,1)S(1)} collective-permute-done((bf16[64,2048]{1,0:T(8,128)(2,1)S(1)}, bf16[64,2048]{1,0:T(8,128)(2,1)S(1)}, u32[]{:S(2)}, u32[]{:S(2)}) %collective-permute-start.3) | collective-permute-done | bytes 262176 | tf_op jit(solution)/shard_map/cond/branch_1_fun/ppermute | solution.py:212
  104.1 0.7 copy-done.26
  104.8 2.5 %branch_1_fun.1 = bf16[4,2,64,2048]{3,2,1,0:T(8,128)(2,1)} custom-call(s32[1]{0:T(128)} %get-tuple-element.62.refs_0_, s32[16]{0:T(128)S(1)} %get-tuple-element.63.refs_1_, s32[1,16]{1,0:T(1,128)S(1)} %get-tuple-element.64.refs_2_, bf16[4,2,64,2048]{3,2,1,0:T(8,128)(2,1)} %get-tuple-element.65.refs_3_, ...), custom_call_target="tpu_custom_call", output_to_operand_aliasing={{}: (3, {})} | custom-call | tf_op jit(solution)/shard_map/cond/branch_1_fun/pallas_call | solution.py:367
  (85 shorter events, 0.2 us)
Async XLA Ops:
  0.6 4.8 %copy-start.34 = (bf16[14,2,2048]{2,1,0:T(2,128)(2,1)S(1)}, bf16[14,2,2048]{2,1,0:T(2,128)(2,1)}, u32[]{:S(2)}) copy-start(bf16[14,2,2048]{2,1,0:T(2,128)(2,1)} %param.17) | copy-start | bytes 344068
  0.6 9.6 %copy-start.36 = (s32[16]{0:T(128)S(1)}, s32[16]{0:T(128)}, u32[]{:S(2)}) copy-start(s32[16]{0:T(128)} %refs_1_.7) | copy-start | bytes 196
  0.7 9.6 %copy-start.40 = (s32[16,1]{0,1:T(1,128)S(1)}, s32[16,1]{0,1:T(1,128)}, u32[]{:S(2)}) copy-start(s32[16,1]{0,1:T(1,128)} %param.29) | copy-start | bytes 196
  4.9 29.1 %collective-permute-start.29 = (bf16[4,2,64,2048]{3,2,1,0:T(8,128)(2,1)}, bf16[4,2,64,2048]{3,2,1,0:T(8,128)(2,1)S(1)}, u32[]{:S(2)}, u32[]{:S(2)}) collective-permute-start(bf16[4,2,64,2048]{3,2,1,0:T(8,128)(2,1)} %get-tuple-element.119), channel_id=1, source_target_pairs={{0,4},{4,0},{8,12},{12,8},{1,5},{5,1},{9,13},{13,9},{2,6},{6,2},{1... | collective-permute-start | bytes 6291464 | tf_op jit(solution)/shard_map/ppermute | solution.py:212
  5.5 3.4 %collective-permute-start.18 = (bf16[8,2048]{1,0:T(8,128)(2,1)S(1)}, bf16[8,2048]{1,0:T(8,128)(2,1)S(1)}, u32[]{:S(2)}, u32[]{:S(2)}) collective-permute-start(bf16[8,2048]{1,0:T(8,128)(2,1)S(1)} %pad_slice_fusion), channel_id=1, source_target_pairs={{0,12},{4,8},{8,4},{12,0},{1,13},{5,9},{9,5},{13,1},{2,14},{6,10},... | collective-permute-start | bytes 98312 | tf_op jit(solution)/shard_map/ppermute | solution.py:212
  6.8 2.8 %collective-permute-start.17 = (bf16[8,2048]{1,0:T(8,128)(2,1)S(1)}, bf16[8,2048]{1,0:T(8,128)(2,1)S(1)}, u32[]{:S(2)}, u32[]{:S(2)}) collective-permute-start(bf16[8,2048]{1,0:T(8,128)(2,1)S(1)} %pad_slice_fusion), channel_id=1, source_target_pairs={{0,8},{4,12},{8,0},{12,4},{1,9},{5,13},{9,1},{13,5},{2,10},{6,14},... | collective-permute-start | bytes 98312 | tf_op jit(solution)/shard_map/ppermute | solution.py:212
  7.0 2.6 %collective-permute-start.16 = (bf16[8,2048]{1,0:T(8,128)(2,1)S(1)}, bf16[8,2048]{1,0:T(8,128)(2,1)S(1)}, u32[]{:S(2)}, u32[]{:S(2)}) collective-permute-start(bf16[8,2048]{1,0:T(8,128)(2,1)S(1)} %pad_slice_fusion), channel_id=1, source_target_pairs={{0,4},{4,0},{8,12},{12,8},{1,5},{5,1},{9,13},{13,9},{2,6},{6,2},{1... | collective-permute-start | bytes 98312 | tf_op jit(solution)/shard_map/ppermute | solution.py:212
  8.9 0.7 copy-start.37
  10.2 8.3 %copy-start.1 = (bf16[32,2048]{1,0:T(8,128)(2,1)S(1)}, bf16[32,2048]{1,0:T(8,128)(2,1)}, u32[]{:S(2)}) copy-start(bf16[32,2048]{1,0:T(8,128)(2,1)} %pad.4.refs_5_.refs_0_) | copy-start | bytes 393220
  10.2 12.3 %copy-start.47 = (bf16[4,2,64,256]{3,2,1,0:T(8,128)(2,1)S(1)}, bf16[4,2,64,256]{3,2,1,0:T(8,128)(2,1)}, u32[]{:S(2)}) copy-start(bf16[4,2,64,256]{3,2,1,0:T(8,128)(2,1)} %get-tuple-element.118) | copy-start | bytes 786436
  10.2 23.7 %copy-start.48 = (bf16[128,2,256]{2,1,0:T(2,128)(2,1)S(1)}, bf16[128,2,256]{2,1,0:T(2,128)(2,1)}, u32[]{:S(2)}) copy-start(bf16[128,2,256]{2,1,0:T(2,128)(2,1)} %get-tuple-element.117) | copy-start | bytes 393220
  15.1 7.4 %collective-permute-start.19 = (f32[8,128]{1,0:T(8,128)}, f32[8,128]{1,0:T(8,128)S(1)}, u32[]{:S(2)}, u32[]{:S(2)}) collective-permute-start(f32[8,128]{1,0:T(8,128)} %get-tuple-element.112), channel_id=1, source_target_pairs={{0,4},{4,0},{8,12},{12,8},{1,5},{5,1},{9,13},{13,9},{2,6},{6,2},{1... | collective-permute-start | bytes 12296 | tf_op jit(solution)/shard_map/ppermute | solution.py:212
  16.8 6.2 %collective-permute-start.20 = (f32[8,128]{1,0:T(8,128)}, f32[8,128]{1,0:T(8,128)S(1)}, u32[]{:S(2)}, u32[]{:S(2)}) collective-permute-start(f32[8,128]{1,0:T(8,128)} %get-tuple-element.113), channel_id=1, source_target_pairs={{0,8},{4,12},{8,0},{12,4},{1,9},{5,13},{9,1},{13,5},{2,10},{6,14},... | collective-permute-start | bytes 12296 | tf_op jit(solution)/shard_map/ppermute | solution.py:212
  16.9 6.1 %collective-permute-start.21 = (f32[8,128]{1,0:T(8,128)}, f32[8,128]{1,0:T(8,128)S(1)}, u32[]{:S(2)}, u32[]{:S(2)}) collective-permute-start(f32[8,128]{1,0:T(8,128)} %get-tuple-element.114), channel_id=1, source_target_pairs={{0,12},{4,8},{8,4},{12,0},{1,13},{5,9},{9,5},{13,1},{2,14},{6,10},... | collective-permute-start | bytes 12296 | tf_op jit(solution)/shard_map/ppermute | solution.py:212
  18.5 12.2 %collective-permute-start.33 = (bf16[32,2048]{1,0:T(8,128)(2,1)S(1)}, bf16[32,2048]{1,0:T(8,128)(2,1)S(1)}, u32[]{:S(2)}, u32[]{:S(2)}) collective-permute-start(bf16[32,2048]{1,0:T(8,128)(2,1)S(1)} %copy-done.1), channel_id=1, source_target_pairs={{0,3},{1,0},{2,1},{3,2},{4,7},{5,4},{6,5},{7,6},{8,11},{9,8},{10,9... | collective-permute-start | bytes 393224 | tf_op jit(solution)/shard_map/ppermute | solution.py:217
  22.6 10.9 %collective-permute-start.28 = (bf16[4,2,64,256]{3,2,1,0:T(8,128)(2,1)S(1)}, bf16[4,2,64,256]{3,2,1,0:T(8,128)(2,1)S(1)}, u32[]{:S(2)}, u32[]{:S(2)}) collective-permute-start(bf16[4,2,64,256]{3,2,1,0:T(8,128)(2,1)S(1)} %copy-done.47), channel_id=1, source_target_pairs={{0,4},{4,0},{8,12},{12,8},{1,5},{5,1},{9,13},{13,9},{2,6},{6,2},{1... | collective-permute-start | bytes 786440 | tf_op jit(solution)/shard_map/ppermute | solution.py:212
  23.7 54.4 %copy-start.35 = (f32[32,128]{1,0:T(8,128)}, f32[32,128]{1,0:T(8,128)S(1)}, u32[]{:S(2)}) copy-start(f32[32,128]{1,0:T(8,128)S(1)} %pad_maximum_fusion.refs_8_) | copy-start | bytes 49156
  23.7 2.6 %collective-permute-start.24 = (f32[32,128]{1,0:T(8,128)S(1)}, f32[32,128]{1,0:T(8,128)S(1)}, u32[]{:S(2)}, u32[]{:S(2)}) collective-permute-start(f32[32,128]{1,0:T(8,128)S(1)} %pad_maximum_fusion.refs_8_), channel_id=1, source_target_pairs={{0,3},{1,0},{2,1},{3,2},{4,7},{5,4},{6,5},{7,6},{8,11},{9,8},{10,9... | collective-permute-start | bytes 49160 | tf_op jit(solution)/shard_map/ppermute | solution.py:217
  24.3 3.5 %collective-permute-start.23 = (f32[32,128]{1,0:T(8,128)S(1)}, f32[32,128]{1,0:T(8,128)S(1)}, u32[]{:S(2)}, u32[]{:S(2)}) collective-permute-start(f32[32,128]{1,0:T(8,128)S(1)} %pad_maximum_fusion.refs_8_), channel_id=1, source_target_pairs={{0,2},{1,3},{2,0},{3,1},{4,6},{5,7},{6,4},{7,5},{8,10},{9,11},{10,... | collective-permute-start | bytes 49160 | tf_op jit(solution)/shard_map/ppermute | solution.py:217
  26.3 51.8 %copy-start.41 = (f32[32,128]{1,0:T(8,128)}, f32[32,128]{1,0:T(8,128)S(1)}, u32[]{:S(2)}) copy-start(f32[32,128]{1,0:T(8,128)S(1)} %collective-permute-done.24.refs_11_) | copy-start | bytes 49156
  26.3 4.4 %collective-permute-start.22 = (f32[32,128]{1,0:T(8,128)S(1)}, f32[32,128]{1,0:T(8,128)S(1)}, u32[]{:S(2)}, u32[]{:S(2)}) collective-permute-start(f32[32,128]{1,0:T(8,128)S(1)} %pad_maximum_fusion.refs_8_), channel_id=1, source_target_pairs={{0,1},{1,2},{2,3},{3,0},{4,5},{5,6},{6,7},{7,4},{8,9},{9,10},{10,1... | collective-permute-start | bytes 49160 | tf_op jit(solution)/shard_map/ppermute | solution.py:217
  27.8 50.2 %copy-start.42 = (f32[32,128]{1,0:T(8,128)}, f32[32,128]{1,0:T(8,128)S(1)}, u32[]{:S(2)}) copy-start(f32[32,128]{1,0:T(8,128)S(1)} %collective-permute-done.23.refs_10_) | copy-start | bytes 49156
  27.8 11.3 %collective-permute-start.32 = (bf16[32,2048]{1,0:T(8,128)(2,1)S(1)}, bf16[32,2048]{1,0:T(8,128)(2,1)S(1)}, u32[]{:S(2)}, u32[]{:S(2)}) collective-permute-start(bf16[32,2048]{1,0:T(8,128)(2,1)S(1)} %copy-done.1), channel_id=1, source_target_pairs={{0,2},{1,3},{2,0},{3,1},{4,6},{5,7},{6,4},{7,5},{8,10},{9,11},{10,... | collective-permute-start | bytes 393224 | tf_op jit(solution)/shard_map/ppermute | solution.py:217
  30.7 47.4 %copy-start.43 = (f32[32,128]{1,0:T(8,128)}, f32[32,128]{1,0:T(8,128)S(1)}, u32[]{:S(2)}) copy-start(f32[32,128]{1,0:T(8,128)S(1)} %collective-permute-done.22.refs_9_) | copy-start | bytes 49156
  30.7 9.6 %collective-permute-start.31 = (bf16[32,2048]{1,0:T(8,128)(2,1)S(1)}, bf16[32,2048]{1,0:T(8,128)(2,1)S(1)}, u32[]{:S(2)}, u32[]{:S(2)}) collective-permute-start(bf16[32,2048]{1,0:T(8,128)(2,1)S(1)} %copy-done.1), channel_id=1, source_target_pairs={{0,1},{1,2},{2,3},{3,0},{4,5},{5,6},{6,7},{7,4},{8,9},{9,10},{10,1... | collective-permute-start | bytes 393224 | tf_op jit(solution)/shard_map/ppermute | solution.py:217
  30.7 12.6 %copy-start.31 = (bf16[32,2048]{1,0:T(8,128)(2,1)}, bf16[32,2048]{1,0:T(8,128)(2,1)S(1)}, u32[]{:S(2)}) copy-start(bf16[32,2048]{1,0:T(8,128)(2,1)S(1)} %collective-permute-done.33.refs_3_) | copy-start | bytes 393220
  30.7 9.9 %collective-permute-start.25 = (bf16[128,2,256]{2,1,0:T(2,128)(2,1)}, bf16[128,2,256]{2,1,0:T(2,128)(2,1)S(1)}, u32[]{:S(2)}, u32[]{:S(2)}) collective-permute-start(bf16[128,2,256]{2,1,0:T(2,128)(2,1)} %get-tuple-element.115), channel_id=1, source_target_pairs={{0,4},{4,0},{8,12},{12,8},{1,5},{5,1},{9,13},{13,9},{2,6},{6,2},{1... | collective-permute-start | bytes 393224 | tf_op jit(solution)/shard_map/ppermute | solution.py:212
  33.4 1.8 %copy-start.2 = (bf16[4,2,64,256]{3,2,1,0:T(8,128)(2,1)}, bf16[4,2,64,256]{3,2,1,0:T(8,128)(2,1)S(1)}, u32[]{:S(2)}) copy-start(bf16[4,2,64,256]{3,2,1,0:T(8,128)(2,1)S(1)} %collective-permute-done.28.refs_6_) | copy-start | bytes 786436
  33.4 8.4 %collective-permute-start.26 = (bf16[128,2,256]{2,1,0:T(2,128)(2,1)}, bf16[128,2,256]{2,1,0:T(2,128)(2,1)S(1)}, u32[]{:S(2)}, u32[]{:S(2)}) collective-permute-start(bf16[128,2,256]{2,1,0:T(2,128)(2,1)} %get-tuple-element.116), channel_id=1, source_target_pairs={{0,8},{4,12},{8,0},{12,4},{1,9},{5,13},{9,1},{13,5},{2,10},{6,14},... | collective-permute-start | bytes 393224 | tf_op jit(solution)/shard_map/ppermute | solution.py:212
  33.9 1.3 %copy-start = (bf16[4,2,64,2048]{3,2,1,0:T(8,128)(2,1)}, bf16[4,2,64,2048]{3,2,1,0:T(8,128)(2,1)S(1)}, u32[]{:S(2)}) copy-start(bf16[4,2,64,2048]{3,2,1,0:T(8,128)(2,1)S(1)} %collective-permute-done.29.refs_5_.refs_3_) | copy-start | bytes 6291460
  33.9 8.2 %collective-permute-start.27 = (bf16[128,2,256]{2,1,0:T(2,128)(2,1)S(1)}, bf16[128,2,256]{2,1,0:T(2,128)(2,1)S(1)}, u32[]{:S(2)}, u32[]{:S(2)}) collective-permute-start(bf16[128,2,256]{2,1,0:T(2,128)(2,1)S(1)} %copy-done.48), channel_id=1, source_target_pairs={{0,12},{4,8},{8,4},{12,0},{1,13},{5,9},{9,5},{13,1},{2,14},{6,10},... | collective-permute-start | bytes 393224 | tf_op jit(solution)/shard_map/ppermute | solution.py:212
  39.1 4.2 %copy-start.32 = (bf16[32,2048]{1,0:T(8,128)(2,1)}, bf16[32,2048]{1,0:T(8,128)(2,1)S(1)}, u32[]{:S(2)}) copy-start(bf16[32,2048]{1,0:T(8,128)(2,1)S(1)} %collective-permute-done.32.refs_2_) | copy-start | bytes 393220
  39.1 6.9 %collective-permute-start.30 = (bf16[4,2,64,256]{3,2,1,0:T(8,128)(2,1)}, bf16[4,2,64,256]{3,2,1,0:T(8,128)(2,1)S(1)}, u32[]{:S(2)}, u32[]{:S(2)}) collective-permute-start(bf16[4,2,64,256]{3,2,1,0:T(8,128)(2,1)} %get-tuple-element.120), channel_id=1, source_target_pairs={{0,8},{4,12},{8,0},{12,4},{1,9},{5,13},{9,1},{13,5},{2,10},{6,14},... | collective-permute-start | bytes 786440 | tf_op jit(solution)/shard_map/ppermute | solution.py:212
  40.3 3.0 %copy-start.33 = (bf16[32,2048]{1,0:T(8,128)(2,1)}, bf16[32,2048]{1,0:T(8,128)(2,1)S(1)}, u32[]{:S(2)}) copy-start(bf16[32,2048]{1,0:T(8,128)(2,1)S(1)} %collective-permute-done.31.refs_1_) | copy-start | bytes 393220
  40.3 11.3 %collective-permute-start.35 = (bf16[64,2048]{1,0:T(8,128)(2,1)}, bf16[64,2048]{1,0:T(8,128)(2,1)S(1)}, u32[]{:S(2)}, u32[]{:S(2)}) collective-permute-start(bf16[64,2048]{1,0:T(8,128)(2,1)} %get-tuple-element.126), channel_id=1, source_target_pairs={{0,8},{4,12},{8,0},{12,4},{1,9},{5,13},{9,1},{13,5},{2,10},{6,14},... | collective-permute-start | bytes 786440 | tf_op jit(solution)/shard_map/ppermute | solution.py:212
  40.7 37.4 %copy-start.28 = (bf16[128,2,256]{2,1,0:T(2,128)(2,1)}, bf16[128,2,256]{2,1,0:T(2,128)(2,1)S(1)}, u32[]{:S(2)}) copy-start(bf16[128,2,256]{2,1,0:T(2,128)(2,1)S(1)} %collective-permute-done.25.refs_12_) | copy-start | bytes 393220
  40.7 16.6 %collective-permute-start.36 = (bf16[64,2048]{1,0:T(8,128)(2,1)}, bf16[64,2048]{1,0:T(8,128)(2,1)S(1)}, u32[]{:S(2)}, u32[]{:S(2)}) collective-permute-start(bf16[64,2048]{1,0:T(8,128)(2,1)} %get-tuple-element.127), channel_id=1, source_target_pairs={{0,8},{4,12},{8,0},{12,4},{1,9},{5,13},{9,1},{13,5},{2,10},{6,14},... | collective-permute-start | bytes 786440 | tf_op jit(solution)/shard_map/ppermute | solution.py:212
  41.8 36.3 %copy-start.29 = (bf16[128,2,256]{2,1,0:T(2,128)(2,1)}, bf16[128,2,256]{2,1,0:T(2,128)(2,1)S(1)}, u32[]{:S(2)}) copy-start(bf16[128,2,256]{2,1,0:T(2,128)(2,1)S(1)} %collective-permute-done.26.refs_13_) | copy-start | bytes 393220
  41.8 21.0 %collective-permute-start.37 = (bf16[64,2048]{1,0:T(8,128)(2,1)}, bf16[64,2048]{1,0:T(8,128)(2,1)S(1)}, u32[]{:S(2)}, u32[]{:S(2)}) collective-permute-start(bf16[64,2048]{1,0:T(8,128)(2,1)} %get-tuple-element.128), channel_id=1, source_target_pairs={{0,8},{4,12},{8,0},{12,4},{1,9},{5,13},{9,1},{13,5},{2,10},{6,14},... | collective-permute-start | bytes 786440 | tf_op jit(solution)/shard_map/ppermute | solution.py:212
  42.1 36.0 %copy-start.30 = (bf16[128,2,256]{2,1,0:T(2,128)(2,1)}, bf16[128,2,256]{2,1,0:T(2,128)(2,1)S(1)}, u32[]{:S(2)}) copy-start(bf16[128,2,256]{2,1,0:T(2,128)(2,1)S(1)} %collective-permute-done.27.refs_14_) | copy-start | bytes 393220
  42.1 26.3 %collective-permute-start.38 = (bf16[64,2048]{1,0:T(8,128)(2,1)}, bf16[64,2048]{1,0:T(8,128)(2,1)S(1)}, u32[]{:S(2)}, u32[]{:S(2)}) collective-permute-start(bf16[64,2048]{1,0:T(8,128)(2,1)} %get-tuple-element.129), channel_id=1, source_target_pairs={{0,8},{4,12},{8,0},{12,4},{1,9},{5,13},{9,1},{13,5},{2,10},{6,14},... | collective-permute-start | bytes 786440 | tf_op jit(solution)/shard_map/ppermute | solution.py:212
  46.0 32.1 %copy-start.5 = (bf16[4,2,64,256]{3,2,1,0:T(8,128)(2,1)}, bf16[4,2,64,256]{3,2,1,0:T(8,128)(2,1)S(1)}, u32[]{:S(2)}) copy-start(bf16[4,2,64,256]{3,2,1,0:T(8,128)(2,1)S(1)} %collective-permute-done.30) | copy-start | bytes 786436
  46.0 48.1 %collective-permute-start.34 = (bf16[64,2048]{1,0:T(8,128)(2,1)}, bf16[64,2048]{1,0:T(8,128)(2,1)S(1)}, u32[]{:S(2)}, u32[]{:S(2)}) collective-permute-start(bf16[64,2048]{1,0:T(8,128)(2,1)} %get-tuple-element.125), channel_id=1, source_target_pairs={{0,8},{4,12},{8,0},{12,4},{1,9},{5,13},{9,1},{13,5},{2,10},{6,14},... | collective-permute-start | bytes 786440 | tf_op jit(solution)/shard_map/ppermute | solution.py:212
  51.6 26.5 %copy-start.3 = (bf16[64,2048]{1,0:T(8,128)(2,1)}, bf16[64,2048]{1,0:T(8,128)(2,1)S(1)}, u32[]{:S(2)}) copy-start(bf16[64,2048]{1,0:T(8,128)(2,1)S(1)} %collective-permute-done.35.refs_4_) | copy-start | bytes 786436
  51.6 38.0 %collective-permute-start.39 = (bf16[64,2048]{1,0:T(8,128)(2,1)S(1)}, bf16[64,2048]{1,0:T(8,128)(2,1)S(1)}, u32[]{:S(2)}, u32[]{:S(2)}) collective-permute-start(bf16[64,2048]{1,0:T(8,128)(2,1)S(1)} %collective-permute-done.35.refs_4_), channel_id=1, source_target_pairs={{0,4},{4,0},{8,12},{12,8},{1,5},{5,1},{9,13},{13,9},{2,6},{6,2},{1... | collective-permute-start | bytes 786440 | tf_op jit(solution)/shard_map/ppermute | solution.py:212
  57.2 20.9 %copy-start.4 = (bf16[64,2048]{1,0:T(8,128)(2,1)}, bf16[64,2048]{1,0:T(8,128)(2,1)S(1)}, u32[]{:S(2)}) copy-start(bf16[64,2048]{1,0:T(8,128)(2,1)S(1)} %collective-permute-done.36.refs_5_) | copy-start | bytes 786436
  57.2 32.4 %collective-permute-start.40 = (bf16[64,2048]{1,0:T(8,128)(2,1)S(1)}, bf16[64,2048]{1,0:T(8,128)(2,1)S(1)}, u32[]{:S(2)}, u32[]{:S(2)}) collective-permute-start(bf16[64,2048]{1,0:T(8,128)(2,1)S(1)} %collective-permute-done.36.refs_5_), channel_id=1, source_target_pairs={{0,4},{4,0},{8,12},{12,8},{1,5},{5,1},{9,13},{13,9},{2,6},{6,2},{1... | collective-permute-start | bytes 786440 | tf_op jit(solution)/shard_map/ppermute | solution.py:212
  62.8 15.3 %copy-start.6 = (bf16[64,2048]{1,0:T(8,128)(2,1)}, bf16[64,2048]{1,0:T(8,128)(2,1)S(1)}, u32[]{:S(2)}) copy-start(bf16[64,2048]{1,0:T(8,128)(2,1)S(1)} %collective-permute-done.37.refs_6_) | copy-start | bytes 786436
  62.8 26.8 %collective-permute-start.41 = (bf16[64,2048]{1,0:T(8,128)(2,1)S(1)}, bf16[64,2048]{1,0:T(8,128)(2,1)S(1)}, u32[]{:S(2)}, u32[]{:S(2)}) collective-permute-start(bf16[64,2048]{1,0:T(8,128)(2,1)S(1)} %collective-permute-done.37.refs_6_), channel_id=1, source_target_pairs={{0,4},{4,0},{8,12},{12,8},{1,5},{5,1},{9,13},{13,9},{2,6},{6,2},{1... | collective-permute-start | bytes 786440 | tf_op jit(solution)/shard_map/ppermute | solution.py:212
  68.5 9.7 %copy-start.7 = (bf16[64,2048]{1,0:T(8,128)(2,1)}, bf16[64,2048]{1,0:T(8,128)(2,1)S(1)}, u32[]{:S(2)}) copy-start(bf16[64,2048]{1,0:T(8,128)(2,1)S(1)} %collective-permute-done.38.refs_7_) | copy-start | bytes 786436
  68.5 21.2 %collective-permute-start.42 = (bf16[64,2048]{1,0:T(8,128)(2,1)S(1)}, bf16[64,2048]{1,0:T(8,128)(2,1)S(1)}, u32[]{:S(2)}, u32[]{:S(2)}) collective-permute-start(bf16[64,2048]{1,0:T(8,128)(2,1)S(1)} %collective-permute-done.38.refs_7_), channel_id=1, source_target_pairs={{0,4},{4,0},{8,12},{12,8},{1,5},{5,1},{9,13},{13,9},{2,6},{6,2},{1... | collective-permute-start | bytes 786440 | tf_op jit(solution)/shard_map/ppermute | solution.py:212
  89.6 4.5 %copy-start.44 = (bf16[64,2048]{1,0:T(8,128)(2,1)S(1)}, bf16[64,2048]{1,0:T(8,128)(2,1)}, u32[]{:S(2)}) copy-start(bf16[64,2048]{1,0:T(8,128)(2,1)} %get-tuple-element.130) | copy-start | bytes 786436
  89.6 4.5 %copy-start.45 = (bf16[64,2048]{1,0:T(8,128)(2,1)S(1)}, bf16[64,2048]{1,0:T(8,128)(2,1)}, u32[]{:S(2)}) copy-start(bf16[64,2048]{1,0:T(8,128)(2,1)} %get-tuple-element.131) | copy-start | bytes 786436
  89.6 4.5 %copy-start.46 = (bf16[64,2048]{1,0:T(8,128)(2,1)S(1)}, bf16[64,2048]{1,0:T(8,128)(2,1)}, u32[]{:S(2)}) copy-start(bf16[64,2048]{1,0:T(8,128)(2,1)} %get-tuple-element.132) | copy-start | bytes 786436
  89.6 0.7 copy-start.8
  89.6 0.8 copy-start.9
  89.6 0.9 copy-start.10
  90.5 0.7 copy-start.12
  94.1 7.8 %collective-permute-start.1 = (bf16[64,2048]{1,0:T(8,128)(2,1)S(1)}, bf16[64,2048]{1,0:T(8,128)(2,1)S(1)}, u32[]{:S(2)}, u32[]{:S(2)}) collective-permute-start(bf16[64,2048]{1,0:T(8,128)(2,1)S(1)} %get-tuple-element.67), channel_id=1, source_target_pairs={{0,8},{4,12},{8,0},{12,4},{1,9},{5,13},{9,1},{13,5},{2,10},{6,14},... | collective-permute-start | bytes 786440 | tf_op jit(solution)/shard_map/cond/branch_1_fun/ppermute | solution.py:212
  94.8 8.2 %collective-permute-start.2 = (bf16[64,2048]{1,0:T(8,128)(2,1)S(1)}, bf16[64,2048]{1,0:T(8,128)(2,1)S(1)}, u32[]{:S(2)}, u32[]{:S(2)}) collective-permute-start(bf16[64,2048]{1,0:T(8,128)(2,1)S(1)} %get-tuple-element.66.refs_4_), channel_id=1, source_target_pairs={{0,4},{4,0},{8,12},{12,8},{1,5},{5,1},{9,13},{13,9},{2,6},{6,2},{1... | collective-permute-start | bytes 786440 | tf_op jit(solution)/shard_map/cond/branch_1_fun/ppermute | solution.py:212
  101.9 2.1 %copy-start.23 = (bf16[64,2048]{1,0:T(8,128)(2,1)}, bf16[64,2048]{1,0:T(8,128)(2,1)S(1)}, u32[]{:S(2)}) copy-start(bf16[64,2048]{1,0:T(8,128)(2,1)S(1)} %collective-permute-done.1.refs_5_) | copy-start | bytes 786436 | tf_op jit(solution)/shard_map/cond
  101.9 2.1 %collective-permute-start.3 = (bf16[64,2048]{1,0:T(8,128)(2,1)S(1)}, bf16[64,2048]{1,0:T(8,128)(2,1)S(1)}, u32[]{:S(2)}, u32[]{:S(2)}) collective-permute-start(bf16[64,2048]{1,0:T(8,128)(2,1)S(1)} %collective-permute-done.1.refs_5_), channel_id=1, source_target_pairs={{0,4},{4,0},{8,12},{12,8},{1,5},{5,1},{9,13},{13,9},{2,6},{6,2},{1... | collective-permute-start | bytes 786440 | tf_op jit(solution)/shard_map/cond/branch_1_fun/ppermute | solution.py:212
  102.9 1.2 %copy-start.24 = (bf16[64,2048]{1,0:T(8,128)(2,1)}, bf16[64,2048]{1,0:T(8,128)(2,1)S(1)}, u32[]{:S(2)}) copy-start(bf16[64,2048]{1,0:T(8,128)(2,1)S(1)} %collective-permute-done.2.refs_6_) | copy-start | bytes 786436 | tf_op jit(solution)/shard_map/cond
  104.1 0.7 copy-start.26
  (2 other events, 1.2 us)

commit v2 on v1

--- a/solution.py
+++ b/solution.py
@@ -217,8 +217,8 @@
     return lax.ppermute(array, "tensor", [(i, (i + step) % size) for i in range(size)])
 
 
-HEAD_UNITS = 5
-EARLY_UNITS = 4
+ALWAYS = ((0, 2), (2, 3), (5, 1))
+AT_NEED = ((6, 1), (7, 1))
 SMEM = pl.BlockSpec(memory_space=pltpu.SMEM)
 VMEM = pl.BlockSpec(memory_space=pltpu.VMEM)
 
@@ -242,7 +242,7 @@
     return items
 
 
-def staged(groups):
+def staged(groups, meanwhile=None):
     def when(condition, action):
         if condition is None:
             action()
@@ -264,6 +264,8 @@
     for moves, buffer, sems in groups:
         for at, (condition, sources, _) in enumerate(moves):
             when(condition, functools.partial(begin, at, sources, buffer, sems))
+    if meanwhile is not None:
+        meanwhile()
     for moves, buffer, sems in groups:
         for at, (condition, _, targets) in enumerate(moves):
             when(condition, functools.partial(forward, at, targets, buffer, sems))
@@ -273,9 +275,9 @@
 
 
 def collect_kernel(spans, slot_total, masks, *refs):
-    (me_ref, arrival_from, arrival_slot, holder, kv_cache, store_a, store_b) = refs[:7]
-    leaving, (rows_b, rows_a) = refs[7 : 7 + len(masks)], refs[7 + len(masks) : 9 + len(masks)]
-    buffers, semaphores = refs[9 + len(masks) : 12 + len(masks)], refs[12 + len(masks) :]
+    (me_ref, arrival_from, arrival_slot, holder, kv_cache, store_a, store_b, hidden) = refs[:8]
+    *leaving, rows_a, rows_b, rows, asking = refs[8 : 12 + len(masks)]
+    buffers, semaphores = refs[12 + len(masks) : 15 + len(masks)], refs[15 + len(masks) :]
     me = me_ref[0]
     moves = []
     for i, mask in enumerate(masks):
@@ -292,19 +294,29 @@
             row = holder[copy_id * spans + span]
             slot += jnp.where(row // slot_total == me, row % slot_total, 0)
         held.append(slot)
-    for table, rows in ((store_a, rows_a), (store_b, rows_b)):
+    for table, target in ((store_a, rows_a), (store_b, rows_b)):
         groups.append(
             [
-                (None, [(None, table.at[slot])], [(None, rows.at[copy_id])])
+                (None, [(None, table.at[slot])], [(None, target.at[copy_id])])
                 for copy_id, slot in enumerate(held)
             ]
         )
-    staged(list(zip(groups, buffers, semaphores)))
+
+    def regroup():
+        count = hidden.shape[0] * hidden.shape[1]
+        start = rows.shape[0] - asking.shape[0]
+        blank = jnp.zeros((rows.shape[0] - count, rows.shape[1]), rows.dtype)
+        every = hidden[...].reshape(count, rows.shape[1])
+        rows[...] = jnp.concatenate([every, blank], axis=0)
+        asking[...] = rows[start:]
+
+    staged(list(zip(groups, buffers, semaphores)), regroup)
 
 
 def pack_kernel(spans, slot_total, *refs):
     (me_ref, holder, dest, store_a, store_b, sibling_a, sibling_b) = refs[:7]
     across_b, *units = refs[7:-5]
+    spread = ALWAYS + AT_NEED
     extra, buffer_b, buffer_a, sems_b, sems_a = refs[-5:]
     me = me_ref[0]
     core = me % 2
@@ -325,55 +337,68 @@
             (own, store_a.at[row % slot_total, core]),
             (jnp.logical_not(own), sibling_a.at[copy_id, core]),
         ]
-        targets = [(unit == i, units[i]) for i in range(at + 1)]
+        targets = [
+            (
+                jnp.logical_and(unit >= start, unit < start + size),
+                array.at[jnp.clip(unit - start, 0, size - 1)],
+            )
+            for array, (start, size) in zip(units, spread)
+            if start <= at
+        ]
         moves_a.append((crosses, sources, targets))
     count = items[-1][4] + items[-1][3].astype(jnp.int32)
-    extra[0] = jnp.clip(count - HEAD_UNITS, 0, len(units) - HEAD_UNITS)
+    extra[0] = jnp.clip(count - AT_NEED[0][0], 0, len(AT_NEED))
     staged([(moves_b, buffer_b, sems_b), (moves_a, buffer_a, sems_a)])
 
 
-def place_kernel(spans, slot_total, first_unit, unit_count, *refs):
+def place_kernel(spans, slot_total, spread, *refs):
     (me_ref, holder, dest, earlier) = refs[:4]
-    got, other = refs[4 : 4 + unit_count], refs[4 + unit_count : 4 + 2 * unit_count]
+    got, other = refs[4 : 4 + len(spread)], refs[4 + len(spread) : 4 + 2 * len(spread)]
     out, buffer, sems = refs[-3:]
     me = me_ref[0]
     core = me % 2
+    first_unit = spread[0][0]
+    past_unit = spread[-1][0] + spread[-1][1]
     items = crossing(holder, dest, spans, slot_total, me // 2)
     moves = []
     for copy_id in range(COPIES):
         one, two = items[2 * copy_id], items[2 * copy_id + 1]
         crosses = jnp.where(core == 0, one[3].astype(jnp.int32), two[3].astype(jnp.int32)) != 0
         unit = jnp.where(core == 0, one[4], two[4])
-        possible = [i for i in range(unit_count) if first_unit + i <= 2 * copy_id + 1]
+        possible = [i for i, (start, _) in enumerate(spread) if start <= 2 * copy_id + 1]
         if first_unit and not possible:
             continue
+        here = jnp.logical_and(unit >= first_unit, unit < past_unit)
         for half, arrays in ((core, got), (1 - core, other)):
             sources = []
-            if first_unit:
-                active = jnp.logical_and(crosses, unit >= first_unit)
-            else:
+            active = jnp.logical_and(crosses, here)
+            if not first_unit:
                 near = jnp.logical_not(crosses)
-                active = jnp.logical_or(near, unit < unit_count)
+                active = jnp.logical_or(near, here)
                 sources.append((near, earlier.at[copy_id, half]))
             for i in possible:
-                hit = jnp.logical_and(crosses, unit == first_unit + i)
-                sources.append((hit, arrays[i]))
+                start, size = spread[i]
+                hit = jnp.logical_and(unit >= start, unit < start + size)
+                source = arrays[i].at[jnp.clip(unit - start, 0, size - 1)]
+                sources.append((jnp.logical_and(crosses, hit), source))
             moves.append((active, sources, [(None, out.at[copy_id, half])]))
     staged([(moves, buffer, sems)])
 
 
-def copy_call(kernel, tables, arrays, shapes, scratch, scalars=(), aliases=None):
-    hbm = pl.BlockSpec(memory_space=pltpu.HBM)
+def copy_call(kernel, tables, arrays, shapes, scratch, scalars=(), aliases=None, given=(), made=()):
+    hbm = pl.BlockSpec(memory_space=pl.ANY)
+    dtype = arrays[0].dtype
     return pl.pallas_call(
         kernel,
-        out_shape=[pltpu.HBM(shape, arrays[0].dtype) for shape in shapes]
+        out_shape=[pltpu.HBM(shape, dtype) for shape in shapes]
+        + [jax.ShapeDtypeStruct(shape, dtype) for shape in made]
         + [jax.ShapeDtypeStruct(shape, jnp.int32) for shape in scalars],
-        in_specs=[SMEM] * len(tables) + [hbm] * len(arrays),
-        out_specs=[hbm] * len(shapes) + [SMEM] * len(scalars),
-        scratch_shapes=[pltpu.VMEM(shape, arrays[0].dtype) for shape in scratch]
+        in_specs=[SMEM] * len(tables) + [hbm] * len(arrays) + [VMEM] * len(given),
+        out_specs=[hbm] * len(shapes) + [VMEM] * len(made) + [SMEM] * len(scalars),
+        scratch_shapes=[pltpu.VMEM(shape, dtype) for shape in scratch]
         + [pltpu.SemaphoreType.DMA((2, shape[0])) for shape in scratch],
         input_output_aliases=aliases or {},
-    )(*tables, *arrays)
+    )(*tables, *arrays, *given)
 
 
 def project_kernel(spans, slot_total, resident, steps, masks, *refs):
@@ -434,10 +459,10 @@
 
 def attend_kernel(spans, masks, resident, steps, kv_heads, head_length, *refs):
     (me_ref, lengths, arrival_from, arrival_slot, resident_adapter, arrival_adapter) = refs[:6]
-    holder, dest, *parts = refs[6 : -11 - len(masks)]
-    came = refs[-11 - len(masks) : -11]
-    store_b, sibling_b, across_b, base, queries, cache = refs[-11:-5]
-    out, new_kv, arrived, installed_b, fresh_ref = refs[-5:]
+    holder, dest, *parts = refs[6 : -12 - len(masks)]
+    came = refs[-12 - len(masks) : -12]
+    store_b, sibling_b, across_b, base, queries, cache = refs[-12:-6]
+    out, new_kv, arrived, installed_b, fresh_ref, mixed_ref = refs[-6:]
     me = me_ref[0]
     arrive = arrival_from.shape[0]
     replicas = arrival_from.shape[1]
@@ -526,7 +551,9 @@
             spot = slice(at + part * head_length, at + (part + 1) * head_length)
             rounded = piece.astype(jnp.bfloat16)
             fresh_ref[:, spot] = rounded.astype(jnp.float32)
-            new_kv[:, spot] = jnp.where(dead, jnp.zeros_like(rounded), rounded)
+            kept = jnp.where(dead, 0.0, rounded.astype(jnp.float32))[: slots * steps]
+            lanes = slice(part * head_length, (part + 1) * head_length)
+            new_kv[:, :, g, lanes] = kept.reshape(slots, steps, head_length).astype(jnp.bfloat16)
 
     query_rows = queries.shape[1]
     heads = query_rows // steps
@@ -581,7 +608,11 @@
             mixed = mixed + (term / denom).astype(jnp.bfloat16).astype(jnp.float32) * value
         if n < resident:
             mixed = jnp.where(gone[n] != 0, 0.0, mixed)
-        out[n] = mixed.astype(jnp.bfloat16)
+        mixed_ref[n * query_rows : (n + 1) * query_rows] = mixed
+        for head in range(heads):
+            lanes = slice(head * head_length, (head + 1) * head_length)
+            pair = mixed_ref[pl.ds(n * query_rows + head, steps, stride=heads)]
+            out[n, :, lanes] = pair.astype(jnp.bfloat16)
 
 
 def pairs_layer(
@@ -620,20 +651,21 @@
 
     used = slots * steps
     padded = -(-used // 8) * 8
-    rows = jnp.pad(hidden.reshape(used, features), ((0, padded - used), (0, 0)))
     first = resident * steps
     block = padded - first
-    other_rows = [partner(rows[first:], mask) for mask in masks]
-
-    *leaving, rows_b, rows_a = copy_call(
+
+    *leaving, rows_a, rows_b, rows, asking = copy_call(
         functools.partial(collect_kernel, spans, slot_total, masks),
         (me_table, from_table, slot_table, hot_holder),
         (kv_cache, store_a, store_b),
-        [kv_cache.shape[1:]] * len(masks) + [(COPIES,) + row_b, (COPIES,) + row_a],
+        [kv_cache.shape[1:]] * len(masks) + [(COPIES,) + row_a, (COPIES,) + row_b],
         [(len(masks),) + kv_cache.shape[1:], (COPIES,) + row_a, (COPIES,) + row_b],
+        given=(hidden,),
+        made=[(padded, features), (block, features)],
     )
     sibling_a = partner(rows_a, 1)
     sibling_b = partner(rows_b, 1)
+    other_rows = [partner(asking, mask) for mask in masks]
     came = [partner(array, mask) for array, mask in zip(leaving, masks)]
     around = [rows] + [shifted(rows, step) for step in range(1, shards)]
 
@@ -679,13 +711,14 @@
         functools.partial(pack_kernel, spans, slot_total),
         (me_table, hot_holder, dest_table),
         (store_a, store_b, sibling_a, sibling_b),
-        [(COPIES,) + row_b] + [unit_shape] * unit_total,
+        [(COPIES,) + row_b] + [(size,) + unit_shape for _, size in ALWAYS + AT_NEED],
         [(COPIES,) + row_b, (unit_total,) + unit_shape],
         [(1,)],
     )
     across_b = partner(across_b, 2)
-    got = [partner(array, 2) for array in units[:EARLY_UNITS]]
-    got += [partner(array, 2) for array in units[EARLY_UNITS:HEAD_UNITS]]
+    got = []
+    for array in units[: len(ALWAYS)]:
+        got.append(partner(array, 2))
 
     full = pl.pallas_call(
         gather_kernel,
@@ -699,14 +732,17 @@
     attn_out, new_kv, arrived, installed_b = pl.pallas_call(
         functools.partial(attend_kernel, spans, masks, resident, steps, kv_heads, head_length),
         out_shape=[
-            jax.ShapeDtypeStruct((slots, steps * heads, head_length), jnp.bfloat16),
-            jax.ShapeDtypeStruct((padded, kv_heads * head_pair), jnp.bfloat16),
+            jax.ShapeDtypeStruct((slots, steps, heads * head_length), jnp.bfloat16),
+            jax.ShapeDtypeStruct((slots, steps, kv_heads, head_pair), jnp.bfloat16),
             jax.ShapeDtypeStruct((arrive,) + kv_cache.shape[1:], jnp.bfloat16),
             jax.ShapeDtypeStruct((COPIES, 2 * rank, columns), jnp.bfloat16),
         ],
         in_specs=[SMEM] * 8 + [VMEM] * (shards + len(masks) + 6),
         out_specs=[VMEM] * 4,
-        scratch_shapes=[pltpu.VMEM((padded, kv_heads * head_pair), jnp.float32)],
+        scratch_shapes=[
+            pltpu.VMEM((padded, kv_heads * head_pair), jnp.float32),
+            pltpu.VMEM((slots * steps * heads, head_length), jnp.float32),
+        ],
         name="attend",
     )(
         me_table,
@@ -727,26 +763,25 @@
         kv_cache,
     )
     installed_b = installed_b.reshape((COPIES,) + row_b)
-    attn_out = attn_out.reshape(slots, steps, heads * head_length)
-    new_kv = new_kv[:used].reshape(slots, steps, kv_heads, head_pair)
 
     tables = (me_table, hot_holder, dest_table)
-    other = [partner(array, 1) for array in got[:EARLY_UNITS]]
+    early = len(ALWAYS) - 1
+    other = [partner(array, 1) for array in got[:early]]
     (placed,) = copy_call(
-        functools.partial(place_kernel, spans, slot_total, 0, EARLY_UNITS),
+        functools.partial(place_kernel, spans, slot_total, ALWAYS[:early]),
         tables,
-        (sibling_a, *got[:EARLY_UNITS], *other),
+        (sibling_a, *got[:early], *other),
         [(COPIES,) + row_a],
         [(unit_total,) + unit_shape],
     )
 
     def finish(count):
         def branch(placed, *arrays):
-            late = list(arrays[: HEAD_UNITS - EARLY_UNITS])
-            late += [partner(array, 2) for array in arrays[len(late) :][:count]]
+            late = [arrays[0]] + [partner(array, 2) for array in arrays[1:][:count]]
             other = [partner(array, 1) for array in late]
+            spread = (ALWAYS[early:] + AT_NEED)[: len(late)]
             return copy_call(
-                functools.partial(place_kernel, spans, slot_total, EARLY_UNITS, len(late)),
+                functools.partial(place_kernel, spans, slot_total, spread),
                 tables,
                 (placed, *late, *other),
                 [(COPIES,) + row_a],
@@ -756,10 +791,8 @@
 
         return branch
 
-    branches = [finish(count) for count in range(unit_total - HEAD_UNITS + 1)]
-    installed_a = lax.switch(
-        extra[0], branches, placed, *got[EARLY_UNITS:], *units[HEAD_UNITS:]
-    )
+    branches = [finish(count) for count in range(len(AT_NEED) + 1)]
+    installed_a = lax.switch(extra[0], branches, placed, got[early], *units[len(ALWAYS) :])
     return (attn_out, new_kv, arrived, installed_a, installed_b)
 
 

time: 108 us -> 104 us (0.963)
  the two profiles are of different devices: /device:TPU:5 before, /device:TPU:0 now
where the time goes in v2:
time: 104 us; the launch traced here: 103 us
  waiting for transfers between devices  35 us (34%)
  Pallas kernels  27 us (26%)
  starting transfers between devices  26.9 us (26%)
  local copies, waits for them, and re-layouts  5.94 us (6%)
  matrix products  5.77 us (6%)
  between operations  1.51 us (1%)
    ppermute x18, waiting for transfers between devices, partner(): lax.ppermute(array, 'replica', [(i, i ^ mask) for i in range(lax.axis_siz...  25.8 us
    ppermute x6, starting transfers between devices, shifted(): lax.ppermute(array, 'tensor', [(i, (i + step) % size) for i in range(size)])  14.1 us
    ppermute x18, starting transfers between devices, partner(): lax.ppermute(array, 'replica', [(i, i ^ mask) for i in range(lax.axis_siz...  12.8 us
    pallas_call x4, Pallas kernels, copy_call(): pl.pallas_call(kernel, out_shape=[pltpu.HBM(shape, dtype) for shape in sh...  12.2 us
    ppermute x6, waiting for transfers between devices, shifted(): lax.ppermute(array, 'tensor', [(i, (i + step) % size) for i in range(size)])  9.24 us
    pallas_call x1, Pallas kernels, pairs_layer(): pl.pallas_call(functools.partial(attend_kernel, spans, masks, resident, s...  7.89 us
    dot_general x1, matrix products, pairs_layer(): jnp.einsum('md,dgc->gmc', full, w_kv, preferred_element_type=jnp.float32)  5.77 us
    pallas_call x1, Pallas kernels, pairs_layer(): pl.pallas_call(functools.partial(project_kernel, spans, slot_total, resid...  4.93 us
  transfers between devices with their start and end apart: 24, of which 9 were waited for; matrix products, arithmetic and copies ran while one was open for 7% of the time, Pallas kernels for 17%

profile of v2, /device:TPU:0, one launch (start us, length us, event | category | flops | bytes accessed | tf_op | source)
XLA Modules:
  0.0 102.9 jit_solution(486927788822343925)
XLA Ops:
  0.6 0.0 copy-start.27
  0.6 0.0 copy-start.29
  0.7 4.8 %shard_map.164 = (bf16[128,2,256]{2,1,0:T(2,128)(2,1)}, bf16[128,2,256]{2,1,0:T(2,128)(2,1)}, bf16[128,2,256]{2,1,0:T(2,128)(2,1)}, bf16[4,2,64,2048]{3,2,1,0:T(...) custom-call(s32[1]{0:T(128)} %bitcast.refs_0_, s32[2,4]{1,0:T(2,128)} %bitcast.30, ...), custom_call_target="tpu_custom_call" | custom-call | tf_op jit(solution)/shard_map/pallas_call | solution.py:391
  5.4 0.6 collective-permute-start.22
  6.0 0.1 collective-permute-start.21
  6.1 4.3 %collective-permute-done.21.refs_6_ = bf16[4,2,64,256]{3,2,1,0:T(8,128)(2,1)S(1)} collective-permute-done((bf16[4,2,64,256]{3,2,1,0:T(8,128)(2,1)}, bf16[4,2,64,256]{3,2,1,0:T(8,128)(2,1)S(1)}, u32[]{:S(2)}, u32[]{:S(2)}) %collective-permute-start.21) | collective-permute-done | bytes 262176 | tf_op jit(solution)/shard_map/ppermute | solution.py:212
  10.4 0.0 collective-permute-done.22.refs_5_.refs_3_
  10.4 0.7 copy-done.1
  11.1 0.7 copy-done
  11.8 3.7 %shard_map.165 = (bf16[4,2,64,256]{3,2,1,0:T(8,128)(2,1)}, bf16[2,64,2048]{2,1,0:T(8,128)(2,1)}, bf16[3,64,2048]{2,1,0:T(8,128)(2,1)}, bf16[1,64,2048]{2,1,0:T(8...) custom-call(s32[1]{0:T(128)} %bitcast.refs_0_, s32[16]{0:T(128)S(1)} %copy-done.27, ...), custom_call_target="tpu_custom_call" | custom-call | tf_op jit(solution)/shard_map/pallas_call | solution.py:391
  15.5 2.9 %collective-permute-start.29 = (bf16[3,64,2048]{2,1,0:T(8,128)(2,1)}, bf16[3,64,2048]{2,1,0:T(8,128)(2,1)S(1)}, u32[]{:S(2)}, u32[]{:S(2)}) collective-permute-start(bf16[3,64,2048]{2,1,0:T(8,128)(2,1)} %get-tuple-element.103), channel_id=1, source_target_pairs={{0,8},{4,12},{8,0},{12,4},{1,9},{5,13},{9,1},{13,5},{2,10},{6,14},... | collective-permute-start | bytes 2359304 | tf_op jit(solution)/shard_map/ppermute | solution.py:212
  18.4 0.0 collective-permute-start.11
  18.4 1.5 %collective-permute-start.10 = (bf16[8,2048]{1,0:T(8,128)(2,1)S(1)}, bf16[8,2048]{1,0:T(8,128)(2,1)S(1)}, u32[]{:S(2)}, u32[]{:S(2)}) collective-permute-start(bf16[8,2048]{1,0:T(8,128)(2,1)S(1)} %copy-done.38), channel_id=1, source_target_pairs={{0,8},{4,12},{8,0},{12,4},{1,9},{5,13},{9,1},{13,5},{2,10},{6,14},... | collective-permute-start | bytes 98312 | tf_op jit(solution)/shard_map/ppermute | solution.py:212
  19.9 0.3 collective-permute-start.9
  20.3 0.3 collective-permute-start.28
  20.5 16.7 %collective-permute-done.11.refs_8_ = bf16[8,2048]{1,0:T(8,128)(2,1)S(1)} collective-permute-done((bf16[8,2048]{1,0:T(8,128)(2,1)S(1)}, bf16[8,2048]{1,0:T(8,128)(2,1)S(1)}, u32[]{:S(2)}, u32[]{:S(2)}) %collective-permute-start.11) | collective-permute-done | bytes 32800 | tf_op jit(solution)/shard_map/ppermute | solution.py:212
  37.2 1.2 %collective-permute-done.10.refs_7_ = bf16[8,2048]{1,0:T(8,128)(2,1)S(1)} collective-permute-done((bf16[8,2048]{1,0:T(8,128)(2,1)S(1)}, bf16[8,2048]{1,0:T(8,128)(2,1)S(1)}, u32[]{:S(2)}, u32[]{:S(2)}) %collective-permute-start.10) | collective-permute-done | bytes 32800 | tf_op jit(solution)/shard_map/ppermute | solution.py:212
  38.4 0.0 collective-permute-done.9.refs_6_
  38.4 0.6 copy-done.25
  39.0 0.0 copy-done.26
  39.0 4.9 %project.1 = (f32[32,128]{1,0:T(8,128)}, f32[8,128]{1,0:T(8,128)}, f32[8,128]{1,0:T(8,128)}, f32[8,128]{1,0:T(8,128)}) custom-call(s32[1]{0:T(128)} %bitcast.refs_0_, s32[48]{0:T(128)} %refs_4_.5, s32[2,4]{1,0:T(2,128)} %bitcast.34, s32[16]{0:T(128)S(1)} %copy-done.27, s32[1,16]{1,0:T(1,128)S(1)} %bitcast.25, ...), custom_call_target="tpu_custom_call" | custom-call | tf_op jit(solution)/shard_map/project/pallas_call | solution.py:674
  44.0 0.1 collective-permute-start.12
  44.0 2.1 %collective-permute-start.13 = (f32[8,128]{1,0:T(8,128)}, f32[8,128]{1,0:T(8,128)S(1)}, u32[]{:S(2)}, u32[]{:S(2)}) collective-permute-start(f32[8,128]{1,0:T(8,128)} %get-tuple-element.89), channel_id=1, source_target_pairs={{0,8},{4,12},{8,0},{12,4},{1,9},{5,13},{9,1},{13,5},{2,10},{6,14},... | collective-permute-start | bytes 12296 | tf_op jit(solution)/shard_map/ppermute | solution.py:212
  46.1 0.0 collective-permute-start.14
  46.2 0.7 slice.6
  46.9 0.0 collective-permute-done.12
  46.9 3.9 %collective-permute-start.26 = (bf16[32,2048]{1,0:T(8,128)(2,1)S(1)}, bf16[32,2048]{1,0:T(8,128)(2,1)S(1)}, u32[]{:S(2)}, u32[]{:S(2)}) collective-permute-start(bf16[32,2048]{1,0:T(8,128)(2,1)S(1)} %copy-done.6), channel_id=1, source_target_pairs={{0,3},{1,0},{2,1},{3,2},{4,7},{5,4},{6,5},{7,6},{8,11},{9,8},{10,9... | collective-permute-start | bytes 393224 | tf_op jit(solution)/shard_map/ppermute | solution.py:217
  50.7 1.3 %collective-permute-start.25 = (bf16[32,2048]{1,0:T(8,128)(2,1)S(1)}, bf16[32,2048]{1,0:T(8,128)(2,1)S(1)}, u32[]{:S(2)}, u32[]{:S(2)}) collective-permute-start(bf16[32,2048]{1,0:T(8,128)(2,1)S(1)} %copy-done.6), channel_id=1, source_target_pairs={{0,2},{1,3},{2,0},{3,1},{4,6},{5,7},{6,4},{7,5},{8,10},{9,11},{10,... | collective-permute-start | bytes 393224 | tf_op jit(solution)/shard_map/ppermute | solution.py:217
  52.1 0.7 add_add_fusion
  52.8 0.0 collective-permute-done.29.refs_5_
  52.8 0.1 collective-permute-start.31
  52.9 1.4 %collective-permute-start.17 = (f32[32,128]{1,0:T(8,128)S(1)}, f32[32,128]{1,0:T(8,128)S(1)}, u32[]{:S(2)}, u32[]{:S(2)}) collective-permute-start(f32[32,128]{1,0:T(8,128)S(1)} %pad_maximum_fusion.refs_8_), channel_id=1, source_target_pairs={{0,3},{1,0},{2,1},{3,2},{4,7},{5,4},{6,5},{7,6},{8,11},{9,8},{10,9... | collective-permute-start | bytes 49160 | tf_op jit(solution)/shard_map/ppermute | solution.py:217
  54.3 3.0 %collective-permute-done.17.refs_11_ = f32[32,128]{1,0:T(8,128)S(1)} collective-permute-done((f32[32,128]{1,0:T(8,128)S(1)}, f32[32,128]{1,0:T(8,128)S(1)}, u32[]{:S(2)}, u32[]{:S(2)}) %collective-permute-start.17) | collective-permute-done | bytes 16416 | tf_op jit(solution)/shard_map/ppermute | solution.py:217
  57.2 2.6 %collective-permute-start.16 = (f32[32,128]{1,0:T(8,128)S(1)}, f32[32,128]{1,0:T(8,128)S(1)}, u32[]{:S(2)}, u32[]{:S(2)}) collective-permute-start(f32[32,128]{1,0:T(8,128)S(1)} %pad_maximum_fusion.refs_8_), channel_id=1, source_target_pairs={{0,2},{1,3},{2,0},{3,1},{4,6},{5,7},{6,4},{7,5},{8,10},{9,11},{10,... | collective-permute-start | bytes 49160 | tf_op jit(solution)/shard_map/ppermute | solution.py:217
  59.8 2.0 %collective-permute-done.16.refs_10_ = f32[32,128]{1,0:T(8,128)S(1)} collective-permute-done((f32[32,128]{1,0:T(8,128)S(1)}, f32[32,128]{1,0:T(8,128)S(1)}, u32[]{:S(2)}, u32[]{:S(2)}) %collective-permute-start.16) | collective-permute-done | bytes 16416 | tf_op jit(solution)/shard_map/ppermute | solution.py:217
  61.9 3.6 %collective-permute-start.24 = (bf16[32,2048]{1,0:T(8,128)(2,1)S(1)}, bf16[32,2048]{1,0:T(8,128)(2,1)S(1)}, u32[]{:S(2)}, u32[]{:S(2)}) collective-permute-start(bf16[32,2048]{1,0:T(8,128)(2,1)S(1)} %copy-done.6), channel_id=1, source_target_pairs={{0,1},{1,2},{2,3},{3,0},{4,5},{5,6},{6,7},{7,4},{8,9},{9,10},{10,1... | collective-permute-start | bytes 393224 | tf_op jit(solution)/shard_map/ppermute | solution.py:217
  65.5 0.1 collective-permute-start.18
  65.6 1.6 %collective-permute-start.19 = (bf16[128,2,256]{2,1,0:T(2,128)(2,1)S(1)}, bf16[128,2,256]{2,1,0:T(2,128)(2,1)S(1)}, u32[]{:S(2)}, u32[]{:S(2)}) collective-permute-start(bf16[128,2,256]{2,1,0:T(2,128)(2,1)S(1)} %copy-done.36), channel_id=1, source_target_pairs={{0,8},{4,12},{8,0},{12,4},{1,9},{5,13},{9,1},{13,5},{2,10},{6,14},... | collective-permute-start | bytes 393224 | tf_op jit(solution)/shard_map/ppermute | solution.py:212
  67.2 2.0 %collective-permute-done.24.refs_1_ = bf16[32,2048]{1,0:T(8,128)(2,1)S(1)} collective-permute-done((bf16[32,2048]{1,0:T(8,128)(2,1)S(1)}, bf16[32,2048]{1,0:T(8,128)(2,1)S(1)}, u32[]{:S(2)}, u32[]{:S(2)}) %collective-permute-start.24) | collective-permute-done | bytes 131104 | tf_op jit(solution)/shard_map/ppermute | solution.py:217
  69.2 1.3 %collective-permute-start.15 = (f32[32,128]{1,0:T(8,128)S(1)}, f32[32,128]{1,0:T(8,128)S(1)}, u32[]{:S(2)}, u32[]{:S(2)}) collective-permute-start(f32[32,128]{1,0:T(8,128)S(1)} %pad_maximum_fusion.refs_8_), channel_id=1, source_target_pairs={{0,1},{1,2},{2,3},{3,0},{4,5},{5,6},{6,7},{7,4},{8,9},{9,10},{10,1... | collective-permute-start | bytes 49160 | tf_op jit(solution)/shard_map/ppermute | solution.py:217
  70.5 1.9 %gather.1 = bf16[32,8192]{1,0:T(8,128)(2,1)} custom-call(s32[1]{0:T(128)} %bitcast.9.shard_ref, bf16[32,2048]{1,0:T(8,128)(2,1)} %get-tuple-element.85.refs_5_.refs_0_, bf16[32,2048]{1,0:T(8,128)(2,1)} %copy-done.22, bf16[32,2048]{1,0:T(8,128)(2,1)} %copy-done.21, bf16[32,2048]{1,0:T(8,128)(2,1)} %copy-done.20), custom_call_target="tpu_custom_call" | custom-call | tf_op jit(solution)/shard_map/gather/pallas_call | solution.py:723
  72.4 2.3 %collective-permute-done.15.refs_9_ = f32[32,128]{1,0:T(8,128)S(1)} collective-permute-done((f32[32,128]{1,0:T(8,128)S(1)}, f32[32,128]{1,0:T(8,128)S(1)}, u32[]{:S(2)}, u32[]{:S(2)}) %collective-permute-start.15) | collective-permute-done | bytes 16416 | tf_op jit(solution)/shard_map/ppermute | solution.py:217
  74.7 0.0 collective-permute-start.20
  74.7 0.0 collective-permute-done.18.refs_12_
  74.7 1.6 %collective-permute-start.23 = (bf16[4,2,64,256]{3,2,1,0:T(8,128)(2,1)}, bf16[4,2,64,256]{3,2,1,0:T(8,128)(2,1)S(1)}, u32[]{:S(2)}, u32[]{:S(2)}) collective-permute-start(bf16[4,2,64,256]{3,2,1,0:T(8,128)(2,1)} %get-tuple-element.96), channel_id=1, source_target_pairs={{0,8},{4,12},{8,0},{12,4},{1,9},{5,13},{9,1},{13,5},{2,10},{6,14},... | collective-permute-start | bytes 786440 | tf_op jit(solution)/shard_map/ppermute | solution.py:212
  76.3 0.0 collective-permute-done.19.refs_13_
  76.3 0.6 collective-permute-start.27
  76.9 1.0 collective-permute-start.30
  77.8 5.8 %fusion.2.refs_18_ = f32[2,32,256]{2,1,0:T(8,128)} fusion(bf16[8192,2,256]{2,1,0:T(2,128)(2,1)} %param.19, bf16[32,8192]{1,0:T(8,128)(2,1)} %gather.1), kind=kOutput, calls=%fused_computation.2 | convolution fusion | flops 268435456 | bytes 8978432 | tf_op jit(solution)/shard_map/md,dgc->gmc/dot_general | solution.py:730
  83.6 0.0 copy-start.28
  83.6 0.0 copy-start.30
  84.3 2.1 %collective-permute-done.23 = bf16[4,2,64,256]{3,2,1,0:T(8,128)(2,1)S(1)} collective-permute-done((bf16[4,2,64,256]{3,2,1,0:T(8,128)(2,1)}, bf16[4,2,64,256]{3,2,1,0:T(8,128)(2,1)S(1)}, u32[]{:S(2)}, u32[]{:S(2)}) %collective-permute-start.23) | collective-permute-done | bytes 262176 | tf_op jit(solution)/shard_map/ppermute | solution.py:212
  86.4 0.7 copy-done.7
  87.1 7.9 %attend.1 = (bf16[14,2,2048]{2,1,0:T(2,128)(2,1)}, bf16[14,2,2,256]{3,2,1,0:T(2,128)(2,1)}, bf16[2,128,2,256]{3,2,1,0:T(2,128)(2,1)}, bf16[4,128,256]{2,1,0:T(8,128)(2,1)}) custom-call(s32[1]{0:T(128)} %bitcast.refs_0_, s32[48]{0:T(128)} %refs_1_.6, s32[2,4]{1,0:T(2,128)} %bitcast.31, s32[2,4]{1,0:T(2,128)} %bitcast.33, s32[48]{0:T(128)} %refs_4_.5, ...), custom_call_target="tpu_custom_call" | custom-call | tf_op jit(solution)/shard_map/attend/pallas_call | solution.py:732
  95.0 0.0 collective-permute-done.31.refs_7_
  95.0 0.8 copy-done.5
  95.8 0.9 copy-done.3
  96.7 3.0 %shard_map.166 = bf16[4,2,64,2048]{3,2,1,0:T(8,128)(2,1)} custom-call(s32[1]{0:T(128)} %bitcast.refs_0_, s32[16]{0:T(128)S(1)} %copy-done.28, s32[1,16]{1,0:T(1,128)S(1)} %bitcast.26, bf16[4,2,64,2048]{3,2,1,0:T(8,128)(2,1)} %copy-done, bf16[2,64,2048]{2,1,0:T(8,128)(2,1)} %copy-done.4, bf16[3,64,2048]{2,1,0:T(8,128)(2,1)} %copy-done.2, ...), custom_call_target="tpu_custom_call" | custom-call | tf_op jit(solution)/shard_map/pallas_call | solution.py:391
  99.7 0.0 collective-permute-done.27
  99.7 3.1 %conditional.1 = (bf16[4,2,64,2048]{3,2,1,0:T(8,128)(2,1)}) conditional(s32[]{:T(128)} %bitcast.13, (bf16[1,64,2048]{2,1,0:T(8,128)(2,1)S(1)}, s32[1]{0:T(128)}, s32[16]{0:T(128)S(1)}, s32[1,16]{1,0:T(1,128)S(1)}, bf16[4,2,64,2048]{3,2,1,0:T(8,128)(2,1)}) %tuple.27, (bf16[1,64,2048]{2,1,0:T(8,128)(2,1)S(1)}, ...), branch_computations={%region_0.0_spmd, %region_1.0_spmd, %region_2.0_spmd} | conditional | bytes 10486108 | solution.py:795
  99.7 0.1 collective-permute-start
  99.9 1.5 %collective-permute-done.refs_5_ = bf16[1,64,2048]{2,1,0:T(8,128)(2,1)S(1)} collective-permute-done((bf16[1,64,2048]{2,1,0:T(8,128)(2,1)S(1)}, bf16[1,64,2048]{2,1,0:T(8,128)(2,1)S(1)}, u32[]{:S(2)}, u32[]{:S(2)}) %collective-permute-start) | collective-permute-done | bytes 262176 | tf_op jit(solution)/shard_map/cond/branch_0_fun/ppermute | solution.py:212
  101.4 0.7 copy-done.16
  102.1 0.8 branch_0_fun.1
  (58 shorter events, 0.1 us)
Async XLA Ops:
  0.6 11.1 %copy-start.27 = (s32[16]{0:T(128)S(1)}, s32[16]{0:T(128)}, u32[]{:S(2)}) copy-start(s32[16]{0:T(128)} %refs_1_.7) | copy-start | bytes 196
  0.6 11.1 %copy-start.29 = (s32[16,1]{0,1:T(1,128)S(1)}, s32[16,1]{0,1:T(1,128)}, u32[]{:S(2)}) copy-start(s32[16,1]{0,1:T(1,128)} %param.28) | copy-start | bytes 196
  5.4 4.9 %collective-permute-start.22 = (bf16[4,2,64,2048]{3,2,1,0:T(8,128)(2,1)}, bf16[4,2,64,2048]{3,2,1,0:T(8,128)(2,1)S(1)}, u32[]{:S(2)}, u32[]{:S(2)}) collective-permute-start(bf16[4,2,64,2048]{3,2,1,0:T(8,128)(2,1)} %get-tuple-element.95), channel_id=1, source_target_pairs={{0,4},{4,0},{8,12},{12,8},{1,5},{5,1},{9,13},{13,9},{2,6},{6,2},{1... | collective-permute-start | bytes 6291464 | tf_op jit(solution)/shard_map/ppermute | solution.py:212
  6.0 4.4 %collective-permute-start.21 = (bf16[4,2,64,256]{3,2,1,0:T(8,128)(2,1)}, bf16[4,2,64,256]{3,2,1,0:T(8,128)(2,1)S(1)}, u32[]{:S(2)}, u32[]{:S(2)}) collective-permute-start(bf16[4,2,64,256]{3,2,1,0:T(8,128)(2,1)} %get-tuple-element.94), channel_id=1, source_target_pairs={{0,4},{4,0},{8,12},{12,8},{1,5},{5,1},{9,13},{13,9},{2,6},{6,2},{1... | collective-permute-start | bytes 786440 | tf_op jit(solution)/shard_map/ppermute | solution.py:212
  10.4 0.7 copy-start.1
  10.4 1.4 %copy-start = (bf16[4,2,64,2048]{3,2,1,0:T(8,128)(2,1)}, bf16[4,2,64,2048]{3,2,1,0:T(8,128)(2,1)S(1)}, u32[]{:S(2)}) copy-start(bf16[4,2,64,2048]{3,2,1,0:T(8,128)(2,1)S(1)} %collective-permute-done.22.refs_5_.refs_3_) | copy-start | bytes 6291460
  11.8 6.6 %copy-start.38 = (bf16[8,2048]{1,0:T(8,128)(2,1)S(1)}, bf16[8,2048]{1,0:T(8,128)(2,1)}, u32[]{:S(2)}) copy-start(bf16[8,2048]{1,0:T(8,128)(2,1)} %get-tuple-element.86) | copy-start | bytes 98308
  15.5 37.3 %collective-permute-start.29 = (bf16[3,64,2048]{2,1,0:T(8,128)(2,1)}, bf16[3,64,2048]{2,1,0:T(8,128)(2,1)S(1)}, u32[]{:S(2)}, u32[]{:S(2)}) collective-permute-start(bf16[3,64,2048]{2,1,0:T(8,128)(2,1)} %get-tuple-element.103), channel_id=1, source_target_pairs={{0,8},{4,12},{8,0},{12,4},{1,9},{5,13},{9,1},{13,5},{2,10},{6,14},... | collective-permute-start | bytes 2359304 | tf_op jit(solution)/shard_map/ppermute | solution.py:212
  18.4 18.8 %collective-permute-start.11 = (bf16[8,2048]{1,0:T(8,128)(2,1)S(1)}, bf16[8,2048]{1,0:T(8,128)(2,1)S(1)}, u32[]{:S(2)}, u32[]{:S(2)}) collective-permute-start(bf16[8,2048]{1,0:T(8,128)(2,1)S(1)} %copy-done.38), channel_id=1, source_target_pairs={{0,12},{4,8},{8,4},{12,0},{1,13},{5,9},{9,5},{13,1},{2,14},{6,10},... | collective-permute-start | bytes 98312 | tf_op jit(solution)/shard_map/ppermute | solution.py:212
  18.4 20.0 %collective-permute-start.10 = (bf16[8,2048]{1,0:T(8,128)(2,1)S(1)}, bf16[8,2048]{1,0:T(8,128)(2,1)S(1)}, u32[]{:S(2)}, u32[]{:S(2)}) collective-permute-start(bf16[8,2048]{1,0:T(8,128)(2,1)S(1)} %copy-done.38), channel_id=1, source_target_pairs={{0,8},{4,12},{8,0},{12,4},{1,9},{5,13},{9,1},{13,5},{2,10},{6,14},... | collective-permute-start | bytes 98312 | tf_op jit(solution)/shard_map/ppermute | solution.py:212
  19.9 18.5 %collective-permute-start.9 = (bf16[8,2048]{1,0:T(8,128)(2,1)S(1)}, bf16[8,2048]{1,0:T(8,128)(2,1)S(1)}, u32[]{:S(2)}, u32[]{:S(2)}) collective-permute-start(bf16[8,2048]{1,0:T(8,128)(2,1)S(1)} %copy-done.38), channel_id=1, source_target_pairs={{0,4},{4,0},{8,12},{12,8},{1,5},{5,1},{9,13},{13,9},{2,6},{6,2},{1... | collective-permute-start | bytes 98312 | tf_op jit(solution)/shard_map/ppermute | solution.py:212
  20.3 56.6 %collective-permute-start.28 = (bf16[2,64,2048]{2,1,0:T(8,128)(2,1)}, bf16[2,64,2048]{2,1,0:T(8,128)(2,1)S(1)}, u32[]{:S(2)}, u32[]{:S(2)}) collective-permute-start(bf16[2,64,2048]{2,1,0:T(8,128)(2,1)} %get-tuple-element.102), channel_id=1, source_target_pairs={{0,8},{4,12},{8,0},{12,4},{1,9},{5,13},{9,1},{13,5},{2,10},{6,14},... | collective-permute-start | bytes 1572872 | tf_op jit(solution)/shard_map/ppermute | solution.py:212
  37.2 1.2 %copy-start.24 = (bf16[8,2048]{1,0:T(8,128)(2,1)}, bf16[8,2048]{1,0:T(8,128)(2,1)S(1)}, u32[]{:S(2)}) copy-start(bf16[8,2048]{1,0:T(8,128)(2,1)S(1)} %collective-permute-done.11.refs_8_) | copy-start | bytes 98308
  38.4 0.6 copy-start.25
  38.4 0.6 copy-start.26
  39.0 7.9 %copy-start.6 = (bf16[32,2048]{1,0:T(8,128)(2,1)S(1)}, bf16[32,2048]{1,0:T(8,128)(2,1)}, u32[]{:S(2)}) copy-start(bf16[32,2048]{1,0:T(8,128)(2,1)} %get-tuple-element.85.refs_5_.refs_0_) | copy-start | bytes 393220
  39.0 26.5 %copy-start.37 = (bf16[128,2,256]{2,1,0:T(2,128)(2,1)S(1)}, bf16[128,2,256]{2,1,0:T(2,128)(2,1)}, u32[]{:S(2)}) copy-start(bf16[128,2,256]{2,1,0:T(2,128)(2,1)} %get-tuple-element.91) | copy-start | bytes 393220
  39.0 26.6 %copy-start.36 = (bf16[128,2,256]{2,1,0:T(2,128)(2,1)S(1)}, bf16[128,2,256]{2,1,0:T(2,128)(2,1)}, u32[]{:S(2)}) copy-start(bf16[128,2,256]{2,1,0:T(2,128)(2,1)} %get-tuple-element.92) | copy-start | bytes 393220
  44.0 2.9 %collective-permute-start.12 = (f32[8,128]{1,0:T(8,128)}, f32[8,128]{1,0:T(8,128)S(1)}, u32[]{:S(2)}, u32[]{:S(2)}) collective-permute-start(f32[8,128]{1,0:T(8,128)} %get-tuple-element.88), channel_id=1, source_target_pairs={{0,4},{4,0},{8,12},{12,8},{1,5},{5,1},{9,13},{13,9},{2,6},{6,2},{1... | collective-permute-start | bytes 12296 | tf_op jit(solution)/shard_map/ppermute | solution.py:212
  44.0 6.7 %collective-permute-start.13 = (f32[8,128]{1,0:T(8,128)}, f32[8,128]{1,0:T(8,128)S(1)}, u32[]{:S(2)}, u32[]{:S(2)}) collective-permute-start(f32[8,128]{1,0:T(8,128)} %get-tuple-element.89), channel_id=1, source_target_pairs={{0,8},{4,12},{8,0},{12,4},{1,9},{5,13},{9,1},{13,5},{2,10},{6,14},... | collective-permute-start | bytes 12296 | tf_op jit(solution)/shard_map/ppermute | solution.py:212
  46.1 5.9 %collective-permute-start.14 = (f32[8,128]{1,0:T(8,128)}, f32[8,128]{1,0:T(8,128)S(1)}, u32[]{:S(2)}, u32[]{:S(2)}) collective-permute-start(f32[8,128]{1,0:T(8,128)} %get-tuple-element.90), channel_id=1, source_target_pairs={{0,12},{4,8},{8,4},{12,0},{1,13},{5,9},{9,5},{13,1},{2,14},{6,10},... | collective-permute-start | bytes 12296 | tf_op jit(solution)/shard_map/ppermute | solution.py:212
  46.9 18.6 %collective-permute-start.26 = (bf16[32,2048]{1,0:T(8,128)(2,1)S(1)}, bf16[32,2048]{1,0:T(8,128)(2,1)S(1)}, u32[]{:S(2)}, u32[]{:S(2)}) collective-permute-start(bf16[32,2048]{1,0:T(8,128)(2,1)S(1)} %copy-done.6), channel_id=1, source_target_pairs={{0,3},{1,0},{2,1},{3,2},{4,7},{5,4},{6,5},{7,6},{8,11},{9,8},{10,9... | collective-permute-start | bytes 393224 | tf_op jit(solution)/shard_map/ppermute | solution.py:217
  50.7 14.9 %collective-permute-start.25 = (bf16[32,2048]{1,0:T(8,128)(2,1)S(1)}, bf16[32,2048]{1,0:T(8,128)(2,1)S(1)}, u32[]{:S(2)}, u32[]{:S(2)}) collective-permute-start(bf16[32,2048]{1,0:T(8,128)(2,1)S(1)} %copy-done.6), channel_id=1, source_target_pairs={{0,2},{1,3},{2,0},{3,1},{4,6},{5,7},{6,4},{7,5},{8,10},{9,11},{10,... | collective-permute-start | bytes 393224 | tf_op jit(solution)/shard_map/ppermute | solution.py:217
  52.8 30.8 %copy-start.2 = (bf16[3,64,2048]{2,1,0:T(8,128)(2,1)}, bf16[3,64,2048]{2,1,0:T(8,128)(2,1)S(1)}, u32[]{:S(2)}) copy-start(bf16[3,64,2048]{2,1,0:T(8,128)(2,1)S(1)} %collective-permute-done.29.refs_5_) | copy-start | bytes 2359300
  52.8 42.2 %collective-permute-start.31 = (bf16[3,64,2048]{2,1,0:T(8,128)(2,1)S(1)}, bf16[3,64,2048]{2,1,0:T(8,128)(2,1)S(1)}, u32[]{:S(2)}, u32[]{:S(2)}) collective-permute-start(bf16[3,64,2048]{2,1,0:T(8,128)(2,1)S(1)} %collective-permute-done.29.refs_5_), channel_id=1, source_target_pairs={{0,4},{4,0},{8,12},{12,8},{1,5},{5,1},{9,13},{13,9},{2,6},{6,2},{1... | collective-permute-start | bytes 2359304 | tf_op jit(solution)/shard_map/ppermute | solution.py:212
  52.9 33.5 %copy-start.23 = (f32[32,128]{1,0:T(8,128)}, f32[32,128]{1,0:T(8,128)S(1)}, u32[]{:S(2)}) copy-start(f32[32,128]{1,0:T(8,128)S(1)} %pad_maximum_fusion.refs_8_) | copy-start | bytes 49156
  52.9 4.4 %collective-permute-start.17 = (f32[32,128]{1,0:T(8,128)S(1)}, f32[32,128]{1,0:T(8,128)S(1)}, u32[]{:S(2)}, u32[]{:S(2)}) collective-permute-start(f32[32,128]{1,0:T(8,128)S(1)} %pad_maximum_fusion.refs_8_), channel_id=1, source_target_pairs={{0,3},{1,0},{2,1},{3,2},{4,7},{5,4},{6,5},{7,6},{8,11},{9,8},{10,9... | collective-permute-start | bytes 49160 | tf_op jit(solution)/shard_map/ppermute | solution.py:217
  57.2 8.3 %copy-start.31 = (f32[32,128]{1,0:T(8,128)}, f32[32,128]{1,0:T(8,128)S(1)}, u32[]{:S(2)}) copy-start(f32[32,128]{1,0:T(8,128)S(1)} %collective-permute-done.17.refs_11_) | copy-start | bytes 49156
  57.2 4.6 %collective-permute-start.16 = (f32[32,128]{1,0:T(8,128)S(1)}, f32[32,128]{1,0:T(8,128)S(1)}, u32[]{:S(2)}, u32[]{:S(2)}) collective-permute-start(f32[32,128]{1,0:T(8,128)S(1)} %pad_maximum_fusion.refs_8_), channel_id=1, source_target_pairs={{0,2},{1,3},{2,0},{3,1},{4,6},{5,7},{6,4},{7,5},{8,10},{9,11},{10,... | collective-permute-start | bytes 49160 | tf_op jit(solution)/shard_map/ppermute | solution.py:217
  61.9 3.6 %copy-start.32 = (f32[32,128]{1,0:T(8,128)}, f32[32,128]{1,0:T(8,128)S(1)}, u32[]{:S(2)}) copy-start(f32[32,128]{1,0:T(8,128)S(1)} %collective-permute-done.16.refs_10_) | copy-start | bytes 49156
  61.9 7.3 %collective-permute-start.24 = (bf16[32,2048]{1,0:T(8,128)(2,1)S(1)}, bf16[32,2048]{1,0:T(8,128)(2,1)S(1)}, u32[]{:S(2)}, u32[]{:S(2)}) collective-permute-start(bf16[32,2048]{1,0:T(8,128)(2,1)S(1)} %copy-done.6), channel_id=1, source_target_pairs={{0,1},{1,2},{2,3},{3,0},{4,5},{5,6},{6,7},{7,4},{8,9},{9,10},{10,1... | collective-permute-start | bytes 393224 | tf_op jit(solution)/shard_map/ppermute | solution.py:217
  65.5 5.0 %copy-start.20 = (bf16[32,2048]{1,0:T(8,128)(2,1)}, bf16[32,2048]{1,0:T(8,128)(2,1)S(1)}, u32[]{:S(2)}) copy-start(bf16[32,2048]{1,0:T(8,128)(2,1)S(1)} %collective-permute-done.26.refs_3_) | copy-start | bytes 393220
  65.5 9.2 %collective-permute-start.18 = (bf16[128,2,256]{2,1,0:T(2,128)(2,1)S(1)}, bf16[128,2,256]{2,1,0:T(2,128)(2,1)S(1)}, u32[]{:S(2)}, u32[]{:S(2)}) collective-permute-start(bf16[128,2,256]{2,1,0:T(2,128)(2,1)S(1)} %copy-done.37), channel_id=1, source_target_pairs={{0,4},{4,0},{8,12},{12,8},{1,5},{5,1},{9,13},{13,9},{2,6},{6,2},{1... | collective-permute-start | bytes 393224 | tf_op jit(solution)/shard_map/ppermute | solution.py:212
  65.6 4.9 %copy-start.21 = (bf16[32,2048]{1,0:T(8,128)(2,1)}, bf16[32,2048]{1,0:T(8,128)(2,1)S(1)}, u32[]{:S(2)}) copy-start(bf16[32,2048]{1,0:T(8,128)(2,1)S(1)} %collective-permute-done.25.refs_2_) | copy-start | bytes 393220
  65.6 10.6 %collective-permute-start.19 = (bf16[128,2,256]{2,1,0:T(2,128)(2,1)S(1)}, bf16[128,2,256]{2,1,0:T(2,128)(2,1)S(1)}, u32[]{:S(2)}, u32[]{:S(2)}) collective-permute-start(bf16[128,2,256]{2,1,0:T(2,128)(2,1)S(1)} %copy-done.36), channel_id=1, source_target_pairs={{0,8},{4,12},{8,0},{12,4},{1,9},{5,13},{9,1},{13,5},{2,10},{6,14},... | collective-permute-start | bytes 393224 | tf_op jit(solution)/shard_map/ppermute | solution.py:212
  69.2 1.3 %copy-start.22 = (bf16[32,2048]{1,0:T(8,128)(2,1)}, bf16[32,2048]{1,0:T(8,128)(2,1)S(1)}, u32[]{:S(2)}) copy-start(bf16[32,2048]{1,0:T(8,128)(2,1)S(1)} %collective-permute-done.24.refs_1_) | copy-start | bytes 393220
  69.2 5.5 %collective-permute-start.15 = (f32[32,128]{1,0:T(8,128)S(1)}, f32[32,128]{1,0:T(8,128)S(1)}, u32[]{:S(2)}, u32[]{:S(2)}) collective-permute-start(f32[32,128]{1,0:T(8,128)S(1)} %pad_maximum_fusion.refs_8_), channel_id=1, source_target_pairs={{0,1},{1,2},{2,3},{3,0},{4,5},{5,6},{6,7},{7,4},{8,9},{9,10},{10,1... | collective-permute-start | bytes 49160 | tf_op jit(solution)/shard_map/ppermute | solution.py:217
  74.7 1.6 %copy-start.33 = (f32[32,128]{1,0:T(8,128)}, f32[32,128]{1,0:T(8,128)S(1)}, u32[]{:S(2)}) copy-start(f32[32,128]{1,0:T(8,128)S(1)} %collective-permute-done.15.refs_9_) | copy-start | bytes 49156
  74.7 9.5 %collective-permute-start.20 = (bf16[128,2,256]{2,1,0:T(2,128)(2,1)}, bf16[128,2,256]{2,1,0:T(2,128)(2,1)S(1)}, u32[]{:S(2)}, u32[]{:S(2)}) collective-permute-start(bf16[128,2,256]{2,1,0:T(2,128)(2,1)} %get-tuple-element.93), channel_id=1, source_target_pairs={{0,12},{4,8},{8,4},{12,0},{1,13},{5,9},{9,5},{13,1},{2,14},{6,10},... | collective-permute-start | bytes 393224 | tf_op jit(solution)/shard_map/ppermute | solution.py:212
  74.7 8.9 %copy-start.17 = (bf16[128,2,256]{2,1,0:T(2,128)(2,1)}, bf16[128,2,256]{2,1,0:T(2,128)(2,1)S(1)}, u32[]{:S(2)}) copy-start(bf16[128,2,256]{2,1,0:T(2,128)(2,1)S(1)} %collective-permute-done.18.refs_12_) | copy-start | bytes 393220
  74.7 11.6 %collective-permute-start.23 = (bf16[4,2,64,256]{3,2,1,0:T(8,128)(2,1)}, bf16[4,2,64,256]{3,2,1,0:T(8,128)(2,1)S(1)}, u32[]{:S(2)}, u32[]{:S(2)}) collective-permute-start(bf16[4,2,64,256]{3,2,1,0:T(8,128)(2,1)} %get-tuple-element.96), channel_id=1, source_target_pairs={{0,8},{4,12},{8,0},{12,4},{1,9},{5,13},{9,1},{13,5},{2,10},{6,14},... | collective-permute-start | bytes 786440 | tf_op jit(solution)/shard_map/ppermute | solution.py:212
  76.3 7.3 %copy-start.18 = (bf16[128,2,256]{2,1,0:T(2,128)(2,1)}, bf16[128,2,256]{2,1,0:T(2,128)(2,1)S(1)}, u32[]{:S(2)}) copy-start(bf16[128,2,256]{2,1,0:T(2,128)(2,1)S(1)} %collective-permute-done.19.refs_13_) | copy-start | bytes 393220
  76.3 23.4 %collective-permute-start.27 = (bf16[1,64,2048]{2,1,0:T(8,128)(2,1)}, bf16[1,64,2048]{2,1,0:T(8,128)(2,1)S(1)}, u32[]{:S(2)}, u32[]{:S(2)}) collective-permute-start(bf16[1,64,2048]{2,1,0:T(8,128)(2,1)} %get-tuple-element.101), channel_id=1, source_target_pairs={{0,8},{4,12},{8,0},{12,4},{1,9},{5,13},{9,1},{13,5},{2,10},{6,14},... | collective-permute-start | bytes 786440 | tf_op jit(solution)/shard_map/ppermute | solution.py:212
  76.9 6.7 %copy-start.4 = (bf16[2,64,2048]{2,1,0:T(8,128)(2,1)}, bf16[2,64,2048]{2,1,0:T(8,128)(2,1)S(1)}, u32[]{:S(2)}) copy-start(bf16[2,64,2048]{2,1,0:T(8,128)(2,1)S(1)} %collective-permute-done.28.refs_4_) | copy-start | bytes 1572868
  76.9 18.1 %collective-permute-start.30 = (bf16[2,64,2048]{2,1,0:T(8,128)(2,1)S(1)}, bf16[2,64,2048]{2,1,0:T(8,128)(2,1)S(1)}, u32[]{:S(2)}, u32[]{:S(2)}) collective-permute-start(bf16[2,64,2048]{2,1,0:T(8,128)(2,1)S(1)} %collective-permute-done.28.refs_4_), channel_id=1, source_target_pairs={{0,4},{4,0},{8,12},{12,8},{1,5},{5,1},{9,13},{13,9},{2,6},{6,2},{1... | collective-permute-start | bytes 1572872 | tf_op jit(solution)/shard_map/ppermute | solution.py:212
  83.6 13.1 %copy-start.28 = (s32[16]{0:T(128)S(1)}, s32[16]{0:T(128)}, u32[]{:S(2)}) copy-start(s32[16]{0:T(128)} %refs_1_.7) | copy-start | bytes 196
  83.6 13.1 %copy-start.30 = (s32[16,1]{0,1:T(1,128)S(1)}, s32[16,1]{0,1:T(1,128)}, u32[]{:S(2)}) copy-start(s32[16,1]{0,1:T(1,128)} %param.28) | copy-start | bytes 196
  84.2 2.1 %copy-start.19 = (bf16[128,2,256]{2,1,0:T(2,128)(2,1)}, bf16[128,2,256]{2,1,0:T(2,128)(2,1)S(1)}, u32[]{:S(2)}) copy-start(bf16[128,2,256]{2,1,0:T(2,128)(2,1)S(1)} %collective-permute-done.20.refs_14_) | copy-start | bytes 393220
  86.4 0.7 copy-start.7
  95.0 4.8 %copy-start.34 = (bf16[1,64,2048]{2,1,0:T(8,128)(2,1)S(1)}, bf16[1,64,2048]{2,1,0:T(8,128)(2,1)}, u32[]{:S(2)}) copy-start(bf16[1,64,2048]{2,1,0:T(8,128)(2,1)} %get-tuple-element.104) | copy-start | bytes 786436
  95.0 4.8 %copy-start.35 = (bf16[1,64,2048]{2,1,0:T(8,128)(2,1)S(1)}, bf16[1,64,2048]{2,1,0:T(8,128)(2,1)}, u32[]{:S(2)}) copy-start(bf16[1,64,2048]{2,1,0:T(8,128)(2,1)} %get-tuple-element.105) | copy-start | bytes 786436
  95.0 0.8 copy-start.5
  95.8 0.9 copy-start.3
  99.7 1.6 %collective-permute-start = (bf16[1,64,2048]{2,1,0:T(8,128)(2,1)S(1)}, bf16[1,64,2048]{2,1,0:T(8,128)(2,1)S(1)}, u32[]{:S(2)}, u32[]{:S(2)}) collective-permute-start(bf16[1,64,2048]{2,1,0:T(8,128)(2,1)S(1)} %get-tuple-element.44.refs_4_), channel_id=1, source_target_pairs={{0,4},{4,0},{8,12},{12,8},{1,5},{5,1},{9,13},{13,9},{2,6},{6,2},{1... | collective-permute-start | bytes 786440 | tf_op jit(solution)/shard_map/cond/branch_0_fun/ppermute | solution.py:212
  101.3 0.7 copy-start.16

commit v3 on v2

--- a/solution.py
+++ b/solution.py
@@ -217,7 +217,7 @@
     return lax.ppermute(array, "tensor", [(i, (i + step) % size) for i in range(size)])
 
 
-ALWAYS = ((0, 2), (2, 3), (5, 1))
+ALWAYS = ((0, 1), (1, 4), (5, 1))
 AT_NEED = ((6, 1), (7, 1))
 SMEM = pl.BlockSpec(memory_space=pltpu.SMEM)
 VMEM = pl.BlockSpec(memory_space=pltpu.VMEM)
@@ -459,10 +459,11 @@
 
 def attend_kernel(spans, masks, resident, steps, kv_heads, head_length, *refs):
     (me_ref, lengths, arrival_from, arrival_slot, resident_adapter, arrival_adapter) = refs[:6]
-    holder, dest, *parts = refs[6 : -12 - len(masks)]
-    came = refs[-12 - len(masks) : -12]
-    store_b, sibling_b, across_b, base, queries, cache = refs[-12:-6]
-    out, new_kv, arrived, installed_b, fresh_ref, mixed_ref = refs[-6:]
+    holder, dest, *parts = refs[6 : -14 - len(masks)]
+    came = refs[-14 - len(masks) : -14]
+    store_b, sibling_b, across_b, base, queries, cache = refs[-14:-8]
+    out, new_kv, arrived, installed_b = refs[-8:-4]
+    fresh_ref, mixed_ref, score_ref, weight_ref = refs[-4:]
     me = me_ref[0]
     arrive = arrival_from.shape[0]
     replicas = arrival_from.shape[1]
@@ -541,74 +542,80 @@
             for n in range(resident):
                 gone[n] = jnp.where(jnp.logical_and(mine, slot == n), 1, gone[n])
     for g in range(kv_heads):
-        at = g * 2 * head_length
         columns = slice(g * head_length, (g + 1) * head_length)
         key = base[g, :, :head_length] + ADAPTER_SCALE * deltas[0][:, columns]
         value = base[g, :, head_length:] + ADAPTER_SCALE * deltas[1][:, columns]
         u, w = key[:, :half], key[:, half:]
         key = jnp.concatenate([u * cosine - w * sine, w * cosine + u * sine], axis=1)
         for part, piece in enumerate((key, value)):
-            spot = slice(at + part * head_length, at + (part + 1) * head_length)
-            rounded = piece.astype(jnp.bfloat16)
-            fresh_ref[:, spot] = rounded.astype(jnp.float32)
-            kept = jnp.where(dead, 0.0, rounded.astype(jnp.float32))[: slots * steps]
+            rounded = piece.astype(jnp.bfloat16).astype(jnp.float32)
             lanes = slice(part * head_length, (part + 1) * head_length)
+            fresh_ref[part, pl.ds(g, row_count, stride=kv_heads)] = rounded
+            kept = jnp.where(dead, 0.0, rounded)[: slots * steps]
             new_kv[:, :, g, lanes] = kept.reshape(slots, steps, head_length).astype(jnp.bfloat16)
 
     query_rows = queries.shape[1]
     heads = query_rows // steps
+    cache_rows = cache.shape[1] * kv_heads
+    new_rows = steps * kv_heads
+    pad_rows = 16 - new_rows
     row = lax.broadcasted_iota(jnp.int32, (query_rows, 1), 0)
     step_of = row // heads
     group_of = row % heads // (heads // kv_heads)
-    cache_rows = cache.shape[1] * kv_heads
     column = lax.broadcasted_iota(jnp.int32, (query_rows, cache_rows), 1)
     same = column % kv_heads == group_of
     past_row = column // kv_heads
+    late = lax.broadcasted_iota(jnp.int32, (query_rows, 128), 1)
+    allowed = jnp.logical_and(late % kv_heads == group_of, late // kv_heads <= step_of)
+    allowed = jnp.logical_and(allowed, late < new_rows)
     scale = 1.0 / math.sqrt(head_length)
+
+    def cached(n):
+        stored = cache[n] if n < resident else arrived[n - resident]
+        return stored.reshape(cache_rows, 2 * head_length)
+
+    def fresh_rows(n, part):
+        lines = fresh_ref[part, n * new_rows : (n + 1) * new_rows]
+        blank = jnp.zeros((pad_rows, head_length), jnp.float32)
+        return jnp.concatenate([lines, blank], axis=0).astype(jnp.bfloat16)
+
+    def against(query, keys):
+        return lax.dot_general(
+            query, keys, (((1,), (1,)), ((), ())), preferred_element_type=jnp.float32
+        )
+
     for n in range(slots):
-        stored = cache[n] if n < resident else arrived[n - resident]
-        stored = stored.reshape(cache_rows, 2 * head_length)
+        lines = slice(n * query_rows, (n + 1) * query_rows)
         query = queries[n]
-        score = (
-            lax.dot_general(
-                query,
-                stored[:, :head_length],
-                (((1,), (1,)), ((), ())),
-                preferred_element_type=jnp.float32,
-            )
-            * scale
+        score = against(query, cached(n)[:, :head_length]) * scale
+        score = jnp.where(jnp.logical_and(same, past_row < seen[n]), score, -jnp.inf)
+        score_ref[lines, :cache_rows] = score
+        keys = jnp.concatenate(
+            [fresh_rows(n, 0), jnp.zeros((128 - 16, head_length), jnp.bfloat16)], axis=0
         )
-        score = jnp.where(jnp.logical_and(same, past_row < seen[n]), score, -jnp.inf)
-        query = query.astype(jnp.float32)
-        recent, values = [], []
-        for t in range(steps):
-            line = fresh_ref[n * steps + t : n * steps + t + 1]
-            key = jnp.zeros((query_rows, head_length), jnp.float32)
-            value = key
-            for g in range(kv_heads):
-                at = g * 2 * head_length
-                key = jnp.where(group_of == g, line[:, at : at + head_length], key)
-                value = jnp.where(
-                    group_of == g, line[:, at + head_length : at + 2 * head_length], value
-                )
-            fit = jnp.sum(query * key, axis=1, keepdims=True) * scale
-            recent.append(jnp.where(step_of >= t, fit, -jnp.inf))
-            values.append(value)
-        peak = jnp.max(score, axis=1, keepdims=True)
-        for fit in recent:
-            peak = jnp.maximum(peak, fit)
-        past_exp = jnp.exp(score - peak)
-        recent_exp = [jnp.exp(fit - peak) for fit in recent]
-        denom = jnp.sum(past_exp, axis=1, keepdims=True)
-        for term in recent_exp:
-            denom = denom + term
-        weight = (past_exp / denom).astype(jnp.bfloat16)
-        mixed = jnp.dot(weight, stored[:, head_length:], preferred_element_type=jnp.float32)
-        for term, value in zip(recent_exp, values):
-            mixed = mixed + (term / denom).astype(jnp.bfloat16).astype(jnp.float32) * value
+        score = against(query, keys) * scale
+        score_ref[lines, cache_rows:] = jnp.where(allowed, score, -jnp.inf)
+    for n in range(slots):
+        lines = slice(n * query_rows, (n + 1) * query_rows)
+        score = score_ref[lines]
+        term = jnp.exp(score - jnp.max(score, axis=1, keepdims=True))
+        inverse = 1.0 / jnp.sum(term, axis=1, keepdims=True)
+        weight_ref[lines] = (term * inverse).astype(jnp.bfloat16)
+    for n in range(slots):
+        lines = slice(n * query_rows, (n + 1) * query_rows)
+        weight = weight_ref[lines]
+        mixed = jnp.dot(
+            weight[:, :cache_rows], cached(n)[:, head_length:], preferred_element_type=jnp.float32
+        )
+        mixed = mixed + jnp.dot(
+            weight[:, cache_rows : cache_rows + 16],
+            fresh_rows(n, 1),
+            preferred_element_type=jnp.float32,
+        )
         if n < resident:
             mixed = jnp.where(gone[n] != 0, 0.0, mixed)
-        mixed_ref[n * query_rows : (n + 1) * query_rows] = mixed
+        mixed_ref[lines] = mixed
+    for n in range(slots):
         for head in range(heads):
             lanes = slice(head * head_length, (head + 1) * head_length)
             pair = mixed_ref[pl.ds(n * query_rows + head, steps, stride=heads)]
@@ -633,7 +640,7 @@
     me = lax.axis_index("replica")
     replicas = lax.axis_size("replica")
     shards = lax.axis_size("tensor")
-    resident, _, kv_heads, head_pair = kv_cache.shape
+    resident, cap, kv_heads, head_pair = kv_cache.shape
     arrive = arrival_from.shape[1]
     slots = resident + arrive
     steps, features = hidden.shape[1:]
@@ -740,8 +747,10 @@
         in_specs=[SMEM] * 8 + [VMEM] * (shards + len(masks) + 6),
         out_specs=[VMEM] * 4,
         scratch_shapes=[
-            pltpu.VMEM((padded, kv_heads * head_pair), jnp.float32),
+            pltpu.VMEM((2, padded * kv_heads, head_length), jnp.float32),
             pltpu.VMEM((slots * steps * heads, head_length), jnp.float32),
+            pltpu.VMEM((slots * steps * heads, cap * kv_heads + 128), jnp.float32),
+            pltpu.VMEM((slots * steps * heads, cap * kv_heads + 128), jnp.bfloat16),
         ],
         name="attend",
     )(

time: 104 us -> 105 us (level)
  waiting for transfers between devices: 35 us -> 39 us
  Pallas kernels: 27 us -> 23.7 us
    ppermute x18, waiting for transfers between devices: 25.8 us -> 31.1 us  [partner(): lax.ppermute(array, 'replica', [(i, i ^ mask) for i in range(lax.axis_siz...]
    pallas_call x1, Pallas kernels: 7.89 us -> 4.67 us  [pairs_layer(): pl.pallas_call(functools.partial(attend_kernel, spans, masks, resident, s...]
    ppermute x6, waiting for transfers between devices: 9.24 us -> 7.88 us  [shifted(): lax.ppermute(array, 'tensor', [(i, (i + step) % size) for i in range(size)])]
    ppermute x18, starting transfers between devices: 12.8 us -> 14 us  [partner(): lax.ppermute(array, 'replica', [(i, i ^ mask) for i in range(lax.axis_siz...]
    ppermute x6, starting transfers between devices: 14.1 us -> 13 us  [shifted(): lax.ppermute(array, 'tensor', [(i, (i + step) % size) for i in range(size)])]
  transfers between devices with their start and end apart: 24 -> 24, of which waited for: 9 -> 9; matrix products, arithmetic and copies ran while one was open for 7% -> 7% of each run, Pallas kernels for 17% -> 14%
where the time goes in v3:
time: 105 us; the launch traced here: 104 us
  waiting for transfers between devices  39 us (37%)
  starting transfers between devices  27 us (26%)
  Pallas kernels  23.7 us (23%)
  local copies, waits for them, and re-layouts  5.9 us (6%)
  matrix products  5.76 us (5%)
  between operations  1.58 us (2%)
    ppermute x18, waiting for transfers between devices, partner(): lax.ppermute(array, 'replica', [(i, i ^ mask) for i in range(lax.axis_siz...  31.1 us
    ppermute x18, starting transfers between devices, partner(): lax.ppermute(array, 'replica', [(i, i ^ mask) for i in range(lax.axis_siz...  14 us
    ppermute x6, starting transfers between devices, shifted(): lax.ppermute(array, 'tensor', [(i, (i + step) % size) for i in range(size)])  13 us
    pallas_call x4, Pallas kernels, copy_call(): pl.pallas_call(kernel, out_shape=[pltpu.HBM(shape, dtype) for shape in sh...  12.2 us
    ppermute x6, waiting for transfers between devices, shifted(): lax.ppermute(array, 'tensor', [(i, (i + step) % size) for i in range(size)])  7.88 us
    dot_general x1, matrix products, pairs_layer(): jnp.einsum('md,dgc->gmc', full, w_kv, preferred_element_type=jnp.float32)  5.76 us
    pallas_call x1, Pallas kernels, pairs_layer(): pl.pallas_call(functools.partial(project_kernel, spans, slot_total, resid...  4.87 us
    pallas_call x1, Pallas kernels, pairs_layer(): pl.pallas_call(functools.partial(attend_kernel, spans, masks, resident, s...  4.67 us
  transfers between devices with their start and end apart: 24, of which 9 were waited for; matrix products, arithmetic and copies ran while one was open for 7% of the time, Pallas kernels for 14%

profile of v3, /device:TPU:0, one launch (start us, length us, event | category | flops | bytes accessed | tf_op | source)
XLA Modules:
  0.0 103.8 jit_solution(4653099178796265570)
XLA Ops:
  0.6 0.0 copy-start.27
  0.6 0.0 copy-start.29
  0.7 4.8 %shard_map.164 = (bf16[128,2,256]{2,1,0:T(2,128)(2,1)}, bf16[128,2,256]{2,1,0:T(2,128)(2,1)}, bf16[128,2,256]{2,1,0:T(2,128)(2,1)}, bf16[4,2,64,2048]{3,2,1,0:T(...) custom-call(s32[1]{0:T(128)} %bitcast.refs_0_, s32[2,4]{1,0:T(2,128)} %bitcast.30, ...), custom_call_target="tpu_custom_call" | custom-call | tf_op jit(solution)/shard_map/pallas_call | solution.py:391
  5.4 0.6 collective-permute-start.22
  6.0 0.1 collective-permute-start.21
  6.1 4.3 %collective-permute-done.21.refs_6_ = bf16[4,2,64,256]{3,2,1,0:T(8,128)(2,1)S(1)} collective-permute-done((bf16[4,2,64,256]{3,2,1,0:T(8,128)(2,1)}, bf16[4,2,64,256]{3,2,1,0:T(8,128)(2,1)S(1)}, u32[]{:S(2)}, u32[]{:S(2)}) %collective-permute-start.21) | collective-permute-done | bytes 262176 | tf_op jit(solution)/shard_map/ppermute | solution.py:212
  10.4 0.0 collective-permute-done.22.refs_5_.refs_3_
  10.4 0.7 copy-done.3
  11.1 0.7 copy-done
  11.8 3.7 %shard_map.165 = (bf16[4,2,64,256]{3,2,1,0:T(8,128)(2,1)}, bf16[1,64,2048]{2,1,0:T(8,128)(2,1)}, bf16[4,64,2048]{2,1,0:T(8,128)(2,1)}, bf16[1,64,2048]{2,1,0:T(8...) custom-call(s32[1]{0:T(128)} %bitcast.refs_0_, s32[16]{0:T(128)S(1)} %copy-done.27, ...), custom_call_target="tpu_custom_call" | custom-call | tf_op jit(solution)/shard_map/pallas_call | solution.py:391
  15.5 2.9 %collective-permute-start.29 = (bf16[4,64,2048]{2,1,0:T(8,128)(2,1)}, bf16[4,64,2048]{2,1,0:T(8,128)(2,1)S(1)}, u32[]{:S(2)}, u32[]{:S(2)}) collective-permute-start(bf16[4,64,2048]{2,1,0:T(8,128)(2,1)} %get-tuple-element.103), channel_id=1, source_target_pairs={{0,8},{4,12},{8,0},{12,4},{1,9},{5,13},{9,1},{13,5},{2,10},{6,14},... | collective-permute-start | bytes 3145736 | tf_op jit(solution)/shard_map/ppermute | solution.py:212
  18.4 0.0 collective-permute-start.11
  18.4 1.6 %collective-permute-start.10 = (bf16[8,2048]{1,0:T(8,128)(2,1)S(1)}, bf16[8,2048]{1,0:T(8,128)(2,1)S(1)}, u32[]{:S(2)}, u32[]{:S(2)}) collective-permute-start(bf16[8,2048]{1,0:T(8,128)(2,1)S(1)} %copy-done.38), channel_id=1, source_target_pairs={{0,8},{4,12},{8,0},{12,4},{1,9},{5,13},{9,1},{13,5},{2,10},{6,14},... | collective-permute-start | bytes 98312 | tf_op jit(solution)/shard_map/ppermute | solution.py:212
  20.0 0.3 collective-permute-start.9
  20.3 22.2 %collective-permute-done.11.refs_8_ = bf16[8,2048]{1,0:T(8,128)(2,1)S(1)} collective-permute-done((bf16[8,2048]{1,0:T(8,128)(2,1)S(1)}, bf16[8,2048]{1,0:T(8,128)(2,1)S(1)}, u32[]{:S(2)}, u32[]{:S(2)}) %collective-permute-start.11) | collective-permute-done | bytes 32800 | tf_op jit(solution)/shard_map/ppermute | solution.py:212
  42.5 1.1 %collective-permute-done.10.refs_7_ = bf16[8,2048]{1,0:T(8,128)(2,1)S(1)} collective-permute-done((bf16[8,2048]{1,0:T(8,128)(2,1)S(1)}, bf16[8,2048]{1,0:T(8,128)(2,1)S(1)}, u32[]{:S(2)}, u32[]{:S(2)}) %collective-permute-start.10) | collective-permute-done | bytes 32800 | tf_op jit(solution)/shard_map/ppermute | solution.py:212
  43.6 0.6 copy-done.25
  44.2 0.0 copy-done.26
  44.2 4.9 %project.1 = (f32[32,128]{1,0:T(8,128)}, f32[8,128]{1,0:T(8,128)}, f32[8,128]{1,0:T(8,128)}, f32[8,128]{1,0:T(8,128)}) custom-call(s32[1]{0:T(128)} %bitcast.refs_0_, s32[48]{0:T(128)} %refs_4_.5, s32[2,4]{1,0:T(2,128)} %bitcast.34, s32[16]{0:T(128)S(1)} %copy-done.27, s32[1,16]{1,0:T(1,128)S(1)} %bitcast.25, ...), custom_call_target="tpu_custom_call" | custom-call | tf_op jit(solution)/shard_map/project/pallas_call | solution.py:681
  49.1 0.1 collective-permute-start.12
  49.1 1.8 %collective-permute-start.13 = (f32[8,128]{1,0:T(8,128)}, f32[8,128]{1,0:T(8,128)S(1)}, u32[]{:S(2)}, u32[]{:S(2)}) collective-permute-start(f32[8,128]{1,0:T(8,128)} %get-tuple-element.89), channel_id=1, source_target_pairs={{0,8},{4,12},{8,0},{12,4},{1,9},{5,13},{9,1},{13,5},{2,10},{6,14},... | collective-permute-start | bytes 12296 | tf_op jit(solution)/shard_map/ppermute | solution.py:212
  51.0 0.0 collective-permute-start.14
  51.0 3.8 %collective-permute-start.26 = (bf16[32,2048]{1,0:T(8,128)(2,1)S(1)}, bf16[32,2048]{1,0:T(8,128)(2,1)S(1)}, u32[]{:S(2)}, u32[]{:S(2)}) collective-permute-start(bf16[32,2048]{1,0:T(8,128)(2,1)S(1)} %copy-done.4), channel_id=1, source_target_pairs={{0,3},{1,0},{2,1},{3,2},{4,7},{5,4},{6,5},{7,6},{8,11},{9,8},{10,9... | collective-permute-start | bytes 393224 | tf_op jit(solution)/shard_map/ppermute | solution.py:217
  54.8 0.7 slice.6
  55.5 0.0 collective-permute-start.25
  55.5 0.0 collective-permute-done.29.refs_5_
  55.5 0.1 collective-permute-start.31
  55.7 0.0 collective-permute-done.13
  55.7 0.0 collective-permute-done.14
  55.7 0.7 add_add_fusion
  56.4 1.6 %collective-permute-start.28 = (bf16[1,64,2048]{2,1,0:T(8,128)(2,1)S(1)}, bf16[1,64,2048]{2,1,0:T(8,128)(2,1)S(1)}, u32[]{:S(2)}, u32[]{:S(2)}) collective-permute-start(bf16[1,64,2048]{2,1,0:T(8,128)(2,1)S(1)} %copy-done.36), channel_id=1, source_target_pairs={{0,8},{4,12},{8,0},{12,4},{1,9},{5,13},{9,1},{13,5},{2,10},{6,14},... | collective-permute-start | bytes 786440 | tf_op jit(solution)/shard_map/ppermute | solution.py:212
  58.0 1.1 %collective-permute-start.17 = (f32[32,128]{1,0:T(8,128)S(1)}, f32[32,128]{1,0:T(8,128)S(1)}, u32[]{:S(2)}, u32[]{:S(2)}) collective-permute-start(f32[32,128]{1,0:T(8,128)S(1)} %pad_maximum_fusion.refs_8_), channel_id=1, source_target_pairs={{0,3},{1,0},{2,1},{3,2},{4,7},{5,4},{6,5},{7,6},{8,11},{9,8},{10,9... | collective-permute-start | bytes 49160 | tf_op jit(solution)/shard_map/ppermute | solution.py:217
  59.1 2.6 %collective-permute-done.17.refs_11_ = f32[32,128]{1,0:T(8,128)S(1)} collective-permute-done((f32[32,128]{1,0:T(8,128)S(1)}, f32[32,128]{1,0:T(8,128)S(1)}, u32[]{:S(2)}, u32[]{:S(2)}) %collective-permute-start.17) | collective-permute-done | bytes 16416 | tf_op jit(solution)/shard_map/ppermute | solution.py:217
  61.7 2.8 %collective-permute-start.16 = (f32[32,128]{1,0:T(8,128)S(1)}, f32[32,128]{1,0:T(8,128)S(1)}, u32[]{:S(2)}, u32[]{:S(2)}) collective-permute-start(f32[32,128]{1,0:T(8,128)S(1)} %pad_maximum_fusion.refs_8_), channel_id=1, source_target_pairs={{0,2},{1,3},{2,0},{3,1},{4,6},{5,7},{6,4},{7,5},{8,10},{9,11},{10,... | collective-permute-start | bytes 49160 | tf_op jit(solution)/shard_map/ppermute | solution.py:217
  64.5 1.8 %collective-permute-done.16.refs_10_ = f32[32,128]{1,0:T(8,128)S(1)} collective-permute-done((f32[32,128]{1,0:T(8,128)S(1)}, f32[32,128]{1,0:T(8,128)S(1)}, u32[]{:S(2)}, u32[]{:S(2)}) %collective-permute-start.16) | collective-permute-done | bytes 16416 | tf_op jit(solution)/shard_map/ppermute | solution.py:217
  66.3 3.6 %collective-permute-start.24 = (bf16[32,2048]{1,0:T(8,128)(2,1)S(1)}, bf16[32,2048]{1,0:T(8,128)(2,1)S(1)}, u32[]{:S(2)}, u32[]{:S(2)}) collective-permute-start(bf16[32,2048]{1,0:T(8,128)(2,1)S(1)} %copy-done.4), channel_id=1, source_target_pairs={{0,1},{1,2},{2,3},{3,0},{4,5},{5,6},{6,7},{7,4},{8,9},{9,10},{10,1... | collective-permute-start | bytes 393224 | tf_op jit(solution)/shard_map/ppermute | solution.py:217
  69.9 0.1 collective-permute-start.18
  70.0 0.0 collective-permute-done.25.refs_2_
  70.0 1.6 %collective-permute-start.19 = (bf16[128,2,256]{2,1,0:T(2,128)(2,1)}, bf16[128,2,256]{2,1,0:T(2,128)(2,1)S(1)}, u32[]{:S(2)}, u32[]{:S(2)}) collective-permute-start(bf16[128,2,256]{2,1,0:T(2,128)(2,1)} %get-tuple-element.92), channel_id=1, source_target_pairs={{0,8},{4,12},{8,0},{12,4},{1,9},{5,13},{9,1},{13,5},{2,10},{6,14},... | collective-permute-start | bytes 393224 | tf_op jit(solution)/shard_map/ppermute | solution.py:212
  71.7 1.5 %collective-permute-done.24.refs_1_ = bf16[32,2048]{1,0:T(8,128)(2,1)S(1)} collective-permute-done((bf16[32,2048]{1,0:T(8,128)(2,1)S(1)}, bf16[32,2048]{1,0:T(8,128)(2,1)S(1)}, u32[]{:S(2)}, u32[]{:S(2)}) %collective-permute-start.24) | collective-permute-done | bytes 131104 | tf_op jit(solution)/shard_map/ppermute | solution.py:217
  73.2 1.8 %collective-permute-start.15 = (f32[32,128]{1,0:T(8,128)S(1)}, f32[32,128]{1,0:T(8,128)S(1)}, u32[]{:S(2)}, u32[]{:S(2)}) collective-permute-start(f32[32,128]{1,0:T(8,128)S(1)} %pad_maximum_fusion.refs_8_), channel_id=1, source_target_pairs={{0,1},{1,2},{2,3},{3,0},{4,5},{5,6},{6,7},{7,4},{8,9},{9,10},{10,1... | collective-permute-start | bytes 49160 | tf_op jit(solution)/shard_map/ppermute | solution.py:217
  75.0 1.9 %gather.1 = bf16[32,8192]{1,0:T(8,128)(2,1)} custom-call(s32[1]{0:T(128)} %bitcast.9.shard_ref, bf16[32,2048]{1,0:T(8,128)(2,1)} %get-tuple-element.85.refs_5_.refs_0_, bf16[32,2048]{1,0:T(8,128)(2,1)} %copy-done.22, bf16[32,2048]{1,0:T(8,128)(2,1)} %copy-done.21, bf16[32,2048]{1,0:T(8,128)(2,1)} %copy-done.20), custom_call_target="tpu_custom_call" | custom-call | tf_op jit(solution)/shard_map/gather/pallas_call | solution.py:730
  76.9 1.9 %collective-permute-done.15.refs_9_ = f32[32,128]{1,0:T(8,128)S(1)} collective-permute-done((f32[32,128]{1,0:T(8,128)S(1)}, f32[32,128]{1,0:T(8,128)S(1)}, u32[]{:S(2)}, u32[]{:S(2)}) %collective-permute-start.15) | collective-permute-done | bytes 16416 | tf_op jit(solution)/shard_map/ppermute | solution.py:217
  78.8 0.0 collective-permute-start.20
  78.8 0.0 collective-permute-done.18.refs_12_
  78.8 1.6 %collective-permute-start.23 = (bf16[4,2,64,256]{3,2,1,0:T(8,128)(2,1)}, bf16[4,2,64,256]{3,2,1,0:T(8,128)(2,1)S(1)}, u32[]{:S(2)}, u32[]{:S(2)}) collective-permute-start(bf16[4,2,64,256]{3,2,1,0:T(8,128)(2,1)} %get-tuple-element.96), channel_id=1, source_target_pairs={{0,8},{4,12},{8,0},{12,4},{1,9},{5,13},{9,1},{13,5},{2,10},{6,14},... | collective-permute-start | bytes 786440 | tf_op jit(solution)/shard_map/ppermute | solution.py:212
  80.4 0.0 collective-permute-done.19.refs_13_
  80.4 0.5 collective-permute-start.27
  81.0 0.0 collective-permute-done.28.refs_4_
  81.0 1.0 %collective-permute-start.30 = (bf16[1,64,2048]{2,1,0:T(8,128)(2,1)S(1)}, bf16[1,64,2048]{2,1,0:T(8,128)(2,1)S(1)}, u32[]{:S(2)}, u32[]{:S(2)}) collective-permute-start(bf16[1,64,2048]{2,1,0:T(8,128)(2,1)S(1)} %collective-permute-done.28.refs_4_), channel_id=1, source_target_pairs={{0,4},{4,0},{8,12},{12,8},{1,5},{5,1},{9,13},{13,9},{2,6},{6,2},{1... | collective-permute-start | bytes 786440 | tf_op jit(solution)/shard_map/ppermute | solution.py:212
  82.0 5.8 %fusion.2.refs_18_ = f32[2,32,256]{2,1,0:T(8,128)} fusion(bf16[8192,2,256]{2,1,0:T(2,128)(2,1)} %param.19, bf16[32,8192]{1,0:T(8,128)(2,1)} %gather.1), kind=kOutput, calls=%fused_computation.2 | convolution fusion | flops 268435456 | bytes 8978432 | tf_op jit(solution)/shard_map/md,dgc->gmc/dot_general | solution.py:737
  87.8 0.0 copy-start.28
  87.8 0.0 copy-start.30
  88.5 2.0 %collective-permute-done.23 = bf16[4,2,64,256]{3,2,1,0:T(8,128)(2,1)S(1)} collective-permute-done((bf16[4,2,64,256]{3,2,1,0:T(8,128)(2,1)}, bf16[4,2,64,256]{3,2,1,0:T(8,128)(2,1)S(1)}, u32[]{:S(2)}, u32[]{:S(2)}) %collective-permute-start.23) | collective-permute-done | bytes 262176 | tf_op jit(solution)/shard_map/ppermute | solution.py:212
  90.5 0.7 copy-done.6
  91.2 4.7 %attend.1 = (bf16[14,2,2048]{2,1,0:T(2,128)(2,1)}, bf16[14,2,2,256]{3,2,1,0:T(2,128)(2,1)}, bf16[2,128,2,256]{3,2,1,0:T(2,128)(2,1)}, bf16[4,128,256]{2,1,0:T(8,128)(2,1)}) custom-call(s32[1]{0:T(128)} %bitcast.refs_0_, s32[48]{0:T(128)} %refs_1_.6, s32[2,4]{1,0:T(2,128)} %bitcast.31, s32[2,4]{1,0:T(2,128)} %bitcast.33, s32[48]{0:T(128)} %refs_4_.5, ...), custom_call_target="tpu_custom_call" | custom-call | tf_op jit(solution)/shard_map/attend/pallas_call | solution.py:739
  96.0 0.7 copy-done.7
  96.6 1.0 copy-done.2
  97.6 3.0 %shard_map.166 = bf16[4,2,64,2048]{3,2,1,0:T(8,128)(2,1)} custom-call(s32[1]{0:T(128)} %bitcast.refs_0_, s32[16]{0:T(128)S(1)} %copy-done.28, s32[1,16]{1,0:T(1,128)S(1)} %bitcast.26, bf16[4,2,64,2048]{3,2,1,0:T(8,128)(2,1)} %copy-done, bf16[1,64,2048]{2,1,0:T(8,128)(2,1)} %copy-done.5, bf16[4,64,2048]{2,1,0:T(8,128)(2,1)} %copy-done.1, ...), custom_call_target="tpu_custom_call" | custom-call | tf_op jit(solution)/shard_map/pallas_call | solution.py:391
  100.6 3.1 %conditional.1 = (bf16[4,2,64,2048]{3,2,1,0:T(8,128)(2,1)}) conditional(s32[]{:T(128)} %bitcast.13, (bf16[1,64,2048]{2,1,0:T(8,128)(2,1)S(1)}, s32[1]{0:T(128)}, s32[16]{0:T(128)S(1)}, s32[1,16]{1,0:T(1,128)S(1)}, bf16[4,2,64,2048]{3,2,1,0:T(8,128)(2,1)}) %tuple.27, (bf16[1,64,2048]{2,1,0:T(8,128)(2,1)S(1)}, ...), branch_computations={%region_0.0_spmd, %region_1.0_spmd, %region_2.0_spmd} | conditional | bytes 10486108 | solution.py:804
  100.6 0.1 collective-permute-start
  100.7 1.5 %collective-permute-done.refs_5_ = bf16[1,64,2048]{2,1,0:T(8,128)(2,1)S(1)} collective-permute-done((bf16[1,64,2048]{2,1,0:T(8,128)(2,1)S(1)}, bf16[1,64,2048]{2,1,0:T(8,128)(2,1)S(1)}, u32[]{:S(2)}, u32[]{:S(2)}) %collective-permute-start) | collective-permute-done | bytes 262176 | tf_op jit(solution)/shard_map/cond/branch_0_fun/ppermute | solution.py:212
  102.2 0.7 copy-done.16
  103.0 0.8 branch_0_fun.1
  (58 shorter events, 0.1 us)
Async XLA Ops:
  0.6 11.2 %copy-start.27 = (s32[16]{0:T(128)S(1)}, s32[16]{0:T(128)}, u32[]{:S(2)}) copy-start(s32[16]{0:T(128)} %refs_1_.7) | copy-start | bytes 196
  0.6 11.1 %copy-start.29 = (s32[16,1]{0,1:T(1,128)S(1)}, s32[16,1]{0,1:T(1,128)}, u32[]{:S(2)}) copy-start(s32[16,1]{0,1:T(1,128)} %param.28) | copy-start | bytes 196
  5.4 4.9 %collective-permute-start.22 = (bf16[4,2,64,2048]{3,2,1,0:T(8,128)(2,1)}, bf16[4,2,64,2048]{3,2,1,0:T(8,128)(2,1)S(1)}, u32[]{:S(2)}, u32[]{:S(2)}) collective-permute-start(bf16[4,2,64,2048]{3,2,1,0:T(8,128)(2,1)} %get-tuple-element.95), channel_id=1, source_target_pairs={{0,4},{4,0},{8,12},{12,8},{1,5},{5,1},{9,13},{13,9},{2,6},{6,2},{1... | collective-permute-start | bytes 6291464 | tf_op jit(solution)/shard_map/ppermute | solution.py:212
  6.0 4.4 %collective-permute-start.21 = (bf16[4,2,64,256]{3,2,1,0:T(8,128)(2,1)}, bf16[4,2,64,256]{3,2,1,0:T(8,128)(2,1)S(1)}, u32[]{:S(2)}, u32[]{:S(2)}) collective-permute-start(bf16[4,2,64,256]{3,2,1,0:T(8,128)(2,1)} %get-tuple-element.94), channel_id=1, source_target_pairs={{0,4},{4,0},{8,12},{12,8},{1,5},{5,1},{9,13},{13,9},{2,6},{6,2},{1... | collective-permute-start | bytes 786440 | tf_op jit(solution)/shard_map/ppermute | solution.py:212
  10.4 0.7 copy-start.3
  10.4 1.4 %copy-start = (bf16[4,2,64,2048]{3,2,1,0:T(8,128)(2,1)}, bf16[4,2,64,2048]{3,2,1,0:T(8,128)(2,1)S(1)}, u32[]{:S(2)}) copy-start(bf16[4,2,64,2048]{3,2,1,0:T(8,128)(2,1)S(1)} %collective-permute-done.22.refs_5_.refs_3_) | copy-start | bytes 6291460
  11.8 6.6 %copy-start.38 = (bf16[8,2048]{1,0:T(8,128)(2,1)S(1)}, bf16[8,2048]{1,0:T(8,128)(2,1)}, u32[]{:S(2)}) copy-start(bf16[8,2048]{1,0:T(8,128)(2,1)} %get-tuple-element.86) | copy-start | bytes 98308
  15.5 40.0 %collective-permute-start.29 = (bf16[4,64,2048]{2,1,0:T(8,128)(2,1)}, bf16[4,64,2048]{2,1,0:T(8,128)(2,1)S(1)}, u32[]{:S(2)}, u32[]{:S(2)}) collective-permute-start(bf16[4,64,2048]{2,1,0:T(8,128)(2,1)} %get-tuple-element.103), channel_id=1, source_target_pairs={{0,8},{4,12},{8,0},{12,4},{1,9},{5,13},{9,1},{13,5},{2,10},{6,14},... | collective-permute-start | bytes 3145736 | tf_op jit(solution)/shard_map/ppermute | solution.py:212
  18.4 24.1 %collective-permute-start.11 = (bf16[8,2048]{1,0:T(8,128)(2,1)S(1)}, bf16[8,2048]{1,0:T(8,128)(2,1)S(1)}, u32[]{:S(2)}, u32[]{:S(2)}) collective-permute-start(bf16[8,2048]{1,0:T(8,128)(2,1)S(1)} %copy-done.38), channel_id=1, source_target_pairs={{0,12},{4,8},{8,4},{12,0},{1,13},{5,9},{9,5},{13,1},{2,14},{6,10},... | collective-permute-start | bytes 98312 | tf_op jit(solution)/shard_map/ppermute | solution.py:212
  18.4 25.1 %collective-permute-start.10 = (bf16[8,2048]{1,0:T(8,128)(2,1)S(1)}, bf16[8,2048]{1,0:T(8,128)(2,1)S(1)}, u32[]{:S(2)}, u32[]{:S(2)}) collective-permute-start(bf16[8,2048]{1,0:T(8,128)(2,1)S(1)} %copy-done.38), channel_id=1, source_target_pairs={{0,8},{4,12},{8,0},{12,4},{1,9},{5,13},{9,1},{13,5},{2,10},{6,14},... | collective-permute-start | bytes 98312 | tf_op jit(solution)/shard_map/ppermute | solution.py:212
  20.0 23.6 %collective-permute-start.9 = (bf16[8,2048]{1,0:T(8,128)(2,1)S(1)}, bf16[8,2048]{1,0:T(8,128)(2,1)S(1)}, u32[]{:S(2)}, u32[]{:S(2)}) collective-permute-start(bf16[8,2048]{1,0:T(8,128)(2,1)S(1)} %copy-done.38), channel_id=1, source_target_pairs={{0,4},{4,0},{8,12},{12,8},{1,5},{5,1},{9,13},{13,9},{2,6},{6,2},{1... | collective-permute-start | bytes 98312 | tf_op jit(solution)/shard_map/ppermute | solution.py:212
  42.5 1.1 %copy-start.24 = (bf16[8,2048]{1,0:T(8,128)(2,1)}, bf16[8,2048]{1,0:T(8,128)(2,1)S(1)}, u32[]{:S(2)}) copy-start(bf16[8,2048]{1,0:T(8,128)(2,1)S(1)} %collective-permute-done.11.refs_8_) | copy-start | bytes 98308
  43.6 0.6 copy-start.25
  43.6 0.6 copy-start.26
  44.2 6.8 %copy-start.4 = (bf16[32,2048]{1,0:T(8,128)(2,1)S(1)}, bf16[32,2048]{1,0:T(8,128)(2,1)}, u32[]{:S(2)}) copy-start(bf16[32,2048]{1,0:T(8,128)(2,1)} %get-tuple-element.85.refs_5_.refs_0_) | copy-start | bytes 393220
  44.2 12.2 %copy-start.36 = (bf16[1,64,2048]{2,1,0:T(8,128)(2,1)S(1)}, bf16[1,64,2048]{2,1,0:T(8,128)(2,1)}, u32[]{:S(2)}) copy-start(bf16[1,64,2048]{2,1,0:T(8,128)(2,1)} %get-tuple-element.102) | copy-start | bytes 786436
  44.2 25.7 %copy-start.37 = (bf16[128,2,256]{2,1,0:T(2,128)(2,1)S(1)}, bf16[128,2,256]{2,1,0:T(2,128)(2,1)}, u32[]{:S(2)}) copy-start(bf16[128,2,256]{2,1,0:T(2,128)(2,1)} %get-tuple-element.91) | copy-start | bytes 393220
  49.1 6.4 %collective-permute-start.12 = (f32[8,128]{1,0:T(8,128)}, f32[8,128]{1,0:T(8,128)S(1)}, u32[]{:S(2)}, u32[]{:S(2)}) collective-permute-start(f32[8,128]{1,0:T(8,128)} %get-tuple-element.88), channel_id=1, source_target_pairs={{0,4},{4,0},{8,12},{12,8},{1,5},{5,1},{9,13},{13,9},{2,6},{6,2},{1... | collective-permute-start | bytes 12296 | tf_op jit(solution)/shard_map/ppermute | solution.py:212
  49.1 6.5 %collective-permute-start.13 = (f32[8,128]{1,0:T(8,128)}, f32[8,128]{1,0:T(8,128)S(1)}, u32[]{:S(2)}, u32[]{:S(2)}) collective-permute-start(f32[8,128]{1,0:T(8,128)} %get-tuple-element.89), channel_id=1, source_target_pairs={{0,8},{4,12},{8,0},{12,4},{1,9},{5,13},{9,1},{13,5},{2,10},{6,14},... | collective-permute-start | bytes 12296 | tf_op jit(solution)/shard_map/ppermute | solution.py:212
  51.0 4.7 %collective-permute-start.14 = (f32[8,128]{1,0:T(8,128)}, f32[8,128]{1,0:T(8,128)S(1)}, u32[]{:S(2)}, u32[]{:S(2)}) collective-permute-start(f32[8,128]{1,0:T(8,128)} %get-tuple-element.90), channel_id=1, source_target_pairs={{0,12},{4,8},{8,4},{12,0},{1,13},{5,9},{9,5},{13,1},{2,14},{6,10},... | collective-permute-start | bytes 12296 | tf_op jit(solution)/shard_map/ppermute | solution.py:212
  51.0 18.9 %collective-permute-start.26 = (bf16[32,2048]{1,0:T(8,128)(2,1)S(1)}, bf16[32,2048]{1,0:T(8,128)(2,1)S(1)}, u32[]{:S(2)}, u32[]{:S(2)}) collective-permute-start(bf16[32,2048]{1,0:T(8,128)(2,1)S(1)} %copy-done.4), channel_id=1, source_target_pairs={{0,3},{1,0},{2,1},{3,2},{4,7},{5,4},{6,5},{7,6},{8,11},{9,8},{10,9... | collective-permute-start | bytes 393224 | tf_op jit(solution)/shard_map/ppermute | solution.py:217
  55.5 14.5 %collective-permute-start.25 = (bf16[32,2048]{1,0:T(8,128)(2,1)S(1)}, bf16[32,2048]{1,0:T(8,128)(2,1)S(1)}, u32[]{:S(2)}, u32[]{:S(2)}) collective-permute-start(bf16[32,2048]{1,0:T(8,128)(2,1)S(1)} %copy-done.4), channel_id=1, source_target_pairs={{0,2},{1,3},{2,0},{3,1},{4,6},{5,7},{6,4},{7,5},{8,10},{9,11},{10,... | collective-permute-start | bytes 393224 | tf_op jit(solution)/shard_map/ppermute | solution.py:217
  55.5 32.3 %copy-start.1 = (bf16[4,64,2048]{2,1,0:T(8,128)(2,1)}, bf16[4,64,2048]{2,1,0:T(8,128)(2,1)S(1)}, u32[]{:S(2)}) copy-start(bf16[4,64,2048]{2,1,0:T(8,128)(2,1)S(1)} %collective-permute-done.29.refs_5_) | copy-start | bytes 3145732
  55.5 40.4 %collective-permute-start.31 = (bf16[4,64,2048]{2,1,0:T(8,128)(2,1)S(1)}, bf16[4,64,2048]{2,1,0:T(8,128)(2,1)S(1)}, u32[]{:S(2)}, u32[]{:S(2)}) collective-permute-start(bf16[4,64,2048]{2,1,0:T(8,128)(2,1)S(1)} %collective-permute-done.29.refs_5_), channel_id=1, source_target_pairs={{0,4},{4,0},{8,12},{12,8},{1,5},{5,1},{9,13},{13,9},{2,6},{6,2},{1... | collective-permute-start | bytes 3145736 | tf_op jit(solution)/shard_map/ppermute | solution.py:212
  56.4 24.6 %collective-permute-start.28 = (bf16[1,64,2048]{2,1,0:T(8,128)(2,1)S(1)}, bf16[1,64,2048]{2,1,0:T(8,128)(2,1)S(1)}, u32[]{:S(2)}, u32[]{:S(2)}) collective-permute-start(bf16[1,64,2048]{2,1,0:T(8,128)(2,1)S(1)} %copy-done.36), channel_id=1, source_target_pairs={{0,8},{4,12},{8,0},{12,4},{1,9},{5,13},{9,1},{13,5},{2,10},{6,14},... | collective-permute-start | bytes 786440 | tf_op jit(solution)/shard_map/ppermute | solution.py:212
  58.0 32.6 %copy-start.23 = (f32[32,128]{1,0:T(8,128)}, f32[32,128]{1,0:T(8,128)S(1)}, u32[]{:S(2)}) copy-start(f32[32,128]{1,0:T(8,128)S(1)} %pad_maximum_fusion.refs_8_) | copy-start | bytes 49156
  58.0 3.7 %collective-permute-start.17 = (f32[32,128]{1,0:T(8,128)S(1)}, f32[32,128]{1,0:T(8,128)S(1)}, u32[]{:S(2)}, u32[]{:S(2)}) collective-permute-start(f32[32,128]{1,0:T(8,128)S(1)} %pad_maximum_fusion.refs_8_), channel_id=1, source_target_pairs={{0,3},{1,0},{2,1},{3,2},{4,7},{5,4},{6,5},{7,6},{8,11},{9,8},{10,9... | collective-permute-start | bytes 49160 | tf_op jit(solution)/shard_map/ppermute | solution.py:217
  61.7 11.5 %copy-start.31 = (f32[32,128]{1,0:T(8,128)}, f32[32,128]{1,0:T(8,128)S(1)}, u32[]{:S(2)}) copy-start(f32[32,128]{1,0:T(8,128)S(1)} %collective-permute-done.17.refs_11_) | copy-start | bytes 49156
  61.7 4.6 %collective-permute-start.16 = (f32[32,128]{1,0:T(8,128)S(1)}, f32[32,128]{1,0:T(8,128)S(1)}, u32[]{:S(2)}, u32[]{:S(2)}) collective-permute-start(f32[32,128]{1,0:T(8,128)S(1)} %pad_maximum_fusion.refs_8_), channel_id=1, source_target_pairs={{0,2},{1,3},{2,0},{3,1},{4,6},{5,7},{6,4},{7,5},{8,10},{9,11},{10,... | collective-permute-start | bytes 49160 | tf_op jit(solution)/shard_map/ppermute | solution.py:217
  66.3 6.8 %copy-start.32 = (f32[32,128]{1,0:T(8,128)}, f32[32,128]{1,0:T(8,128)S(1)}, u32[]{:S(2)}) copy-start(f32[32,128]{1,0:T(8,128)S(1)} %collective-permute-done.16.refs_10_) | copy-start | bytes 49156
  66.3 6.8 %collective-permute-start.24 = (bf16[32,2048]{1,0:T(8,128)(2,1)S(1)}, bf16[32,2048]{1,0:T(8,128)(2,1)S(1)}, u32[]{:S(2)}, u32[]{:S(2)}) collective-permute-start(bf16[32,2048]{1,0:T(8,128)(2,1)S(1)} %copy-done.4), channel_id=1, source_target_pairs={{0,1},{1,2},{2,3},{3,0},{4,5},{5,6},{6,7},{7,4},{8,9},{9,10},{10,1... | collective-permute-start | bytes 393224 | tf_op jit(solution)/shard_map/ppermute | solution.py:217
  69.9 5.0 %copy-start.20 = (bf16[32,2048]{1,0:T(8,128)(2,1)}, bf16[32,2048]{1,0:T(8,128)(2,1)S(1)}, u32[]{:S(2)}) copy-start(bf16[32,2048]{1,0:T(8,128)(2,1)S(1)} %collective-permute-done.26.refs_3_) | copy-start | bytes 393220
  69.9 8.8 %collective-permute-start.18 = (bf16[128,2,256]{2,1,0:T(2,128)(2,1)S(1)}, bf16[128,2,256]{2,1,0:T(2,128)(2,1)S(1)}, u32[]{:S(2)}, u32[]{:S(2)}) collective-permute-start(bf16[128,2,256]{2,1,0:T(2,128)(2,1)S(1)} %copy-done.37), channel_id=1, source_target_pairs={{0,4},{4,0},{8,12},{12,8},{1,5},{5,1},{9,13},{13,9},{2,6},{6,2},{1... | collective-permute-start | bytes 393224 | tf_op jit(solution)/shard_map/ppermute | solution.py:212
  70.0 4.9 %copy-start.21 = (bf16[32,2048]{1,0:T(8,128)(2,1)}, bf16[32,2048]{1,0:T(8,128)(2,1)S(1)}, u32[]{:S(2)}) copy-start(bf16[32,2048]{1,0:T(8,128)(2,1)S(1)} %collective-permute-done.25.refs_2_) | copy-start | bytes 393220
  70.0 10.4 %collective-permute-start.19 = (bf16[128,2,256]{2,1,0:T(2,128)(2,1)}, bf16[128,2,256]{2,1,0:T(2,128)(2,1)S(1)}, u32[]{:S(2)}, u32[]{:S(2)}) collective-permute-start(bf16[128,2,256]{2,1,0:T(2,128)(2,1)} %get-tuple-element.92), channel_id=1, source_target_pairs={{0,8},{4,12},{8,0},{12,4},{1,9},{5,13},{9,1},{13,5},{2,10},{6,14},... | collective-permute-start | bytes 393224 | tf_op jit(solution)/shard_map/ppermute | solution.py:212
  73.2 1.8 %copy-start.22 = (bf16[32,2048]{1,0:T(8,128)(2,1)}, bf16[32,2048]{1,0:T(8,128)(2,1)S(1)}, u32[]{:S(2)}) copy-start(bf16[32,2048]{1,0:T(8,128)(2,1)S(1)} %collective-permute-done.24.refs_1_) | copy-start | bytes 393220
  73.2 5.6 %collective-permute-start.15 = (f32[32,128]{1,0:T(8,128)S(1)}, f32[32,128]{1,0:T(8,128)S(1)}, u32[]{:S(2)}, u32[]{:S(2)}) collective-permute-start(f32[32,128]{1,0:T(8,128)S(1)} %pad_maximum_fusion.refs_8_), channel_id=1, source_target_pairs={{0,1},{1,2},{2,3},{3,0},{4,5},{5,6},{6,7},{7,4},{8,9},{9,10},{10,1... | collective-permute-start | bytes 49160 | tf_op jit(solution)/shard_map/ppermute | solution.py:217
  78.8 1.7 %copy-start.33 = (f32[32,128]{1,0:T(8,128)}, f32[32,128]{1,0:T(8,128)S(1)}, u32[]{:S(2)}) copy-start(f32[32,128]{1,0:T(8,128)S(1)} %collective-permute-done.15.refs_9_) | copy-start | bytes 49156
  78.8 9.7 %collective-permute-start.20 = (bf16[128,2,256]{2,1,0:T(2,128)(2,1)}, bf16[128,2,256]{2,1,0:T(2,128)(2,1)S(1)}, u32[]{:S(2)}, u32[]{:S(2)}) collective-permute-start(bf16[128,2,256]{2,1,0:T(2,128)(2,1)} %get-tuple-element.93), channel_id=1, source_target_pairs={{0,12},{4,8},{8,4},{12,0},{1,13},{5,9},{9,5},{13,1},{2,14},{6,10},... | collective-permute-start | bytes 393224 | tf_op jit(solution)/shard_map/ppermute | solution.py:212
  78.8 9.0 %copy-start.17 = (bf16[128,2,256]{2,1,0:T(2,128)(2,1)}, bf16[128,2,256]{2,1,0:T(2,128)(2,1)S(1)}, u32[]{:S(2)}) copy-start(bf16[128,2,256]{2,1,0:T(2,128)(2,1)S(1)} %collective-permute-done.18.refs_12_) | copy-start | bytes 393220
  78.8 11.7 %collective-permute-start.23 = (bf16[4,2,64,256]{3,2,1,0:T(8,128)(2,1)}, bf16[4,2,64,256]{3,2,1,0:T(8,128)(2,1)S(1)}, u32[]{:S(2)}, u32[]{:S(2)}) collective-permute-start(bf16[4,2,64,256]{3,2,1,0:T(8,128)(2,1)} %get-tuple-element.96), channel_id=1, source_target_pairs={{0,8},{4,12},{8,0},{12,4},{1,9},{5,13},{9,1},{13,5},{2,10},{6,14},... | collective-permute-start | bytes 786440 | tf_op jit(solution)/shard_map/ppermute | solution.py:212
  80.4 7.3 %copy-start.18 = (bf16[128,2,256]{2,1,0:T(2,128)(2,1)}, bf16[128,2,256]{2,1,0:T(2,128)(2,1)S(1)}, u32[]{:S(2)}) copy-start(bf16[128,2,256]{2,1,0:T(2,128)(2,1)S(1)} %collective-permute-done.19.refs_13_) | copy-start | bytes 393220
  80.4 20.1 %collective-permute-start.27 = (bf16[1,64,2048]{2,1,0:T(8,128)(2,1)}, bf16[1,64,2048]{2,1,0:T(8,128)(2,1)S(1)}, u32[]{:S(2)}, u32[]{:S(2)}) collective-permute-start(bf16[1,64,2048]{2,1,0:T(8,128)(2,1)} %get-tuple-element.101), channel_id=1, source_target_pairs={{0,8},{4,12},{8,0},{12,4},{1,9},{5,13},{9,1},{13,5},{2,10},{6,14},... | collective-permute-start | bytes 786440 | tf_op jit(solution)/shard_map/ppermute | solution.py:212
  81.0 6.8 %copy-start.5 = (bf16[1,64,2048]{2,1,0:T(8,128)(2,1)}, bf16[1,64,2048]{2,1,0:T(8,128)(2,1)S(1)}, u32[]{:S(2)}) copy-start(bf16[1,64,2048]{2,1,0:T(8,128)(2,1)S(1)} %collective-permute-done.28.refs_4_) | copy-start | bytes 786436
  81.0 14.9 %collective-permute-start.30 = (bf16[1,64,2048]{2,1,0:T(8,128)(2,1)S(1)}, bf16[1,64,2048]{2,1,0:T(8,128)(2,1)S(1)}, u32[]{:S(2)}, u32[]{:S(2)}) collective-permute-start(bf16[1,64,2048]{2,1,0:T(8,128)(2,1)S(1)} %collective-permute-done.28.refs_4_), channel_id=1, source_target_pairs={{0,4},{4,0},{8,12},{12,8},{1,5},{5,1},{9,13},{13,9},{2,6},{6,2},{1... | collective-permute-start | bytes 786440 | tf_op jit(solution)/shard_map/ppermute | solution.py:212
  87.8 9.8 %copy-start.28 = (s32[16]{0:T(128)S(1)}, s32[16]{0:T(128)}, u32[]{:S(2)}) copy-start(s32[16]{0:T(128)} %refs_1_.7) | copy-start | bytes 196
  87.8 9.8 %copy-start.30 = (s32[16,1]{0,1:T(1,128)S(1)}, s32[16,1]{0,1:T(1,128)}, u32[]{:S(2)}) copy-start(s32[16,1]{0,1:T(1,128)} %param.28) | copy-start | bytes 196
  88.5 2.0 %copy-start.19 = (bf16[128,2,256]{2,1,0:T(2,128)(2,1)}, bf16[128,2,256]{2,1,0:T(2,128)(2,1)S(1)}, u32[]{:S(2)}) copy-start(bf16[128,2,256]{2,1,0:T(2,128)(2,1)S(1)} %collective-permute-done.20.refs_14_) | copy-start | bytes 393220
  90.5 0.7 copy-start.6
  95.9 4.7 %copy-start.34 = (bf16[1,64,2048]{2,1,0:T(8,128)(2,1)S(1)}, bf16[1,64,2048]{2,1,0:T(8,128)(2,1)}, u32[]{:S(2)}) copy-start(bf16[1,64,2048]{2,1,0:T(8,128)(2,1)} %get-tuple-element.104) | copy-start | bytes 786436
  95.9 0.7 copy-start.7
  95.9 4.7 %copy-start.35 = (bf16[1,64,2048]{2,1,0:T(8,128)(2,1)S(1)}, bf16[1,64,2048]{2,1,0:T(8,128)(2,1)}, u32[]{:S(2)}) copy-start(bf16[1,64,2048]{2,1,0:T(8,128)(2,1)} %get-tuple-element.105) | copy-start | bytes 786436
  96.6 1.0 copy-start.2
  100.6 1.6 %collective-permute-start = (bf16[1,64,2048]{2,1,0:T(8,128)(2,1)S(1)}, bf16[1,64,2048]{2,1,0:T(8,128)(2,1)S(1)}, u32[]{:S(2)}, u32[]{:S(2)}) collective-permute-start(bf16[1,64,2048]{2,1,0:T(8,128)(2,1)S(1)} %get-tuple-element.44.refs_4_), channel_id=1, source_target_pairs={{0,4},{4,0},{8,12},{12,8},{1,5},{5,1},{9,13},{13,9},{2,6},{6,2},{1... | collective-permute-start | bytes 786440 | tf_op jit(solution)/shard_map/cond/branch_0_fun/ppermute | solution.py:212
  102.2 0.7 copy-start.16

commit v4 on v3

--- a/solution.py
+++ b/solution.py
@@ -217,8 +217,8 @@
     return lax.ppermute(array, "tensor", [(i, (i + step) % size) for i in range(size)])
 
 
-ALWAYS = ((0, 1), (1, 4), (5, 1))
-AT_NEED = ((6, 1), (7, 1))
+ALWAYS = ((0, 2), (2, 3))
+AT_NEED = ((5, 1), (6, 1), (7, 1))
 SMEM = pl.BlockSpec(memory_space=pltpu.SMEM)
 VMEM = pl.BlockSpec(memory_space=pltpu.VMEM)
 
@@ -277,7 +277,8 @@
 def collect_kernel(spans, slot_total, masks, *refs):
     (me_ref, arrival_from, arrival_slot, holder, kv_cache, store_a, store_b, hidden) = refs[:8]
     *leaving, rows_a, rows_b, rows, asking = refs[8 : 12 + len(masks)]
-    buffers, semaphores = refs[12 + len(masks) : 15 + len(masks)], refs[15 + len(masks) :]
+    *buffers, raw, even = refs[12 + len(masks) : 17 + len(masks)]
+    *semaphores, raw_sems, even_sems = refs[17 + len(masks) :]
     me = me_ref[0]
     moves = []
     for i, mask in enumerate(masks):
@@ -302,15 +303,26 @@
             ]
         )
 
+    start = rows.shape[0] - asking.shape[0]
+    fetch = pltpu.make_async_copy(hidden, raw, raw_sems.at[0, 0])
+    puts = [
+        pltpu.make_async_copy(even, rows, even_sems.at[0, 0]),
+        pltpu.make_async_copy(even.at[start:], asking, even_sems.at[1, 0]),
+    ]
+
     def regroup():
-        count = hidden.shape[0] * hidden.shape[1]
-        start = rows.shape[0] - asking.shape[0]
+        count = raw.shape[0] * raw.shape[1]
         blank = jnp.zeros((rows.shape[0] - count, rows.shape[1]), rows.dtype)
-        every = hidden[...].reshape(count, rows.shape[1])
-        rows[...] = jnp.concatenate([every, blank], axis=0)
-        asking[...] = rows[start:]
-
+        fetch.wait()
+        every = raw[...].reshape(count, rows.shape[1])
+        even[...] = jnp.concatenate([every, blank], axis=0)
+        for put in puts:
+            put.start()
+
+    fetch.start()
     staged(list(zip(groups, buffers, semaphores)), regroup)
+    for put in puts:
+        put.wait()
 
 
 def pack_kernel(spans, slot_total, *refs):
@@ -385,20 +397,19 @@
     staged([(moves, buffer, sems)])
 
 
-def copy_call(kernel, tables, arrays, shapes, scratch, scalars=(), aliases=None, given=(), made=()):
+def copy_call(kernel, tables, arrays, shapes, scratch, scalars=(), aliases=None):
     hbm = pl.BlockSpec(memory_space=pl.ANY)
     dtype = arrays[0].dtype
     return pl.pallas_call(
         kernel,
         out_shape=[pltpu.HBM(shape, dtype) for shape in shapes]
-        + [jax.ShapeDtypeStruct(shape, dtype) for shape in made]
         + [jax.ShapeDtypeStruct(shape, jnp.int32) for shape in scalars],
-        in_specs=[SMEM] * len(tables) + [hbm] * len(arrays) + [VMEM] * len(given),
-        out_specs=[hbm] * len(shapes) + [VMEM] * len(made) + [SMEM] * len(scalars),
+        in_specs=[SMEM] * len(tables) + [hbm] * len(arrays),
+        out_specs=[hbm] * len(shapes) + [SMEM] * len(scalars),
         scratch_shapes=[pltpu.VMEM(shape, dtype) for shape in scratch]
         + [pltpu.SemaphoreType.DMA((2, shape[0])) for shape in scratch],
         input_output_aliases=aliases or {},
-    )(*tables, *arrays, *given)
+    )(*tables, *arrays)
 
 
 def project_kernel(spans, slot_total, resident, steps, masks, *refs):
@@ -664,11 +675,16 @@
     *leaving, rows_a, rows_b, rows, asking = copy_call(
         functools.partial(collect_kernel, spans, slot_total, masks),
         (me_table, from_table, slot_table, hot_holder),
-        (kv_cache, store_a, store_b),
-        [kv_cache.shape[1:]] * len(masks) + [(COPIES,) + row_a, (COPIES,) + row_b],
-        [(len(masks),) + kv_cache.shape[1:], (COPIES,) + row_a, (COPIES,) + row_b],
-        given=(hidden,),
-        made=[(padded, features), (block, features)],
+        (kv_cache, store_a, store_b, hidden),
+        [kv_cache.shape[1:]] * len(masks)
+        + [(COPIES,) + row_a, (COPIES,) + row_b, (padded, features), (block, features)],
+        [
+            (len(masks),) + kv_cache.shape[1:],
+            (COPIES,) + row_a,
+            (COPIES,) + row_b,
+            hidden.shape,
+            (padded, features),
+        ],
     )
     sibling_a = partner(rows_a, 1)
     sibling_b = partner(rows_b, 1)
@@ -774,34 +790,38 @@
     installed_b = installed_b.reshape((COPIES,) + row_b)
 
     tables = (me_table, hot_holder, dest_table)
-    early = len(ALWAYS) - 1
-    other = [partner(array, 1) for array in got[:early]]
-    (placed,) = copy_call(
-        functools.partial(place_kernel, spans, slot_total, ALWAYS[:early]),
-        tables,
-        (sibling_a, *got[:early], *other),
-        [(COPIES,) + row_a],
-        [(unit_total,) + unit_shape],
-    )
 
     def finish(count):
-        def branch(placed, *arrays):
-            late = [arrays[0]] + [partner(array, 2) for array in arrays[1:][:count]]
+        def branch(sibling_a, first_other, *arrays):
+            got, rest = list(arrays[: len(ALWAYS)]), arrays[len(ALWAYS) :]
+            late = [partner(array, 2) for array in rest[:count]]
+            other = [first_other] + [partner(array, 1) for array in got[1:]]
+            (placed,) = copy_call(
+                functools.partial(place_kernel, spans, slot_total, ALWAYS),
+                tables,
+                (sibling_a, *got, *other),
+                [(COPIES,) + row_a],
+                [(unit_total,) + unit_shape],
+            )
+            if not count:
+                return placed
             other = [partner(array, 1) for array in late]
-            spread = (ALWAYS[early:] + AT_NEED)[: len(late)]
-            return copy_call(
-                functools.partial(place_kernel, spans, slot_total, spread),
+            (placed,) = copy_call(
+                functools.partial(place_kernel, spans, slot_total, AT_NEED[:count]),
                 tables,
                 (placed, *late, *other),
                 [(COPIES,) + row_a],
                 [(unit_total,) + unit_shape],
                 aliases={len(tables): 0},
-            )[0]
+            )
+            return placed
 
         return branch
 
     branches = [finish(count) for count in range(len(AT_NEED) + 1)]
-    installed_a = lax.switch(extra[0], branches, placed, got[early], *units[len(ALWAYS) :])
+    first_other = partner(got[0], 1)
+    *rest, attn_out = lax.optimization_barrier((*units[len(ALWAYS) :], attn_out))
+    installed_a = lax.switch(extra[0], branches, sibling_a, first_other, *got, *rest)
     return (attn_out, new_kv, arrived, installed_a, installed_b)
 
 

time: 105 us -> 84 us (0.80)
  the two profiles are of different devices: /device:TPU:0 before, /device:TPU:4 now
where the time goes in v4:
time: 84 us; the launch traced here: 83.5 us
  waiting for transfers between devices  26.2 us (31%)
  Pallas kernels  25.6 us (30%)
  starting transfers between devices  19.6 us (23%)
  matrix products  5.74 us (7%)
  local copies, waits for them, and re-layouts  4.24 us (5%)
  between operations  1.36 us (2%)
    ppermute x18, waiting for transfers between devices, partner(): lax.ppermute(array, 'replica', [(i, i ^ mask) for i in range(lax.axis_siz...  14.7 us
    pallas_call x4, Pallas kernels, copy_call(): pl.pallas_call(kernel, out_shape=[pltpu.HBM(shape, dtype) for shape in sh...  14.1 us
    ppermute x6, waiting for transfers between devices, shifted(): lax.ppermute(array, 'tensor', [(i, (i + step) % size) for i in range(size)])  11.6 us
    ppermute x18, starting transfers between devices, partner(): lax.ppermute(array, 'replica', [(i, i ^ mask) for i in range(lax.axis_siz...  10.5 us
    ppermute x6, starting transfers between devices, shifted(): lax.ppermute(array, 'tensor', [(i, (i + step) % size) for i in range(size)])  9.05 us
    dot_general x1, matrix products, pairs_layer(): jnp.einsum('md,dgc->gmc', full, w_kv, preferred_element_type=jnp.float32)  5.74 us
    pallas_call x1, Pallas kernels, pairs_layer(): pl.pallas_call(functools.partial(project_kernel, spans, slot_total, resid...  4.9 us
    pallas_call x1, Pallas kernels, pairs_layer(): pl.pallas_call(functools.partial(attend_kernel, spans, masks, resident, s...  4.68 us
  transfers between devices with their start and end apart: 24, of which 8 were waited for; matrix products, arithmetic and copies ran while one was open for 9% of the time, Pallas kernels for 22%

profile of v4, /device:TPU:4, one launch (start us, length us, event | category | flops | bytes accessed | tf_op | source)
XLA Modules:
  0.0 83.5 jit_solution(3417202998437653979)
XLA Ops:
  0.6 0.0 copy-start.11
  0.6 0.0 copy-start.15
  0.7 4.9 %shard_map.164 = (bf16[128,2,256]{2,1,0:T(2,128)(2,1)}, bf16[128,2,256]{2,1,0:T(2,128)(2,1)}, bf16[128,2,256]{2,1,0:T(2,128)(2,1)}, bf16[4,2,64,2048]{3,2,1,0:T(...) custom-call(s32[1]{0:T(128)} %bitcast.refs_0_, s32[2,4]{1,0:T(2,128)} %bitcast.29, ...), custom_call_target="tpu_custom_call" | custom-call | tf_op jit(solution)/shard_map/pallas_call | solution.py:403
  5.5 0.1 collective-permute-start.16
  5.6 0.5 collective-permute-start.17
  6.1 1.3 %collective-permute-start.20 = (bf16[8,2048]{1,0:T(8,128)(2,1)}, bf16[8,2048]{1,0:T(8,128)(2,1)S(1)}, u32[]{:S(2)}, u32[]{:S(2)}) collective-permute-start(bf16[8,2048]{1,0:T(8,128)(2,1)} %get-tuple-element.144), channel_id=1, source_target_pairs={{0,12},{4,8},{8,4},{12,0},{1,13},{5,9},{9,5},{13,1},{2,14},{6,10},... | collective-permute-start | bytes 98312 | tf_op jit(solution)/shard_map/ppermute | solution.py:212
  7.5 0.4 collective-permute-start.19
  7.8 0.2 collective-permute-start.18
  8.0 2.4 %collective-permute-done.17.refs_6_ = bf16[4,2,64,256]{3,2,1,0:T(8,128)(2,1)S(1)} collective-permute-done((bf16[4,2,64,256]{3,2,1,0:T(8,128)(2,1)}, bf16[4,2,64,256]{3,2,1,0:T(8,128)(2,1)S(1)}, u32[]{:S(2)}, u32[]{:S(2)}) %collective-permute-start.17) | collective-permute-done | bytes 262176 | tf_op jit(solution)/shard_map/ppermute | solution.py:212
  10.4 0.0 collective-permute-done.16.refs_5_
  10.4 0.7 copy-done
  11.1 3.6 %shard_map.165 = (bf16[4,2,64,256]{3,2,1,0:T(8,128)(2,1)}, bf16[2,64,2048]{2,1,0:T(8,128)(2,1)}, bf16[3,64,2048]{2,1,0:T(8,128)(2,1)}, bf16[1,64,2048]{2,1,0:T(8...) custom-call(s32[1]{0:T(128)} %bitcast.refs_0_, s32[16]{0:T(128)S(1)} %copy-done.11, ...), custom_call_target="tpu_custom_call" | custom-call | tf_op jit(solution)/shard_map/pallas_call | solution.py:403
  14.7 1.7 %collective-permute-start.35 = (bf16[2,64,2048]{2,1,0:T(8,128)(2,1)}, bf16[2,64,2048]{2,1,0:T(8,128)(2,1)S(1)}, u32[]{:S(2)}, u32[]{:S(2)}) collective-permute-start(bf16[2,64,2048]{2,1,0:T(8,128)(2,1)} %get-tuple-element.159), channel_id=1, source_target_pairs={{0,8},{4,12},{8,0},{12,4},{1,9},{5,13},{9,1},{13,5},{2,10},{6,14},... | collective-permute-start | bytes 1572872 | tf_op jit(solution)/shard_map/ppermute | solution.py:212
  16.4 0.0 collective-permute-done.20.refs_8_
  16.4 0.0 collective-permute-done.19.refs_7_
  16.4 0.0 copy-start.21
  16.4 0.6 copy-done.19
  17.0 0.0 copy-done.20
  17.0 0.0 copy-done.21
  17.0 4.9 %project.1 = (f32[32,128]{1,0:T(8,128)}, f32[8,128]{1,0:T(8,128)}, f32[8,128]{1,0:T(8,128)}, f32[8,128]{1,0:T(8,128)}) custom-call(s32[1]{0:T(128)} %bitcast.refs_0_, s32[48]{0:T(128)} %refs_4_.5, s32[2,4]{1,0:T(2,128)} %bitcast.33, s32[16]{0:T(128)S(1)} %copy-done.11, s32[1,16]{1,0:T(1,128)S(1)} %bitcast.28, ...), custom_call_target="tpu_custom_call" | custom-call | tf_op jit(solution)/shard_map/project/pallas_call | solution.py:697
  21.9 0.1 collective-permute-start.21
  22.0 0.5 collective-permute-start.22
  22.5 1.3 %collective-permute-start.23 = (f32[8,128]{1,0:T(8,128)}, f32[8,128]{1,0:T(8,128)S(1)}, u32[]{:S(2)}, u32[]{:S(2)}) collective-permute-start(f32[8,128]{1,0:T(8,128)} %get-tuple-element.148), channel_id=1, source_target_pairs={{0,12},{4,8},{8,4},{12,0},{1,13},{5,9},{9,5},{13,1},{2,14},{6,10},... | collective-permute-start | bytes 12296 | tf_op jit(solution)/shard_map/ppermute | solution.py:212
  23.8 3.6 %collective-permute-start.33 = (bf16[32,2048]{1,0:T(8,128)(2,1)S(1)}, bf16[32,2048]{1,0:T(8,128)(2,1)S(1)}, u32[]{:S(2)}, u32[]{:S(2)}) collective-permute-start(bf16[32,2048]{1,0:T(8,128)(2,1)S(1)} %copy-done.5), channel_id=1, source_target_pairs={{0,3},{1,0},{2,1},{3,2},{4,7},{5,4},{6,5},{7,6},{8,11},{9,8},{10,9... | collective-permute-start | bytes 393224 | tf_op jit(solution)/shard_map/ppermute | solution.py:217
  27.4 0.7 slice.6
  28.2 0.0 collective-permute-done.21
  28.2 0.8 %collective-permute-done.22 = f32[8,128]{1,0:T(8,128)S(1)} collective-permute-done((f32[8,128]{1,0:T(8,128)}, f32[8,128]{1,0:T(8,128)S(1)}, u32[]{:S(2)}, u32[]{:S(2)}) %collective-permute-start.22) | collective-permute-done | bytes 4128 | tf_op jit(solution)/shard_map/ppermute | solution.py:212
  29.0 0.0 collective-permute-done.23
  29.0 0.7 add_add_fusion
  29.7 1.7 %collective-permute-start.34 = (bf16[3,64,2048]{2,1,0:T(8,128)(2,1)}, bf16[3,64,2048]{2,1,0:T(8,128)(2,1)S(1)}, u32[]{:S(2)}, u32[]{:S(2)}) collective-permute-start(bf16[3,64,2048]{2,1,0:T(8,128)(2,1)} %get-tuple-element.158), channel_id=1, source_target_pairs={{0,8},{4,12},{8,0},{12,4},{1,9},{5,13},{9,1},{13,5},{2,10},{6,14},... | collective-permute-start | bytes 2359304 | tf_op jit(solution)/shard_map/ppermute | solution.py:212
  31.4 3.6 %collective-permute-start.26 = (f32[32,128]{1,0:T(8,128)S(1)}, f32[32,128]{1,0:T(8,128)}, u32[]{:S(2)}, u32[]{:S(2)}) collective-permute-start(f32[32,128]{1,0:T(8,128)S(1)} %pad_maximum_fusion.refs_8_), channel_id=1, source_target_pairs={{0,3},{1,0},{2,1},{3,2},{4,7},{5,4},{6,5},{7,6},{8,11},{9,8},{10,9... | collective-permute-start | bytes 49160 | tf_op jit(solution)/shard_map/ppermute | solution.py:217
  35.0 1.4 %collective-permute-done.26.refs_11_ = f32[32,128]{1,0:T(8,128)} collective-permute-done((f32[32,128]{1,0:T(8,128)S(1)}, f32[32,128]{1,0:T(8,128)}, u32[]{:S(2)}, u32[]{:S(2)}) %collective-permute-start.26) | collective-permute-done | bytes 16416 | tf_op jit(solution)/shard_map/ppermute | solution.py:217
  36.5 1.4 %collective-permute-start.31 = (bf16[32,2048]{1,0:T(8,128)(2,1)S(1)}, bf16[32,2048]{1,0:T(8,128)(2,1)S(1)}, u32[]{:S(2)}, u32[]{:S(2)}) collective-permute-start(bf16[32,2048]{1,0:T(8,128)(2,1)S(1)} %copy-done.5), channel_id=1, source_target_pairs={{0,1},{1,2},{2,3},{3,0},{4,5},{5,6},{6,7},{7,4},{8,9},{9,10},{10,1... | collective-permute-start | bytes 393224 | tf_op jit(solution)/shard_map/ppermute | solution.py:217
  37.9 0.0 collective-permute-done.33.refs_3_
  37.9 0.0 collective-permute-start.27
  37.9 7.0 %collective-permute-done.32.refs_2_ = bf16[32,2048]{1,0:T(8,128)(2,1)S(1)} collective-permute-done((bf16[32,2048]{1,0:T(8,128)(2,1)S(1)}, bf16[32,2048]{1,0:T(8,128)(2,1)S(1)}, u32[]{:S(2)}, u32[]{:S(2)}) %collective-permute-start.32) | collective-permute-done | bytes 131104 | tf_op jit(solution)/shard_map/ppermute | solution.py:217
  44.9 0.0 collective-permute-done.31.refs_1_
  44.9 0.6 copy-done.8
  45.5 0.6 copy-done.9
  46.2 0.4 collective-permute-start.24
  46.6 1.9 %gather.1 = bf16[32,8192]{1,0:T(8,128)(2,1)} custom-call(s32[1]{0:T(128)} %bitcast.9.shard_ref, bf16[32,2048]{1,0:T(8,128)(2,1)} %get-tuple-element.143.refs_5_.refs_0_, bf16[32,2048]{1,0:T(8,128)(2,1)} %copy-done.9, bf16[32,2048]{1,0:T(8,128)(2,1)} %copy-done.8, bf16[32,2048]{1,0:T(8,128)(2,1)} %copy-done.7), custom_call_target="tpu_custom_call" | custom-call | tf_op jit(solution)/shard_map/gather/pallas_call | solution.py:746
  48.5 1.1 %collective-permute-done.25.refs_10_ = f32[32,128]{1,0:T(8,128)} collective-permute-done((f32[32,128]{1,0:T(8,128)S(1)}, f32[32,128]{1,0:T(8,128)}, u32[]{:S(2)}, u32[]{:S(2)}) %collective-permute-start.25) | collective-permute-done | bytes 16416 | tf_op jit(solution)/shard_map/ppermute | solution.py:217
  49.6 0.1 collective-permute-start.28
  49.8 2.1 %collective-permute-done.24.refs_9_ = f32[32,128]{1,0:T(8,128)} collective-permute-done((f32[32,128]{1,0:T(8,128)S(1)}, f32[32,128]{1,0:T(8,128)}, u32[]{:S(2)}, u32[]{:S(2)}) %collective-permute-start.24) | collective-permute-done | bytes 16416 | tf_op jit(solution)/shard_map/ppermute | solution.py:217
  51.8 0.0 collective-permute-start.29
  51.8 0.0 collective-permute-done.27.refs_12_
  51.8 0.1 collective-permute-start.30
  52.0 1.7 %collective-permute-start.36 = (bf16[2,64,2048]{2,1,0:T(8,128)(2,1)S(1)}, bf16[2,64,2048]{2,1,0:T(8,128)(2,1)}, u32[]{:S(2)}, u32[]{:S(2)}) collective-permute-start(bf16[2,64,2048]{2,1,0:T(8,128)(2,1)S(1)} %collective-permute-done.35), channel_id=1, source_target_pairs={{0,4},{4,0},{8,12},{12,8},{1,5},{5,1},{9,13},{13,9},{2,6},{6,2},{1... | collective-permute-start | bytes 1572872 | tf_op jit(solution)/shard_map/ppermute | solution.py:212
  53.7 5.7 %fusion.2.refs_18_ = f32[2,32,256]{2,1,0:T(8,128)} fusion(bf16[8192,2,256]{2,1,0:T(2,128)(2,1)} %param.20, bf16[32,8192]{1,0:T(8,128)(2,1)} %gather.1), kind=kOutput, calls=%fused_computation.2 | convolution fusion | flops 268435456 | bytes 8978432 | tf_op jit(solution)/shard_map/md,dgc->gmc/dot_general | solution.py:753
  60.0 0.0 collective-permute-done.28.refs_13_
  60.0 0.0 collective-permute-done.29.refs_14_
  60.0 3.1 %collective-permute-done.30 = bf16[4,2,64,256]{3,2,1,0:T(8,128)(2,1)} collective-permute-done((bf16[4,2,64,256]{3,2,1,0:T(8,128)(2,1)}, bf16[4,2,64,256]{3,2,1,0:T(8,128)(2,1)}, u32[]{:S(2)}, u32[]{:S(2)}) %collective-permute-start.30) | collective-permute-done | bytes 262176 | tf_op jit(solution)/shard_map/ppermute | solution.py:212
  63.1 4.7 %attend.1 = (bf16[14,2,2048]{2,1,0:T(2,128)(2,1)}, bf16[14,2,2,256]{3,2,1,0:T(2,128)(2,1)}, bf16[2,128,2,256]{3,2,1,0:T(2,128)(2,1)}, bf16[4,128,256]{2,1,0:T(8,128)(2,1)}) custom-call(s32[1]{0:T(128)} %bitcast.refs_0_, s32[48]{0:T(128)} %refs_1_.5, s32[2,4]{1,0:T(2,128)} %bitcast.30, s32[2,4]{1,0:T(2,128)} %bitcast.32, s32[48]{0:T(128)} %refs_4_.5, ...), custom_call_target="tpu_custom_call" | custom-call | tf_op jit(solution)/shard_map/attend/pallas_call | solution.py:755
  67.8 0.0 collective-permute-done.36
  67.8 15.7 %conditional.1 = (bf16[4,2,64,2048]{3,2,1,0:T(8,128)(2,1)}) conditional(s32[]{:T(128)} %bitcast.13, (bf16[3,64,2048]{2,1,0:T(8,128)(2,1)S(1)}, s32[1]{0:T(128)}, s32[16]{0:T(128)}, s32[1,16]{1,0:T(1,128)}, bf16[4,2,64,2048]{3,2,1,0:T(8,128)(2,1)S(1)}, /*index=5*/bf16[2,64,2048]{2,1,0:T(8,128)(2,1)S(1)}, ...), branch_computations={%region_0.0_spmd, %region_1.0_spmd, %region_2.0_spmd, %region_3.0_... | conditional | bytes 12583796 | solution.py:824
  67.9 0.2 collective-permute-start.1
  68.0 0.6 collective-permute-start.2
  68.6 8.4 %collective-permute-done.2.refs_4_ = bf16[1,64,2048]{2,1,0:T(8,128)(2,1)} collective-permute-done((bf16[1,64,2048]{2,1,0:T(8,128)(2,1)}, bf16[1,64,2048]{2,1,0:T(8,128)(2,1)}, u32[]{:S(2)}, u32[]{:S(2)}) %collective-permute-start.2) | collective-permute-done | bytes 262176 | tf_op jit(solution)/shard_map/cond/branch_1_fun/ppermute | solution.py:212
  77.0 0.0 collective-permute-start.3
  77.0 0.0 collective-permute-done.1.refs_7_
  77.0 0.9 %copy-done.3 = bf16[3,64,2048]{2,1,0:T(8,128)(2,1)} copy-done((bf16[3,64,2048]{2,1,0:T(8,128)(2,1)}, bf16[3,64,2048]{2,1,0:T(8,128)(2,1)S(1)}, u32[]{:S(2)}) %copy-start.3) | copy-done | bytes 786456 | tf_op jit(solution)/shard_map/cond
  77.9 3.1 %branch_1_fun.2.refs_3_ = bf16[4,2,64,2048]{3,2,1,0:T(8,128)(2,1)} custom-call(s32[1]{0:T(128)} %get-tuple-element.80.refs_0_, s32[16]{0:T(128)} %get-tuple-element.81.refs_1_, s32[1,16]{1,0:T(1,128)} %get-tuple-element.82.refs_2_, bf16[4,2,64,2048]{3,2,1,0:T(8,128)(2,1)S(1)} %get-tuple-element.83.refs_3_, ...), custom_call_target="tpu_custom_call" | custom-call | tf_op jit(solution)/shard_map/cond/branch_1_fun/pallas_call | solution.py:403
  81.0 0.0 collective-permute-done.3.refs_5_
  81.0 2.5 %branch_1_fun.3 = bf16[4,2,64,2048]{3,2,1,0:T(8,128)(2,1)} custom-call(s32[1]{0:T(128)} %get-tuple-element.80.refs_0_, s32[16]{0:T(128)S(1)} %copy-done.12, s32[1,16]{1,0:T(1,128)S(1)} %copy-done.16, bf16[4,2,64,2048]{3,2,1,0:T(8,128)(2,1)} %branch_1_fun.2.refs_3_, ...), custom_call_target="tpu_custom_call", output_to_operand_aliasing={{}: (3, {})} | custom-call | tf_op jit(solution)/shard_map/cond/branch_1_fun/pallas_call | solution.py:403
  (26 shorter events, 0.1 us)
Async XLA Ops:
  0.6 10.4 %copy-start.11 = (s32[16]{0:T(128)S(1)}, s32[16]{0:T(128)}, u32[]{:S(2)}) copy-start(s32[16]{0:T(128)} %refs_6_.3) | copy-start | bytes 196
  0.6 10.4 %copy-start.15 = (s32[16,1]{0,1:T(1,128)S(1)}, s32[16,1]{0,1:T(1,128)}, u32[]{:S(2)}) copy-start(s32[16,1]{0,1:T(1,128)} %param.29) | copy-start | bytes 196
  5.5 4.8 %collective-permute-start.16 = (bf16[4,2,64,2048]{3,2,1,0:T(8,128)(2,1)}, bf16[4,2,64,2048]{3,2,1,0:T(8,128)(2,1)S(1)}, u32[]{:S(2)}, u32[]{:S(2)}) collective-permute-start(bf16[4,2,64,2048]{3,2,1,0:T(8,128)(2,1)} %get-tuple-element.138), channel_id=1, source_target_pairs={{0,4},{4,0},{8,12},{12,8},{1,5},{5,1},{9,13},{13,9},{2,6},{6,2},{1... | collective-permute-start | bytes 6291464 | tf_op jit(solution)/shard_map/ppermute | solution.py:212
  5.6 4.7 %collective-permute-start.17 = (bf16[4,2,64,256]{3,2,1,0:T(8,128)(2,1)}, bf16[4,2,64,256]{3,2,1,0:T(8,128)(2,1)S(1)}, u32[]{:S(2)}, u32[]{:S(2)}) collective-permute-start(bf16[4,2,64,256]{3,2,1,0:T(8,128)(2,1)} %get-tuple-element.139), channel_id=1, source_target_pairs={{0,4},{4,0},{8,12},{12,8},{1,5},{5,1},{9,13},{13,9},{2,6},{6,2},{1... | collective-permute-start | bytes 786440 | tf_op jit(solution)/shard_map/ppermute | solution.py:212
  6.1 10.2 %collective-permute-start.20 = (bf16[8,2048]{1,0:T(8,128)(2,1)}, bf16[8,2048]{1,0:T(8,128)(2,1)S(1)}, u32[]{:S(2)}, u32[]{:S(2)}) collective-permute-start(bf16[8,2048]{1,0:T(8,128)(2,1)} %get-tuple-element.144), channel_id=1, source_target_pairs={{0,12},{4,8},{8,4},{12,0},{1,13},{5,9},{9,5},{13,1},{2,14},{6,10},... | collective-permute-start | bytes 98312 | tf_op jit(solution)/shard_map/ppermute | solution.py:212
  7.5 8.9 %collective-permute-start.19 = (bf16[8,2048]{1,0:T(8,128)(2,1)}, bf16[8,2048]{1,0:T(8,128)(2,1)S(1)}, u32[]{:S(2)}, u32[]{:S(2)}) collective-permute-start(bf16[8,2048]{1,0:T(8,128)(2,1)} %get-tuple-element.144), channel_id=1, source_target_pairs={{0,8},{4,12},{8,0},{12,4},{1,9},{5,13},{9,1},{13,5},{2,10},{6,14},... | collective-permute-start | bytes 98312 | tf_op jit(solution)/shard_map/ppermute | solution.py:212
  7.8 8.6 %collective-permute-start.18 = (bf16[8,2048]{1,0:T(8,128)(2,1)}, bf16[8,2048]{1,0:T(8,128)(2,1)S(1)}, u32[]{:S(2)}, u32[]{:S(2)}) collective-permute-start(bf16[8,2048]{1,0:T(8,128)(2,1)} %get-tuple-element.144), channel_id=1, source_target_pairs={{0,4},{4,0},{8,12},{12,8},{1,5},{5,1},{9,13},{13,9},{2,6},{6,2},{1... | collective-permute-start | bytes 98312 | tf_op jit(solution)/shard_map/ppermute | solution.py:212
  10.4 0.7 copy-start
  14.7 37.3 %collective-permute-start.35 = (bf16[2,64,2048]{2,1,0:T(8,128)(2,1)}, bf16[2,64,2048]{2,1,0:T(8,128)(2,1)S(1)}, u32[]{:S(2)}, u32[]{:S(2)}) collective-permute-start(bf16[2,64,2048]{2,1,0:T(8,128)(2,1)} %get-tuple-element.159), channel_id=1, source_target_pairs={{0,8},{4,12},{8,0},{12,4},{1,9},{5,13},{9,1},{13,5},{2,10},{6,14},... | collective-permute-start | bytes 1572872 | tf_op jit(solution)/shard_map/ppermute | solution.py:212
  16.4 0.6 copy-start.19
  16.4 0.6 copy-start.20
  16.4 0.6 copy-start.21
  17.0 6.8 %copy-start.5 = (bf16[32,2048]{1,0:T(8,128)(2,1)S(1)}, bf16[32,2048]{1,0:T(8,128)(2,1)}, u32[]{:S(2)}) copy-start(bf16[32,2048]{1,0:T(8,128)(2,1)} %get-tuple-element.143.refs_5_.refs_0_) | copy-start | bytes 393220
  21.9 6.2 %collective-permute-start.21 = (f32[8,128]{1,0:T(8,128)}, f32[8,128]{1,0:T(8,128)S(1)}, u32[]{:S(2)}, u32[]{:S(2)}) collective-permute-start(f32[8,128]{1,0:T(8,128)} %get-tuple-element.146), channel_id=1, source_target_pairs={{0,4},{4,0},{8,12},{12,8},{1,5},{5,1},{9,13},{13,9},{2,6},{6,2},{1... | collective-permute-start | bytes 12296 | tf_op jit(solution)/shard_map/ppermute | solution.py:212
  22.0 7.0 %collective-permute-start.22 = (f32[8,128]{1,0:T(8,128)}, f32[8,128]{1,0:T(8,128)S(1)}, u32[]{:S(2)}, u32[]{:S(2)}) collective-permute-start(f32[8,128]{1,0:T(8,128)} %get-tuple-element.147), channel_id=1, source_target_pairs={{0,8},{4,12},{8,0},{12,4},{1,9},{5,13},{9,1},{13,5},{2,10},{6,14},... | collective-permute-start | bytes 12296 | tf_op jit(solution)/shard_map/ppermute | solution.py:212
  22.5 6.5 %collective-permute-start.23 = (f32[8,128]{1,0:T(8,128)}, f32[8,128]{1,0:T(8,128)S(1)}, u32[]{:S(2)}, u32[]{:S(2)}) collective-permute-start(f32[8,128]{1,0:T(8,128)} %get-tuple-element.148), channel_id=1, source_target_pairs={{0,12},{4,8},{8,4},{12,0},{1,13},{5,9},{9,5},{13,1},{2,14},{6,10},... | collective-permute-start | bytes 12296 | tf_op jit(solution)/shard_map/ppermute | solution.py:212
  23.8 14.1 %collective-permute-start.33 = (bf16[32,2048]{1,0:T(8,128)(2,1)S(1)}, bf16[32,2048]{1,0:T(8,128)(2,1)S(1)}, u32[]{:S(2)}, u32[]{:S(2)}) collective-permute-start(bf16[32,2048]{1,0:T(8,128)(2,1)S(1)} %copy-done.5), channel_id=1, source_target_pairs={{0,3},{1,0},{2,1},{3,2},{4,7},{5,4},{6,5},{7,6},{8,11},{9,8},{10,9... | collective-permute-start | bytes 393224 | tf_op jit(solution)/shard_map/ppermute | solution.py:217
  29.7 38.1 %collective-permute-start.34 = (bf16[3,64,2048]{2,1,0:T(8,128)(2,1)}, bf16[3,64,2048]{2,1,0:T(8,128)(2,1)S(1)}, u32[]{:S(2)}, u32[]{:S(2)}) collective-permute-start(bf16[3,64,2048]{2,1,0:T(8,128)(2,1)} %get-tuple-element.158), channel_id=1, source_target_pairs={{0,8},{4,12},{8,0},{12,4},{1,9},{5,13},{9,1},{13,5},{2,10},{6,14},... | collective-permute-start | bytes 2359304 | tf_op jit(solution)/shard_map/ppermute | solution.py:212
  31.4 31.7 %copy-start.10 = (f32[32,128]{1,0:T(8,128)}, f32[32,128]{1,0:T(8,128)S(1)}, u32[]{:S(2)}) copy-start(f32[32,128]{1,0:T(8,128)S(1)} %pad_maximum_fusion.refs_8_) | copy-start | bytes 49156
  31.4 5.0 %collective-permute-start.26 = (f32[32,128]{1,0:T(8,128)S(1)}, f32[32,128]{1,0:T(8,128)}, u32[]{:S(2)}, u32[]{:S(2)}) collective-permute-start(f32[32,128]{1,0:T(8,128)S(1)} %pad_maximum_fusion.refs_8_), channel_id=1, source_target_pairs={{0,3},{1,0},{2,1},{3,2},{4,7},{5,4},{6,5},{7,6},{8,11},{9,8},{10,9... | collective-permute-start | bytes 49160 | tf_op jit(solution)/shard_map/ppermute | solution.py:217
  35.0 9.8 %collective-permute-start.32 = (bf16[32,2048]{1,0:T(8,128)(2,1)S(1)}, bf16[32,2048]{1,0:T(8,128)(2,1)S(1)}, u32[]{:S(2)}, u32[]{:S(2)}) collective-permute-start(bf16[32,2048]{1,0:T(8,128)(2,1)S(1)} %copy-done.5), channel_id=1, source_target_pairs={{0,2},{1,3},{2,0},{3,1},{4,6},{5,7},{6,4},{7,5},{8,10},{9,11},{10,... | collective-permute-start | bytes 393224 | tf_op jit(solution)/shard_map/ppermute | solution.py:217
  36.5 8.4 %collective-permute-start.31 = (bf16[32,2048]{1,0:T(8,128)(2,1)S(1)}, bf16[32,2048]{1,0:T(8,128)(2,1)S(1)}, u32[]{:S(2)}, u32[]{:S(2)}) collective-permute-start(bf16[32,2048]{1,0:T(8,128)(2,1)S(1)} %copy-done.5), channel_id=1, source_target_pairs={{0,1},{1,2},{2,3},{3,0},{4,5},{5,6},{6,7},{7,4},{8,9},{9,10},{10,1... | collective-permute-start | bytes 393224 | tf_op jit(solution)/shard_map/ppermute | solution.py:217
  37.9 7.0 %copy-start.7 = (bf16[32,2048]{1,0:T(8,128)(2,1)}, bf16[32,2048]{1,0:T(8,128)(2,1)S(1)}, u32[]{:S(2)}) copy-start(bf16[32,2048]{1,0:T(8,128)(2,1)S(1)} %collective-permute-done.33.refs_3_) | copy-start | bytes 393220
  37.9 13.9 %collective-permute-start.27 = (bf16[128,2,256]{2,1,0:T(2,128)(2,1)}, bf16[128,2,256]{2,1,0:T(2,128)(2,1)}, u32[]{:S(2)}, u32[]{:S(2)}) collective-permute-start(bf16[128,2,256]{2,1,0:T(2,128)(2,1)} %get-tuple-element.149), channel_id=1, source_target_pairs={{0,4},{4,0},{8,12},{12,8},{1,5},{5,1},{9,13},{13,9},{2,6},{6,2},{1... | collective-permute-start | bytes 393224 | tf_op jit(solution)/shard_map/ppermute | solution.py:212
  44.9 0.7 copy-start.8
  44.9 4.7 %collective-permute-start.25 = (f32[32,128]{1,0:T(8,128)S(1)}, f32[32,128]{1,0:T(8,128)}, u32[]{:S(2)}, u32[]{:S(2)}) collective-permute-start(f32[32,128]{1,0:T(8,128)S(1)} %pad_maximum_fusion.refs_8_), channel_id=1, source_target_pairs={{0,2},{1,3},{2,0},{3,1},{4,6},{5,7},{6,4},{7,5},{8,10},{9,11},{10,... | collective-permute-start | bytes 49160 | tf_op jit(solution)/shard_map/ppermute | solution.py:217
  45.5 0.7 copy-start.9
  46.2 5.6 %collective-permute-start.24 = (f32[32,128]{1,0:T(8,128)S(1)}, f32[32,128]{1,0:T(8,128)}, u32[]{:S(2)}, u32[]{:S(2)}) collective-permute-start(f32[32,128]{1,0:T(8,128)S(1)} %pad_maximum_fusion.refs_8_), channel_id=1, source_target_pairs={{0,1},{1,2},{2,3},{3,0},{4,5},{5,6},{6,7},{7,4},{8,9},{9,10},{10,1... | collective-permute-start | bytes 49160 | tf_op jit(solution)/shard_map/ppermute | solution.py:217
  49.6 10.4 %collective-permute-start.28 = (bf16[128,2,256]{2,1,0:T(2,128)(2,1)}, bf16[128,2,256]{2,1,0:T(2,128)(2,1)S(1)}, u32[]{:S(2)}, u32[]{:S(2)}) collective-permute-start(bf16[128,2,256]{2,1,0:T(2,128)(2,1)} %get-tuple-element.150), channel_id=1, source_target_pairs={{0,8},{4,12},{8,0},{12,4},{1,9},{5,13},{9,1},{13,5},{2,10},{6,14},... | collective-permute-start | bytes 393224 | tf_op jit(solution)/shard_map/ppermute | solution.py:212
  51.8 8.2 %collective-permute-start.29 = (bf16[128,2,256]{2,1,0:T(2,128)(2,1)}, bf16[128,2,256]{2,1,0:T(2,128)(2,1)}, u32[]{:S(2)}, u32[]{:S(2)}) collective-permute-start(bf16[128,2,256]{2,1,0:T(2,128)(2,1)} %get-tuple-element.151), channel_id=1, source_target_pairs={{0,12},{4,8},{8,4},{12,0},{1,13},{5,9},{9,5},{13,1},{2,14},{6,10},... | collective-permute-start | bytes 393224 | tf_op jit(solution)/shard_map/ppermute | solution.py:212
  51.8 11.3 %collective-permute-start.30 = (bf16[4,2,64,256]{3,2,1,0:T(8,128)(2,1)}, bf16[4,2,64,256]{3,2,1,0:T(8,128)(2,1)}, u32[]{:S(2)}, u32[]{:S(2)}) collective-permute-start(bf16[4,2,64,256]{3,2,1,0:T(8,128)(2,1)} %get-tuple-element.152), channel_id=1, source_target_pairs={{0,8},{4,12},{8,0},{12,4},{1,9},{5,13},{9,1},{13,5},{2,10},{6,14},... | collective-permute-start | bytes 786440 | tf_op jit(solution)/shard_map/ppermute | solution.py:212
  52.0 15.8 %collective-permute-start.36 = (bf16[2,64,2048]{2,1,0:T(8,128)(2,1)S(1)}, bf16[2,64,2048]{2,1,0:T(8,128)(2,1)}, u32[]{:S(2)}, u32[]{:S(2)}) collective-permute-start(bf16[2,64,2048]{2,1,0:T(8,128)(2,1)S(1)} %collective-permute-done.35), channel_id=1, source_target_pairs={{0,4},{4,0},{8,12},{12,8},{1,5},{5,1},{9,13},{13,9},{2,6},{6,2},{1... | collective-permute-start | bytes 1572872 | tf_op jit(solution)/shard_map/ppermute | solution.py:212
  60.0 3.1 %copy-start.6 = (bf16[128,2,256]{2,1,0:T(2,128)(2,1)}, bf16[128,2,256]{2,1,0:T(2,128)(2,1)S(1)}, u32[]{:S(2)}) copy-start(bf16[128,2,256]{2,1,0:T(2,128)(2,1)S(1)} %collective-permute-done.28.refs_13_) | copy-start | bytes 393220
  67.9 9.1 %collective-permute-start.1 = (bf16[3,64,2048]{2,1,0:T(8,128)(2,1)S(1)}, bf16[3,64,2048]{2,1,0:T(8,128)(2,1)S(1)}, u32[]{:S(2)}, u32[]{:S(2)}) collective-permute-start(bf16[3,64,2048]{2,1,0:T(8,128)(2,1)S(1)} %get-tuple-element.85.refs_5_), channel_id=1, source_target_pairs={{0,4},{4,0},{8,12},{12,8},{1,5},{5,1},{9,13},{13,9},{2,6},{6,2},{1... | collective-permute-start | bytes 2359304 | tf_op jit(solution)/shard_map/cond/branch_1_fun/ppermute | solution.py:212
  68.0 8.9 %collective-permute-start.2 = (bf16[1,64,2048]{2,1,0:T(8,128)(2,1)}, bf16[1,64,2048]{2,1,0:T(8,128)(2,1)}, u32[]{:S(2)}, u32[]{:S(2)}) collective-permute-start(bf16[1,64,2048]{2,1,0:T(8,128)(2,1)} %get-tuple-element.87), channel_id=1, source_target_pairs={{0,8},{4,12},{8,0},{12,4},{1,9},{5,13},{9,1},{13,5},{2,10},{6,14},... | collective-permute-start | bytes 786440 | tf_op jit(solution)/shard_map/cond/branch_1_fun/ppermute | solution.py:212
  77.0 4.0 %collective-permute-start.3 = (bf16[1,64,2048]{2,1,0:T(8,128)(2,1)}, bf16[1,64,2048]{2,1,0:T(8,128)(2,1)}, u32[]{:S(2)}, u32[]{:S(2)}) collective-permute-start(bf16[1,64,2048]{2,1,0:T(8,128)(2,1)} %collective-permute-done.2.refs_4_), channel_id=1, source_target_pairs={{0,4},{4,0},{8,12},{12,8},{1,5},{5,1},{9,13},{13,9},{2,6},{6,2},{1... | collective-permute-start | bytes 786440 | tf_op jit(solution)/shard_map/cond/branch_1_fun/ppermute | solution.py:212
  77.0 0.9 %copy-start.3 = (bf16[3,64,2048]{2,1,0:T(8,128)(2,1)}, bf16[3,64,2048]{2,1,0:T(8,128)(2,1)S(1)}, u32[]{:S(2)}) copy-start(bf16[3,64,2048]{2,1,0:T(8,128)(2,1)S(1)} %collective-permute-done.1.refs_7_) | copy-start | bytes 2359300 | tf_op jit(solution)/shard_map/cond
  77.9 3.1 %copy-start.12 = (s32[16]{0:T(128)S(1)}, s32[16]{0:T(128)}, u32[]{:S(2)}) copy-start(s32[16]{0:T(128)} %get-tuple-element.81.refs_1_) | copy-start | bytes 196 | tf_op jit(solution)/shard_map/cond
  77.9 3.1 %copy-start.16 = (s32[1,16]{1,0:T(1,128)S(1)}, s32[1,16]{1,0:T(1,128)}, u32[]{:S(2)}) copy-start(s32[1,16]{1,0:T(1,128)} %get-tuple-element.82.refs_2_) | copy-start | bytes 196 | tf_op jit(solution)/shard_map/cond

commit v5 on v4

--- a/solution.py
+++ b/solution.py
@@ -459,13 +459,18 @@
             out[...] = sums[base + i * block : base + (i + 1) * block]
 
 
-def gather_kernel(shard_ref, *refs):
-    out = refs[-1]
-    count = len(refs) - 1
+def gather_kernel(chunks, shard_ref, *refs):
+    partial, *returned, out, total = refs[chunks:]
     width = refs[0].shape[1]
-    for step, ref in enumerate(refs[:-1]):
-        source = lax.rem(shard_ref[0] + count - step, count)
+    for step, ref in enumerate(refs[:chunks]):
+        source = lax.rem(shard_ref[0] + chunks - step, chunks)
         out[:, pl.ds(pl.multiple_of(source * width, width), width)] = ref[...]
+    first = partial.shape[0] - returned[0].shape[0]
+    last = partial[first:]
+    for ref in returned:
+        last = last + ref[...]
+    total[:first] = partial[:first]
+    total[first:] = last
 
 
 def attend_kernel(spans, masks, resident, steps, kv_heads, head_length, *refs):
@@ -722,12 +727,6 @@
         store_a.reshape(slot_total // per_step, per_step * 2 * rank, features),
     )
     returned = [partner(array, mask) for array, mask in zip(sent, masks)]
-    last = partial[first:]
-    for array in returned:
-        last = last + array
-    partial = jnp.concatenate([partial[:first], last])
-    parts = [partial] + [shifted(partial, step) for step in range(1, shards)]
-
     unit_shape = row_a[1:]
     unit_total = 2 * COPIES
     across_b, *units, extra = copy_call(
@@ -743,13 +742,17 @@
     for array in units[: len(ALWAYS)]:
         got.append(partner(array, 2))
 
-    full = pl.pallas_call(
-        gather_kernel,
-        out_shape=jax.ShapeDtypeStruct((padded, shards * features), hidden.dtype),
-        in_specs=[SMEM] + [VMEM] * shards,
-        out_specs=VMEM,
+    full, partial = pl.pallas_call(
+        functools.partial(gather_kernel, shards),
+        out_shape=[
+            jax.ShapeDtypeStruct((padded, shards * features), hidden.dtype),
+            jax.ShapeDtypeStruct(partial.shape, jnp.float32),
+        ],
+        in_specs=[SMEM] + [VMEM] * (shards + 1 + len(masks)),
+        out_specs=[VMEM] * 2,
         name="gather",
-    )(shard_table, *around)
+    )(shard_table, *around, partial, *returned)
+    parts = [partial] + [shifted(partial, step) for step in range(1, shards)]
     base = jnp.einsum("md,dgc->gmc", full, w_kv, preferred_element_type=jnp.float32)
 
     attn_out, new_kv, arrived, installed_b = pl.pallas_call(

time: 84 us -> 102 us (1.21)
  waiting for transfers between devices: 26.2 us -> 41.8 us
  starting transfers between devices: 19.6 us -> 24.6 us
  local copies, waits for them, and re-layouts: 4.24 us -> 2.86 us
    ppermute x18, waiting for transfers between devices: 14.7 us -> 41.8 us  [partner(): lax.ppermute(array, 'replica', [(i, i ^ mask) for i in range(lax.axis_siz...]
    ppermute x6, waiting for transfers between devices: 11.6 us -> 0.02 us  [shifted(): lax.ppermute(array, 'tensor', [(i, (i + step) % size) for i in range(size)])]
    ppermute x6, starting transfers between devices: 9.05 us -> 12 us  [shifted(): lax.ppermute(array, 'tensor', [(i, (i + step) % size) for i in range(size)])]
    ppermute x18, starting transfers between devices: 10.5 us -> 12.5 us  [partner(): lax.ppermute(array, 'replica', [(i, i ^ mask) for i in range(lax.axis_siz...]
    unnamed x24 -> x26, local copies, waits for them, and re-layouts: 2.62 us -> 1.94 us
  transfers between devices with their start and end apart: 24 -> 24, of which waited for: 8 -> 9; matrix products, arithmetic and copies ran while one was open for 9% -> 6% of each run, Pallas kernels for 22% -> 14%
where the time goes in v5:
time: 102 us
  waiting for transfers between devices  41.8 us (41%)
  Pallas kernels  25.3 us (25%)
  starting transfers between devices  24.6 us (24%)
  matrix products  5.75 us (6%)
  local copies, waits for them, and re-layouts  2.86 us (3%)
  between operations  1.33 us (1%)
    ppermute x18, waiting for transfers between devices, partner(): lax.ppermute(array, 'replica', [(i, i ^ mask) for i in range(lax.axis_siz...  41.8 us
    pallas_call x4, Pallas kernels, copy_call(): pl.pallas_call(kernel, out_shape=[pltpu.HBM(shape, dtype) for shape in sh...  13.8 us
    ppermute x18, starting transfers between devices, partner(): lax.ppermute(array, 'replica', [(i, i ^ mask) for i in range(lax.axis_siz...  12.5 us
    ppermute x6, starting transfers between devices, shifted(): lax.ppermute(array, 'tensor', [(i, (i + step) % size) for i in range(size)])  12 us
    dot_general x1, matrix products, pairs_layer(): jnp.einsum('md,dgc->gmc', full, w_kv, preferred_element_type=jnp.float32)  5.75 us
    pallas_call x1, Pallas kernels, pairs_layer(): pl.pallas_call(functools.partial(project_kernel, spans, slot_total, resid...  4.74 us
    pallas_call x1, Pallas kernels, pairs_layer(): pl.pallas_call(functools.partial(attend_kernel, spans, masks, resident, s...  4.69 us
  transfers between devices with their start and end apart: 24, of which 9 were waited for; matrix products, arithmetic and copies ran while one was open for 6% of the time, Pallas kernels for 14%

profile of v5, /device:TPU:4, one launch (start us, length us, event | category | flops | bytes accessed | tf_op | source)
XLA Modules:
  0.0 101.6 jit_solution(11099655008363546133)
XLA Ops:
  0.6 0.0 copy-start.7
  0.7 4.9 %shard_map.164 = (bf16[128,2,256]{2,1,0:T(2,128)(2,1)}, bf16[128,2,256]{2,1,0:T(2,128)(2,1)}, bf16[128,2,256]{2,1,0:T(2,128)(2,1)}, bf16[4,2,64,2048]{3,2,1,0:T(...) custom-call(s32[1]{0:T(128)} %bitcast.refs_0_, s32[2,4]{1,0:T(2,128)} %bitcast.29, ...), custom_call_target="tpu_custom_call" | custom-call | tf_op jit(solution)/shard_map/pallas_call | solution.py:403
  5.5 0.1 collective-permute-start.16
  5.6 0.5 collective-permute-start.17
  6.1 4.2 %collective-permute-done.17.refs_6_ = bf16[4,2,64,256]{3,2,1,0:T(8,128)(2,1)S(1)} collective-permute-done((bf16[4,2,64,256]{3,2,1,0:T(8,128)(2,1)}, bf16[4,2,64,256]{3,2,1,0:T(8,128)(2,1)S(1)}, u32[]{:S(2)}, u32[]{:S(2)}) %collective-permute-start.17) | collective-permute-done | bytes 262176 | tf_op jit(solution)/shard_map/ppermute | solution.py:212
  10.4 0.0 collective-permute-done.16.refs_5_
  10.4 0.7 copy-done
  11.1 0.0 copy-done.8
  11.1 3.6 %shard_map.165 = (bf16[4,2,64,256]{3,2,1,0:T(8,128)(2,1)}, bf16[2,64,2048]{2,1,0:T(8,128)(2,1)}, bf16[3,64,2048]{2,1,0:T(8,128)(2,1)}, bf16[1,64,2048]{2,1,0:T(8...) custom-call(s32[1]{0:T(128)} %bitcast.refs_0_, s32[16]{0:T(128)S(1)} %copy-done.7, ...), custom_call_target="tpu_custom_call" | custom-call | tf_op jit(solution)/shard_map/pallas_call | solution.py:403
  14.7 1.7 %collective-permute-start.35 = (bf16[2,64,2048]{2,1,0:T(8,128)(2,1)}, bf16[2,64,2048]{2,1,0:T(8,128)(2,1)S(1)}, u32[]{:S(2)}, u32[]{:S(2)}) collective-permute-start(bf16[2,64,2048]{2,1,0:T(8,128)(2,1)} %get-tuple-element.163), channel_id=1, source_target_pairs={{0,8},{4,12},{8,0},{12,4},{1,9},{5,13},{9,1},{13,5},{2,10},{6,14},... | collective-permute-start | bytes 1572872 | tf_op jit(solution)/shard_map/ppermute | solution.py:212
  16.4 0.0 collective-permute-start.23
  16.4 1.6 %collective-permute-start.22 = (bf16[8,2048]{1,0:T(8,128)(2,1)S(1)}, bf16[8,2048]{1,0:T(8,128)(2,1)S(1)}, u32[]{:S(2)}, u32[]{:S(2)}) collective-permute-start(bf16[8,2048]{1,0:T(8,128)(2,1)S(1)} %copy-done.16), channel_id=1, source_target_pairs={{0,8},{4,12},{8,0},{12,4},{1,9},{5,13},{9,1},{13,5},{2,10},{6,14},... | collective-permute-start | bytes 98312 | tf_op jit(solution)/shard_map/ppermute | solution.py:212
  17.9 0.0 copy-done.5
  17.9 3.6 %collective-permute-start.20 = (bf16[32,2048]{1,0:T(8,128)(2,1)S(1)}, bf16[32,2048]{1,0:T(8,128)(2,1)}, u32[]{:S(2)}, u32[]{:S(2)}) collective-permute-start(bf16[32,2048]{1,0:T(8,128)(2,1)S(1)} %copy-done.5), channel_id=1, source_target_pairs={{0,3},{1,0},{2,1},{3,2},{4,7},{5,4},{6,5},{7,6},{8,11},{9,8},{10,9... | collective-permute-start | bytes 393224 | tf_op jit(solution)/shard_map/ppermute | solution.py:217
  21.5 0.0 collective-permute-start.19
  21.5 7.6 %collective-permute-done.23.refs_8_ = bf16[8,2048]{1,0:T(8,128)(2,1)S(1)} collective-permute-done((bf16[8,2048]{1,0:T(8,128)(2,1)S(1)}, bf16[8,2048]{1,0:T(8,128)(2,1)S(1)}, u32[]{:S(2)}, u32[]{:S(2)}) %collective-permute-start.23) | collective-permute-done | bytes 32800 | tf_op jit(solution)/shard_map/ppermute | solution.py:212
  29.2 1.6 %collective-permute-start.18 = (bf16[32,2048]{1,0:T(8,128)(2,1)S(1)}, bf16[32,2048]{1,0:T(8,128)(2,1)}, u32[]{:S(2)}, u32[]{:S(2)}) collective-permute-start(bf16[32,2048]{1,0:T(8,128)(2,1)S(1)} %copy-done.5), channel_id=1, source_target_pairs={{0,1},{1,2},{2,3},{3,0},{4,5},{5,6},{6,7},{7,4},{8,9},{9,10},{10,1... | collective-permute-start | bytes 393224 | tf_op jit(solution)/shard_map/ppermute | solution.py:217
  30.8 0.0 collective-permute-done.22.refs_7_
  30.8 0.3 collective-permute-start.21
  31.1 0.9 collective-permute-done.21.refs_6_
  32.0 0.6 copy-done.11
  32.6 4.7 %project.1 = (f32[32,128]{1,0:T(8,128)}, f32[8,128]{1,0:T(8,128)}, f32[8,128]{1,0:T(8,128)}, f32[8,128]{1,0:T(8,128)}) custom-call(s32[1]{0:T(128)} %bitcast.refs_0_, s32[48]{0:T(128)} %refs_4_.5, s32[2,4]{1,0:T(2,128)} %bitcast.33, s32[16]{0:T(128)S(1)} %copy-done.7, s32[1,16]{1,0:T(1,128)S(1)} %bitcast.23, ...), custom_call_target="tpu_custom_call" | custom-call | tf_op jit(solution)/shard_map/project/pallas_call | solution.py:702
  37.3 0.3 collective-permute-start.24
  37.7 1.1 %collective-permute-done.24.refs_5_ = f32[8,128]{1,0:T(8,128)S(1)} collective-permute-done((f32[8,128]{1,0:T(8,128)}, f32[8,128]{1,0:T(8,128)S(1)}, u32[]{:S(2)}, u32[]{:S(2)}) %collective-permute-start.24) | collective-permute-done | bytes 4128 | tf_op jit(solution)/shard_map/ppermute | solution.py:212
  38.8 1.7 %collective-permute-start.25 = (f32[8,128]{1,0:T(8,128)}, f32[8,128]{1,0:T(8,128)S(1)}, u32[]{:S(2)}, u32[]{:S(2)}) collective-permute-start(f32[8,128]{1,0:T(8,128)} %get-tuple-element.149), channel_id=1, source_target_pairs={{0,8},{4,12},{8,0},{12,4},{1,9},{5,13},{9,1},{13,5},{2,10},{6,14},... | collective-permute-start | bytes 12296 | tf_op jit(solution)/shard_map/ppermute | solution.py:212
  40.5 2.1 %collective-permute-done.25.refs_6_ = f32[8,128]{1,0:T(8,128)S(1)} collective-permute-done((f32[8,128]{1,0:T(8,128)}, f32[8,128]{1,0:T(8,128)S(1)}, u32[]{:S(2)}, u32[]{:S(2)}) %collective-permute-start.25) | collective-permute-done | bytes 4128 | tf_op jit(solution)/shard_map/ppermute | solution.py:212
  42.6 0.5 collective-permute-start.26
  43.1 2.8 %collective-permute-done.26.refs_7_ = f32[8,128]{1,0:T(8,128)S(1)} collective-permute-done((f32[8,128]{1,0:T(8,128)}, f32[8,128]{1,0:T(8,128)S(1)}, u32[]{:S(2)}, u32[]{:S(2)}) %collective-permute-start.26) | collective-permute-done | bytes 4128 | tf_op jit(solution)/shard_map/ppermute | solution.py:212
  45.8 0.6 copy-done.15
  46.4 1.7 %collective-permute-start.34 = (bf16[3,64,2048]{2,1,0:T(8,128)(2,1)}, bf16[3,64,2048]{2,1,0:T(8,128)(2,1)S(1)}, u32[]{:S(2)}, u32[]{:S(2)}) collective-permute-start(bf16[3,64,2048]{2,1,0:T(8,128)(2,1)} %get-tuple-element.162), channel_id=1, source_target_pairs={{0,8},{4,12},{8,0},{12,4},{1,9},{5,13},{9,1},{13,5},{2,10},{6,14},... | collective-permute-start | bytes 2359304 | tf_op jit(solution)/shard_map/ppermute | solution.py:212
  48.1 0.0 collective-permute-done.20.refs_3_
  48.1 0.0 collective-permute-start.30
  48.1 0.0 collective-permute-done.19.refs_2_
  48.1 0.4 collective-permute-start.31
  48.5 0.0 collective-permute-done.18.refs_1_
  48.5 1.4 %collective-permute-start.32 = (bf16[128,2,256]{2,1,0:T(2,128)(2,1)}, bf16[128,2,256]{2,1,0:T(2,128)(2,1)S(1)}, u32[]{:S(2)}, u32[]{:S(2)}) collective-permute-start(bf16[128,2,256]{2,1,0:T(2,128)(2,1)} %get-tuple-element.154), channel_id=1, source_target_pairs={{0,12},{4,8},{8,4},{12,0},{1,13},{5,9},{9,5},{13,1},{2,14},{6,10},... | collective-permute-start | bytes 393224 | tf_op jit(solution)/shard_map/ppermute | solution.py:212
  50.0 2.0 %gather.1 = (bf16[32,8192]{1,0:T(8,128)(2,1)}, f32[32,128]{1,0:T(8,128)}) custom-call(s32[1]{0:T(128)} %bitcast.5.shard_ref, bf16[32,2048]{1,0:T(8,128)(2,1)} %get-tuple-element.145.refs_5_.refs_0_, bf16[32,2048]{1,0:T(8,128)(2,1)} %collective-permute-done.18.refs_1_, bf16[32,2048]{1,0:T(8,128)(2,1)} %collective-permute-done.19.refs_2_, ...), custom_call_target="tpu_custom_call" | custom-call | tf_op jit(solution)/shard_map/gather/pallas_call | solution.py:745
  52.0 0.0 collective-permute-done.30.refs_12_
  52.0 3.2 %collective-permute-start.29 = (f32[32,128]{1,0:T(8,128)}, f32[32,128]{1,0:T(8,128)S(1)}, u32[]{:S(2)}, u32[]{:S(2)}) collective-permute-start(f32[32,128]{1,0:T(8,128)} %get-tuple-element.151.refs_8_), channel_id=1, source_target_pairs={{0,3},{1,0},{2,1},{3,2},{4,7},{5,4},{6,5},{7,6},{8,11},{9,8},{10,9... | collective-permute-start | bytes 49160 | tf_op jit(solution)/shard_map/ppermute | solution.py:217
  55.2 14.8 %collective-permute-done.31.refs_13_ = bf16[128,2,256]{2,1,0:T(2,128)(2,1)} collective-permute-done((bf16[128,2,256]{2,1,0:T(2,128)(2,1)}, bf16[128,2,256]{2,1,0:T(2,128)(2,1)}, u32[]{:S(2)}, u32[]{:S(2)}) %collective-permute-start.31) | collective-permute-done | bytes 131104 | tf_op jit(solution)/shard_map/ppermute | solution.py:212
  70.0 2.9 %collective-permute-start.28 = (f32[32,128]{1,0:T(8,128)}, f32[32,128]{1,0:T(8,128)}, u32[]{:S(2)}, u32[]{:S(2)}) collective-permute-start(f32[32,128]{1,0:T(8,128)} %get-tuple-element.151.refs_8_), channel_id=1, source_target_pairs={{0,2},{1,3},{2,0},{3,1},{4,6},{5,7},{6,4},{7,5},{8,10},{9,11},{10,... | collective-permute-start | bytes 49160 | tf_op jit(solution)/shard_map/ppermute | solution.py:217
  72.9 0.0 collective-permute-done.32.refs_14_
  72.9 0.7 collective-permute-start.27
  73.7 0.0 collective-permute-done.29.refs_11_
  73.7 1.2 %collective-permute-start.33 = (bf16[4,2,64,256]{3,2,1,0:T(8,128)(2,1)}, bf16[4,2,64,256]{3,2,1,0:T(8,128)(2,1)}, u32[]{:S(2)}, u32[]{:S(2)}) collective-permute-start(bf16[4,2,64,256]{3,2,1,0:T(8,128)(2,1)} %get-tuple-element.155), channel_id=1, source_target_pairs={{0,8},{4,12},{8,0},{12,4},{1,9},{5,13},{9,1},{13,5},{2,10},{6,14},... | collective-permute-start | bytes 786440 | tf_op jit(solution)/shard_map/ppermute | solution.py:212
  74.9 0.0 collective-permute-done.35
  74.9 0.0 collective-permute-start.36
  74.9 5.7 %fusion.2.refs_18_ = f32[2,32,256]{2,1,0:T(8,128)} fusion(bf16[8192,2,256]{2,1,0:T(2,128)(2,1)} %param.20, bf16[32,8192]{1,0:T(8,128)(2,1)} %get-tuple-element.156), kind=kOutput, calls=%fused_computation.2 | convolution fusion | flops 268435456 | bytes 8978432 | tf_op jit(solution)/shard_map/md,dgc->gmc/dot_general | solution.py:756
  81.2 0.0 collective-permute-done.28.refs_10_
  81.2 0.0 collective-permute-done.27.refs_9_
  81.2 0.2 collective-permute-done.33
  81.5 4.7 %attend.1 = (bf16[14,2,2048]{2,1,0:T(2,128)(2,1)}, bf16[14,2,2,256]{3,2,1,0:T(2,128)(2,1)}, bf16[2,128,2,256]{3,2,1,0:T(2,128)(2,1)}, bf16[4,128,256]{2,1,0:T(8,128)(2,1)}) custom-call(s32[1]{0:T(128)} %bitcast.refs_0_, s32[48]{0:T(128)} %refs_1_.5, s32[2,4]{1,0:T(2,128)} %bitcast.30, s32[2,4]{1,0:T(2,128)} %bitcast.32, s32[48]{0:T(128)} %refs_4_.5, ...), custom_call_target="tpu_custom_call" | custom-call | tf_op jit(solution)/shard_map/attend/pallas_call | solution.py:758
  86.2 0.0 collective-permute-done.34
  86.2 0.0 collective-permute-done.36
  86.2 15.4 %conditional.1 = (bf16[4,2,64,2048]{3,2,1,0:T(8,128)(2,1)}) conditional(s32[]{:T(128)} %bitcast.13, (bf16[3,64,2048]{2,1,0:T(8,128)(2,1)S(1)}, s32[1]{0:T(128)}, s32[16]{0:T(128)S(1)}, s32[1,16]{1,0:T(1,128)S(1)}, bf16[4,2,64,2048]{3,2,1,0:T(8,128)(2,1)S(1)}, /*index=5*/bf16[2,64,2048]{2,1,0:T(8,128)(2,1)S(1)}, ...), branch_computations={%region_0.0_spmd, %region_1.0_spmd, %region_2.0_spmd, %region_3.0_... | conditional | bytes 12583228 | solution.py:827
  86.2 0.3 collective-permute-start.1
  86.5 0.9 collective-permute-start.2
  87.5 7.9 %collective-permute-done.2.refs_4_ = bf16[1,64,2048]{2,1,0:T(8,128)(2,1)} collective-permute-done((bf16[1,64,2048]{2,1,0:T(8,128)(2,1)}, bf16[1,64,2048]{2,1,0:T(8,128)(2,1)}, u32[]{:S(2)}, u32[]{:S(2)}) %collective-permute-start.2) | collective-permute-done | bytes 262176 | tf_op jit(solution)/shard_map/cond/branch_1_fun/ppermute | solution.py:212
  95.3 0.0 collective-permute-start.3
  95.3 0.0 collective-permute-done.1.refs_7_
  95.3 0.9 copy-done.3
  96.3 2.8 %branch_1_fun.2.refs_3_ = bf16[4,2,64,2048]{3,2,1,0:T(8,128)(2,1)} custom-call(s32[1]{0:T(128)} %get-tuple-element.80.refs_0_, s32[16]{0:T(128)S(1)} %get-tuple-element.81.refs_1_, s32[1,16]{1,0:T(1,128)S(1)} %get-tuple-element.82.refs_2_, bf16[4,2,64,2048]{3,2,1,0:T(8,128)(2,1)S(1)} %get-tuple-element.83.refs_3_, ...), custom_call_target="tpu_custom_call" | custom-call | tf_op jit(solution)/shard_map/cond/branch_1_fun/pallas_call | solution.py:403
  99.1 0.0 collective-permute-done.3.refs_5_
  99.1 2.5 %branch_1_fun.3 = bf16[4,2,64,2048]{3,2,1,0:T(8,128)(2,1)} custom-call(s32[1]{0:T(128)} %get-tuple-element.80.refs_0_, s32[16]{0:T(128)S(1)} %get-tuple-element.81.refs_1_, s32[1,16]{1,0:T(1,128)S(1)} %get-tuple-element.82.refs_2_, bf16[4,2,64,2048]{3,2,1,0:T(8,128)(2,1)} %branch_1_fun.2.refs_3_, ...), custom_call_target="tpu_custom_call", output_to_operand_aliasing={{}: (3, {})} | custom-call | tf_op jit(solution)/shard_map/cond/branch_1_fun/pallas_call | solution.py:403
  (21 shorter events, 0.0 us)
Async XLA Ops:
  0.6 10.4 %copy-start.7 = (s32[16]{0:T(128)S(1)}, s32[16]{0:T(128)}, u32[]{:S(2)}) copy-start(s32[16]{0:T(128)} %refs_6_.3) | copy-start | bytes 196
  0.6 10.4 %copy-start.8 = (s32[16,1]{0,1:T(1,128)S(1)}, s32[16,1]{0,1:T(1,128)}, u32[]{:S(2)}) copy-start(s32[16,1]{0,1:T(1,128)} %param.29) | copy-start | bytes 196
  5.5 4.8 %collective-permute-start.16 = (bf16[4,2,64,2048]{3,2,1,0:T(8,128)(2,1)}, bf16[4,2,64,2048]{3,2,1,0:T(8,128)(2,1)S(1)}, u32[]{:S(2)}, u32[]{:S(2)}) collective-permute-start(bf16[4,2,64,2048]{3,2,1,0:T(8,128)(2,1)} %get-tuple-element.140), channel_id=1, source_target_pairs={{0,4},{4,0},{8,12},{12,8},{1,5},{5,1},{9,13},{13,9},{2,6},{6,2},{1... | collective-permute-start | bytes 6291464 | tf_op jit(solution)/shard_map/ppermute | solution.py:212
  5.6 4.7 %collective-permute-start.17 = (bf16[4,2,64,256]{3,2,1,0:T(8,128)(2,1)}, bf16[4,2,64,256]{3,2,1,0:T(8,128)(2,1)S(1)}, u32[]{:S(2)}, u32[]{:S(2)}) collective-permute-start(bf16[4,2,64,256]{3,2,1,0:T(8,128)(2,1)} %get-tuple-element.141), channel_id=1, source_target_pairs={{0,4},{4,0},{8,12},{12,8},{1,5},{5,1},{9,13},{13,9},{2,6},{6,2},{1... | collective-permute-start | bytes 786440 | tf_op jit(solution)/shard_map/ppermute | solution.py:212
  10.4 0.7 copy-start
  11.1 5.3 %copy-start.16 = (bf16[8,2048]{1,0:T(8,128)(2,1)S(1)}, bf16[8,2048]{1,0:T(8,128)(2,1)}, u32[]{:S(2)}) copy-start(bf16[8,2048]{1,0:T(8,128)(2,1)} %get-tuple-element.146) | copy-start | bytes 98308
  11.1 6.9 %copy-start.5 = (bf16[32,2048]{1,0:T(8,128)(2,1)S(1)}, bf16[32,2048]{1,0:T(8,128)(2,1)}, u32[]{:S(2)}) copy-start(bf16[32,2048]{1,0:T(8,128)(2,1)} %get-tuple-element.145.refs_5_.refs_0_) | copy-start | bytes 393220
  14.7 60.2 %collective-permute-start.35 = (bf16[2,64,2048]{2,1,0:T(8,128)(2,1)}, bf16[2,64,2048]{2,1,0:T(8,128)(2,1)S(1)}, u32[]{:S(2)}, u32[]{:S(2)}) collective-permute-start(bf16[2,64,2048]{2,1,0:T(8,128)(2,1)} %get-tuple-element.163), channel_id=1, source_target_pairs={{0,8},{4,12},{8,0},{12,4},{1,9},{5,13},{9,1},{13,5},{2,10},{6,14},... | collective-permute-start | bytes 1572872 | tf_op jit(solution)/shard_map/ppermute | solution.py:212
  16.4 12.8 %collective-permute-start.23 = (bf16[8,2048]{1,0:T(8,128)(2,1)S(1)}, bf16[8,2048]{1,0:T(8,128)(2,1)S(1)}, u32[]{:S(2)}, u32[]{:S(2)}) collective-permute-start(bf16[8,2048]{1,0:T(8,128)(2,1)S(1)} %copy-done.16), channel_id=1, source_target_pairs={{0,12},{4,8},{8,4},{12,0},{1,13},{5,9},{9,5},{13,1},{2,14},{6,10},... | collective-permute-start | bytes 98312 | tf_op jit(solution)/shard_map/ppermute | solution.py:212
  16.4 14.4 %collective-permute-start.22 = (bf16[8,2048]{1,0:T(8,128)(2,1)S(1)}, bf16[8,2048]{1,0:T(8,128)(2,1)S(1)}, u32[]{:S(2)}, u32[]{:S(2)}) collective-permute-start(bf16[8,2048]{1,0:T(8,128)(2,1)S(1)} %copy-done.16), channel_id=1, source_target_pairs={{0,8},{4,12},{8,0},{12,4},{1,9},{5,13},{9,1},{13,5},{2,10},{6,14},... | collective-permute-start | bytes 98312 | tf_op jit(solution)/shard_map/ppermute | solution.py:212
  17.9 30.2 %collective-permute-start.20 = (bf16[32,2048]{1,0:T(8,128)(2,1)S(1)}, bf16[32,2048]{1,0:T(8,128)(2,1)}, u32[]{:S(2)}, u32[]{:S(2)}) collective-permute-start(bf16[32,2048]{1,0:T(8,128)(2,1)S(1)} %copy-done.5), channel_id=1, source_target_pairs={{0,3},{1,0},{2,1},{3,2},{4,7},{5,4},{6,5},{7,6},{8,11},{9,8},{10,9... | collective-permute-start | bytes 393224 | tf_op jit(solution)/shard_map/ppermute | solution.py:217
  21.5 26.6 %collective-permute-start.19 = (bf16[32,2048]{1,0:T(8,128)(2,1)S(1)}, bf16[32,2048]{1,0:T(8,128)(2,1)}, u32[]{:S(2)}, u32[]{:S(2)}) collective-permute-start(bf16[32,2048]{1,0:T(8,128)(2,1)S(1)} %copy-done.5), channel_id=1, source_target_pairs={{0,2},{1,3},{2,0},{3,1},{4,6},{5,7},{6,4},{7,5},{8,10},{9,11},{10,... | collective-permute-start | bytes 393224 | tf_op jit(solution)/shard_map/ppermute | solution.py:217
  29.2 2.8 %copy-start.9 = (bf16[8,2048]{1,0:T(8,128)(2,1)}, bf16[8,2048]{1,0:T(8,128)(2,1)S(1)}, u32[]{:S(2)}) copy-start(bf16[8,2048]{1,0:T(8,128)(2,1)S(1)} %collective-permute-done.23.refs_8_) | copy-start | bytes 98308
  29.2 19.4 %collective-permute-start.18 = (bf16[32,2048]{1,0:T(8,128)(2,1)S(1)}, bf16[32,2048]{1,0:T(8,128)(2,1)}, u32[]{:S(2)}, u32[]{:S(2)}) collective-permute-start(bf16[32,2048]{1,0:T(8,128)(2,1)S(1)} %copy-done.5), channel_id=1, source_target_pairs={{0,1},{1,2},{2,3},{3,0},{4,5},{5,6},{6,7},{7,4},{8,9},{9,10},{10,1... | collective-permute-start | bytes 393224 | tf_op jit(solution)/shard_map/ppermute | solution.py:217
  30.8 1.2 %copy-start.10 = (bf16[8,2048]{1,0:T(8,128)(2,1)}, bf16[8,2048]{1,0:T(8,128)(2,1)S(1)}, u32[]{:S(2)}) copy-start(bf16[8,2048]{1,0:T(8,128)(2,1)S(1)} %collective-permute-done.22.refs_7_) | copy-start | bytes 98308
  30.8 1.2 %collective-permute-start.21 = (bf16[8,2048]{1,0:T(8,128)(2,1)S(1)}, bf16[8,2048]{1,0:T(8,128)(2,1)S(1)}, u32[]{:S(2)}, u32[]{:S(2)}) collective-permute-start(bf16[8,2048]{1,0:T(8,128)(2,1)S(1)} %copy-done.16), channel_id=1, source_target_pairs={{0,4},{4,0},{8,12},{12,8},{1,5},{5,1},{9,13},{13,9},{2,6},{6,2},{1... | collective-permute-start | bytes 98312 | tf_op jit(solution)/shard_map/ppermute | solution.py:212
  32.0 0.6 copy-start.11
  37.3 1.4 %collective-permute-start.24 = (f32[8,128]{1,0:T(8,128)}, f32[8,128]{1,0:T(8,128)S(1)}, u32[]{:S(2)}, u32[]{:S(2)}) collective-permute-start(f32[8,128]{1,0:T(8,128)} %get-tuple-element.148), channel_id=1, source_target_pairs={{0,4},{4,0},{8,12},{12,8},{1,5},{5,1},{9,13},{13,9},{2,6},{6,2},{1... | collective-permute-start | bytes 12296 | tf_op jit(solution)/shard_map/ppermute | solution.py:212
  38.8 11.2 %copy-start.13 = (f32[8,128]{1,0:T(8,128)}, f32[8,128]{1,0:T(8,128)S(1)}, u32[]{:S(2)}) copy-start(f32[8,128]{1,0:T(8,128)S(1)} %collective-permute-done.24.refs_5_) | copy-start | bytes 12292
  38.8 3.8 %collective-permute-start.25 = (f32[8,128]{1,0:T(8,128)}, f32[8,128]{1,0:T(8,128)S(1)}, u32[]{:S(2)}, u32[]{:S(2)}) collective-permute-start(f32[8,128]{1,0:T(8,128)} %get-tuple-element.149), channel_id=1, source_target_pairs={{0,8},{4,12},{8,0},{12,4},{1,9},{5,13},{9,1},{13,5},{2,10},{6,14},... | collective-permute-start | bytes 12296 | tf_op jit(solution)/shard_map/ppermute | solution.py:212
  42.6 7.4 %copy-start.14 = (f32[8,128]{1,0:T(8,128)}, f32[8,128]{1,0:T(8,128)S(1)}, u32[]{:S(2)}) copy-start(f32[8,128]{1,0:T(8,128)S(1)} %collective-permute-done.25.refs_6_) | copy-start | bytes 12292
  42.6 3.2 %collective-permute-start.26 = (f32[8,128]{1,0:T(8,128)}, f32[8,128]{1,0:T(8,128)S(1)}, u32[]{:S(2)}, u32[]{:S(2)}) collective-permute-start(f32[8,128]{1,0:T(8,128)} %get-tuple-element.150), channel_id=1, source_target_pairs={{0,12},{4,8},{8,4},{12,0},{1,13},{5,9},{9,5},{13,1},{2,14},{6,10},... | collective-permute-start | bytes 12296 | tf_op jit(solution)/shard_map/ppermute | solution.py:212
  45.8 0.6 copy-start.15
  46.4 39.7 %collective-permute-start.34 = (bf16[3,64,2048]{2,1,0:T(8,128)(2,1)}, bf16[3,64,2048]{2,1,0:T(8,128)(2,1)S(1)}, u32[]{:S(2)}, u32[]{:S(2)}) collective-permute-start(bf16[3,64,2048]{2,1,0:T(8,128)(2,1)} %get-tuple-element.162), channel_id=1, source_target_pairs={{0,8},{4,12},{8,0},{12,4},{1,9},{5,13},{9,1},{13,5},{2,10},{6,14},... | collective-permute-start | bytes 2359304 | tf_op jit(solution)/shard_map/ppermute | solution.py:212
  48.1 3.9 %collective-permute-start.30 = (bf16[128,2,256]{2,1,0:T(2,128)(2,1)}, bf16[128,2,256]{2,1,0:T(2,128)(2,1)}, u32[]{:S(2)}, u32[]{:S(2)}) collective-permute-start(bf16[128,2,256]{2,1,0:T(2,128)(2,1)} %get-tuple-element.152), channel_id=1, source_target_pairs={{0,4},{4,0},{8,12},{12,8},{1,5},{5,1},{9,13},{13,9},{2,6},{6,2},{1... | collective-permute-start | bytes 393224 | tf_op jit(solution)/shard_map/ppermute | solution.py:212
  48.1 21.9 %collective-permute-start.31 = (bf16[128,2,256]{2,1,0:T(2,128)(2,1)}, bf16[128,2,256]{2,1,0:T(2,128)(2,1)}, u32[]{:S(2)}, u32[]{:S(2)}) collective-permute-start(bf16[128,2,256]{2,1,0:T(2,128)(2,1)} %get-tuple-element.153), channel_id=1, source_target_pairs={{0,8},{4,12},{8,0},{12,4},{1,9},{5,13},{9,1},{13,5},{2,10},{6,14},... | collective-permute-start | bytes 393224 | tf_op jit(solution)/shard_map/ppermute | solution.py:212
  48.5 24.4 %collective-permute-start.32 = (bf16[128,2,256]{2,1,0:T(2,128)(2,1)}, bf16[128,2,256]{2,1,0:T(2,128)(2,1)S(1)}, u32[]{:S(2)}, u32[]{:S(2)}) collective-permute-start(bf16[128,2,256]{2,1,0:T(2,128)(2,1)} %get-tuple-element.154), channel_id=1, source_target_pairs={{0,12},{4,8},{8,4},{12,0},{1,13},{5,9},{9,5},{13,1},{2,14},{6,10},... | collective-permute-start | bytes 393224 | tf_op jit(solution)/shard_map/ppermute | solution.py:212
  52.0 21.7 %collective-permute-start.29 = (f32[32,128]{1,0:T(8,128)}, f32[32,128]{1,0:T(8,128)S(1)}, u32[]{:S(2)}, u32[]{:S(2)}) collective-permute-start(f32[32,128]{1,0:T(8,128)} %get-tuple-element.151.refs_8_), channel_id=1, source_target_pairs={{0,3},{1,0},{2,1},{3,2},{4,7},{5,4},{6,5},{7,6},{8,11},{9,8},{10,9... | collective-permute-start | bytes 49160 | tf_op jit(solution)/shard_map/ppermute | solution.py:217
  70.0 11.2 %collective-permute-start.28 = (f32[32,128]{1,0:T(8,128)}, f32[32,128]{1,0:T(8,128)}, u32[]{:S(2)}, u32[]{:S(2)}) collective-permute-start(f32[32,128]{1,0:T(8,128)} %get-tuple-element.151.refs_8_), channel_id=1, source_target_pairs={{0,2},{1,3},{2,0},{3,1},{4,6},{5,7},{6,4},{7,5},{8,10},{9,11},{10,... | collective-permute-start | bytes 49160 | tf_op jit(solution)/shard_map/ppermute | solution.py:217
  72.9 7.7 %copy-start.6 = (bf16[128,2,256]{2,1,0:T(2,128)(2,1)}, bf16[128,2,256]{2,1,0:T(2,128)(2,1)S(1)}, u32[]{:S(2)}) copy-start(bf16[128,2,256]{2,1,0:T(2,128)(2,1)S(1)} %collective-permute-done.32.refs_14_) | copy-start | bytes 393220
  72.9 8.3 %collective-permute-start.27 = (f32[32,128]{1,0:T(8,128)}, f32[32,128]{1,0:T(8,128)}, u32[]{:S(2)}, u32[]{:S(2)}) collective-permute-start(f32[32,128]{1,0:T(8,128)} %get-tuple-element.151.refs_8_), channel_id=1, source_target_pairs={{0,1},{1,2},{2,3},{3,0},{4,5},{5,6},{6,7},{7,4},{8,9},{9,10},{10,1... | collective-permute-start | bytes 49160 | tf_op jit(solution)/shard_map/ppermute | solution.py:217
  73.7 1.2 %copy-start.12 = (f32[32,128]{1,0:T(8,128)}, f32[32,128]{1,0:T(8,128)S(1)}, u32[]{:S(2)}) copy-start(f32[32,128]{1,0:T(8,128)S(1)} %collective-permute-done.29.refs_11_) | copy-start | bytes 49156
  73.7 7.8 %collective-permute-start.33 = (bf16[4,2,64,256]{3,2,1,0:T(8,128)(2,1)}, bf16[4,2,64,256]{3,2,1,0:T(8,128)(2,1)}, u32[]{:S(2)}, u32[]{:S(2)}) collective-permute-start(bf16[4,2,64,256]{3,2,1,0:T(8,128)(2,1)} %get-tuple-element.155), channel_id=1, source_target_pairs={{0,8},{4,12},{8,0},{12,4},{1,9},{5,13},{9,1},{13,5},{2,10},{6,14},... | collective-permute-start | bytes 786440 | tf_op jit(solution)/shard_map/ppermute | solution.py:212
  74.9 11.3 %collective-permute-start.36 = (bf16[2,64,2048]{2,1,0:T(8,128)(2,1)S(1)}, bf16[2,64,2048]{2,1,0:T(8,128)(2,1)}, u32[]{:S(2)}, u32[]{:S(2)}) collective-permute-start(bf16[2,64,2048]{2,1,0:T(8,128)(2,1)S(1)} %collective-permute-done.35), channel_id=1, source_target_pairs={{0,4},{4,0},{8,12},{12,8},{1,5},{5,1},{9,13},{13,9},{2,6},{6,2},{1... | collective-permute-start | bytes 1572872 | tf_op jit(solution)/shard_map/ppermute | solution.py:212
  86.2 9.1 %collective-permute-start.1 = (bf16[3,64,2048]{2,1,0:T(8,128)(2,1)S(1)}, bf16[3,64,2048]{2,1,0:T(8,128)(2,1)S(1)}, u32[]{:S(2)}, u32[]{:S(2)}) collective-permute-start(bf16[3,64,2048]{2,1,0:T(8,128)(2,1)S(1)} %get-tuple-element.85.refs_5_), channel_id=1, source_target_pairs={{0,4},{4,0},{8,12},{12,8},{1,5},{5,1},{9,13},{13,9},{2,6},{6,2},{1... | collective-permute-start | bytes 2359304 | tf_op jit(solution)/shard_map/cond/branch_1_fun/ppermute | solution.py:212
  86.5 8.8 %collective-permute-start.2 = (bf16[1,64,2048]{2,1,0:T(8,128)(2,1)}, bf16[1,64,2048]{2,1,0:T(8,128)(2,1)}, u32[]{:S(2)}, u32[]{:S(2)}) collective-permute-start(bf16[1,64,2048]{2,1,0:T(8,128)(2,1)} %get-tuple-element.87), channel_id=1, source_target_pairs={{0,8},{4,12},{8,0},{12,4},{1,9},{5,13},{9,1},{13,5},{2,10},{6,14},... | collective-permute-start | bytes 786440 | tf_op jit(solution)/shard_map/cond/branch_1_fun/ppermute | solution.py:212
  95.3 3.8 %collective-permute-start.3 = (bf16[1,64,2048]{2,1,0:T(8,128)(2,1)}, bf16[1,64,2048]{2,1,0:T(8,128)(2,1)}, u32[]{:S(2)}, u32[]{:S(2)}) collective-permute-start(bf16[1,64,2048]{2,1,0:T(8,128)(2,1)} %collective-permute-done.2.refs_4_), channel_id=1, source_target_pairs={{0,4},{4,0},{8,12},{12,8},{1,5},{5,1},{9,13},{13,9},{2,6},{6,2},{1... | collective-permute-start | bytes 786440 | tf_op jit(solution)/shard_map/cond/branch_1_fun/ppermute | solution.py:212
  95.3 0.9 copy-start.3

commit v6 on v5

--- a/solution.py
+++ b/solution.py
@@ -274,11 +274,30 @@
             when(condition, functools.partial(finish, at, buffer, sems))
 
 
+def held_slots(me, holder, spans, slot_total):
+    slots = []
+    for copy_id in range(COPIES):
+        slot = jnp.int32(0)
+        for span in range(spans):
+            row = holder[copy_id * spans + span]
+            slot += jnp.where(row // slot_total == me, row % slot_total, 0)
+        slots.append(slot)
+    return slots
+
+
+def collect_down_kernel(spans, slot_total, me_ref, holder, store_a, rows_a, buffer, sems):
+    moves = [
+        (None, [(None, store_a.at[slot])], [(None, rows_a.at[copy_id])])
+        for copy_id, slot in enumerate(held_slots(me_ref[0], holder, spans, slot_total))
+    ]
+    staged([(moves, buffer, sems)])
+
+
 def collect_kernel(spans, slot_total, masks, *refs):
-    (me_ref, arrival_from, arrival_slot, holder, kv_cache, store_a, store_b, hidden) = refs[:8]
-    *leaving, rows_a, rows_b, rows, asking = refs[8 : 12 + len(masks)]
-    *buffers, raw, even = refs[12 + len(masks) : 17 + len(masks)]
-    *semaphores, raw_sems, even_sems = refs[17 + len(masks) :]
+    (me_ref, arrival_from, arrival_slot, holder, kv_cache, store_b, hidden) = refs[:7]
+    *leaving, rows_b, rows, asking = refs[7 : 10 + len(masks)]
+    *buffers, raw, even = refs[10 + len(masks) : 14 + len(masks)]
+    *semaphores, raw_sems, even_sems = refs[14 + len(masks) :]
     me = me_ref[0]
     moves = []
     for i, mask in enumerate(masks):
@@ -287,21 +306,13 @@
         for a in range(arrival_from.shape[0]):
             slot += jnp.where(arrival_from[a, to] == me, arrival_slot[a, to], 0)
         moves.append((None, [(None, kv_cache.at[slot])], [(None, leaving[i])]))
-    groups = [moves]
-    held = []
-    for copy_id in range(COPIES):
-        slot = jnp.int32(0)
-        for span in range(spans):
-            row = holder[copy_id * spans + span]
-            slot += jnp.where(row // slot_total == me, row % slot_total, 0)
-        held.append(slot)
-    for table, target in ((store_a, rows_a), (store_b, rows_b)):
-        groups.append(
-            [
-                (None, [(None, table.at[slot])], [(None, target.at[copy_id])])
-                for copy_id, slot in enumerate(held)
-            ]
-        )
+    groups = [
+        moves,
+        [
+            (None, [(None, store_b.at[slot])], [(None, rows_b.at[copy_id])])
+            for copy_id, slot in enumerate(held_slots(me, holder, spans, slot_total))
+        ],
+    ]
 
     start = rows.shape[0] - asking.shape[0]
     fetch = pltpu.make_async_copy(hidden, raw, raw_sems.at[0, 0])
@@ -677,21 +688,22 @@
     first = resident * steps
     block = padded - first
 
-    *leaving, rows_a, rows_b, rows, asking = copy_call(
+    (rows_a,) = copy_call(
+        functools.partial(collect_down_kernel, spans, slot_total),
+        (me_table, hot_holder),
+        (store_a,),
+        [(COPIES,) + row_a],
+        [(COPIES,) + row_a],
+    )
+    sibling_a = partner(rows_a, 1)
+    *leaving, rows_b, rows, asking = copy_call(
         functools.partial(collect_kernel, spans, slot_total, masks),
         (me_table, from_table, slot_table, hot_holder),
-        (kv_cache, store_a, store_b, hidden),
+        (kv_cache, store_b, hidden),
         [kv_cache.shape[1:]] * len(masks)
-        + [(COPIES,) + row_a, (COPIES,) + row_b, (padded, features), (block, features)],
-        [
-            (len(masks),) + kv_cache.shape[1:],
-            (COPIES,) + row_a,
-            (COPIES,) + row_b,
-            hidden.shape,
-            (padded, features),
-        ],
-    )
-    sibling_a = partner(rows_a, 1)
+        + [(COPIES,) + row_b, (padded, features), (block, features)],
+        [(len(masks),) + kv_cache.shape[1:], (COPIES,) + row_b, hidden.shape, (padded, features)],
+    )
     sibling_b = partner(rows_b, 1)
     other_rows = [partner(asking, mask) for mask in masks]
     came = [partner(array, mask) for array, mask in zip(leaving, masks)]

time: 102 us -> 101 us (level)
  waiting for transfers between devices: 41.8 us -> 39.3 us
  Pallas kernels: 25.3 us -> 27.3 us
    ppermute x18, waiting for transfers between devices: 41.8 us -> 39.3 us  [partner(): lax.ppermute(array, 'replica', [(i, i ^ mask) for i in range(lax.axis_siz...]
    pallas_call x4 -> x5, Pallas kernels: 13.8 us -> 15.9 us  [copy_call(): pl.pallas_call(kernel, out_shape=[pltpu.HBM(shape, dtype) for shape in sh...]
  transfers between devices with their start and end apart: 24 -> 24, of which waited for: 9 -> 9; matrix products, arithmetic and copies ran while one was open for 6% -> 6% of each run, Pallas kernels for 14% -> 18%
where the time goes in v6:
time: 101 us
  waiting for transfers between devices  39.3 us (39%)
  Pallas kernels  27.3 us (27%)
  starting transfers between devices  24.4 us (24%)
  matrix products  5.75 us (6%)
  local copies, waits for them, and re-layouts  2.86 us (3%)
  between operations  1.34 us (1%)
    ppermute x18, waiting for transfers between devices, partner(): lax.ppermute(array, 'replica', [(i, i ^ mask) for i in range(lax.axis_siz...  39.3 us
    pallas_call x5, Pallas kernels, copy_call(): pl.pallas_call(kernel, out_shape=[pltpu.HBM(shape, dtype) for shape in sh...  15.9 us
    ppermute x18, starting transfers between devices, partner(): lax.ppermute(array, 'replica', [(i, i ^ mask) for i in range(lax.axis_siz...  12.3 us
    ppermute x6, starting transfers between devices, shifted(): lax.ppermute(array, 'tensor', [(i, (i + step) % size) for i in range(size)])  12.1 us
    dot_general x1, matrix products, pairs_layer(): jnp.einsum('md,dgc->gmc', full, w_kv, preferred_element_type=jnp.float32)  5.75 us
    pallas_call x1, Pallas kernels, pairs_layer(): pl.pallas_call(functools.partial(project_kernel, spans, slot_total, resid...  4.73 us
    pallas_call x1, Pallas kernels, pairs_layer(): pl.pallas_call(functools.partial(attend_kernel, spans, masks, resident, s...  4.69 us
  transfers between devices with their start and end apart: 24, of which 9 were waited for; matrix products, arithmetic and copies ran while one was open for 6% of the time, Pallas kernels for 18%

profile of v6, /device:TPU:4, one launch (start us, length us, event | category | flops | bytes accessed | tf_op | source)
XLA Modules:
  0.0 101.0 jit_solution(14492061970872885559)
XLA Ops:
  0.6 3.2 %shard_map.164 = bf16[4,2,64,2048]{3,2,1,0:T(8,128)(2,1)} custom-call(s32[1]{0:T(128)} %bitcast.me_ref.refs_0_, s32[16]{0:T(128)} %refs_6_.3, bf16[8,2,64,2048]{3,2,1,0:T(8,128)(2,1)} %refs_3_.4), custom_call_target="tpu_custom_call" | custom-call | tf_op jit(solution)/shard_map/pallas_call | solution.py:414
  3.9 0.0 copy-start.8
  3.9 0.4 collective-permute-start.16
  4.3 3.7 %shard_map.165 = (bf16[128,2,256]{2,1,0:T(2,128)(2,1)}, bf16[128,2,256]{2,1,0:T(2,128)(2,1)}, bf16[128,2,256]{2,1,0:T(2,128)(2,1)}, bf16[4,2,64,256]{3,2,1,0:T(8...) custom-call(s32[1]{0:T(128)} %bitcast.me_ref.refs_0_, s32[2,4]{1,0:T(2,128)} %bitcast.29, s32[2,4]{1,0:T(2,128)} %bitcast.31, ...), custom_call_target="tpu_custom_call" | custom-call | tf_op jit(solution)/shard_map/pallas_call | solution.py:414
  8.0 0.3 collective-permute-start.17
  8.2 1.5 %collective-permute-done.17.refs_6_ = bf16[4,2,64,256]{3,2,1,0:T(8,128)(2,1)S(1)} collective-permute-done((bf16[4,2,64,256]{3,2,1,0:T(8,128)(2,1)}, bf16[4,2,64,256]{3,2,1,0:T(8,128)(2,1)S(1)}, u32[]{:S(2)}, u32[]{:S(2)}) %collective-permute-start.17) | collective-permute-done | bytes 262176 | tf_op jit(solution)/shard_map/ppermute | solution.py:212
  9.8 0.0 collective-permute-done.16.refs_5_
  9.8 0.7 copy-done
  10.5 3.6 %shard_map.166 = (bf16[4,2,64,256]{3,2,1,0:T(8,128)(2,1)}, bf16[2,64,2048]{2,1,0:T(8,128)(2,1)}, bf16[3,64,2048]{2,1,0:T(8,128)(2,1)}, bf16[1,64,2048]{2,1,0:T(8...) custom-call(s32[1]{0:T(128)} %bitcast.me_ref.refs_0_, s32[16]{0:T(128)S(1)} %copy-done.7, ...), custom_call_target="tpu_custom_call" | custom-call | tf_op jit(solution)/shard_map/pallas_call | solution.py:414
  14.1 1.4 %collective-permute-start.35 = (bf16[2,64,2048]{2,1,0:T(8,128)(2,1)}, bf16[2,64,2048]{2,1,0:T(8,128)(2,1)S(1)}, u32[]{:S(2)}, u32[]{:S(2)}) collective-permute-start(bf16[2,64,2048]{2,1,0:T(8,128)(2,1)} %get-tuple-element.161), channel_id=1, source_target_pairs={{0,8},{4,12},{8,0},{12,4},{1,9},{5,13},{9,1},{13,5},{2,10},{6,14},... | collective-permute-start | bytes 1572872 | tf_op jit(solution)/shard_map/ppermute | solution.py:212
  15.5 0.2 collective-permute-start.23
  15.7 1.6 %collective-permute-start.22 = (bf16[8,2048]{1,0:T(8,128)(2,1)S(1)}, bf16[8,2048]{1,0:T(8,128)(2,1)S(1)}, u32[]{:S(2)}, u32[]{:S(2)}) collective-permute-start(bf16[8,2048]{1,0:T(8,128)(2,1)S(1)} %copy-done.16), channel_id=1, source_target_pairs={{0,8},{4,12},{8,0},{12,4},{1,9},{5,13},{9,1},{13,5},{2,10},{6,14},... | collective-permute-start | bytes 98312 | tf_op jit(solution)/shard_map/ppermute | solution.py:212
  17.2 3.6 %collective-permute-start.20 = (bf16[32,2048]{1,0:T(8,128)(2,1)S(1)}, bf16[32,2048]{1,0:T(8,128)(2,1)}, u32[]{:S(2)}, u32[]{:S(2)}) collective-permute-start(bf16[32,2048]{1,0:T(8,128)(2,1)S(1)} %copy-done.5), channel_id=1, source_target_pairs={{0,3},{1,0},{2,1},{3,2},{4,7},{5,4},{6,5},{7,6},{8,11},{9,8},{10,9... | collective-permute-start | bytes 393224 | tf_op jit(solution)/shard_map/ppermute | solution.py:217
  20.8 0.0 collective-permute-start.19
  20.8 7.6 %collective-permute-done.23.refs_8_ = bf16[8,2048]{1,0:T(8,128)(2,1)S(1)} collective-permute-done((bf16[8,2048]{1,0:T(8,128)(2,1)S(1)}, bf16[8,2048]{1,0:T(8,128)(2,1)S(1)}, u32[]{:S(2)}, u32[]{:S(2)}) %collective-permute-start.23) | collective-permute-done | bytes 32800 | tf_op jit(solution)/shard_map/ppermute | solution.py:212
  28.5 1.6 %collective-permute-start.18 = (bf16[32,2048]{1,0:T(8,128)(2,1)S(1)}, bf16[32,2048]{1,0:T(8,128)(2,1)}, u32[]{:S(2)}, u32[]{:S(2)}) collective-permute-start(bf16[32,2048]{1,0:T(8,128)(2,1)S(1)} %copy-done.5), channel_id=1, source_target_pairs={{0,1},{1,2},{2,3},{3,0},{4,5},{5,6},{6,7},{7,4},{8,9},{9,10},{10,1... | collective-permute-start | bytes 393224 | tf_op jit(solution)/shard_map/ppermute | solution.py:217
  30.1 0.0 collective-permute-done.22.refs_7_
  30.1 0.5 collective-permute-start.21
  30.5 0.9 collective-permute-done.21.refs_6_
  31.4 0.0 copy-done.9
  31.4 0.6 copy-done.11
  32.0 4.7 %project.1 = (f32[32,128]{1,0:T(8,128)}, f32[8,128]{1,0:T(8,128)}, f32[8,128]{1,0:T(8,128)}, f32[8,128]{1,0:T(8,128)}) custom-call(s32[1]{0:T(128)} %bitcast.me_ref.refs_0_, s32[48]{0:T(128)} %refs_4_.5, s32[2,4]{1,0:T(2,128)} %bitcast.33, s32[16]{0:T(128)S(1)} %copy-done.7, s32[1,16]{1,0:T(1,128)S(1)} %bitcast.23, ...), custom_call_target="tpu_custom_call" | custom-call | tf_op jit(solution)/shard_map/project/pallas_call | solution.py:714
  36.7 0.4 collective-permute-start.24
  37.2 1.0 %collective-permute-done.24.refs_5_ = f32[8,128]{1,0:T(8,128)S(1)} collective-permute-done((f32[8,128]{1,0:T(8,128)}, f32[8,128]{1,0:T(8,128)S(1)}, u32[]{:S(2)}, u32[]{:S(2)}) %collective-permute-start.24) | collective-permute-done | bytes 4128 | tf_op jit(solution)/shard_map/ppermute | solution.py:212
  38.2 1.6 %collective-permute-start.25 = (f32[8,128]{1,0:T(8,128)}, f32[8,128]{1,0:T(8,128)S(1)}, u32[]{:S(2)}, u32[]{:S(2)}) collective-permute-start(f32[8,128]{1,0:T(8,128)} %get-tuple-element.147), channel_id=1, source_target_pairs={{0,8},{4,12},{8,0},{12,4},{1,9},{5,13},{9,1},{13,5},{2,10},{6,14},... | collective-permute-start | bytes 12296 | tf_op jit(solution)/shard_map/ppermute | solution.py:212
  39.8 2.3 %collective-permute-done.25.refs_6_ = f32[8,128]{1,0:T(8,128)S(1)} collective-permute-done((f32[8,128]{1,0:T(8,128)}, f32[8,128]{1,0:T(8,128)S(1)}, u32[]{:S(2)}, u32[]{:S(2)}) %collective-permute-start.25) | collective-permute-done | bytes 4128 | tf_op jit(solution)/shard_map/ppermute | solution.py:212
  42.0 0.4 collective-permute-start.26
  42.4 2.9 %collective-permute-done.26.refs_7_ = f32[8,128]{1,0:T(8,128)S(1)} collective-permute-done((f32[8,128]{1,0:T(8,128)}, f32[8,128]{1,0:T(8,128)S(1)}, u32[]{:S(2)}, u32[]{:S(2)}) %collective-permute-start.26) | collective-permute-done | bytes 4128 | tf_op jit(solution)/shard_map/ppermute | solution.py:212
  45.3 0.6 copy-done.15
  45.9 1.6 %collective-permute-start.34 = (bf16[3,64,2048]{2,1,0:T(8,128)(2,1)}, bf16[3,64,2048]{2,1,0:T(8,128)(2,1)S(1)}, u32[]{:S(2)}, u32[]{:S(2)}) collective-permute-start(bf16[3,64,2048]{2,1,0:T(8,128)(2,1)} %get-tuple-element.160), channel_id=1, source_target_pairs={{0,8},{4,12},{8,0},{12,4},{1,9},{5,13},{9,1},{13,5},{2,10},{6,14},... | collective-permute-start | bytes 2359304 | tf_op jit(solution)/shard_map/ppermute | solution.py:212
  47.4 0.0 collective-permute-done.20.refs_3_
  47.4 0.0 collective-permute-start.30
  47.4 0.0 collective-permute-done.19.refs_2_
  47.4 0.5 collective-permute-start.31
  48.0 0.0 collective-permute-done.18.refs_1_
  48.0 1.3 %collective-permute-start.32 = (bf16[128,2,256]{2,1,0:T(2,128)(2,1)}, bf16[128,2,256]{2,1,0:T(2,128)(2,1)S(1)}, u32[]{:S(2)}, u32[]{:S(2)}) collective-permute-start(bf16[128,2,256]{2,1,0:T(2,128)(2,1)} %get-tuple-element.152), channel_id=1, source_target_pairs={{0,12},{4,8},{8,4},{12,0},{1,13},{5,9},{9,5},{13,1},{2,14},{6,10},... | collective-permute-start | bytes 393224 | tf_op jit(solution)/shard_map/ppermute | solution.py:212
  49.3 2.0 %gather.1 = (bf16[32,8192]{1,0:T(8,128)(2,1)}, f32[32,128]{1,0:T(8,128)}) custom-call(s32[1]{0:T(128)} %bitcast.5.shard_ref, bf16[32,2048]{1,0:T(8,128)(2,1)} %get-tuple-element.143.refs_5_.refs_0_, bf16[32,2048]{1,0:T(8,128)(2,1)} %collective-permute-done.18.refs_1_, bf16[32,2048]{1,0:T(8,128)(2,1)} %collective-permute-done.19.refs_2_, ...), custom_call_target="tpu_custom_call" | custom-call | tf_op jit(solution)/shard_map/gather/pallas_call | solution.py:757
  51.3 0.0 collective-permute-done.30.refs_12_
  51.3 3.2 %collective-permute-start.29 = (f32[32,128]{1,0:T(8,128)}, f32[32,128]{1,0:T(8,128)S(1)}, u32[]{:S(2)}, u32[]{:S(2)}) collective-permute-start(f32[32,128]{1,0:T(8,128)} %get-tuple-element.149.refs_8_), channel_id=1, source_target_pairs={{0,3},{1,0},{2,1},{3,2},{4,7},{5,4},{6,5},{7,6},{8,11},{9,8},{10,9... | collective-permute-start | bytes 49160 | tf_op jit(solution)/shard_map/ppermute | solution.py:217
  54.5 14.9 %collective-permute-done.31.refs_13_ = bf16[128,2,256]{2,1,0:T(2,128)(2,1)} collective-permute-done((bf16[128,2,256]{2,1,0:T(2,128)(2,1)}, bf16[128,2,256]{2,1,0:T(2,128)(2,1)}, u32[]{:S(2)}, u32[]{:S(2)}) %collective-permute-start.31) | collective-permute-done | bytes 131104 | tf_op jit(solution)/shard_map/ppermute | solution.py:212
  69.4 3.0 %collective-permute-start.28 = (f32[32,128]{1,0:T(8,128)}, f32[32,128]{1,0:T(8,128)}, u32[]{:S(2)}, u32[]{:S(2)}) collective-permute-start(f32[32,128]{1,0:T(8,128)} %get-tuple-element.149.refs_8_), channel_id=1, source_target_pairs={{0,2},{1,3},{2,0},{3,1},{4,6},{5,7},{6,4},{7,5},{8,10},{9,11},{10,... | collective-permute-start | bytes 49160 | tf_op jit(solution)/shard_map/ppermute | solution.py:217
  72.4 0.0 collective-permute-done.32.refs_14_
  72.4 0.8 collective-permute-start.27
  73.1 0.0 collective-permute-done.29.refs_11_
  73.1 1.0 %collective-permute-start.33 = (bf16[4,2,64,256]{3,2,1,0:T(8,128)(2,1)}, bf16[4,2,64,256]{3,2,1,0:T(8,128)(2,1)}, u32[]{:S(2)}, u32[]{:S(2)}) collective-permute-start(bf16[4,2,64,256]{3,2,1,0:T(8,128)(2,1)} %get-tuple-element.153), channel_id=1, source_target_pairs={{0,8},{4,12},{8,0},{12,4},{1,9},{5,13},{9,1},{13,5},{2,10},{6,14},... | collective-permute-start | bytes 786440 | tf_op jit(solution)/shard_map/ppermute | solution.py:212
  74.2 0.0 collective-permute-done.35
  74.2 0.0 collective-permute-start.36
  74.2 5.7 %fusion.2.refs_18_ = f32[2,32,256]{2,1,0:T(8,128)} fusion(bf16[8192,2,256]{2,1,0:T(2,128)(2,1)} %param.20, bf16[32,8192]{1,0:T(8,128)(2,1)} %get-tuple-element.154), kind=kOutput, calls=%fused_computation.2 | convolution fusion | flops 268435456 | bytes 8978432 | tf_op jit(solution)/shard_map/md,dgc->gmc/dot_general | solution.py:768
  80.5 0.0 collective-permute-done.28.refs_10_
  80.5 0.0 collective-permute-done.27.refs_9_
  80.5 0.4 collective-permute-done.33
  80.9 4.7 %attend.1 = (bf16[14,2,2048]{2,1,0:T(2,128)(2,1)}, bf16[14,2,2,256]{3,2,1,0:T(2,128)(2,1)}, bf16[2,128,2,256]{3,2,1,0:T(2,128)(2,1)}, bf16[4,128,256]{2,1,0:T(8,128)(2,1)}) custom-call(s32[1]{0:T(128)} %bitcast.me_ref.refs_0_, s32[48]{0:T(128)} %refs_1_.5, s32[2,4]{1,0:T(2,128)} %bitcast.30, s32[2,4]{1,0:T(2,128)} %bitcast.32, s32[48]{0:T(128)} %refs_4_.5, ...), custom_call_target="tpu_custom_call" | custom-call | tf_op jit(solution)/shard_map/attend/pallas_call | solution.py:770
  85.6 0.0 collective-permute-done.34
  85.6 0.0 collective-permute-done.36
  85.6 15.4 %conditional.1 = (bf16[4,2,64,2048]{3,2,1,0:T(8,128)(2,1)}) conditional(s32[]{:T(128)} %bitcast.13, (bf16[3,64,2048]{2,1,0:T(8,128)(2,1)S(1)}, s32[1]{0:T(128)}, s32[16]{0:T(128)S(1)}, s32[1,16]{1,0:T(1,128)S(1)}, bf16[4,2,64,2048]{3,2,1,0:T(8,128)(2,1)S(1)}, /*index=5*/bf16[2,64,2048]{2,1,0:T(8,128)(2,1)S(1)}, ...), branch_computations={%region_0.0_spmd, %region_1.0_spmd, %region_2.0_spmd, %region_3.0_... | conditional | bytes 12583228 | solution.py:839
  85.6 0.2 collective-permute-start.1
  85.9 1.1 %collective-permute-start.2 = (bf16[1,64,2048]{2,1,0:T(8,128)(2,1)}, bf16[1,64,2048]{2,1,0:T(8,128)(2,1)}, u32[]{:S(2)}, u32[]{:S(2)}) collective-permute-start(bf16[1,64,2048]{2,1,0:T(8,128)(2,1)} %get-tuple-element.87), channel_id=1, source_target_pairs={{0,8},{4,12},{8,0},{12,4},{1,9},{5,13},{9,1},{13,5},{2,10},{6,14},... | collective-permute-start | bytes 786440 | tf_op jit(solution)/shard_map/cond/branch_1_fun/ppermute | solution.py:212
  86.9 7.8 %collective-permute-done.2.refs_4_ = bf16[1,64,2048]{2,1,0:T(8,128)(2,1)} collective-permute-done((bf16[1,64,2048]{2,1,0:T(8,128)(2,1)}, bf16[1,64,2048]{2,1,0:T(8,128)(2,1)}, u32[]{:S(2)}, u32[]{:S(2)}) %collective-permute-start.2) | collective-permute-done | bytes 262176 | tf_op jit(solution)/shard_map/cond/branch_1_fun/ppermute | solution.py:212
  94.7 0.0 collective-permute-start.3
  94.8 0.0 collective-permute-done.1.refs_7_
  94.8 0.9 copy-done.3
  95.7 2.8 %branch_1_fun.2.refs_3_ = bf16[4,2,64,2048]{3,2,1,0:T(8,128)(2,1)} custom-call(s32[1]{0:T(128)} %get-tuple-element.80.refs_0_, s32[16]{0:T(128)S(1)} %get-tuple-element.81.refs_1_, s32[1,16]{1,0:T(1,128)S(1)} %get-tuple-element.82.refs_2_, bf16[4,2,64,2048]{3,2,1,0:T(8,128)(2,1)S(1)} %get-tuple-element.83.refs_3_, ...), custom_call_target="tpu_custom_call" | custom-call | tf_op jit(solution)/shard_map/cond/branch_1_fun/pallas_call | solution.py:414
  98.5 0.0 collective-permute-done.3.refs_5_
  98.5 2.5 %branch_1_fun.3 = bf16[4,2,64,2048]{3,2,1,0:T(8,128)(2,1)} custom-call(s32[1]{0:T(128)} %get-tuple-element.80.refs_0_, s32[16]{0:T(128)S(1)} %get-tuple-element.81.refs_1_, s32[1,16]{1,0:T(1,128)S(1)} %get-tuple-element.82.refs_2_, bf16[4,2,64,2048]{3,2,1,0:T(8,128)(2,1)} %branch_1_fun.2.refs_3_, ...), custom_call_target="tpu_custom_call", output_to_operand_aliasing={{}: (3, {})} | custom-call | tf_op jit(solution)/shard_map/cond/branch_1_fun/pallas_call | solution.py:414
  (22 shorter events, 0.0 us)
Async XLA Ops:
  0.6 3.6 %copy-start.7 = (s32[16]{0:T(128)S(1)}, s32[16]{0:T(128)}, u32[]{:S(2)}) copy-start(s32[16]{0:T(128)} %refs_6_.3) | copy-start | bytes 196
  3.9 6.6 %copy-start.8 = (s32[16,1]{0,1:T(1,128)S(1)}, s32[16,1]{0,1:T(1,128)}, u32[]{:S(2)}) copy-start(s32[16,1]{0,1:T(1,128)} %param.29) | copy-start | bytes 196
  3.9 5.9 %collective-permute-start.16 = (bf16[4,2,64,2048]{3,2,1,0:T(8,128)(2,1)}, bf16[4,2,64,2048]{3,2,1,0:T(8,128)(2,1)S(1)}, u32[]{:S(2)}, u32[]{:S(2)}) collective-permute-start(bf16[4,2,64,2048]{3,2,1,0:T(8,128)(2,1)} %shard_map.164), channel_id=1, source_target_pairs={{0,4},{4,0},{8,12},{12,8},{1,5},{5,1},{9,13},{13,9},{2,6},{6,2},{1... | collective-permute-start | bytes 6291464 | tf_op jit(solution)/shard_map/ppermute | solution.py:212
  8.0 1.8 %collective-permute-start.17 = (bf16[4,2,64,256]{3,2,1,0:T(8,128)(2,1)}, bf16[4,2,64,256]{3,2,1,0:T(8,128)(2,1)S(1)}, u32[]{:S(2)}, u32[]{:S(2)}) collective-permute-start(bf16[4,2,64,256]{3,2,1,0:T(8,128)(2,1)} %get-tuple-element.139), channel_id=1, source_target_pairs={{0,4},{4,0},{8,12},{12,8},{1,5},{5,1},{9,13},{13,9},{2,6},{6,2},{1... | collective-permute-start | bytes 786440 | tf_op jit(solution)/shard_map/ppermute | solution.py:212
  9.8 0.7 copy-start
  10.5 5.0 %copy-start.16 = (bf16[8,2048]{1,0:T(8,128)(2,1)S(1)}, bf16[8,2048]{1,0:T(8,128)(2,1)}, u32[]{:S(2)}) copy-start(bf16[8,2048]{1,0:T(8,128)(2,1)} %get-tuple-element.144) | copy-start | bytes 98308
  10.5 6.8 %copy-start.5 = (bf16[32,2048]{1,0:T(8,128)(2,1)S(1)}, bf16[32,2048]{1,0:T(8,128)(2,1)}, u32[]{:S(2)}) copy-start(bf16[32,2048]{1,0:T(8,128)(2,1)} %get-tuple-element.143.refs_5_.refs_0_) | copy-start | bytes 393220
  14.1 60.1 %collective-permute-start.35 = (bf16[2,64,2048]{2,1,0:T(8,128)(2,1)}, bf16[2,64,2048]{2,1,0:T(8,128)(2,1)S(1)}, u32[]{:S(2)}, u32[]{:S(2)}) collective-permute-start(bf16[2,64,2048]{2,1,0:T(8,128)(2,1)} %get-tuple-element.161), channel_id=1, source_target_pairs={{0,8},{4,12},{8,0},{12,4},{1,9},{5,13},{9,1},{13,5},{2,10},{6,14},... | collective-permute-start | bytes 1572872 | tf_op jit(solution)/shard_map/ppermute | solution.py:212
  15.5 13.0 %collective-permute-start.23 = (bf16[8,2048]{1,0:T(8,128)(2,1)S(1)}, bf16[8,2048]{1,0:T(8,128)(2,1)S(1)}, u32[]{:S(2)}, u32[]{:S(2)}) collective-permute-start(bf16[8,2048]{1,0:T(8,128)(2,1)S(1)} %copy-done.16), channel_id=1, source_target_pairs={{0,12},{4,8},{8,4},{12,0},{1,13},{5,9},{9,5},{13,1},{2,14},{6,10},... | collective-permute-start | bytes 98312 | tf_op jit(solution)/shard_map/ppermute | solution.py:212
  15.7 14.4 %collective-permute-start.22 = (bf16[8,2048]{1,0:T(8,128)(2,1)S(1)}, bf16[8,2048]{1,0:T(8,128)(2,1)S(1)}, u32[]{:S(2)}, u32[]{:S(2)}) collective-permute-start(bf16[8,2048]{1,0:T(8,128)(2,1)S(1)} %copy-done.16), channel_id=1, source_target_pairs={{0,8},{4,12},{8,0},{12,4},{1,9},{5,13},{9,1},{13,5},{2,10},{6,14},... | collective-permute-start | bytes 98312 | tf_op jit(solution)/shard_map/ppermute | solution.py:212
  17.2 30.2 %collective-permute-start.20 = (bf16[32,2048]{1,0:T(8,128)(2,1)S(1)}, bf16[32,2048]{1,0:T(8,128)(2,1)}, u32[]{:S(2)}, u32[]{:S(2)}) collective-permute-start(bf16[32,2048]{1,0:T(8,128)(2,1)S(1)} %copy-done.5), channel_id=1, source_target_pairs={{0,3},{1,0},{2,1},{3,2},{4,7},{5,4},{6,5},{7,6},{8,11},{9,8},{10,9... | collective-permute-start | bytes 393224 | tf_op jit(solution)/shard_map/ppermute | solution.py:217
  20.8 26.6 %collective-permute-start.19 = (bf16[32,2048]{1,0:T(8,128)(2,1)S(1)}, bf16[32,2048]{1,0:T(8,128)(2,1)}, u32[]{:S(2)}, u32[]{:S(2)}) collective-permute-start(bf16[32,2048]{1,0:T(8,128)(2,1)S(1)} %copy-done.5), channel_id=1, source_target_pairs={{0,2},{1,3},{2,0},{3,1},{4,6},{5,7},{6,4},{7,5},{8,10},{9,11},{10,... | collective-permute-start | bytes 393224 | tf_op jit(solution)/shard_map/ppermute | solution.py:217
  28.5 2.9 %copy-start.9 = (bf16[8,2048]{1,0:T(8,128)(2,1)}, bf16[8,2048]{1,0:T(8,128)(2,1)S(1)}, u32[]{:S(2)}) copy-start(bf16[8,2048]{1,0:T(8,128)(2,1)S(1)} %collective-permute-done.23.refs_8_) | copy-start | bytes 98308
  28.5 19.5 %collective-permute-start.18 = (bf16[32,2048]{1,0:T(8,128)(2,1)S(1)}, bf16[32,2048]{1,0:T(8,128)(2,1)}, u32[]{:S(2)}, u32[]{:S(2)}) collective-permute-start(bf16[32,2048]{1,0:T(8,128)(2,1)S(1)} %copy-done.5), channel_id=1, source_target_pairs={{0,1},{1,2},{2,3},{3,0},{4,5},{5,6},{6,7},{7,4},{8,9},{9,10},{10,1... | collective-permute-start | bytes 393224 | tf_op jit(solution)/shard_map/ppermute | solution.py:217
  30.1 1.3 %copy-start.10 = (bf16[8,2048]{1,0:T(8,128)(2,1)}, bf16[8,2048]{1,0:T(8,128)(2,1)S(1)}, u32[]{:S(2)}) copy-start(bf16[8,2048]{1,0:T(8,128)(2,1)S(1)} %collective-permute-done.22.refs_7_) | copy-start | bytes 98308
  30.1 1.3 %collective-permute-start.21 = (bf16[8,2048]{1,0:T(8,128)(2,1)S(1)}, bf16[8,2048]{1,0:T(8,128)(2,1)S(1)}, u32[]{:S(2)}, u32[]{:S(2)}) collective-permute-start(bf16[8,2048]{1,0:T(8,128)(2,1)S(1)} %copy-done.16), channel_id=1, source_target_pairs={{0,4},{4,0},{8,12},{12,8},{1,5},{5,1},{9,13},{13,9},{2,6},{6,2},{1... | collective-permute-start | bytes 98312 | tf_op jit(solution)/shard_map/ppermute | solution.py:212
  31.4 0.6 copy-start.11
  36.7 1.4 %collective-permute-start.24 = (f32[8,128]{1,0:T(8,128)}, f32[8,128]{1,0:T(8,128)S(1)}, u32[]{:S(2)}, u32[]{:S(2)}) collective-permute-start(f32[8,128]{1,0:T(8,128)} %get-tuple-element.146), channel_id=1, source_target_pairs={{0,4},{4,0},{8,12},{12,8},{1,5},{5,1},{9,13},{13,9},{2,6},{6,2},{1... | collective-permute-start | bytes 12296 | tf_op jit(solution)/shard_map/ppermute | solution.py:212
  38.2 11.1 %copy-start.13 = (f32[8,128]{1,0:T(8,128)}, f32[8,128]{1,0:T(8,128)S(1)}, u32[]{:S(2)}) copy-start(f32[8,128]{1,0:T(8,128)S(1)} %collective-permute-done.24.refs_5_) | copy-start | bytes 12292
  38.2 3.8 %collective-permute-start.25 = (f32[8,128]{1,0:T(8,128)}, f32[8,128]{1,0:T(8,128)S(1)}, u32[]{:S(2)}, u32[]{:S(2)}) collective-permute-start(f32[8,128]{1,0:T(8,128)} %get-tuple-element.147), channel_id=1, source_target_pairs={{0,8},{4,12},{8,0},{12,4},{1,9},{5,13},{9,1},{13,5},{2,10},{6,14},... | collective-permute-start | bytes 12296 | tf_op jit(solution)/shard_map/ppermute | solution.py:212
  42.0 7.3 %copy-start.14 = (f32[8,128]{1,0:T(8,128)}, f32[8,128]{1,0:T(8,128)S(1)}, u32[]{:S(2)}) copy-start(f32[8,128]{1,0:T(8,128)S(1)} %collective-permute-done.25.refs_6_) | copy-start | bytes 12292
  42.0 3.2 %collective-permute-start.26 = (f32[8,128]{1,0:T(8,128)}, f32[8,128]{1,0:T(8,128)S(1)}, u32[]{:S(2)}, u32[]{:S(2)}) collective-permute-start(f32[8,128]{1,0:T(8,128)} %get-tuple-element.148), channel_id=1, source_target_pairs={{0,12},{4,8},{8,4},{12,0},{1,13},{5,9},{9,5},{13,1},{2,14},{6,10},... | collective-permute-start | bytes 12296 | tf_op jit(solution)/shard_map/ppermute | solution.py:212
  45.3 0.6 copy-start.15
  45.9 39.7 %collective-permute-start.34 = (bf16[3,64,2048]{2,1,0:T(8,128)(2,1)}, bf16[3,64,2048]{2,1,0:T(8,128)(2,1)S(1)}, u32[]{:S(2)}, u32[]{:S(2)}) collective-permute-start(bf16[3,64,2048]{2,1,0:T(8,128)(2,1)} %get-tuple-element.160), channel_id=1, source_target_pairs={{0,8},{4,12},{8,0},{12,4},{1,9},{5,13},{9,1},{13,5},{2,10},{6,14},... | collective-permute-start | bytes 2359304 | tf_op jit(solution)/shard_map/ppermute | solution.py:212
  47.4 3.9 %collective-permute-start.30 = (bf16[128,2,256]{2,1,0:T(2,128)(2,1)}, bf16[128,2,256]{2,1,0:T(2,128)(2,1)}, u32[]{:S(2)}, u32[]{:S(2)}) collective-permute-start(bf16[128,2,256]{2,1,0:T(2,128)(2,1)} %get-tuple-element.150), channel_id=1, source_target_pairs={{0,4},{4,0},{8,12},{12,8},{1,5},{5,1},{9,13},{13,9},{2,6},{6,2},{1... | collective-permute-start | bytes 393224 | tf_op jit(solution)/shard_map/ppermute | solution.py:212
  47.4 22.0 %collective-permute-start.31 = (bf16[128,2,256]{2,1,0:T(2,128)(2,1)}, bf16[128,2,256]{2,1,0:T(2,128)(2,1)}, u32[]{:S(2)}, u32[]{:S(2)}) collective-permute-start(bf16[128,2,256]{2,1,0:T(2,128)(2,1)} %get-tuple-element.151), channel_id=1, source_target_pairs={{0,8},{4,12},{8,0},{12,4},{1,9},{5,13},{9,1},{13,5},{2,10},{6,14},... | collective-permute-start | bytes 393224 | tf_op jit(solution)/shard_map/ppermute | solution.py:212
  48.0 24.4 %collective-permute-start.32 = (bf16[128,2,256]{2,1,0:T(2,128)(2,1)}, bf16[128,2,256]{2,1,0:T(2,128)(2,1)S(1)}, u32[]{:S(2)}, u32[]{:S(2)}) collective-permute-start(bf16[128,2,256]{2,1,0:T(2,128)(2,1)} %get-tuple-element.152), channel_id=1, source_target_pairs={{0,12},{4,8},{8,4},{12,0},{1,13},{5,9},{9,5},{13,1},{2,14},{6,10},... | collective-permute-start | bytes 393224 | tf_op jit(solution)/shard_map/ppermute | solution.py:212
  51.3 21.9 %collective-permute-start.29 = (f32[32,128]{1,0:T(8,128)}, f32[32,128]{1,0:T(8,128)S(1)}, u32[]{:S(2)}, u32[]{:S(2)}) collective-permute-start(f32[32,128]{1,0:T(8,128)} %get-tuple-element.149.refs_8_), channel_id=1, source_target_pairs={{0,3},{1,0},{2,1},{3,2},{4,7},{5,4},{6,5},{7,6},{8,11},{9,8},{10,9... | collective-permute-start | bytes 49160 | tf_op jit(solution)/shard_map/ppermute | solution.py:217
  69.4 11.1 %collective-permute-start.28 = (f32[32,128]{1,0:T(8,128)}, f32[32,128]{1,0:T(8,128)}, u32[]{:S(2)}, u32[]{:S(2)}) collective-permute-start(f32[32,128]{1,0:T(8,128)} %get-tuple-element.149.refs_8_), channel_id=1, source_target_pairs={{0,2},{1,3},{2,0},{3,1},{4,6},{5,7},{6,4},{7,5},{8,10},{9,11},{10,... | collective-permute-start | bytes 49160 | tf_op jit(solution)/shard_map/ppermute | solution.py:217
  72.4 7.6 %copy-start.6 = (bf16[128,2,256]{2,1,0:T(2,128)(2,1)}, bf16[128,2,256]{2,1,0:T(2,128)(2,1)S(1)}, u32[]{:S(2)}) copy-start(bf16[128,2,256]{2,1,0:T(2,128)(2,1)S(1)} %collective-permute-done.32.refs_14_) | copy-start | bytes 393220
  72.4 8.2 %collective-permute-start.27 = (f32[32,128]{1,0:T(8,128)}, f32[32,128]{1,0:T(8,128)}, u32[]{:S(2)}, u32[]{:S(2)}) collective-permute-start(f32[32,128]{1,0:T(8,128)} %get-tuple-element.149.refs_8_), channel_id=1, source_target_pairs={{0,1},{1,2},{2,3},{3,0},{4,5},{5,6},{6,7},{7,4},{8,9},{9,10},{10,1... | collective-permute-start | bytes 49160 | tf_op jit(solution)/shard_map/ppermute | solution.py:217
  73.1 1.0 %copy-start.12 = (f32[32,128]{1,0:T(8,128)}, f32[32,128]{1,0:T(8,128)S(1)}, u32[]{:S(2)}) copy-start(f32[32,128]{1,0:T(8,128)S(1)} %collective-permute-done.29.refs_11_) | copy-start | bytes 49156
  73.1 7.8 %collective-permute-start.33 = (bf16[4,2,64,256]{3,2,1,0:T(8,128)(2,1)}, bf16[4,2,64,256]{3,2,1,0:T(8,128)(2,1)}, u32[]{:S(2)}, u32[]{:S(2)}) collective-permute-start(bf16[4,2,64,256]{3,2,1,0:T(8,128)(2,1)} %get-tuple-element.153), channel_id=1, source_target_pairs={{0,8},{4,12},{8,0},{12,4},{1,9},{5,13},{9,1},{13,5},{2,10},{6,14},... | collective-permute-start | bytes 786440 | tf_op jit(solution)/shard_map/ppermute | solution.py:212
  74.2 11.4 %collective-permute-start.36 = (bf16[2,64,2048]{2,1,0:T(8,128)(2,1)S(1)}, bf16[2,64,2048]{2,1,0:T(8,128)(2,1)}, u32[]{:S(2)}, u32[]{:S(2)}) collective-permute-start(bf16[2,64,2048]{2,1,0:T(8,128)(2,1)S(1)} %collective-permute-done.35), channel_id=1, source_target_pairs={{0,4},{4,0},{8,12},{12,8},{1,5},{5,1},{9,13},{13,9},{2,6},{6,2},{1... | collective-permute-start | bytes 1572872 | tf_op jit(solution)/shard_map/ppermute | solution.py:212
  85.6 9.1 %collective-permute-start.1 = (bf16[3,64,2048]{2,1,0:T(8,128)(2,1)S(1)}, bf16[3,64,2048]{2,1,0:T(8,128)(2,1)S(1)}, u32[]{:S(2)}, u32[]{:S(2)}) collective-permute-start(bf16[3,64,2048]{2,1,0:T(8,128)(2,1)S(1)} %get-tuple-element.85.refs_5_), channel_id=1, source_target_pairs={{0,4},{4,0},{8,12},{12,8},{1,5},{5,1},{9,13},{13,9},{2,6},{6,2},{1... | collective-permute-start | bytes 2359304 | tf_op jit(solution)/shard_map/cond/branch_1_fun/ppermute | solution.py:212
  85.9 8.9 %collective-permute-start.2 = (bf16[1,64,2048]{2,1,0:T(8,128)(2,1)}, bf16[1,64,2048]{2,1,0:T(8,128)(2,1)}, u32[]{:S(2)}, u32[]{:S(2)}) collective-permute-start(bf16[1,64,2048]{2,1,0:T(8,128)(2,1)} %get-tuple-element.87), channel_id=1, source_target_pairs={{0,8},{4,12},{8,0},{12,4},{1,9},{5,13},{9,1},{13,5},{2,10},{6,14},... | collective-permute-start | bytes 786440 | tf_op jit(solution)/shard_map/cond/branch_1_fun/ppermute | solution.py:212
  94.7 3.8 %collective-permute-start.3 = (bf16[1,64,2048]{2,1,0:T(8,128)(2,1)}, bf16[1,64,2048]{2,1,0:T(8,128)(2,1)}, u32[]{:S(2)}, u32[]{:S(2)}) collective-permute-start(bf16[1,64,2048]{2,1,0:T(8,128)(2,1)} %collective-permute-done.2.refs_4_), channel_id=1, source_target_pairs={{0,4},{4,0},{8,12},{12,8},{1,5},{5,1},{9,13},{13,9},{2,6},{6,2},{1... | collective-permute-start | bytes 786440 | tf_op jit(solution)/shard_map/cond/branch_1_fun/ppermute | solution.py:212
  94.8 0.9 copy-start.3

commit v7 on v5

--- a/solution.py
+++ b/solution.py
@@ -217,7 +217,7 @@
     return lax.ppermute(array, "tensor", [(i, (i + step) % size) for i in range(size)])
 
 
-ALWAYS = ((0, 2), (2, 3))
+ALWAYS = ((0, 2), (2, 2), (4, 1))
 AT_NEED = ((5, 1), (6, 1), (7, 1))
 SMEM = pl.BlockSpec(memory_space=pltpu.SMEM)
 VMEM = pl.BlockSpec(memory_space=pltpu.VMEM)
@@ -793,38 +793,36 @@
     installed_b = installed_b.reshape((COPIES,) + row_b)
 
     tables = (me_table, hot_holder, dest_table)
+    early = len(ALWAYS) - 1
+    other = [partner(array, 1) for array in got[:early]]
+    (placed,) = copy_call(
+        functools.partial(place_kernel, spans, slot_total, ALWAYS[:early]),
+        tables,
+        (sibling_a, *got[:early], *other),
+        [(COPIES,) + row_a],
+        [(unit_total,) + unit_shape],
+    )
 
     def finish(count):
-        def branch(sibling_a, first_other, *arrays):
-            got, rest = list(arrays[: len(ALWAYS)]), arrays[len(ALWAYS) :]
-            late = [partner(array, 2) for array in rest[:count]]
-            other = [first_other] + [partner(array, 1) for array in got[1:]]
-            (placed,) = copy_call(
-                functools.partial(place_kernel, spans, slot_total, ALWAYS),
-                tables,
-                (sibling_a, *got, *other),
-                [(COPIES,) + row_a],
-                [(unit_total,) + unit_shape],
-            )
-            if not count:
-                return placed
-            other = [partner(array, 1) for array in late]
-            (placed,) = copy_call(
-                functools.partial(place_kernel, spans, slot_total, AT_NEED[:count]),
+        def branch(placed, *arrays):
+            late = [partner(array, 2) for array in arrays[1:][:count]]
+            other = [partner(arrays[0], 1)]
+            late = [arrays[0]] + late
+            other += [partner(array, 1) for array in late[1:]]
+            return copy_call(
+                functools.partial(place_kernel, spans, slot_total, (ALWAYS + AT_NEED)[early:][: count + 1]),
                 tables,
                 (placed, *late, *other),
                 [(COPIES,) + row_a],
                 [(unit_total,) + unit_shape],
                 aliases={len(tables): 0},
-            )
-            return placed
+            )[0]
 
         return branch
 
     branches = [finish(count) for count in range(len(AT_NEED) + 1)]
-    first_other = partner(got[0], 1)
     *rest, attn_out = lax.optimization_barrier((*units[len(ALWAYS) :], attn_out))
-    installed_a = lax.switch(extra[0], branches, sibling_a, first_other, *got, *rest)
+    installed_a = lax.switch(extra[0], branches, placed, got[early], *rest)
     return (attn_out, new_kv, arrived, installed_a, installed_b)
 
 

time: 102 us -> 106 us (1.039)
  the two profiles are of different devices: /device:TPU:4 before, /device:TPU:13 now
where the time goes in v7:
time: 106 us
  waiting for transfers between devices  40.4 us (38%)
  starting transfers between devices  27.3 us (26%)
  Pallas kernels  25.8 us (24%)
  matrix products  5.83 us (6%)
  local copies, waits for them, and re-layouts  5.11 us (5%)
  between operations  1.51 us (1%)
    ppermute x20, waiting for transfers between devices, partner(): lax.ppermute(array, 'replica', [(i, i ^ mask) for i in range(lax.axis_siz...  37.4 us
    ppermute x20, starting transfers between devices, partner(): lax.ppermute(array, 'replica', [(i, i ^ mask) for i in range(lax.axis_siz...  20.4 us
    pallas_call x4, Pallas kernels, copy_call(): pl.pallas_call(kernel, out_shape=[pltpu.HBM(shape, dtype) for shape in sh...  14.3 us
    ppermute x6, starting transfers between devices, shifted(): lax.ppermute(array, 'tensor', [(i, (i + step) % size) for i in range(size)])  6.95 us
    dot_general x1, matrix products, pairs_layer(): jnp.einsum('md,dgc->gmc', full, w_kv, preferred_element_type=jnp.float32)  5.83 us
    pallas_call x1, Pallas kernels, pairs_layer(): pl.pallas_call(functools.partial(project_kernel, spans, slot_total, resid...  4.88 us
    pallas_call x1, Pallas kernels, pairs_layer(): pl.pallas_call(functools.partial(attend_kernel, spans, masks, resident, s...  4.66 us
    unnamed x66, local copies, waits for them, and re-layouts  4.38 us
  transfers between devices with their start and end apart: 26, of which 9 were waited for; matrix products, arithmetic and copies ran while one was open for 6% of the time, Pallas kernels for 13%

profile of v7, /device:TPU:13, one launch (start us, length us, event | category | flops | bytes accessed | tf_op | source)
XLA Modules:
  0.0 106.0 jit_solution(308122323954631196)
XLA Ops:
  0.7 5.1 %shard_map.164 = (bf16[128,2,256]{2,1,0:T(2,128)(2,1)}, bf16[128,2,256]{2,1,0:T(2,128)(2,1)}, bf16[128,2,256]{2,1,0:T(2,128)(2,1)}, bf16[4,2,64,2048]{3,2,1,0:T(...) custom-call(s32[1]{0:T(128)} %bitcast.refs_0_, s32[2,4]{1,0:T(2,128)} %bitcast.31, ...), custom_call_target="tpu_custom_call" | custom-call | tf_op jit(solution)/shard_map/pallas_call | solution.py:403
  5.7 0.6 collective-permute-start.16
  6.3 0.1 collective-permute-start.17
  6.4 4.3 %collective-permute-done.17.refs_6_ = bf16[4,2,64,256]{3,2,1,0:T(8,128)(2,1)S(1)} collective-permute-done((bf16[4,2,64,256]{3,2,1,0:T(8,128)(2,1)}, bf16[4,2,64,256]{3,2,1,0:T(8,128)(2,1)S(1)}, u32[]{:S(2)}, u32[]{:S(2)}) %collective-permute-start.17) | collective-permute-done | bytes 262176 | tf_op jit(solution)/shard_map/ppermute | solution.py:212
  10.7 0.0 collective-permute-done.16.refs_5_.refs_3_
  10.7 0.7 copy-done.1
  11.4 0.7 copy-done
  12.0 3.9 %shard_map.165 = (bf16[4,2,64,256]{3,2,1,0:T(8,128)(2,1)}, bf16[2,64,2048]{2,1,0:T(8,128)(2,1)}, bf16[2,64,2048]{2,1,0:T(8,128)(2,1)}, bf16[1,64,2048]{2,1,0:T(8...) custom-call(s32[1]{0:T(128)} %bitcast.refs_0_, ...), custom_call_target="tpu_custom_call" | custom-call | tf_op jit(solution)/shard_map/pallas_call | solution.py:403
  15.9 1.5 %collective-permute-start.35 = (bf16[2,64,2048]{2,1,0:T(8,128)(2,1)}, bf16[2,64,2048]{2,1,0:T(8,128)(2,1)S(1)}, u32[]{:S(2)}, u32[]{:S(2)}) collective-permute-start(bf16[2,64,2048]{2,1,0:T(8,128)(2,1)} %get-tuple-element.140), channel_id=1, source_target_pairs={{0,8},{4,12},{8,0},{12,4},{1,9},{5,13},{9,1},{13,5},{2,10},{6,14},... | collective-permute-start | bytes 1572872 | tf_op jit(solution)/shard_map/ppermute | solution.py:212
  17.4 0.1 collective-permute-start.36
  17.5 2.2 %collective-permute-start.23 = (bf16[8,2048]{1,0:T(8,128)(2,1)S(1)}, bf16[8,2048]{1,0:T(8,128)(2,1)S(1)}, u32[]{:S(2)}, u32[]{:S(2)}) collective-permute-start(bf16[8,2048]{1,0:T(8,128)(2,1)S(1)} %copy-done.48), channel_id=1, source_target_pairs={{0,12},{4,8},{8,4},{12,0},{1,13},{5,9},{9,5},{13,1},{2,14},{6,10},... | collective-permute-start | bytes 98312 | tf_op jit(solution)/shard_map/ppermute | solution.py:212
  19.7 0.1 collective-permute-start.22
  19.8 0.3 collective-permute-start.21
  20.1 22.1 %collective-permute-done.23.refs_8_ = bf16[8,2048]{1,0:T(8,128)(2,1)S(1)} collective-permute-done((bf16[8,2048]{1,0:T(8,128)(2,1)S(1)}, bf16[8,2048]{1,0:T(8,128)(2,1)S(1)}, u32[]{:S(2)}, u32[]{:S(2)}) %collective-permute-start.23) | collective-permute-done | bytes 32800 | tf_op jit(solution)/shard_map/ppermute | solution.py:212
  42.1 0.2 collective-permute-start.20
  42.3 0.0 collective-permute-done.22.refs_7_
  42.3 2.3 %collective-permute-start.19 = (bf16[32,2048]{1,0:T(8,128)(2,1)S(1)}, bf16[32,2048]{1,0:T(8,128)(2,1)S(1)}, u32[]{:S(2)}, u32[]{:S(2)}) collective-permute-start(bf16[32,2048]{1,0:T(8,128)(2,1)S(1)} %copy-done.2), channel_id=1, source_target_pairs={{0,2},{1,3},{2,0},{3,1},{4,6},{5,7},{6,4},{7,5},{8,10},{9,11},{10,... | collective-permute-start | bytes 393224 | tf_op jit(solution)/shard_map/ppermute | solution.py:217
  44.6 0.0 collective-permute-done.21.refs_6_
  44.6 0.6 copy-done.34
  45.2 0.0 copy-start.44
  45.3 4.9 %project.1 = (f32[32,128]{1,0:T(8,128)}, f32[8,128]{1,0:T(8,128)}, f32[8,128]{1,0:T(8,128)}, f32[8,128]{1,0:T(8,128)}) custom-call(s32[1]{0:T(128)} %bitcast.refs_0_, s32[48]{0:T(128)} %refs_4_.5, s32[2,4]{1,0:T(2,128)} %bitcast.35, s32[16]{0:T(128)S(1)} %copy-done.31, s32[1,16]{1,0:T(1,128)S(1)} %bitcast.24, ...), custom_call_target="tpu_custom_call" | custom-call | tf_op jit(solution)/shard_map/project/pallas_call | solution.py:702
  50.1 1.2 %collective-permute-start.24 = (f32[8,128]{1,0:T(8,128)}, f32[8,128]{1,0:T(8,128)S(1)}, u32[]{:S(2)}, u32[]{:S(2)}) collective-permute-start(f32[8,128]{1,0:T(8,128)} %get-tuple-element.125), channel_id=1, source_target_pairs={{0,4},{4,0},{8,12},{12,8},{1,5},{5,1},{9,13},{13,9},{2,6},{6,2},{1... | collective-permute-start | bytes 12296 | tf_op jit(solution)/shard_map/ppermute | solution.py:212
  51.4 1.0 collective-permute-done.24.refs_5_
  52.4 1.4 %collective-permute-start.25 = (f32[8,128]{1,0:T(8,128)}, f32[8,128]{1,0:T(8,128)S(1)}, u32[]{:S(2)}, u32[]{:S(2)}) collective-permute-start(f32[8,128]{1,0:T(8,128)} %get-tuple-element.126), channel_id=1, source_target_pairs={{0,8},{4,12},{8,0},{12,4},{1,9},{5,13},{9,1},{13,5},{2,10},{6,14},... | collective-permute-start | bytes 12296 | tf_op jit(solution)/shard_map/ppermute | solution.py:212
  53.8 1.3 %collective-permute-done.25.refs_6_ = f32[8,128]{1,0:T(8,128)S(1)} collective-permute-done((f32[8,128]{1,0:T(8,128)}, f32[8,128]{1,0:T(8,128)S(1)}, u32[]{:S(2)}, u32[]{:S(2)}) %collective-permute-start.25) | collective-permute-done | bytes 4128 | tf_op jit(solution)/shard_map/ppermute | solution.py:212
  55.1 2.8 %collective-permute-start.26 = (f32[8,128]{1,0:T(8,128)}, f32[8,128]{1,0:T(8,128)S(1)}, u32[]{:S(2)}, u32[]{:S(2)}) collective-permute-start(f32[8,128]{1,0:T(8,128)} %get-tuple-element.127), channel_id=1, source_target_pairs={{0,12},{4,8},{8,4},{12,0},{1,13},{5,9},{9,5},{13,1},{2,14},{6,10},... | collective-permute-start | bytes 12296 | tf_op jit(solution)/shard_map/ppermute | solution.py:212
  57.8 1.6 %collective-permute-done.26.refs_7_ = f32[8,128]{1,0:T(8,128)S(1)} collective-permute-done((f32[8,128]{1,0:T(8,128)}, f32[8,128]{1,0:T(8,128)S(1)}, u32[]{:S(2)}, u32[]{:S(2)}) %collective-permute-start.26) | collective-permute-done | bytes 4128 | tf_op jit(solution)/shard_map/ppermute | solution.py:212
  59.4 1.2 %collective-permute-start.18 = (bf16[32,2048]{1,0:T(8,128)(2,1)S(1)}, bf16[32,2048]{1,0:T(8,128)(2,1)S(1)}, u32[]{:S(2)}, u32[]{:S(2)}) collective-permute-start(bf16[32,2048]{1,0:T(8,128)(2,1)S(1)} %copy-done.3), channel_id=1, source_target_pairs={{0,1},{1,2},{2,3},{3,0},{4,5},{5,6},{6,7},{7,4},{8,9},{9,10},{10,1... | collective-permute-start | bytes 393224 | tf_op jit(solution)/shard_map/ppermute | solution.py:217
  60.6 1.1 %collective-permute-start.30 = (bf16[128,2,256]{2,1,0:T(2,128)(2,1)S(1)}, bf16[128,2,256]{2,1,0:T(2,128)(2,1)S(1)}, u32[]{:S(2)}, u32[]{:S(2)}) collective-permute-start(bf16[128,2,256]{2,1,0:T(2,128)(2,1)S(1)} %copy-done.47), channel_id=1, source_target_pairs={{0,4},{4,0},{8,12},{12,8},{1,5},{5,1},{9,13},{13,9},{2,6},{6,2},{1... | collective-permute-start | bytes 393224 | tf_op jit(solution)/shard_map/ppermute | solution.py:212
  61.6 0.0 collective-permute-done.19.refs_2_
  61.7 1.2 %collective-permute-start.31 = (bf16[128,2,256]{2,1,0:T(2,128)(2,1)S(1)}, bf16[128,2,256]{2,1,0:T(2,128)(2,1)S(1)}, u32[]{:S(2)}, u32[]{:S(2)}) collective-permute-start(bf16[128,2,256]{2,1,0:T(2,128)(2,1)S(1)} %copy-done.46), channel_id=1, source_target_pairs={{0,8},{4,12},{8,0},{12,4},{1,9},{5,13},{9,1},{13,5},{2,10},{6,14},... | collective-permute-start | bytes 393224 | tf_op jit(solution)/shard_map/ppermute | solution.py:212
  62.8 1.2 %collective-permute-done.18.refs_1_ = bf16[32,2048]{1,0:T(8,128)(2,1)S(1)} collective-permute-done((bf16[32,2048]{1,0:T(8,128)(2,1)S(1)}, bf16[32,2048]{1,0:T(8,128)(2,1)S(1)}, u32[]{:S(2)}, u32[]{:S(2)}) %collective-permute-start.18) | collective-permute-done | bytes 131104 | tf_op jit(solution)/shard_map/ppermute | solution.py:217
  64.1 2.0 %collective-permute-start.32 = (bf16[128,2,256]{2,1,0:T(2,128)(2,1)S(1)}, bf16[128,2,256]{2,1,0:T(2,128)(2,1)S(1)}, u32[]{:S(2)}, u32[]{:S(2)}) collective-permute-start(bf16[128,2,256]{2,1,0:T(2,128)(2,1)S(1)} %copy-done.45), channel_id=1, source_target_pairs={{0,12},{4,8},{8,4},{12,0},{1,13},{5,9},{9,5},{13,1},{2,14},{6,10},... | collective-permute-start | bytes 393224 | tf_op jit(solution)/shard_map/ppermute | solution.py:212
  66.1 2.0 %gather.1 = (bf16[32,8192]{1,0:T(8,128)(2,1)}, f32[32,128]{1,0:T(8,128)}) custom-call(s32[1]{0:T(128)} %bitcast.5.shard_ref, bf16[32,2048]{1,0:T(8,128)(2,1)} %get-tuple-element.122.refs_5_.refs_0_, bf16[32,2048]{1,0:T(8,128)(2,1)} %copy-done.30, bf16[32,2048]{1,0:T(8,128)(2,1)} %copy-done.29, bf16[32,2048]{1,0:T(8,128)(2,1)} %copy-done.28, ...), custom_call_target="tpu_custom_call" | custom-call | tf_op jit(solution)/shard_map/gather/pallas_call | solution.py:745
  68.0 0.0 collective-permute-done.30.refs_12_
  68.1 2.0 %collective-permute-start.29 = (f32[32,128]{1,0:T(8,128)}, f32[32,128]{1,0:T(8,128)S(1)}, u32[]{:S(2)}, u32[]{:S(2)}) collective-permute-start(f32[32,128]{1,0:T(8,128)} %get-tuple-element.128.refs_8_), channel_id=1, source_target_pairs={{0,3},{1,0},{2,1},{3,2},{4,7},{5,4},{6,5},{7,6},{8,11},{9,8},{10,9... | collective-permute-start | bytes 49160 | tf_op jit(solution)/shard_map/ppermute | solution.py:217
  70.1 0.4 collective-permute-start.28
  70.5 0.0 collective-permute-done.32.refs_14_
  70.5 0.8 collective-permute-start.27
  71.4 0.0 collective-permute-done.29.refs_11_
  71.4 0.7 collective-permute-start.33
  72.0 1.7 %collective-permute-done.28.refs_10_ = f32[32,128]{1,0:T(8,128)S(1)} collective-permute-done((f32[32,128]{1,0:T(8,128)}, f32[32,128]{1,0:T(8,128)S(1)}, u32[]{:S(2)}, u32[]{:S(2)}) %collective-permute-start.28) | collective-permute-done | bytes 16416 | tf_op jit(solution)/shard_map/ppermute | solution.py:217
  73.8 0.6 collective-permute-start.34
  74.4 0.0 collective-permute-done.35.refs_4_
  74.4 1.8 %collective-permute-start.37 = (bf16[2,64,2048]{2,1,0:T(8,128)(2,1)S(1)}, bf16[2,64,2048]{2,1,0:T(8,128)(2,1)S(1)}, u32[]{:S(2)}, u32[]{:S(2)}) collective-permute-start(bf16[2,64,2048]{2,1,0:T(8,128)(2,1)S(1)} %collective-permute-done.35.refs_4_), channel_id=1, source_target_pairs={{0,4},{4,0},{8,12},{12,8},{1,5},{5,1},{9,13},{13,9},{2,6},{6,2},{1... | collective-permute-start | bytes 1572872 | tf_op jit(solution)/shard_map/ppermute | solution.py:212
  76.2 0.0 collective-permute-done.36.refs_5_
  76.2 0.1 collective-permute-start.38
  76.3 5.8 %fusion.2.refs_18_ = f32[2,32,256]{2,1,0:T(8,128)} fusion(bf16[8192,2,256]{2,1,0:T(2,128)(2,1)} %param.20, bf16[32,8192]{1,0:T(8,128)(2,1)} %get-tuple-element.133), kind=kOutput, calls=%fused_computation.2 | convolution fusion | flops 268435456 | bytes 8978432 | tf_op jit(solution)/shard_map/md,dgc->gmc/dot_general | solution.py:756
  82.8 0.0 collective-permute-done.33
  82.8 0.0 copy-start.8
  82.9 0.6 copy-done.38
  83.4 0.1 copy-done.8
  83.5 4.7 %attend.1 = (bf16[14,2,2048]{2,1,0:T(2,128)(2,1)}, bf16[14,2,2,256]{3,2,1,0:T(2,128)(2,1)}, bf16[2,128,2,256]{3,2,1,0:T(2,128)(2,1)}, bf16[4,128,256]{2,1,0:T(8,128)(2,1)}) custom-call(s32[1]{0:T(128)} %bitcast.refs_0_, s32[48]{0:T(128)} %refs_1_.6, s32[2,4]{1,0:T(2,128)} %bitcast.32, s32[2,4]{1,0:T(2,128)} %bitcast.34, s32[48]{0:T(128)} %refs_4_.5, ...), custom_call_target="tpu_custom_call" | custom-call | tf_op jit(solution)/shard_map/attend/pallas_call | solution.py:758
  88.3 0.8 copy-done.6
  89.1 0.8 copy-done.7
  89.9 2.8 %shard_map.166 = bf16[4,2,64,2048]{3,2,1,0:T(8,128)(2,1)} custom-call(s32[1]{0:T(128)} %bitcast.refs_0_, s32[16]{0:T(128)S(1)} %copy-done.31, s32[1,16]{1,0:T(1,128)S(1)} %bitcast.26, bf16[4,2,64,2048]{3,2,1,0:T(8,128)(2,1)} %copy-done, bf16[2,64,2048]{2,1,0:T(8,128)(2,1)} %copy-done.4, bf16[2,64,2048]{2,1,0:T(8,128)(2,1)} %copy-done.5, ...), custom_call_target="tpu_custom_call" | custom-call | tf_op jit(solution)/shard_map/pallas_call | solution.py:403
  92.7 13.3 %conditional.1 = (bf16[4,2,64,2048]{3,2,1,0:T(8,128)(2,1)}) conditional(s32[]{:T(128)} %bitcast.13, (bf16[1,64,2048]{2,1,0:T(8,128)(2,1)S(1)}, s32[1]{0:T(128)}, s32[16]{0:T(128)S(1)}, s32[1,16]{1,0:T(1,128)S(1)}, bf16[4,2,64,2048]{3,2,1,0:T(8,128)(2,1)}) %tuple.35, (bf16[1,64,2048]{2,1,0:T(8,128)(2,1)S(1)}, ...), branch_computations={%region_0.0_spmd, %region_1.0_spmd, %region_2.0_spmd, %region_3.0_... | conditional | bytes 14680548 | solution.py:825
  92.7 0.6 collective-permute-start.1
  93.3 0.9 collective-permute-start.2
  94.3 6.0 %collective-permute-done.1.refs_5_ = bf16[1,64,2048]{2,1,0:T(8,128)(2,1)S(1)} collective-permute-done((bf16[1,64,2048]{2,1,0:T(8,128)(2,1)S(1)}, bf16[1,64,2048]{2,1,0:T(8,128)(2,1)S(1)}, u32[]{:S(2)}, u32[]{:S(2)}) %collective-permute-start.1) | collective-permute-done | bytes 262176 | tf_op jit(solution)/shard_map/cond/branch_1_fun/ppermute | solution.py:212
  100.3 1.2 %collective-permute-start.3 = (bf16[1,64,2048]{2,1,0:T(8,128)(2,1)S(1)}, bf16[1,64,2048]{2,1,0:T(8,128)(2,1)S(1)}, u32[]{:S(2)}, u32[]{:S(2)}) collective-permute-start(bf16[1,64,2048]{2,1,0:T(8,128)(2,1)S(1)} %collective-permute-done.1.refs_5_), channel_id=1, source_target_pairs={{0,4},{4,0},{8,12},{12,8},{1,5},{5,1},{9,13},{13,9},{2,6},{6,2},{1... | collective-permute-start | bytes 786440 | tf_op jit(solution)/shard_map/cond/branch_1_fun/ppermute | solution.py:212
  101.5 1.2 %collective-permute-done.3.refs_7_ = bf16[1,64,2048]{2,1,0:T(8,128)(2,1)S(1)} collective-permute-done((bf16[1,64,2048]{2,1,0:T(8,128)(2,1)S(1)}, bf16[1,64,2048]{2,1,0:T(8,128)(2,1)S(1)}, u32[]{:S(2)}, u32[]{:S(2)}) %collective-permute-start.3) | collective-permute-done | bytes 262176 | tf_op jit(solution)/shard_map/cond/branch_1_fun/ppermute | solution.py:212
  102.7 0.7 copy-done.23
  103.4 2.5 %branch_1_fun.1 = bf16[4,2,64,2048]{3,2,1,0:T(8,128)(2,1)} custom-call(s32[1]{0:T(128)} %get-tuple-element.62.refs_0_, s32[16]{0:T(128)S(1)} %get-tuple-element.63.refs_1_, s32[1,16]{1,0:T(1,128)S(1)} %get-tuple-element.64.refs_2_, bf16[4,2,64,2048]{3,2,1,0:T(8,128)(2,1)} %get-tuple-element.65.refs_3_, ...), custom_call_target="tpu_custom_call", output_to_operand_aliasing={{}: (3, {})} | custom-call | tf_op jit(solution)/shard_map/cond/branch_1_fun/pallas_call | solution.py:403
  (69 shorter events, 0.1 us)
Async XLA Ops:
  0.6 11.4 %copy-start.31 = (s32[16]{0:T(128)S(1)}, s32[16]{0:T(128)}, u32[]{:S(2)}) copy-start(s32[16]{0:T(128)} %refs_1_.7) | copy-start | bytes 196
  0.6 11.4 %copy-start.35 = (s32[16,1]{0,1:T(1,128)S(1)}, s32[16,1]{0,1:T(1,128)}, u32[]{:S(2)}) copy-start(s32[16,1]{0,1:T(1,128)} %param.29) | copy-start | bytes 196
  5.7 4.9 %collective-permute-start.16 = (bf16[4,2,64,2048]{3,2,1,0:T(8,128)(2,1)}, bf16[4,2,64,2048]{3,2,1,0:T(8,128)(2,1)S(1)}, u32[]{:S(2)}, u32[]{:S(2)}) collective-permute-start(bf16[4,2,64,2048]{3,2,1,0:T(8,128)(2,1)} %get-tuple-element.117), channel_id=1, source_target_pairs={{0,4},{4,0},{8,12},{12,8},{1,5},{5,1},{9,13},{13,9},{2,6},{6,2},{1... | collective-permute-start | bytes 6291464 | tf_op jit(solution)/shard_map/ppermute | solution.py:212
  6.3 4.4 %collective-permute-start.17 = (bf16[4,2,64,256]{3,2,1,0:T(8,128)(2,1)}, bf16[4,2,64,256]{3,2,1,0:T(8,128)(2,1)S(1)}, u32[]{:S(2)}, u32[]{:S(2)}) collective-permute-start(bf16[4,2,64,256]{3,2,1,0:T(8,128)(2,1)} %get-tuple-element.118), channel_id=1, source_target_pairs={{0,4},{4,0},{8,12},{12,8},{1,5},{5,1},{9,13},{13,9},{2,6},{6,2},{1... | collective-permute-start | bytes 786440 | tf_op jit(solution)/shard_map/ppermute | solution.py:212
  10.7 0.7 copy-start.1
  10.7 1.4 %copy-start = (bf16[4,2,64,2048]{3,2,1,0:T(8,128)(2,1)}, bf16[4,2,64,2048]{3,2,1,0:T(8,128)(2,1)S(1)}, u32[]{:S(2)}) copy-start(bf16[4,2,64,2048]{3,2,1,0:T(8,128)(2,1)S(1)} %collective-permute-done.16.refs_5_.refs_3_) | copy-start | bytes 6291460
  12.0 5.4 %copy-start.48 = (bf16[8,2048]{1,0:T(8,128)(2,1)S(1)}, bf16[8,2048]{1,0:T(8,128)(2,1)}, u32[]{:S(2)}) copy-start(bf16[8,2048]{1,0:T(8,128)(2,1)} %get-tuple-element.123) | copy-start | bytes 98308
  12.0 30.1 %copy-start.2 = (bf16[32,2048]{1,0:T(8,128)(2,1)S(1)}, bf16[32,2048]{1,0:T(8,128)(2,1)}, u32[]{:S(2)}) copy-start(bf16[32,2048]{1,0:T(8,128)(2,1)} %get-tuple-element.122.refs_5_.refs_0_) | copy-start | bytes 393220
  15.9 58.5 %collective-permute-start.35 = (bf16[2,64,2048]{2,1,0:T(8,128)(2,1)}, bf16[2,64,2048]{2,1,0:T(8,128)(2,1)S(1)}, u32[]{:S(2)}, u32[]{:S(2)}) collective-permute-start(bf16[2,64,2048]{2,1,0:T(8,128)(2,1)} %get-tuple-element.140), channel_id=1, source_target_pairs={{0,8},{4,12},{8,0},{12,4},{1,9},{5,13},{9,1},{13,5},{2,10},{6,14},... | collective-permute-start | bytes 1572872 | tf_op jit(solution)/shard_map/ppermute | solution.py:212
  17.4 58.8 %collective-permute-start.36 = (bf16[2,64,2048]{2,1,0:T(8,128)(2,1)}, bf16[2,64,2048]{2,1,0:T(8,128)(2,1)S(1)}, u32[]{:S(2)}, u32[]{:S(2)}) collective-permute-start(bf16[2,64,2048]{2,1,0:T(8,128)(2,1)} %get-tuple-element.141), channel_id=1, source_target_pairs={{0,8},{4,12},{8,0},{12,4},{1,9},{5,13},{9,1},{13,5},{2,10},{6,14},... | collective-permute-start | bytes 1572872 | tf_op jit(solution)/shard_map/ppermute | solution.py:212
  17.5 24.7 %collective-permute-start.23 = (bf16[8,2048]{1,0:T(8,128)(2,1)S(1)}, bf16[8,2048]{1,0:T(8,128)(2,1)S(1)}, u32[]{:S(2)}, u32[]{:S(2)}) collective-permute-start(bf16[8,2048]{1,0:T(8,128)(2,1)S(1)} %copy-done.48), channel_id=1, source_target_pairs={{0,12},{4,8},{8,4},{12,0},{1,13},{5,9},{9,5},{13,1},{2,14},{6,10},... | collective-permute-start | bytes 98312 | tf_op jit(solution)/shard_map/ppermute | solution.py:212
  19.7 22.6 %collective-permute-start.22 = (bf16[8,2048]{1,0:T(8,128)(2,1)S(1)}, bf16[8,2048]{1,0:T(8,128)(2,1)S(1)}, u32[]{:S(2)}, u32[]{:S(2)}) collective-permute-start(bf16[8,2048]{1,0:T(8,128)(2,1)S(1)} %copy-done.48), channel_id=1, source_target_pairs={{0,8},{4,12},{8,0},{12,4},{1,9},{5,13},{9,1},{13,5},{2,10},{6,14},... | collective-permute-start | bytes 98312 | tf_op jit(solution)/shard_map/ppermute | solution.py:212
  19.8 24.9 %collective-permute-start.21 = (bf16[8,2048]{1,0:T(8,128)(2,1)S(1)}, bf16[8,2048]{1,0:T(8,128)(2,1)S(1)}, u32[]{:S(2)}, u32[]{:S(2)}) collective-permute-start(bf16[8,2048]{1,0:T(8,128)(2,1)S(1)} %copy-done.48), channel_id=1, source_target_pairs={{0,4},{4,0},{8,12},{12,8},{1,5},{5,1},{9,13},{13,9},{2,6},{6,2},{1... | collective-permute-start | bytes 98312 | tf_op jit(solution)/shard_map/ppermute | solution.py:212
  42.1 2.5 %copy-start.32 = (bf16[8,2048]{1,0:T(8,128)(2,1)}, bf16[8,2048]{1,0:T(8,128)(2,1)S(1)}, u32[]{:S(2)}) copy-start(bf16[8,2048]{1,0:T(8,128)(2,1)S(1)} %collective-permute-done.23.refs_8_) | copy-start | bytes 98308
  42.1 18.4 %collective-permute-start.20 = (bf16[32,2048]{1,0:T(8,128)(2,1)S(1)}, bf16[32,2048]{1,0:T(8,128)(2,1)S(1)}, u32[]{:S(2)}, u32[]{:S(2)}) collective-permute-start(bf16[32,2048]{1,0:T(8,128)(2,1)S(1)} %copy-done.2), channel_id=1, source_target_pairs={{0,3},{1,0},{2,1},{3,2},{4,7},{5,4},{6,5},{7,6},{8,11},{9,8},{10,9... | collective-permute-start | bytes 393224 | tf_op jit(solution)/shard_map/ppermute | solution.py:217
  42.3 2.3 %copy-start.33 = (bf16[8,2048]{1,0:T(8,128)(2,1)}, bf16[8,2048]{1,0:T(8,128)(2,1)S(1)}, u32[]{:S(2)}) copy-start(bf16[8,2048]{1,0:T(8,128)(2,1)S(1)} %collective-permute-done.22.refs_7_) | copy-start | bytes 98308
  42.3 19.3 %collective-permute-start.19 = (bf16[32,2048]{1,0:T(8,128)(2,1)S(1)}, bf16[32,2048]{1,0:T(8,128)(2,1)S(1)}, u32[]{:S(2)}, u32[]{:S(2)}) collective-permute-start(bf16[32,2048]{1,0:T(8,128)(2,1)S(1)} %copy-done.2), channel_id=1, source_target_pairs={{0,2},{1,3},{2,0},{3,1},{4,6},{5,7},{6,4},{7,5},{8,10},{9,11},{10,... | collective-permute-start | bytes 393224 | tf_op jit(solution)/shard_map/ppermute | solution.py:217
  44.6 0.6 copy-start.34
  45.2 14.2 %copy-start.3 = (bf16[32,2048]{1,0:T(8,128)(2,1)S(1)}, bf16[32,2048]{1,0:T(8,128)(2,1)}, u32[]{:S(2)}) copy-start(bf16[32,2048]{1,0:T(8,128)(2,1)} %get-tuple-element.122.refs_5_.refs_0_) | copy-start | bytes 393220
  45.2 15.3 %copy-start.47 = (bf16[128,2,256]{2,1,0:T(2,128)(2,1)S(1)}, bf16[128,2,256]{2,1,0:T(2,128)(2,1)}, u32[]{:S(2)}) copy-start(bf16[128,2,256]{2,1,0:T(2,128)(2,1)} %get-tuple-element.129) | copy-start | bytes 393220
  45.2 16.4 %copy-start.46 = (bf16[128,2,256]{2,1,0:T(2,128)(2,1)S(1)}, bf16[128,2,256]{2,1,0:T(2,128)(2,1)}, u32[]{:S(2)}) copy-start(bf16[128,2,256]{2,1,0:T(2,128)(2,1)} %get-tuple-element.130) | copy-start | bytes 393220
  45.2 18.8 %copy-start.45 = (bf16[128,2,256]{2,1,0:T(2,128)(2,1)S(1)}, bf16[128,2,256]{2,1,0:T(2,128)(2,1)}, u32[]{:S(2)}) copy-start(bf16[128,2,256]{2,1,0:T(2,128)(2,1)} %get-tuple-element.131) | copy-start | bytes 393220
  45.2 26.1 %copy-start.44 = (bf16[4,2,64,256]{3,2,1,0:T(8,128)(2,1)S(1)}, bf16[4,2,64,256]{3,2,1,0:T(8,128)(2,1)}, u32[]{:S(2)}) copy-start(bf16[4,2,64,256]{3,2,1,0:T(8,128)(2,1)} %get-tuple-element.132) | copy-start | bytes 786436
  50.1 2.2 %collective-permute-start.24 = (f32[8,128]{1,0:T(8,128)}, f32[8,128]{1,0:T(8,128)S(1)}, u32[]{:S(2)}, u32[]{:S(2)}) collective-permute-start(f32[8,128]{1,0:T(8,128)} %get-tuple-element.125), channel_id=1, source_target_pairs={{0,4},{4,0},{8,12},{12,8},{1,5},{5,1},{9,13},{13,9},{2,6},{6,2},{1... | collective-permute-start | bytes 12296 | tf_op jit(solution)/shard_map/ppermute | solution.py:212
  52.4 13.7 %copy-start.39 = (f32[8,128]{1,0:T(8,128)}, f32[8,128]{1,0:T(8,128)S(1)}, u32[]{:S(2)}) copy-start(f32[8,128]{1,0:T(8,128)S(1)} %collective-permute-done.24.refs_5_) | copy-start | bytes 12292
  52.4 2.7 %collective-permute-start.25 = (f32[8,128]{1,0:T(8,128)}, f32[8,128]{1,0:T(8,128)S(1)}, u32[]{:S(2)}, u32[]{:S(2)}) collective-permute-start(f32[8,128]{1,0:T(8,128)} %get-tuple-element.126), channel_id=1, source_target_pairs={{0,8},{4,12},{8,0},{12,4},{1,9},{5,13},{9,1},{13,5},{2,10},{6,14},... | collective-permute-start | bytes 12296 | tf_op jit(solution)/shard_map/ppermute | solution.py:212
  55.1 11.0 %copy-start.40 = (f32[8,128]{1,0:T(8,128)}, f32[8,128]{1,0:T(8,128)S(1)}, u32[]{:S(2)}) copy-start(f32[8,128]{1,0:T(8,128)S(1)} %collective-permute-done.25.refs_6_) | copy-start | bytes 12292
  55.1 4.3 %collective-permute-start.26 = (f32[8,128]{1,0:T(8,128)}, f32[8,128]{1,0:T(8,128)S(1)}, u32[]{:S(2)}, u32[]{:S(2)}) collective-permute-start(f32[8,128]{1,0:T(8,128)} %get-tuple-element.127), channel_id=1, source_target_pairs={{0,12},{4,8},{8,4},{12,0},{1,13},{5,9},{9,5},{13,1},{2,14},{6,10},... | collective-permute-start | bytes 12296 | tf_op jit(solution)/shard_map/ppermute | solution.py:212
  59.4 6.7 %copy-start.41 = (f32[8,128]{1,0:T(8,128)}, f32[8,128]{1,0:T(8,128)S(1)}, u32[]{:S(2)}) copy-start(f32[8,128]{1,0:T(8,128)S(1)} %collective-permute-done.26.refs_7_) | copy-start | bytes 12292
  59.4 4.7 %collective-permute-start.18 = (bf16[32,2048]{1,0:T(8,128)(2,1)S(1)}, bf16[32,2048]{1,0:T(8,128)(2,1)S(1)}, u32[]{:S(2)}, u32[]{:S(2)}) collective-permute-start(bf16[32,2048]{1,0:T(8,128)(2,1)S(1)} %copy-done.3), channel_id=1, source_target_pairs={{0,1},{1,2},{2,3},{3,0},{4,5},{5,6},{6,7},{7,4},{8,9},{9,10},{10,1... | collective-permute-start | bytes 393224 | tf_op jit(solution)/shard_map/ppermute | solution.py:217
  60.6 5.5 %copy-start.28 = (bf16[32,2048]{1,0:T(8,128)(2,1)}, bf16[32,2048]{1,0:T(8,128)(2,1)S(1)}, u32[]{:S(2)}) copy-start(bf16[32,2048]{1,0:T(8,128)(2,1)S(1)} %collective-permute-done.20.refs_3_) | copy-start | bytes 393220
  60.6 7.5 %collective-permute-start.30 = (bf16[128,2,256]{2,1,0:T(2,128)(2,1)S(1)}, bf16[128,2,256]{2,1,0:T(2,128)(2,1)S(1)}, u32[]{:S(2)}, u32[]{:S(2)}) collective-permute-start(bf16[128,2,256]{2,1,0:T(2,128)(2,1)S(1)} %copy-done.47), channel_id=1, source_target_pairs={{0,4},{4,0},{8,12},{12,8},{1,5},{5,1},{9,13},{13,9},{2,6},{6,2},{1... | collective-permute-start | bytes 393224 | tf_op jit(solution)/shard_map/ppermute | solution.py:212
  61.7 4.4 %copy-start.29 = (bf16[32,2048]{1,0:T(8,128)(2,1)}, bf16[32,2048]{1,0:T(8,128)(2,1)S(1)}, u32[]{:S(2)}) copy-start(bf16[32,2048]{1,0:T(8,128)(2,1)S(1)} %collective-permute-done.19.refs_2_) | copy-start | bytes 393220
  61.7 8.4 %collective-permute-start.31 = (bf16[128,2,256]{2,1,0:T(2,128)(2,1)S(1)}, bf16[128,2,256]{2,1,0:T(2,128)(2,1)S(1)}, u32[]{:S(2)}, u32[]{:S(2)}) collective-permute-start(bf16[128,2,256]{2,1,0:T(2,128)(2,1)S(1)} %copy-done.46), channel_id=1, source_target_pairs={{0,8},{4,12},{8,0},{12,4},{1,9},{5,13},{9,1},{13,5},{2,10},{6,14},... | collective-permute-start | bytes 393224 | tf_op jit(solution)/shard_map/ppermute | solution.py:212
  64.1 2.0 %copy-start.30 = (bf16[32,2048]{1,0:T(8,128)(2,1)}, bf16[32,2048]{1,0:T(8,128)(2,1)S(1)}, u32[]{:S(2)}) copy-start(bf16[32,2048]{1,0:T(8,128)(2,1)S(1)} %collective-permute-done.18.refs_1_) | copy-start | bytes 393220
  64.1 6.5 %collective-permute-start.32 = (bf16[128,2,256]{2,1,0:T(2,128)(2,1)S(1)}, bf16[128,2,256]{2,1,0:T(2,128)(2,1)S(1)}, u32[]{:S(2)}, u32[]{:S(2)}) collective-permute-start(bf16[128,2,256]{2,1,0:T(2,128)(2,1)S(1)} %copy-done.45), channel_id=1, source_target_pairs={{0,12},{4,8},{8,4},{12,0},{1,13},{5,9},{9,5},{13,1},{2,14},{6,10},... | collective-permute-start | bytes 393224 | tf_op jit(solution)/shard_map/ppermute | solution.py:212
  68.1 14.1 %copy-start.25 = (bf16[128,2,256]{2,1,0:T(2,128)(2,1)}, bf16[128,2,256]{2,1,0:T(2,128)(2,1)S(1)}, u32[]{:S(2)}) copy-start(bf16[128,2,256]{2,1,0:T(2,128)(2,1)S(1)} %collective-permute-done.30.refs_12_) | copy-start | bytes 393220
  68.1 3.3 %collective-permute-start.29 = (f32[32,128]{1,0:T(8,128)}, f32[32,128]{1,0:T(8,128)S(1)}, u32[]{:S(2)}, u32[]{:S(2)}) collective-permute-start(f32[32,128]{1,0:T(8,128)} %get-tuple-element.128.refs_8_), channel_id=1, source_target_pairs={{0,3},{1,0},{2,1},{3,2},{4,7},{5,4},{6,5},{7,6},{8,11},{9,8},{10,9... | collective-permute-start | bytes 49160 | tf_op jit(solution)/shard_map/ppermute | solution.py:217
  70.1 12.1 %copy-start.26 = (bf16[128,2,256]{2,1,0:T(2,128)(2,1)}, bf16[128,2,256]{2,1,0:T(2,128)(2,1)S(1)}, u32[]{:S(2)}) copy-start(bf16[128,2,256]{2,1,0:T(2,128)(2,1)S(1)} %collective-permute-done.31.refs_13_) | copy-start | bytes 393220
  70.1 3.7 %collective-permute-start.28 = (f32[32,128]{1,0:T(8,128)}, f32[32,128]{1,0:T(8,128)S(1)}, u32[]{:S(2)}, u32[]{:S(2)}) collective-permute-start(f32[32,128]{1,0:T(8,128)} %get-tuple-element.128.refs_8_), channel_id=1, source_target_pairs={{0,2},{1,3},{2,0},{3,1},{4,6},{5,7},{6,4},{7,5},{8,10},{9,11},{10,... | collective-permute-start | bytes 49160 | tf_op jit(solution)/shard_map/ppermute | solution.py:217
  70.5 11.6 %copy-start.27 = (bf16[128,2,256]{2,1,0:T(2,128)(2,1)}, bf16[128,2,256]{2,1,0:T(2,128)(2,1)S(1)}, u32[]{:S(2)}) copy-start(bf16[128,2,256]{2,1,0:T(2,128)(2,1)S(1)} %collective-permute-done.32.refs_14_) | copy-start | bytes 393220
  70.5 12.3 %collective-permute-start.27 = (f32[32,128]{1,0:T(8,128)}, f32[32,128]{1,0:T(8,128)S(1)}, u32[]{:S(2)}, u32[]{:S(2)}) collective-permute-start(f32[32,128]{1,0:T(8,128)} %get-tuple-element.128.refs_8_), channel_id=1, source_target_pairs={{0,1},{1,2},{2,3},{3,0},{4,5},{5,6},{6,7},{7,4},{8,9},{9,10},{10,1... | collective-permute-start | bytes 49160 | tf_op jit(solution)/shard_map/ppermute | solution.py:217
  71.4 10.8 %copy-start.36 = (f32[32,128]{1,0:T(8,128)}, f32[32,128]{1,0:T(8,128)S(1)}, u32[]{:S(2)}) copy-start(f32[32,128]{1,0:T(8,128)S(1)} %collective-permute-done.29.refs_11_) | copy-start | bytes 49156
  71.4 11.4 %collective-permute-start.33 = (bf16[4,2,64,256]{3,2,1,0:T(8,128)(2,1)S(1)}, bf16[4,2,64,256]{3,2,1,0:T(8,128)(2,1)S(1)}, u32[]{:S(2)}, u32[]{:S(2)}) collective-permute-start(bf16[4,2,64,256]{3,2,1,0:T(8,128)(2,1)S(1)} %copy-done.44), channel_id=1, source_target_pairs={{0,8},{4,12},{8,0},{12,4},{1,9},{5,13},{9,1},{13,5},{2,10},{6,14},... | collective-permute-start | bytes 786440 | tf_op jit(solution)/shard_map/ppermute | solution.py:212
  73.8 8.4 %copy-start.37 = (f32[32,128]{1,0:T(8,128)}, f32[32,128]{1,0:T(8,128)S(1)}, u32[]{:S(2)}) copy-start(f32[32,128]{1,0:T(8,128)S(1)} %collective-permute-done.28.refs_10_) | copy-start | bytes 49156
  73.8 18.9 %collective-permute-start.34 = (bf16[1,64,2048]{2,1,0:T(8,128)(2,1)}, bf16[1,64,2048]{2,1,0:T(8,128)(2,1)S(1)}, u32[]{:S(2)}, u32[]{:S(2)}) collective-permute-start(bf16[1,64,2048]{2,1,0:T(8,128)(2,1)} %get-tuple-element.139), channel_id=1, source_target_pairs={{0,8},{4,12},{8,0},{12,4},{1,9},{5,13},{9,1},{13,5},{2,10},{6,14},... | collective-permute-start | bytes 786440 | tf_op jit(solution)/shard_map/ppermute | solution.py:212
  74.4 7.8 %copy-start.4 = (bf16[2,64,2048]{2,1,0:T(8,128)(2,1)}, bf16[2,64,2048]{2,1,0:T(8,128)(2,1)S(1)}, u32[]{:S(2)}) copy-start(bf16[2,64,2048]{2,1,0:T(8,128)(2,1)S(1)} %collective-permute-done.35.refs_4_) | copy-start | bytes 1572868
  74.4 13.8 %collective-permute-start.37 = (bf16[2,64,2048]{2,1,0:T(8,128)(2,1)S(1)}, bf16[2,64,2048]{2,1,0:T(8,128)(2,1)S(1)}, u32[]{:S(2)}, u32[]{:S(2)}) collective-permute-start(bf16[2,64,2048]{2,1,0:T(8,128)(2,1)S(1)} %collective-permute-done.35.refs_4_), channel_id=1, source_target_pairs={{0,4},{4,0},{8,12},{12,8},{1,5},{5,1},{9,13},{13,9},{2,6},{6,2},{1... | collective-permute-start | bytes 1572872 | tf_op jit(solution)/shard_map/ppermute | solution.py:212
  76.2 6.0 %copy-start.5 = (bf16[2,64,2048]{2,1,0:T(8,128)(2,1)}, bf16[2,64,2048]{2,1,0:T(8,128)(2,1)S(1)}, u32[]{:S(2)}) copy-start(bf16[2,64,2048]{2,1,0:T(8,128)(2,1)S(1)} %collective-permute-done.36.refs_5_) | copy-start | bytes 1572868
  76.2 12.0 %collective-permute-start.38 = (bf16[2,64,2048]{2,1,0:T(8,128)(2,1)S(1)}, bf16[2,64,2048]{2,1,0:T(8,128)(2,1)S(1)}, u32[]{:S(2)}, u32[]{:S(2)}) collective-permute-start(bf16[2,64,2048]{2,1,0:T(8,128)(2,1)S(1)} %collective-permute-done.36.refs_5_), channel_id=1, source_target_pairs={{0,4},{4,0},{8,12},{12,8},{1,5},{5,1},{9,13},{13,9},{2,6},{6,2},{1... | collective-permute-start | bytes 1572872 | tf_op jit(solution)/shard_map/ppermute | solution.py:212
  82.8 0.6 copy-start.38
  82.8 0.7 copy-start.8
  88.2 4.5 %copy-start.42 = (bf16[1,64,2048]{2,1,0:T(8,128)(2,1)S(1)}, bf16[1,64,2048]{2,1,0:T(8,128)(2,1)}, u32[]{:S(2)}) copy-start(bf16[1,64,2048]{2,1,0:T(8,128)(2,1)} %get-tuple-element.142) | copy-start | bytes 786436
  88.2 4.5 %copy-start.43 = (bf16[1,64,2048]{2,1,0:T(8,128)(2,1)S(1)}, bf16[1,64,2048]{2,1,0:T(8,128)(2,1)}, u32[]{:S(2)}) copy-start(bf16[1,64,2048]{2,1,0:T(8,128)(2,1)} %get-tuple-element.143) | copy-start | bytes 786436
  88.2 0.8 copy-start.6
  89.1 0.8 copy-start.7
  92.7 7.6 %collective-permute-start.1 = (bf16[1,64,2048]{2,1,0:T(8,128)(2,1)S(1)}, bf16[1,64,2048]{2,1,0:T(8,128)(2,1)S(1)}, u32[]{:S(2)}, u32[]{:S(2)}) collective-permute-start(bf16[1,64,2048]{2,1,0:T(8,128)(2,1)S(1)} %get-tuple-element.67), channel_id=1, source_target_pairs={{0,8},{4,12},{8,0},{12,4},{1,9},{5,13},{9,1},{13,5},{2,10},{6,14},... | collective-permute-start | bytes 786440 | tf_op jit(solution)/shard_map/cond/branch_1_fun/ppermute | solution.py:212
  93.3 8.2 %collective-permute-start.2 = (bf16[1,64,2048]{2,1,0:T(8,128)(2,1)S(1)}, bf16[1,64,2048]{2,1,0:T(8,128)(2,1)S(1)}, u32[]{:S(2)}, u32[]{:S(2)}) collective-permute-start(bf16[1,64,2048]{2,1,0:T(8,128)(2,1)S(1)} %get-tuple-element.66.refs_4_), channel_id=1, source_target_pairs={{0,4},{4,0},{8,12},{12,8},{1,5},{5,1},{9,13},{13,9},{2,6},{6,2},{1... | collective-permute-start | bytes 786440 | tf_op jit(solution)/shard_map/cond/branch_1_fun/ppermute | solution.py:212
  100.3 2.4 %copy-start.20 = (bf16[1,64,2048]{2,1,0:T(8,128)(2,1)}, bf16[1,64,2048]{2,1,0:T(8,128)(2,1)S(1)}, u32[]{:S(2)}) copy-start(bf16[1,64,2048]{2,1,0:T(8,128)(2,1)S(1)} %collective-permute-done.1.refs_5_) | copy-start | bytes 786436 | tf_op jit(solution)/shard_map/cond
  100.3 2.4 %collective-permute-start.3 = (bf16[1,64,2048]{2,1,0:T(8,128)(2,1)S(1)}, bf16[1,64,2048]{2,1,0:T(8,128)(2,1)S(1)}, u32[]{:S(2)}, u32[]{:S(2)}) collective-permute-start(bf16[1,64,2048]{2,1,0:T(8,128)(2,1)S(1)} %collective-permute-done.1.refs_5_), channel_id=1, source_target_pairs={{0,4},{4,0},{8,12},{12,8},{1,5},{5,1},{9,13},{13,9},{2,6},{6,2},{1... | collective-permute-start | bytes 786440 | tf_op jit(solution)/shard_map/cond/branch_1_fun/ppermute | solution.py:212
  101.5 1.2 %copy-start.21 = (bf16[1,64,2048]{2,1,0:T(8,128)(2,1)}, bf16[1,64,2048]{2,1,0:T(8,128)(2,1)S(1)}, u32[]{:S(2)}) copy-start(bf16[1,64,2048]{2,1,0:T(8,128)(2,1)S(1)} %collective-permute-done.2.refs_6_) | copy-start | bytes 786436 | tf_op jit(solution)/shard_map/cond
  102.7 0.7 copy-start.23

commit v8 on v5

--- a/solution.py
+++ b/solution.py
@@ -217,7 +217,7 @@
     return lax.ppermute(array, "tensor", [(i, (i + step) % size) for i in range(size)])
 
 
-ALWAYS = ((0, 2), (2, 3))
+ALWAYS = ((0, 2), (2, 2), (4, 1))
 AT_NEED = ((5, 1), (6, 1), (7, 1))
 SMEM = pl.BlockSpec(memory_space=pltpu.SMEM)
 VMEM = pl.BlockSpec(memory_space=pltpu.VMEM)
@@ -793,12 +793,14 @@
     installed_b = installed_b.reshape((COPIES,) + row_b)
 
     tables = (me_table, hot_holder, dest_table)
+    early = len(ALWAYS) - 1
 
     def finish(count):
-        def branch(sibling_a, first_other, *arrays):
+        def branch(sibling_a, *arrays):
+            swapped, arrays = list(arrays[:early]), arrays[early:]
             got, rest = list(arrays[: len(ALWAYS)]), arrays[len(ALWAYS) :]
             late = [partner(array, 2) for array in rest[:count]]
-            other = [first_other] + [partner(array, 1) for array in got[1:]]
+            other = swapped + [partner(array, 1) for array in got[early:]]
             (placed,) = copy_call(
                 functools.partial(place_kernel, spans, slot_total, ALWAYS),
                 tables,
@@ -822,9 +824,9 @@
         return branch
 
     branches = [finish(count) for count in range(len(AT_NEED) + 1)]
-    first_other = partner(got[0], 1)
+    swapped = [partner(array, 1) for array in got[:early]]
     *rest, attn_out = lax.optimization_barrier((*units[len(ALWAYS) :], attn_out))
-    installed_a = lax.switch(extra[0], branches, sibling_a, first_other, *got, *rest)
+    installed_a = lax.switch(extra[0], branches, sibling_a, *swapped, *got, *rest)
     return (attn_out, new_kv, arrived, installed_a, installed_b)
 
 

time: 102 us -> 102 us (level)
  the two profiles are of different devices: /device:TPU:4 before, /device:TPU:7 now
where the time goes in v8:
time: 102 us; the launch traced here: 101 us
  waiting for transfers between devices  44.3 us (43%)
  Pallas kernels  25.4 us (25%)
  starting transfers between devices  21.7 us (21%)
  matrix products  5.77 us (6%)
  local copies, waits for them, and re-layouts  2.68 us (3%)
  between operations  1.36 us (1%)
    ppermute x20, waiting for transfers between devices, partner(): lax.ppermute(array, 'replica', [(i, i ^ mask) for i in range(lax.axis_siz...  39.7 us
    ppermute x20, starting transfers between devices, partner(): lax.ppermute(array, 'replica', [(i, i ^ mask) for i in range(lax.axis_siz...  16.4 us
    pallas_call x4, Pallas kernels, copy_call(): pl.pallas_call(kernel, out_shape=[pltpu.HBM(shape, dtype) for shape in sh...  13.9 us
    dot_general x1, matrix products, pairs_layer(): jnp.einsum('md,dgc->gmc', full, w_kv, preferred_element_type=jnp.float32)  5.77 us
    ppermute x6, starting transfers between devices, shifted(): lax.ppermute(array, 'tensor', [(i, (i + step) % size) for i in range(size)])  5.29 us
    pallas_call x1, Pallas kernels, pairs_layer(): pl.pallas_call(functools.partial(attend_kernel, spans, masks, resident, s...  4.77 us
    pallas_call x1, Pallas kernels, pairs_layer(): pl.pallas_call(functools.partial(project_kernel, spans, slot_total, resid...  4.74 us
    ppermute x6, waiting for transfers between devices, shifted(): lax.ppermute(array, 'tensor', [(i, (i + step) % size) for i in range(size)])  4.57 us
  transfers between devices with their start and end apart: 26, of which 10 were waited for; matrix products, arithmetic and copies ran while one was open for 6% of the time, Pallas kernels for 14%

profile of v8, /device:TPU:7, one launch (start us, length us, event | category | flops | bytes accessed | tf_op | source)
XLA Modules:
  0.0 101.3 jit_solution(2215847322941207434)
XLA Ops:
  0.7 5.0 %shard_map.164 = (bf16[128,2,256]{2,1,0:T(2,128)(2,1)}, bf16[128,2,256]{2,1,0:T(2,128)(2,1)}, bf16[128,2,256]{2,1,0:T(2,128)(2,1)}, bf16[4,2,64,2048]{3,2,1,0:T(...) custom-call(s32[1]{0:T(128)} %bitcast.refs_0_, s32[2,4]{1,0:T(2,128)} %bitcast.29, ...), custom_call_target="tpu_custom_call" | custom-call | tf_op jit(solution)/shard_map/pallas_call | solution.py:403
  5.7 0.8 collective-permute-start.16
  6.5 0.1 collective-permute-start.17
  6.5 4.3 %collective-permute-done.17.refs_6_ = bf16[4,2,64,256]{3,2,1,0:T(8,128)(2,1)S(1)} collective-permute-done((bf16[4,2,64,256]{3,2,1,0:T(8,128)(2,1)}, bf16[4,2,64,256]{3,2,1,0:T(8,128)(2,1)S(1)}, u32[]{:S(2)}, u32[]{:S(2)}) %collective-permute-start.17) | collective-permute-done | bytes 262176 | tf_op jit(solution)/shard_map/ppermute | solution.py:212
  10.8 0.0 collective-permute-done.16.refs_5_
  10.8 0.7 copy-done
  11.5 3.6 %shard_map.165 = (bf16[4,2,64,256]{3,2,1,0:T(8,128)(2,1)}, bf16[2,64,2048]{2,1,0:T(8,128)(2,1)}, bf16[2,64,2048]{2,1,0:T(8,128)(2,1)}, bf16[1,64,2048]{2,1,0:T(8...) custom-call(s32[1]{0:T(128)} %bitcast.refs_0_, ...), custom_call_target="tpu_custom_call" | custom-call | tf_op jit(solution)/shard_map/pallas_call | solution.py:403
  15.2 0.1 collective-permute-start.35
  15.2 1.5 %collective-permute-start.36 = (bf16[2,64,2048]{2,1,0:T(8,128)(2,1)}, bf16[2,64,2048]{2,1,0:T(8,128)(2,1)S(1)}, u32[]{:S(2)}, u32[]{:S(2)}) collective-permute-start(bf16[2,64,2048]{2,1,0:T(8,128)(2,1)} %get-tuple-element.189), channel_id=1, source_target_pairs={{0,8},{4,12},{8,0},{12,4},{1,9},{5,13},{9,1},{13,5},{2,10},{6,14},... | collective-permute-start | bytes 1572872 | tf_op jit(solution)/shard_map/ppermute | solution.py:212
  16.7 0.9 collective-permute-start.23
  17.6 1.3 %collective-permute-start.22 = (bf16[8,2048]{1,0:T(8,128)(2,1)S(1)}, bf16[8,2048]{1,0:T(8,128)(2,1)S(1)}, u32[]{:S(2)}, u32[]{:S(2)}) collective-permute-start(bf16[8,2048]{1,0:T(8,128)(2,1)S(1)} %copy-done.21), channel_id=1, source_target_pairs={{0,8},{4,12},{8,0},{12,4},{1,9},{5,13},{9,1},{13,5},{2,10},{6,14},... | collective-permute-start | bytes 98312 | tf_op jit(solution)/shard_map/ppermute | solution.py:212
  18.9 0.0 collective-permute-start.21
  18.9 22.5 %collective-permute-done.23.refs_8_ = bf16[8,2048]{1,0:T(8,128)(2,1)S(1)} collective-permute-done((bf16[8,2048]{1,0:T(8,128)(2,1)S(1)}, bf16[8,2048]{1,0:T(8,128)(2,1)S(1)}, u32[]{:S(2)}, u32[]{:S(2)}) %collective-permute-start.23) | collective-permute-done | bytes 32800 | tf_op jit(solution)/shard_map/ppermute | solution.py:212
  41.4 3.3 %collective-permute-start.20 = (bf16[32,2048]{1,0:T(8,128)(2,1)}, bf16[32,2048]{1,0:T(8,128)(2,1)S(1)}, u32[]{:S(2)}, u32[]{:S(2)}) collective-permute-start(bf16[32,2048]{1,0:T(8,128)(2,1)} %get-tuple-element.170.refs_5_.refs_0_), channel_id=1, source_target_pairs={{0,3},{1,0},{2,1},{3,2},{4,7},{5,4},{6,5},{7,6},{8,11},{9,8},{10,9... | collective-permute-start | bytes 393224 | tf_op jit(solution)/shard_map/ppermute | solution.py:217
  44.7 0.0 collective-permute-done.22.refs_7_
  44.7 0.0 collective-permute-start.19
  44.7 0.0 collective-permute-done.21.refs_6_
  44.7 0.0 copy-start.15
  44.7 0.6 copy-done.14
  45.3 0.0 copy-done.15
  45.3 4.7 %project.1 = (f32[32,128]{1,0:T(8,128)}, f32[8,128]{1,0:T(8,128)}, f32[8,128]{1,0:T(8,128)}, f32[8,128]{1,0:T(8,128)}) custom-call(s32[1]{0:T(128)} %bitcast.refs_0_, s32[48]{0:T(128)} %refs_4_.5, s32[2,4]{1,0:T(2,128)} %bitcast.33, s32[16]{0:T(128)S(1)} %copy-done.11, s32[1,16]{1,0:T(1,128)S(1)} %bitcast.23, ...), custom_call_target="tpu_custom_call" | custom-call | tf_op jit(solution)/shard_map/project/pallas_call | solution.py:702
  50.1 0.3 collective-permute-start.24
  50.4 1.1 %collective-permute-done.24.refs_5_ = f32[8,128]{1,0:T(8,128)S(1)} collective-permute-done((f32[8,128]{1,0:T(8,128)}, f32[8,128]{1,0:T(8,128)S(1)}, u32[]{:S(2)}, u32[]{:S(2)}) %collective-permute-start.24) | collective-permute-done | bytes 4128 | tf_op jit(solution)/shard_map/ppermute | solution.py:212
  51.5 0.0 collective-permute-start.25
  51.5 2.7 %collective-permute-done.25.refs_6_ = f32[8,128]{1,0:T(8,128)S(1)} collective-permute-done((f32[8,128]{1,0:T(8,128)}, f32[8,128]{1,0:T(8,128)S(1)}, u32[]{:S(2)}, u32[]{:S(2)}) %collective-permute-start.25) | collective-permute-done | bytes 4128 | tf_op jit(solution)/shard_map/ppermute | solution.py:212
  54.2 1.3 %collective-permute-start.26 = (f32[8,128]{1,0:T(8,128)}, f32[8,128]{1,0:T(8,128)S(1)}, u32[]{:S(2)}, u32[]{:S(2)}) collective-permute-start(f32[8,128]{1,0:T(8,128)} %get-tuple-element.175), channel_id=1, source_target_pairs={{0,12},{4,8},{8,4},{12,0},{1,13},{5,9},{9,5},{13,1},{2,14},{6,10},... | collective-permute-start | bytes 12296 | tf_op jit(solution)/shard_map/ppermute | solution.py:212
  55.5 1.9 %collective-permute-done.26.refs_7_ = f32[8,128]{1,0:T(8,128)S(1)} collective-permute-done((f32[8,128]{1,0:T(8,128)}, f32[8,128]{1,0:T(8,128)S(1)}, u32[]{:S(2)}, u32[]{:S(2)}) %collective-permute-start.26) | collective-permute-done | bytes 4128 | tf_op jit(solution)/shard_map/ppermute | solution.py:212
  57.4 1.2 %collective-permute-start.18 = (bf16[32,2048]{1,0:T(8,128)(2,1)}, bf16[32,2048]{1,0:T(8,128)(2,1)S(1)}, u32[]{:S(2)}, u32[]{:S(2)}) collective-permute-start(bf16[32,2048]{1,0:T(8,128)(2,1)} %get-tuple-element.170.refs_5_.refs_0_), channel_id=1, source_target_pairs={{0,1},{1,2},{2,3},{3,0},{4,5},{5,6},{6,7},{7,4},{8,9},{9,10},{10,1... | collective-permute-start | bytes 393224 | tf_op jit(solution)/shard_map/ppermute | solution.py:217
  58.7 0.0 collective-permute-done.20.refs_3_
  58.7 1.8 %collective-permute-start.30 = (bf16[128,2,256]{2,1,0:T(2,128)(2,1)}, bf16[128,2,256]{2,1,0:T(2,128)(2,1)S(1)}, u32[]{:S(2)}, u32[]{:S(2)}) collective-permute-start(bf16[128,2,256]{2,1,0:T(2,128)(2,1)} %get-tuple-element.177), channel_id=1, source_target_pairs={{0,4},{4,0},{8,12},{12,8},{1,5},{5,1},{9,13},{13,9},{2,6},{6,2},{1... | collective-permute-start | bytes 393224 | tf_op jit(solution)/shard_map/ppermute | solution.py:212
  60.5 0.0 collective-permute-done.19.refs_2_
  60.5 0.1 collective-permute-start.31
  60.6 2.7 %collective-permute-done.18.refs_1_ = bf16[32,2048]{1,0:T(8,128)(2,1)S(1)} collective-permute-done((bf16[32,2048]{1,0:T(8,128)(2,1)}, bf16[32,2048]{1,0:T(8,128)(2,1)S(1)}, u32[]{:S(2)}, u32[]{:S(2)}) %collective-permute-start.18) | collective-permute-done | bytes 131104 | tf_op jit(solution)/shard_map/ppermute | solution.py:217
  63.3 0.6 copy-done.10
  63.9 3.0 %collective-permute-start.32 = (bf16[128,2,256]{2,1,0:T(2,128)(2,1)}, bf16[128,2,256]{2,1,0:T(2,128)(2,1)S(1)}, u32[]{:S(2)}, u32[]{:S(2)}) collective-permute-start(bf16[128,2,256]{2,1,0:T(2,128)(2,1)} %get-tuple-element.179), channel_id=1, source_target_pairs={{0,12},{4,8},{8,4},{12,0},{1,13},{5,9},{9,5},{13,1},{2,14},{6,10},... | collective-permute-start | bytes 393224 | tf_op jit(solution)/shard_map/ppermute | solution.py:212
  66.9 2.0 %gather.1 = (bf16[32,8192]{1,0:T(8,128)(2,1)}, f32[32,128]{1,0:T(8,128)}) custom-call(s32[1]{0:T(128)} %bitcast.5.shard_ref, bf16[32,2048]{1,0:T(8,128)(2,1)} %get-tuple-element.170.refs_5_.refs_0_, bf16[32,2048]{1,0:T(8,128)(2,1)} %copy-done.10, bf16[32,2048]{1,0:T(8,128)(2,1)} %copy-done.9, bf16[32,2048]{1,0:T(8,128)(2,1)} %copy-done.8, ...), custom_call_target="tpu_custom_call" | custom-call | tf_op jit(solution)/shard_map/gather/pallas_call | solution.py:745
  68.9 0.0 collective-permute-done.30.refs_12_
  68.9 0.2 collective-permute-start.29
  69.1 0.0 collective-permute-done.31.refs_13_
  69.1 0.5 collective-permute-start.28
  69.6 1.2 %collective-permute-done.32.refs_14_ = bf16[128,2,256]{2,1,0:T(2,128)(2,1)S(1)} collective-permute-done((bf16[128,2,256]{2,1,0:T(2,128)(2,1)}, bf16[128,2,256]{2,1,0:T(2,128)(2,1)S(1)}, u32[]{:S(2)}, u32[]{:S(2)}) %collective-permute-start.32) | collective-permute-done | bytes 131104 | tf_op jit(solution)/shard_map/ppermute | solution.py:212
  70.9 0.0 collective-permute-start.27
  70.9 1.3 %collective-permute-done.29.refs_11_ = f32[32,128]{1,0:T(8,128)S(1)} collective-permute-done((f32[32,128]{1,0:T(8,128)}, f32[32,128]{1,0:T(8,128)S(1)}, u32[]{:S(2)}, u32[]{:S(2)}) %collective-permute-start.29) | collective-permute-done | bytes 16416 | tf_op jit(solution)/shard_map/ppermute | solution.py:217
  72.2 0.5 collective-permute-start.33
  72.7 0.6 collective-permute-done.28.refs_10_
  73.3 0.9 collective-permute-start.34
  74.2 0.0 collective-permute-done.35
  74.2 0.7 collective-permute-start.37
  74.9 0.0 collective-permute-done.36
  74.9 0.1 collective-permute-start.38
  75.0 5.8 %fusion.2.refs_18_ = f32[2,32,256]{2,1,0:T(8,128)} fusion(bf16[8192,2,256]{2,1,0:T(2,128)(2,1)} %param.20, bf16[32,8192]{1,0:T(8,128)(2,1)} %get-tuple-element.181), kind=kOutput, calls=%fused_computation.2 | convolution fusion | flops 268435456 | bytes 8978432 | tf_op jit(solution)/shard_map/md,dgc->gmc/dot_general | solution.py:756
  81.3 0.0 collective-permute-done.27.refs_9_
  81.3 4.8 %attend.1 = (bf16[14,2,2048]{2,1,0:T(2,128)(2,1)}, bf16[14,2,2,256]{3,2,1,0:T(2,128)(2,1)}, bf16[2,128,2,256]{3,2,1,0:T(2,128)(2,1)}, bf16[4,128,256]{2,1,0:T(8,128)(2,1)}) custom-call(s32[1]{0:T(128)} %bitcast.refs_0_, s32[48]{0:T(128)} %refs_1_.5, s32[2,4]{1,0:T(2,128)} %bitcast.30, s32[2,4]{1,0:T(2,128)} %bitcast.32, s32[48]{0:T(128)} %refs_4_.5, ...), custom_call_target="tpu_custom_call" | custom-call | tf_op jit(solution)/shard_map/attend/pallas_call | solution.py:758
  86.1 0.0 collective-permute-done.34
  86.1 0.0 collective-permute-done.37
  86.1 15.2 %conditional.1 = (bf16[4,2,64,2048]{3,2,1,0:T(8,128)(2,1)}) conditional(s32[]{:T(128)} %bitcast.13, (bf16[1,64,2048]{2,1,0:T(8,128)(2,1)S(1)}, s32[1]{0:T(128)}, s32[16]{0:T(128)S(1)}, s32[1,16]{1,0:T(1,128)S(1)}, bf16[4,2,64,2048]{3,2,1,0:T(8,128)(2,1)S(1)}, /*index=5*/bf16[2,64,2048]{2,1,0:T(8,128)(2,1)S(1)}, ...), branch_computations={%region_0.0_spmd, %region_1.0_spmd, %region_2.0_spmd, %region_3.0_... | conditional | bytes 8388924 | solution.py:829
  86.2 0.6 collective-permute-start.2
  86.8 0.9 collective-permute-start.1
  87.6 6.0 %collective-permute-done.2.refs_4_ = bf16[1,64,2048]{2,1,0:T(8,128)(2,1)} collective-permute-done((bf16[1,64,2048]{2,1,0:T(8,128)(2,1)}, bf16[1,64,2048]{2,1,0:T(8,128)(2,1)}, u32[]{:S(2)}, u32[]{:S(2)}) %collective-permute-start.2) | collective-permute-done | bytes 262176 | tf_op jit(solution)/shard_map/cond/branch_1_fun/ppermute | solution.py:212
  93.7 1.6 %collective-permute-start.3 = (bf16[1,64,2048]{2,1,0:T(8,128)(2,1)}, bf16[1,64,2048]{2,1,0:T(8,128)(2,1)}, u32[]{:S(2)}, u32[]{:S(2)}) collective-permute-start(bf16[1,64,2048]{2,1,0:T(8,128)(2,1)} %collective-permute-done.2.refs_4_), channel_id=1, source_target_pairs={{0,4},{4,0},{8,12},{12,8},{1,5},{5,1},{9,13},{13,9},{2,6},{6,2},{1... | collective-permute-start | bytes 786440 | tf_op jit(solution)/shard_map/cond/branch_1_fun/ppermute | solution.py:212
  95.3 0.7 copy-done.3
  95.9 2.8 %branch_1_fun.2.refs_3_ = bf16[4,2,64,2048]{3,2,1,0:T(8,128)(2,1)} custom-call(s32[1]{0:T(128)} %get-tuple-element.98.refs_0_, s32[16]{0:T(128)S(1)} %get-tuple-element.99.refs_1_, s32[1,16]{1,0:T(1,128)S(1)} %get-tuple-element.100.refs_2_, bf16[4,2,64,2048]{3,2,1,0:T(8,128)(2,1)S(1)} %get-tuple-element.101.refs_3_, ...), custom_call_target="tpu_custom_call" | custom-call | tf_op jit(solution)/shard_map/cond/branch_1_fun/pallas_call | solution.py:403
  98.8 0.0 collective-permute-done.3.refs_5_
  98.8 2.5 %branch_1_fun.3 = bf16[4,2,64,2048]{3,2,1,0:T(8,128)(2,1)} custom-call(s32[1]{0:T(128)} %get-tuple-element.98.refs_0_, s32[16]{0:T(128)S(1)} %get-tuple-element.99.refs_1_, s32[1,16]{1,0:T(1,128)S(1)} %get-tuple-element.100.refs_2_, bf16[4,2,64,2048]{3,2,1,0:T(8,128)(2,1)} %branch_1_fun.2.refs_3_, ...), custom_call_target="tpu_custom_call", output_to_operand_aliasing={{}: (3, {})} | custom-call | tf_op jit(solution)/shard_map/cond/branch_1_fun/pallas_call | solution.py:403
  (35 shorter events, 0.1 us)
Async XLA Ops:
  0.6 10.9 %copy-start.11 = (s32[16]{0:T(128)S(1)}, s32[16]{0:T(128)}, u32[]{:S(2)}) copy-start(s32[16]{0:T(128)} %refs_6_.3) | copy-start | bytes 196
  0.6 10.9 %copy-start.12 = (s32[16,1]{0,1:T(1,128)S(1)}, s32[16,1]{0,1:T(1,128)}, u32[]{:S(2)}) copy-start(s32[16,1]{0,1:T(1,128)} %param.29) | copy-start | bytes 196
  5.7 5.2 %collective-permute-start.16 = (bf16[4,2,64,2048]{3,2,1,0:T(8,128)(2,1)}, bf16[4,2,64,2048]{3,2,1,0:T(8,128)(2,1)S(1)}, u32[]{:S(2)}, u32[]{:S(2)}) collective-permute-start(bf16[4,2,64,2048]{3,2,1,0:T(8,128)(2,1)} %get-tuple-element.165), channel_id=1, source_target_pairs={{0,4},{4,0},{8,12},{12,8},{1,5},{5,1},{9,13},{13,9},{2,6},{6,2},{1... | collective-permute-start | bytes 6291464 | tf_op jit(solution)/shard_map/ppermute | solution.py:212
  6.5 4.4 %collective-permute-start.17 = (bf16[4,2,64,256]{3,2,1,0:T(8,128)(2,1)}, bf16[4,2,64,256]{3,2,1,0:T(8,128)(2,1)S(1)}, u32[]{:S(2)}, u32[]{:S(2)}) collective-permute-start(bf16[4,2,64,256]{3,2,1,0:T(8,128)(2,1)} %get-tuple-element.166), channel_id=1, source_target_pairs={{0,4},{4,0},{8,12},{12,8},{1,5},{5,1},{9,13},{13,9},{2,6},{6,2},{1... | collective-permute-start | bytes 786440 | tf_op jit(solution)/shard_map/ppermute | solution.py:212
  10.8 0.7 copy-start
  11.5 5.2 %copy-start.21 = (bf16[8,2048]{1,0:T(8,128)(2,1)S(1)}, bf16[8,2048]{1,0:T(8,128)(2,1)}, u32[]{:S(2)}) copy-start(bf16[8,2048]{1,0:T(8,128)(2,1)} %get-tuple-element.171) | copy-start | bytes 98308
  15.2 59.0 %collective-permute-start.35 = (bf16[2,64,2048]{2,1,0:T(8,128)(2,1)}, bf16[2,64,2048]{2,1,0:T(8,128)(2,1)S(1)}, u32[]{:S(2)}, u32[]{:S(2)}) collective-permute-start(bf16[2,64,2048]{2,1,0:T(8,128)(2,1)} %get-tuple-element.188), channel_id=1, source_target_pairs={{0,8},{4,12},{8,0},{12,4},{1,9},{5,13},{9,1},{13,5},{2,10},{6,14},... | collective-permute-start | bytes 1572872 | tf_op jit(solution)/shard_map/ppermute | solution.py:212
  15.2 59.6 %collective-permute-start.36 = (bf16[2,64,2048]{2,1,0:T(8,128)(2,1)}, bf16[2,64,2048]{2,1,0:T(8,128)(2,1)S(1)}, u32[]{:S(2)}, u32[]{:S(2)}) collective-permute-start(bf16[2,64,2048]{2,1,0:T(8,128)(2,1)} %get-tuple-element.189), channel_id=1, source_target_pairs={{0,8},{4,12},{8,0},{12,4},{1,9},{5,13},{9,1},{13,5},{2,10},{6,14},... | collective-permute-start | bytes 1572872 | tf_op jit(solution)/shard_map/ppermute | solution.py:212
  16.7 24.7 %collective-permute-start.23 = (bf16[8,2048]{1,0:T(8,128)(2,1)S(1)}, bf16[8,2048]{1,0:T(8,128)(2,1)S(1)}, u32[]{:S(2)}, u32[]{:S(2)}) collective-permute-start(bf16[8,2048]{1,0:T(8,128)(2,1)S(1)} %copy-done.21), channel_id=1, source_target_pairs={{0,12},{4,8},{8,4},{12,0},{1,13},{5,9},{9,5},{13,1},{2,14},{6,10},... | collective-permute-start | bytes 98312 | tf_op jit(solution)/shard_map/ppermute | solution.py:212
  17.6 27.1 %collective-permute-start.22 = (bf16[8,2048]{1,0:T(8,128)(2,1)S(1)}, bf16[8,2048]{1,0:T(8,128)(2,1)S(1)}, u32[]{:S(2)}, u32[]{:S(2)}) collective-permute-start(bf16[8,2048]{1,0:T(8,128)(2,1)S(1)} %copy-done.21), channel_id=1, source_target_pairs={{0,8},{4,12},{8,0},{12,4},{1,9},{5,13},{9,1},{13,5},{2,10},{6,14},... | collective-permute-start | bytes 98312 | tf_op jit(solution)/shard_map/ppermute | solution.py:212
  18.9 25.8 %collective-permute-start.21 = (bf16[8,2048]{1,0:T(8,128)(2,1)S(1)}, bf16[8,2048]{1,0:T(8,128)(2,1)S(1)}, u32[]{:S(2)}, u32[]{:S(2)}) collective-permute-start(bf16[8,2048]{1,0:T(8,128)(2,1)S(1)} %copy-done.21), channel_id=1, source_target_pairs={{0,4},{4,0},{8,12},{12,8},{1,5},{5,1},{9,13},{13,9},{2,6},{6,2},{1... | collective-permute-start | bytes 98312 | tf_op jit(solution)/shard_map/ppermute | solution.py:212
  41.4 3.4 %copy-start.13 = (bf16[8,2048]{1,0:T(8,128)(2,1)}, bf16[8,2048]{1,0:T(8,128)(2,1)S(1)}, u32[]{:S(2)}) copy-start(bf16[8,2048]{1,0:T(8,128)(2,1)S(1)} %collective-permute-done.23.refs_8_) | copy-start | bytes 98308
  41.4 17.3 %collective-permute-start.20 = (bf16[32,2048]{1,0:T(8,128)(2,1)}, bf16[32,2048]{1,0:T(8,128)(2,1)S(1)}, u32[]{:S(2)}, u32[]{:S(2)}) collective-permute-start(bf16[32,2048]{1,0:T(8,128)(2,1)} %get-tuple-element.170.refs_5_.refs_0_), channel_id=1, source_target_pairs={{0,3},{1,0},{2,1},{3,2},{4,7},{5,4},{6,5},{7,6},{8,11},{9,8},{10,9... | collective-permute-start | bytes 393224 | tf_op jit(solution)/shard_map/ppermute | solution.py:217
  44.7 0.6 copy-start.14
  44.7 15.8 %collective-permute-start.19 = (bf16[32,2048]{1,0:T(8,128)(2,1)}, bf16[32,2048]{1,0:T(8,128)(2,1)S(1)}, u32[]{:S(2)}, u32[]{:S(2)}) collective-permute-start(bf16[32,2048]{1,0:T(8,128)(2,1)} %get-tuple-element.170.refs_5_.refs_0_), channel_id=1, source_target_pairs={{0,2},{1,3},{2,0},{3,1},{4,6},{5,7},{6,4},{7,5},{8,10},{9,11},{10,... | collective-permute-start | bytes 393224 | tf_op jit(solution)/shard_map/ppermute | solution.py:217
  44.7 0.6 copy-start.15
  50.1 1.4 %collective-permute-start.24 = (f32[8,128]{1,0:T(8,128)}, f32[8,128]{1,0:T(8,128)S(1)}, u32[]{:S(2)}, u32[]{:S(2)}) collective-permute-start(f32[8,128]{1,0:T(8,128)} %get-tuple-element.173), channel_id=1, source_target_pairs={{0,4},{4,0},{8,12},{12,8},{1,5},{5,1},{9,13},{13,9},{2,6},{6,2},{1... | collective-permute-start | bytes 12296 | tf_op jit(solution)/shard_map/ppermute | solution.py:212
  51.5 15.4 %copy-start.18 = (f32[8,128]{1,0:T(8,128)}, f32[8,128]{1,0:T(8,128)S(1)}, u32[]{:S(2)}) copy-start(f32[8,128]{1,0:T(8,128)S(1)} %collective-permute-done.24.refs_5_) | copy-start | bytes 12292
  51.5 2.7 %collective-permute-start.25 = (f32[8,128]{1,0:T(8,128)}, f32[8,128]{1,0:T(8,128)S(1)}, u32[]{:S(2)}, u32[]{:S(2)}) collective-permute-start(f32[8,128]{1,0:T(8,128)} %get-tuple-element.174), channel_id=1, source_target_pairs={{0,8},{4,12},{8,0},{12,4},{1,9},{5,13},{9,1},{13,5},{2,10},{6,14},... | collective-permute-start | bytes 12296 | tf_op jit(solution)/shard_map/ppermute | solution.py:212
  54.2 12.8 %copy-start.19 = (f32[8,128]{1,0:T(8,128)}, f32[8,128]{1,0:T(8,128)S(1)}, u32[]{:S(2)}) copy-start(f32[8,128]{1,0:T(8,128)S(1)} %collective-permute-done.25.refs_6_) | copy-start | bytes 12292
  54.2 3.2 %collective-permute-start.26 = (f32[8,128]{1,0:T(8,128)}, f32[8,128]{1,0:T(8,128)S(1)}, u32[]{:S(2)}, u32[]{:S(2)}) collective-permute-start(f32[8,128]{1,0:T(8,128)} %get-tuple-element.175), channel_id=1, source_target_pairs={{0,12},{4,8},{8,4},{12,0},{1,13},{5,9},{9,5},{13,1},{2,14},{6,10},... | collective-permute-start | bytes 12296 | tf_op jit(solution)/shard_map/ppermute | solution.py:212
  57.4 1.2 %copy-start.20 = (f32[8,128]{1,0:T(8,128)}, f32[8,128]{1,0:T(8,128)S(1)}, u32[]{:S(2)}) copy-start(f32[8,128]{1,0:T(8,128)S(1)} %collective-permute-done.26.refs_7_) | copy-start | bytes 12292
  57.4 5.8 %collective-permute-start.18 = (bf16[32,2048]{1,0:T(8,128)(2,1)}, bf16[32,2048]{1,0:T(8,128)(2,1)S(1)}, u32[]{:S(2)}, u32[]{:S(2)}) collective-permute-start(bf16[32,2048]{1,0:T(8,128)(2,1)} %get-tuple-element.170.refs_5_.refs_0_), channel_id=1, source_target_pairs={{0,1},{1,2},{2,3},{3,0},{4,5},{5,6},{6,7},{7,4},{8,9},{9,10},{10,1... | collective-permute-start | bytes 393224 | tf_op jit(solution)/shard_map/ppermute | solution.py:217
  58.7 1.8 %copy-start.8 = (bf16[32,2048]{1,0:T(8,128)(2,1)}, bf16[32,2048]{1,0:T(8,128)(2,1)S(1)}, u32[]{:S(2)}) copy-start(bf16[32,2048]{1,0:T(8,128)(2,1)S(1)} %collective-permute-done.20.refs_3_) | copy-start | bytes 393220
  58.7 10.2 %collective-permute-start.30 = (bf16[128,2,256]{2,1,0:T(2,128)(2,1)}, bf16[128,2,256]{2,1,0:T(2,128)(2,1)S(1)}, u32[]{:S(2)}, u32[]{:S(2)}) collective-permute-start(bf16[128,2,256]{2,1,0:T(2,128)(2,1)} %get-tuple-element.177), channel_id=1, source_target_pairs={{0,4},{4,0},{8,12},{12,8},{1,5},{5,1},{9,13},{13,9},{2,6},{6,2},{1... | collective-permute-start | bytes 393224 | tf_op jit(solution)/shard_map/ppermute | solution.py:212
  60.5 2.7 %copy-start.9 = (bf16[32,2048]{1,0:T(8,128)(2,1)}, bf16[32,2048]{1,0:T(8,128)(2,1)S(1)}, u32[]{:S(2)}) copy-start(bf16[32,2048]{1,0:T(8,128)(2,1)S(1)} %collective-permute-done.19.refs_2_) | copy-start | bytes 393220
  60.5 8.6 %collective-permute-start.31 = (bf16[128,2,256]{2,1,0:T(2,128)(2,1)}, bf16[128,2,256]{2,1,0:T(2,128)(2,1)S(1)}, u32[]{:S(2)}, u32[]{:S(2)}) collective-permute-start(bf16[128,2,256]{2,1,0:T(2,128)(2,1)} %get-tuple-element.178), channel_id=1, source_target_pairs={{0,8},{4,12},{8,0},{12,4},{1,9},{5,13},{9,1},{13,5},{2,10},{6,14},... | collective-permute-start | bytes 393224 | tf_op jit(solution)/shard_map/ppermute | solution.py:212
  63.3 0.6 copy-start.10
  63.9 7.0 %collective-permute-start.32 = (bf16[128,2,256]{2,1,0:T(2,128)(2,1)}, bf16[128,2,256]{2,1,0:T(2,128)(2,1)S(1)}, u32[]{:S(2)}, u32[]{:S(2)}) collective-permute-start(bf16[128,2,256]{2,1,0:T(2,128)(2,1)} %get-tuple-element.179), channel_id=1, source_target_pairs={{0,12},{4,8},{8,4},{12,0},{1,13},{5,9},{9,5},{13,1},{2,14},{6,10},... | collective-permute-start | bytes 393224 | tf_op jit(solution)/shard_map/ppermute | solution.py:212
  68.9 11.8 %copy-start.5 = (bf16[128,2,256]{2,1,0:T(2,128)(2,1)}, bf16[128,2,256]{2,1,0:T(2,128)(2,1)S(1)}, u32[]{:S(2)}) copy-start(bf16[128,2,256]{2,1,0:T(2,128)(2,1)S(1)} %collective-permute-done.30.refs_12_) | copy-start | bytes 393220
  68.9 3.3 %collective-permute-start.29 = (f32[32,128]{1,0:T(8,128)}, f32[32,128]{1,0:T(8,128)S(1)}, u32[]{:S(2)}, u32[]{:S(2)}) collective-permute-start(f32[32,128]{1,0:T(8,128)} %get-tuple-element.176.refs_8_), channel_id=1, source_target_pairs={{0,3},{1,0},{2,1},{3,2},{4,7},{5,4},{6,5},{7,6},{8,11},{9,8},{10,9... | collective-permute-start | bytes 49160 | tf_op jit(solution)/shard_map/ppermute | solution.py:217
  69.1 4.1 %copy-start.6 = (bf16[128,2,256]{2,1,0:T(2,128)(2,1)}, bf16[128,2,256]{2,1,0:T(2,128)(2,1)S(1)}, u32[]{:S(2)}) copy-start(bf16[128,2,256]{2,1,0:T(2,128)(2,1)S(1)} %collective-permute-done.31.refs_13_) | copy-start | bytes 393220
  69.1 4.1 %collective-permute-start.28 = (f32[32,128]{1,0:T(8,128)}, f32[32,128]{1,0:T(8,128)S(1)}, u32[]{:S(2)}, u32[]{:S(2)}) collective-permute-start(f32[32,128]{1,0:T(8,128)} %get-tuple-element.176.refs_8_), channel_id=1, source_target_pairs={{0,2},{1,3},{2,0},{3,1},{4,6},{5,7},{6,4},{7,5},{8,10},{9,11},{10,... | collective-permute-start | bytes 49160 | tf_op jit(solution)/shard_map/ppermute | solution.py:217
  70.9 2.4 %copy-start.7 = (bf16[128,2,256]{2,1,0:T(2,128)(2,1)}, bf16[128,2,256]{2,1,0:T(2,128)(2,1)S(1)}, u32[]{:S(2)}) copy-start(bf16[128,2,256]{2,1,0:T(2,128)(2,1)S(1)} %collective-permute-done.32.refs_14_) | copy-start | bytes 393220
  70.9 10.4 %collective-permute-start.27 = (f32[32,128]{1,0:T(8,128)}, f32[32,128]{1,0:T(8,128)}, u32[]{:S(2)}, u32[]{:S(2)}) collective-permute-start(f32[32,128]{1,0:T(8,128)} %get-tuple-element.176.refs_8_), channel_id=1, source_target_pairs={{0,1},{1,2},{2,3},{3,0},{4,5},{5,6},{6,7},{7,4},{8,9},{9,10},{10,1... | collective-permute-start | bytes 49160 | tf_op jit(solution)/shard_map/ppermute | solution.py:217
  72.2 2.7 %copy-start.16 = (f32[32,128]{1,0:T(8,128)}, f32[32,128]{1,0:T(8,128)S(1)}, u32[]{:S(2)}) copy-start(f32[32,128]{1,0:T(8,128)S(1)} %collective-permute-done.29.refs_11_) | copy-start | bytes 49156
  72.2 9.1 %collective-permute-start.33 = (bf16[4,2,64,256]{3,2,1,0:T(8,128)(2,1)}, bf16[4,2,64,256]{3,2,1,0:T(8,128)(2,1)}, u32[]{:S(2)}, u32[]{:S(2)}) collective-permute-start(bf16[4,2,64,256]{3,2,1,0:T(8,128)(2,1)} %get-tuple-element.180), channel_id=1, source_target_pairs={{0,8},{4,12},{8,0},{12,4},{1,9},{5,13},{9,1},{13,5},{2,10},{6,14},... | collective-permute-start | bytes 786440 | tf_op jit(solution)/shard_map/ppermute | solution.py:212
  73.3 1.7 %copy-start.17 = (f32[32,128]{1,0:T(8,128)}, f32[32,128]{1,0:T(8,128)S(1)}, u32[]{:S(2)}) copy-start(f32[32,128]{1,0:T(8,128)S(1)} %collective-permute-done.28.refs_10_) | copy-start | bytes 49156
  73.3 12.8 %collective-permute-start.34 = (bf16[1,64,2048]{2,1,0:T(8,128)(2,1)}, bf16[1,64,2048]{2,1,0:T(8,128)(2,1)S(1)}, u32[]{:S(2)}, u32[]{:S(2)}) collective-permute-start(bf16[1,64,2048]{2,1,0:T(8,128)(2,1)} %get-tuple-element.187), channel_id=1, source_target_pairs={{0,8},{4,12},{8,0},{12,4},{1,9},{5,13},{9,1},{13,5},{2,10},{6,14},... | collective-permute-start | bytes 786440 | tf_op jit(solution)/shard_map/ppermute | solution.py:212
  74.2 11.9 %collective-permute-start.37 = (bf16[2,64,2048]{2,1,0:T(8,128)(2,1)S(1)}, bf16[2,64,2048]{2,1,0:T(8,128)(2,1)}, u32[]{:S(2)}, u32[]{:S(2)}) collective-permute-start(bf16[2,64,2048]{2,1,0:T(8,128)(2,1)S(1)} %collective-permute-done.35), channel_id=1, source_target_pairs={{0,4},{4,0},{8,12},{12,8},{1,5},{5,1},{9,13},{13,9},{2,6},{6,2},{1... | collective-permute-start | bytes 1572872 | tf_op jit(solution)/shard_map/ppermute | solution.py:212
  74.9 11.2 %collective-permute-start.38 = (bf16[2,64,2048]{2,1,0:T(8,128)(2,1)S(1)}, bf16[2,64,2048]{2,1,0:T(8,128)(2,1)}, u32[]{:S(2)}, u32[]{:S(2)}) collective-permute-start(bf16[2,64,2048]{2,1,0:T(8,128)(2,1)S(1)} %collective-permute-done.36), channel_id=1, source_target_pairs={{0,4},{4,0},{8,12},{12,8},{1,5},{5,1},{9,13},{13,9},{2,6},{6,2},{1... | collective-permute-start | bytes 1572872 | tf_op jit(solution)/shard_map/ppermute | solution.py:212
  86.2 7.5 %collective-permute-start.2 = (bf16[1,64,2048]{2,1,0:T(8,128)(2,1)}, bf16[1,64,2048]{2,1,0:T(8,128)(2,1)}, u32[]{:S(2)}, u32[]{:S(2)}) collective-permute-start(bf16[1,64,2048]{2,1,0:T(8,128)(2,1)} %get-tuple-element.107), channel_id=1, source_target_pairs={{0,8},{4,12},{8,0},{12,4},{1,9},{5,13},{9,1},{13,5},{2,10},{6,14},... | collective-permute-start | bytes 786440 | tf_op jit(solution)/shard_map/cond/branch_1_fun/ppermute | solution.py:212
  86.8 8.5 %collective-permute-start.1 = (bf16[1,64,2048]{2,1,0:T(8,128)(2,1)S(1)}, bf16[1,64,2048]{2,1,0:T(8,128)(2,1)S(1)}, u32[]{:S(2)}, u32[]{:S(2)}) collective-permute-start(bf16[1,64,2048]{2,1,0:T(8,128)(2,1)S(1)} %get-tuple-element.104.refs_6_), channel_id=1, source_target_pairs={{0,4},{4,0},{8,12},{12,8},{1,5},{5,1},{9,13},{13,9},{2,6},{6,2},{1... | collective-permute-start | bytes 786440 | tf_op jit(solution)/shard_map/cond/branch_1_fun/ppermute | solution.py:212
  93.7 5.1 %collective-permute-start.3 = (bf16[1,64,2048]{2,1,0:T(8,128)(2,1)}, bf16[1,64,2048]{2,1,0:T(8,128)(2,1)}, u32[]{:S(2)}, u32[]{:S(2)}) collective-permute-start(bf16[1,64,2048]{2,1,0:T(8,128)(2,1)} %collective-permute-done.2.refs_4_), channel_id=1, source_target_pairs={{0,4},{4,0},{8,12},{12,8},{1,5},{5,1},{9,13},{13,9},{2,6},{6,2},{1... | collective-permute-start | bytes 786440 | tf_op jit(solution)/shard_map/cond/branch_1_fun/ppermute | solution.py:212
  95.3 0.7 copy-start.3
